TPU v7x, 32 devices: a whole 2x2x4 slice. The times are simulated.
32 devices in a mesh: rep: 4 (over x, core), fsdp: 8 (over z, y).
Axes of the slice: x: 2, y: 2, z: 4, core: 2. Of those that a mesh axis runs over, the one named last changes fastest.
Arguments:
- hidden_in: bfloat16 [16384, 1024], P(('rep', 'fsdp')), may hold values from -6 to 6
- seg_ids: int32 [16384], P(('rep', 'fsdp')), may hold values from 0 to 127, never falling along the last dimension, each value on 1 to 4096 neighbouring positions
- attn_gain: bfloat16 [1024], P('fsdp'), may hold values from 0.5 to 1.5
- qkv_weight: bfloat16 [1024, 3072], P('fsdp'), may hold values from -0.1875 to 0.1875
- beta_weight: bfloat16 [1024, 8], P('fsdp'), may hold values from -0.1875 to 0.1875
- gate_weight: bfloat16 [1024, 1024], P('fsdp'), may hold values from -0.1875 to 0.1875
- conv_taps: bfloat16 [4, 3072], P(None, 'fsdp'), may hold values from -3 to 3
- out_gain: bfloat16 [128], P('fsdp'), may hold values from 0.5 to 1.5
- out_weight: bfloat16 [1024, 1024], P('fsdp'), may hold values from -0.375 to 0.375
- ffn_gain: bfloat16 [1024], P('fsdp'), may hold values from 0.5 to 1.5
- ffn_gate: bfloat16 [1024, 2816], P('fsdp'), may hold values from -0.1875 to 0.1875
- ffn_up: bfloat16 [1024, 2816], P('fsdp'), may hold values from -0.1875 to 0.1875
- ffn_down: bfloat16 [2816, 1024], P('fsdp'), may hold values from -0.109375 to 0.109375
- cotangent: bfloat16 [16384, 1024], P(('rep', 'fsdp')), may hold values from -6 to 6
Outputs:
- output: bfloat16 [16384, 1024], P(('rep', 'fsdp'))
- input_grad: bfloat16 [16384, 1024], P(('rep', 'fsdp'))
- attngain_grad: float32 [1024], P('fsdp')
- qkv_grad: float32 [1024, 3072], P('fsdp')
- beta_grad: float32 [1024, 8], P('fsdp')
- gate_grad: float32 [1024, 1024], P('fsdp')
- taps_grad: float32 [4, 3072], P(None, 'fsdp')
- outgain_grad: float32 [128], P('fsdp')
- outproj_grad: float32 [1024, 1024], P('fsdp')
- ffngain_grad: float32 [1024], P('fsdp')
- hidgate_grad: float32 [1024, 2816], P('fsdp')
- hidup_grad: float32 [1024, 2816], P('fsdp')
- down_grad: float32 [2816, 1024], P('fsdp')
Inputs may be any that keep to these rules, and one draw needn't show every extreme that they name: `seg_ids`: segment ids never fall along the array; each segment covers 1 to 4096 consecutive positions and one covers exactly 4096.
All inputs are finite; a program needn't handle non-finite values.
Results may differ from a plain program's by a relative error of at most 0.022.
Values may be sent and summed in bfloat16 or wider, within the bound.
No kernel may reach another device: no remote copies, remote signals or barrier semaphores. Data moves between devices by JAX's collectives and lax.ppermute only.
A program may use at most 256 MiB of HBM per device.

v0:
```python
from functools import partial

import jax
import jax.numpy as jnp
from jax import lax
from jax.sharding import PartitionSpec as P

SPAN = 64


EPSILON = 1e-06
HIGH = lax.Precision.HIGHEST


def from_behind(value, axis, steps):
    count = lax.axis_size(axis)
    first, last = (max(0, -steps), min(count, count - steps))
    return lax.ppermute(value, axis, [(source, source + steps) for source in range(first, last)])


def entering(array, axis, combine, identity, reverse):
    peers, index = (lax.axis_size(axis), lax.axis_index(axis))
    everything = jax.tree.map(
        lambda part, kind: lax.all_gather(part.astype(kind), axis),
        array,
        (jnp.bfloat16, jnp.bfloat16),
    )
    start = jax.tree.map(
        lambda part, zero: jnp.broadcast_to(jnp.asarray(zero, part.dtype), part.shape),
        array,
        identity,
    )

    def hop(k, before):
        at = peers - 1 - k if reverse else k
        reached = at > index if reverse else at < index
        new = combine(
            before, jax.tree.map(lambda part, own: part[at].astype(own.dtype), everything, array)
        )
        return jax.tree.map(lambda a, b: jnp.where(reached, a, b), new, before)

    return lax.fori_loop(0, peers, hop, start)


def for_sending(array):
    return jax.tree.map(lambda a: a.astype(jnp.bfloat16) if a.dtype == jnp.float32 else a, array)


def hi_einsum(form, left, right):
    return jnp.einsum(form, left, right, precision=HIGH, preferred_element_type=jnp.float32)


def short_einsum(form, left, right):
    return jnp.einsum(form, left, right, preferred_element_type=jnp.float32)


def snap(values):
    kept = lax.optimization_barrier(values.astype(jnp.bfloat16)).astype(jnp.float32)
    return values + lax.stop_gradient(kept - values)


def contract(left, right, left_dim, right_dim):
    return lax.dot_general(
        left, right, (((left_dim,), (right_dim,)), ((), ())), preferred_element_type=jnp.float32
    )


def rms_norm(values, gain):
    return values * lax.rsqrt(jnp.mean(values * values, axis=-1, keepdims=True) + EPSILON) * gain


def span_core(carried, pieces, plain):
    queries, key_unit, values, rates, starts = pieces
    block_len = starts.shape[-1]
    row_ids = lax.broadcasted_iota(jnp.int32, (block_len, block_len), 0)
    col_ids = lax.broadcasted_iota(jnp.int32, (block_len, block_len), 1)
    causal = (row_ids >= col_ids).astype(jnp.float32)
    strict = (row_ids > col_ids).astype(jnp.float32)
    doc_index = hi_einsum("...s,ts->...t", starts, causal)
    first_doc = (doc_index < 0.5).astype(jnp.float32)
    last_doc = (doc_index > doc_index[..., -1:] - 0.5).astype(jnp.float32)
    same_doc = (jnp.abs(doc_index[..., :, None] - doc_index[..., None, :]) < 0.5).astype(
        jnp.float32
    )
    keep_state = first_doc[..., -1]
    query_heads = jnp.swapaxes(queries, -2, -3)
    key_heads = jnp.swapaxes(key_unit, -2, -3)
    value_heads = jnp.swapaxes(values, -2, -3)
    rate_heads = jnp.swapaxes(rates, -1, -2)[..., None]
    lower = (strict * same_doc)[..., None, :, :]
    if plain:
        key_short = key_heads.astype(jnp.bfloat16)
        mixing = (
            rate_heads
            * jnp.einsum(
                "...td,...sd->...ts", key_short, key_short, preferred_element_type=jnp.float32
            )
            * lower
        )
    else:
        mixing = hi_einsum("...td,...sd->...ts", key_heads * rate_heads, key_heads) * lower
    unit_matrix = jnp.eye(block_len, dtype=jnp.float32)
    inverse = unit_matrix - mixing
    powered = mixing
    for level in range(block_len.bit_length() - 2):
        powered = hi_einsum("...ts,...su->...tu", powered, powered)
        inverse = hi_einsum("...ts,...su->...tu", inverse, unit_matrix + powered)
    key_mix = snap(hi_einsum("...ts,...sd->...td", inverse, key_heads * rate_heads))
    value_mix = snap(hi_einsum("...ts,...sd->...td", inverse, value_heads * rate_heads))
    carried_low = snap(carried)
    head_first = first_doc[..., None, :, None]
    fresh_values = snap(
        value_mix - head_first * short_einsum("...td,...de->...te", key_mix, carried_low)
    )
    carried_next = keep_state[..., None, None, None] * carried + short_einsum(
        "...td,...te->...de", key_heads * last_doc[..., None, :, None], fresh_values
    )
    visible = (causal * same_doc)[..., None, :, :]
    return (
        carried_next,
        (
            fresh_values,
            key_mix,
            query_heads,
            key_heads,
            visible,
            head_first,
            keep_state,
            carried_low,
        ),
    )


def span_step(carried, pieces):
    carried_next, inner = span_core(carried, pieces, False)
    fresh_values, key_mix, query_heads, key_heads, visible, head_first, keep_state, carried_low = (
        inner
    )
    scores = snap(short_einsum("...td,...sd->...ts", query_heads, key_heads) * visible)
    outputs = head_first * short_einsum(
        "...td,...de->...te", query_heads, carried_low
    ) + short_einsum("...ts,...se->...te", scores, fresh_values)
    return (carried_next, jnp.swapaxes(outputs, -2, -3))


def summary_step(carry, pieces):
    carried, transfer = carry
    carried_next, inner = span_core(carried, pieces, True)
    fresh_values, key_mix, query_heads, key_heads, visible, head_first, keep_state, carried_low = (
        inner
    )
    unit_state = jnp.eye(key_heads.shape[-1], dtype=jnp.float32)
    span_transfer = keep_state[..., None, None, None] * (
        unit_state - short_einsum("...td,...te->...de", key_heads, key_mix)
    )
    return ((carried_next, hi_einsum("...de,...ef->...df", span_transfer, transfer)), None)


def to_blocks(array):
    blocks = array.shape[0] // SPAN
    return array.reshape((blocks, SPAN) + array.shape[1:])


def run_rule(queries, key_unit, values, rates, carried, starts):
    row_count, head_count, head_dim = queries.shape
    pieces = (
        to_blocks(queries),
        to_blocks(key_unit),
        to_blocks(values),
        to_blocks(rates),
        to_blocks(starts),
    )
    final_state, outputs = lax.scan(jax.checkpoint(span_step), carried, pieces)
    return (outputs.reshape(row_count, head_count, head_dim), final_state)


def summarize(queries, key_unit, values, rates, starts):
    head_count, head_dim = (queries.shape[1], queries.shape[2])
    zero_state = jnp.zeros((head_count, head_dim, head_dim), jnp.float32)
    unit_stack = jnp.broadcast_to(
        jnp.eye(head_dim, dtype=jnp.float32), (head_count, head_dim, head_dim)
    )
    pieces = (
        to_blocks(queries),
        to_blocks(key_unit),
        to_blocks(values),
        to_blocks(rates),
        to_blocks(starts),
    )
    (local_end, transfer), unused = lax.scan(summary_step, (zero_state, unit_stack), pieces)
    return (transfer, local_end)


def state_adjoint(queries, key_unit, values, rates, starts, heads_grad):
    head_count, head_dim = (queries.shape[1], queries.shape[2])
    zero_state = jnp.zeros((head_count, head_dim, head_dim), jnp.float32)
    pieces = (
        to_blocks(queries),
        to_blocks(key_unit),
        to_blocks(values),
        to_blocks(rates),
        to_blocks(starts),
        to_blocks(heads_grad),
    )

    def adjoint_step(later, block):
        part = block[:5]
        unused, step_back = jax.vjp(partial(span_step, pieces=part), zero_state)
        return (step_back((later, block[5]))[0], None)

    earliest, unused = lax.scan(adjoint_step, zero_state, pieces, reverse=True)
    return earliest


def compose(earlier, later):
    return (
        hi_einsum("hde,hef->hdf", later[0], earlier[0]),
        hi_einsum("hde,hef->hdf", later[0], earlier[1]) + later[1],
    )


def make_features(extended, taps, beta_pre, masks, head_count):
    row_count = extended.shape[0] - 3
    mixed = taps[0] * extended[3:] * masks[0]
    for offset in range(1, 4):
        mixed = mixed + taps[offset] * extended[3 - offset : 3 - offset + row_count] * masks[offset]
    active = jax.nn.silu(mixed)
    model_width = active.shape[1] // 3
    head_dim = model_width // head_count
    queries = (active[:, :model_width] * head_dim ** (-0.5)).reshape(
        row_count, head_count, head_dim
    )
    key_raw = active[:, model_width : 2 * model_width].reshape(row_count, head_count, head_dim)
    key_unit = key_raw * lax.rsqrt(jnp.sum(key_raw * key_raw, axis=-1, keepdims=True) + EPSILON)
    values = active[:, 2 * model_width :].reshape(row_count, head_count, head_dim)
    return (queries, key_unit, values, jax.nn.sigmoid(beta_pre))


def gate_output(attn_heads, gain, gate_pre):
    return rms_norm(attn_heads, gain).reshape(gate_pre.shape) * jax.nn.silu(gate_pre)


def swiglu(up_gate, up_lin):
    return jax.nn.silu(up_gate) * up_lin


def rounded(values):
    return lax.optimization_barrier(values.astype(jnp.bfloat16)).astype(jnp.float32)


def on_device(
    hidden_in,
    seg_ids,
    attn_gain,
    qkv_weight,
    beta_weight,
    gate_weight,
    conv_taps,
    out_gain,
    out_weight,
    ffn_gain,
    ffn_gate,
    ffn_up,
    ffn_down,
    cotangent,
):
    gathered = (
        lax.all_gather(attn_gain, "fsdp", axis=0, tiled=True),
        lax.all_gather(qkv_weight, "fsdp", axis=0, tiled=True),
        lax.all_gather(beta_weight, "fsdp", axis=0, tiled=True),
        lax.all_gather(gate_weight, "fsdp", axis=0, tiled=True),
        lax.all_gather(conv_taps, "fsdp", axis=1, tiled=True),
        lax.all_gather(out_gain, "fsdp", axis=0, tiled=True),
        lax.all_gather(out_weight, "fsdp", axis=0, tiled=True),
        lax.all_gather(ffn_gain, "fsdp", axis=0, tiled=True),
        lax.all_gather(ffn_gate, "fsdp", axis=0, tiled=True),
        lax.all_gather(ffn_up, "fsdp", axis=0, tiled=True),
        lax.all_gather(ffn_down, "fsdp", axis=0, tiled=True),
    )
    (
        attn_full,
        qkv_full,
        beta_full,
        gate_full,
        taps_full,
        outgain_full,
        outw_full,
        ffngain_full,
        hidgate_full,
        hidup_full,
        down_full,
    ) = gathered
    row_count = hidden_in.shape[0]
    head_count = beta_weight.shape[1]
    residual = hidden_in.astype(jnp.float32)
    attn_scale = attn_full.astype(jnp.float32)
    normed = rms_norm(residual, attn_scale)
    normed_low = normed.astype(jnp.bfloat16)
    mixed_pre = jnp.dot(normed_low, qkv_full, preferred_element_type=jnp.float32)
    beta_pre = jnp.dot(normed_low, beta_full, preferred_element_type=jnp.float32)
    gate_pre = jnp.dot(normed_low, gate_full, preferred_element_type=jnp.float32)
    seg_float = (seg_ids + 1).astype(jnp.float32)
    rim_rows, rim_ids = (
        from_behind(mixed_pre[row_count - 3 :].astype(jnp.bfloat16), "fsdp", 1).astype(jnp.float32),
        from_behind(seg_float[row_count - 3 :].astype(jnp.bfloat16), "fsdp", 1).astype(jnp.float32),
    )
    extended = jnp.concatenate([rim_rows, mixed_pre], axis=0)
    ext_ids = jnp.concatenate([rim_ids, seg_float])
    starts = (ext_ids[3:] != ext_ids[2 : row_count + 2]).astype(jnp.float32)
    masks = jnp.stack(
        [
            (ext_ids[3 - offset : 3 - offset + row_count] == ext_ids[3:]).astype(jnp.float32)
            for offset in range(4)
        ]
    )[:, :, None]
    taps_scale = taps_full.astype(jnp.float32)
    features, feature_back = jax.vjp(
        partial(make_features, masks=masks, head_count=head_count), extended, taps_scale, beta_pre
    )
    queries, key_unit, values, rates = features
    query_low = rounded(queries)
    key_low = rounded(key_unit)
    value_low = rounded(values)
    transfer, local_end = summarize(query_low, key_low, value_low, rates, starts)
    head_dim = query_low.shape[2]
    zero_stack = jnp.zeros((head_count, head_dim, head_dim), jnp.float32)
    unit_stack = jnp.broadcast_to(
        jnp.eye(head_dim, dtype=jnp.float32), (head_count, head_dim, head_dim)
    )
    scanned = entering((transfer, local_end), "fsdp", compose, (unit_stack, zero_stack), False)
    carried_in = scanned[1]
    rule_out, rule_back = jax.vjp(
        partial(run_rule, starts=starts), query_low, key_low, value_low, rates, carried_in
    )
    attn_heads = rule_out[0]
    outgain_scale = outgain_full.astype(jnp.float32)
    gated, gated_back = jax.vjp(gate_output, attn_heads, outgain_scale, gate_pre)
    gated_low = gated.astype(jnp.bfloat16)
    middle = residual + jnp.dot(gated_low, outw_full, preferred_element_type=jnp.float32)
    ffngain_scale = ffngain_full.astype(jnp.float32)
    normed_two, norm_two_back = jax.vjp(rms_norm, middle, ffngain_scale)
    normed_two_low = normed_two.astype(jnp.bfloat16)
    up_gate = jnp.dot(normed_two_low, hidgate_full, preferred_element_type=jnp.float32)
    up_lin = jnp.dot(normed_two_low, hidup_full, preferred_element_type=jnp.float32)
    hidden_ff, swiglu_back = jax.vjp(swiglu, up_gate, up_lin)
    hidden_low = hidden_ff.astype(jnp.bfloat16)
    output = (middle + jnp.dot(hidden_low, down_full, preferred_element_type=jnp.float32)).astype(
        jnp.bfloat16
    )
    gathered = (
        lax.all_gather(attn_gain, "fsdp", axis=0, tiled=True),
        lax.all_gather(qkv_weight, "fsdp", axis=0, tiled=True),
        lax.all_gather(beta_weight, "fsdp", axis=0, tiled=True),
        lax.all_gather(gate_weight, "fsdp", axis=0, tiled=True),
        lax.all_gather(conv_taps, "fsdp", axis=1, tiled=True),
        lax.all_gather(out_gain, "fsdp", axis=0, tiled=True),
        lax.all_gather(out_weight, "fsdp", axis=0, tiled=True),
        lax.all_gather(ffn_gain, "fsdp", axis=0, tiled=True),
        lax.all_gather(ffn_gate, "fsdp", axis=0, tiled=True),
        lax.all_gather(ffn_up, "fsdp", axis=0, tiled=True),
        lax.all_gather(ffn_down, "fsdp", axis=0, tiled=True),
    )
    (
        attn_full,
        qkv_full,
        beta_full,
        gate_full,
        taps_full,
        outgain_full,
        outw_full,
        ffngain_full,
        hidgate_full,
        hidup_full,
        down_full,
    ) = gathered
    top_grad = cotangent.astype(jnp.float32)
    down_grad = contract(hidden_low, cotangent, 0, 0)
    hidden_grad = contract(cotangent, down_full, 1, 1)
    upgate_grad, uplin_grad = swiglu_back(hidden_grad)
    upgate_low = upgate_grad.astype(jnp.bfloat16)
    uplin_low = uplin_grad.astype(jnp.bfloat16)
    hidgate_grad = contract(normed_two_low, upgate_low, 0, 0)
    hidup_grad = contract(normed_two_low, uplin_low, 0, 0)
    normed_two_grad = contract(upgate_low, hidgate_full, 1, 1) + contract(
        uplin_low, hidup_full, 1, 1
    )
    middle_back, ffngain_grad = norm_two_back(normed_two_grad)
    middle_grad = top_grad + middle_back
    middle_low = middle_grad.astype(jnp.bfloat16)
    outproj_grad = contract(gated_low, middle_low, 0, 0)
    gated_grad = contract(middle_low, outw_full, 1, 1)
    heads_grad, outgain_grad, gatepre_grad = gated_back(gated_grad)
    local_state_grad = state_adjoint(query_low, key_low, value_low, rates, starts, heads_grad)
    later_grad = entering(
        (jnp.swapaxes(transfer, 1, 2), local_state_grad),
        "fsdp",
        compose,
        (unit_stack, zero_stack),
        True,
    )[1]
    query_grad, key_grad, value_grad, rate_grad, state_grad = rule_back((heads_grad, later_grad))
    ext_grad, taps_grad, betapre_grad = feature_back((query_grad, key_grad, value_grad, rate_grad))
    rim_grad = from_behind(for_sending(ext_grad[:3]), "fsdp", -1)
    mixed_grad = ext_grad[3:] + jnp.pad(rim_grad, ((row_count - 3, 0), (0, 0)))
    mixed_low = mixed_grad.astype(jnp.bfloat16)
    betapre_low = betapre_grad.astype(jnp.bfloat16)
    gatepre_low = gatepre_grad.astype(jnp.bfloat16)
    qkv_grad = contract(normed_low, mixed_low, 0, 0)
    beta_grad = contract(normed_low, betapre_low, 0, 0)
    gate_grad = contract(normed_low, gatepre_low, 0, 0)
    normed_grad = (
        contract(mixed_low, qkv_full, 1, 1)
        + contract(betapre_low, beta_full, 1, 1)
        + contract(gatepre_low, gate_full, 1, 1)
    )
    input_back, attngain_grad = jax.vjp(rms_norm, residual, attn_scale)[1](normed_grad)
    input_grad = (middle_grad + input_back).astype(jnp.bfloat16)
    shares = (
        lax.psum_scatter(
            attngain_grad.astype(jnp.bfloat16), "fsdp", scatter_dimension=0, tiled=True
        ).astype(jnp.float32),
        lax.psum_scatter(
            qkv_grad.astype(jnp.bfloat16), "fsdp", scatter_dimension=0, tiled=True
        ).astype(jnp.float32),
        lax.psum_scatter(
            beta_grad.astype(jnp.bfloat16), "fsdp", scatter_dimension=0, tiled=True
        ).astype(jnp.float32),
        lax.psum_scatter(
            gate_grad.astype(jnp.bfloat16), "fsdp", scatter_dimension=0, tiled=True
        ).astype(jnp.float32),
        lax.psum_scatter(
            taps_grad.astype(jnp.bfloat16), "fsdp", scatter_dimension=1, tiled=True
        ).astype(jnp.float32),
        lax.psum_scatter(
            outgain_grad.astype(jnp.bfloat16), "fsdp", scatter_dimension=0, tiled=True
        ).astype(jnp.float32),
        lax.psum_scatter(
            outproj_grad.astype(jnp.bfloat16), "fsdp", scatter_dimension=0, tiled=True
        ).astype(jnp.float32),
        lax.psum_scatter(
            ffngain_grad.astype(jnp.bfloat16), "fsdp", scatter_dimension=0, tiled=True
        ).astype(jnp.float32),
        lax.psum_scatter(
            hidgate_grad.astype(jnp.bfloat16), "fsdp", scatter_dimension=0, tiled=True
        ).astype(jnp.float32),
        lax.psum_scatter(
            hidup_grad.astype(jnp.bfloat16), "fsdp", scatter_dimension=0, tiled=True
        ).astype(jnp.float32),
        lax.psum_scatter(
            down_grad.astype(jnp.bfloat16), "fsdp", scatter_dimension=0, tiled=True
        ).astype(jnp.float32),
    )
    totals = (
        lax.psum(shares[0].astype(jnp.bfloat16), "rep").astype(jnp.float32),
        lax.psum(shares[1].astype(jnp.bfloat16), "rep").astype(jnp.float32),
        lax.psum(shares[2].astype(jnp.bfloat16), "rep").astype(jnp.float32),
        lax.psum(shares[3].astype(jnp.bfloat16), "rep").astype(jnp.float32),
        lax.psum(shares[4].astype(jnp.bfloat16), "rep").astype(jnp.float32),
        lax.psum(shares[5].astype(jnp.bfloat16), "rep").astype(jnp.float32),
        lax.psum(shares[6].astype(jnp.bfloat16), "rep").astype(jnp.float32),
        lax.psum(shares[7].astype(jnp.bfloat16), "rep").astype(jnp.float32),
        lax.psum(shares[8].astype(jnp.bfloat16), "rep").astype(jnp.float32),
        lax.psum(shares[9].astype(jnp.bfloat16), "rep").astype(jnp.float32),
        lax.psum(shares[10].astype(jnp.bfloat16), "rep").astype(jnp.float32),
    )
    return (
        output,
        input_grad,
        totals[0],
        totals[1],
        totals[2],
        totals[3],
        totals[4],
        totals[5],
        totals[6],
        totals[7],
        totals[8],
        totals[9],
        totals[10],
    )


def solution(mesh):
    placed = (
        P(("rep", "fsdp"), None),
        P(("rep", "fsdp")),
        P("fsdp"),
        P("fsdp", None),
        P("fsdp", None),
        P("fsdp", None),
        P(None, "fsdp"),
        P("fsdp"),
        P("fsdp", None),
        P("fsdp"),
        P("fsdp", None),
        P("fsdp", None),
        P("fsdp", None),
        P(("rep", "fsdp"), None),
    )
    return jax.shard_map(
        on_device,
        mesh=mesh,
        in_specs=placed,
        out_specs=(
            P(("rep", "fsdp"), None),
            P(("rep", "fsdp"), None),
            P("fsdp"),
            P("fsdp", None),
            P("fsdp", None),
            P("fsdp", None),
            P(None, "fsdp"),
            P("fsdp"),
            P("fsdp", None),
            P("fsdp"),
            P("fsdp", None),
            P("fsdp", None),
            P("fsdp", None),
        ),
        check_vma=False,
    )
```

profile of v0, /device:TPU:0, one launch (start us, length us, event | category | flops | bytes accessed | tf_op | source)
XLA Modules:
  0.0 1784.4 jit_solution(14377535095292283457)
XLA Ops:
  8.7 4.9 collective-permute-start
  13.6 18.9 %all-gather.4 = bf16[8,1,128]{2,1,0:T(2,128)(2,1)S(1)} all-gather(bf16[1,1,128]{2,1,0:T(2,128)(2,1)} %bitcast.1015), channel_id=1, replica_groups=mesh['rep'=4,'fsdp'=8] {'fsdp'}, dimensions={0}, use_global_device_ids=true | all-gather | bytes 2304 | tf_op jit(solution)/shard_map/all_gather | solution.py:268
  32.5 26.6 %all_gather.67 = bf16[1024,8]{0,1:T(8,128)(2,1)S(1)} all-gather(bf16[128,8]{0,1:T(8,128)(2,1)} %param.30), channel_id=1, replica_groups=mesh['rep'=4,'fsdp'=8] {'fsdp'}, dimensions={0}, use_global_device_ids=true | all-gather | bytes 18432 | tf_op jit(solution)/shard_map/all_gather | solution.py:270
  63.6 30.7 %all_gather.64 = bf16[4,3072]{1,0:T(4,128)(2,1)S(1)} all-gather(bf16[4,384]{1,0:T(4,128)(2,1)S(1)} %copy-done.81), channel_id=1, replica_groups=mesh['rep'=4,'fsdp'=8] {'fsdp'}, dimensions={1}, use_global_device_ids=true | all-gather | bytes 27648 | tf_op jit(solution)/shard_map/all_gather | solution.py:272
  94.6 18.1 %all-gather.17.cloned.1.call-done = bf16[1024,3072]{1,0:T(8,128)(2,1)} async-done(((bf16[128,3072]{1,0:T(8,128)(2,1)}), bf16[1024,3072]{1,0:T(8,128)(2,1)}) %all-gather.17.cloned.1.call-update) | async-done | bytes 6291472 | tf_op jit(solution)/shard_map/all_gather | solution.py:269
  112.7 5.7 fusion.299
  118.5 2.6 copy-done.18
  121.0 2.6 collective-permute-start.1
  125.0 15.6 fusion.253
  150.2 113.6 %while.103 = (s32[]{:T(128)}, f32[8,128,128]{2,1,0:T(8,128)S(1)}, f32[8,128,128]{2,1,0:T(8,128)S(1)}, f32[8,64]{1,0:T(8,128)}, f32[8,64,8,128]{3,1,2,0:T(8,128)S...) while((s32[]{:T(128)}, f32[8,128,128]{2,1,0:T(8,128)S(1)}, ...), condition=%wide.region_3.4_spmd.clone, body=%wide.region_2.3_spmd.clone.sunk | while | flops 615371008 | bytes 13665965 | solution.py:190
  270.3 20.5 %all-reduce.12 = bf16[128]{0:T(256)(128)(2,1)S(1)} all-reduce(bf16[128]{0:T(256)(128)(2,1)S(1)} %dynamic-update-slice), channel_id=1, replica_groups=mesh['rep'=4,'fsdp'=8] {'fsdp'}, use_global_device_ids=true, to_apply=%add.12 | all-reduce | flops 128 | bytes 512
  290.8 16.3 all-gather.5
  310.8 4.2 all-gather.29.cloned.1.call-done
  315.0 50.5 %all-gather.31.cloned.1.call-done = bf16[64,128,128]{2,1,0:T(8,128)(2,1)} async-done(((bf16[8,128,128]{2,1,0:T(8,128)(2,1)}), bf16[64,128,128]{2,1,0:T(8,128)(2,1)}) %all-gather.31.cloned.1.call-update) | async-done | bytes 2097168 | tf_op jit(solution)/shard_map/all_gather | solution.py:24
  365.5 12.6 while.104
  379.8 122.0 %while.102 = (s32[]{:T(128)}, f32[8,128,128]{2,1,0:T(8,128)S(1)}, f32[8,64,8,128]{3,1,2,0:T(8,128)}, f32[8,8,128,128]{3,2,1,0:T(8,128)}, f32[8,64]{1,0:T(8,128)}...) while((s32[]{:T(128)}, f32[8,128,128]{2,1,0:T(8,128)S(1)}, ...), condition=%wide.region_7.8_spmd.clone.clone, body=%wide.region_6.7_spmd.clone.clone.sunk | while | flops 472944896 | bytes 14112157 | solution.py:173
  501.8 2.4 multiply_reduce_fusion.10
  504.2 2.5 copy.246
  508.9 5.7 multiply_convert_fusion.3
  514.6 3.3 multiply_reduce_fusion.9
  519.4 39.2 %all-gather.23.cloned.1.call-done = bf16[1024,2816]{1,0:T(8,128)(2,1)} async-done(((bf16[128,2816]{1,0:T(8,128)(2,1)}), bf16[1024,2816]{1,0:T(8,128)(2,1)}) %all-gather.23.cloned.1.call-update) | async-done | bytes 5767184 | tf_op jit(solution)/shard_map/all_gather | solution.py:276
  558.6 7.7 fusion.359
  566.3 85.4 %all-gather.25.cloned.1.call-done = bf16[1024,2816]{1,0:T(8,128)(2,1)} async-done(((bf16[128,2816]{1,0:T(8,128)(2,1)}), bf16[1024,2816]{1,0:T(8,128)(2,1)}) %all-gather.25.cloned.1.call-update) | async-done | bytes 5767184 | tf_op jit(solution)/shard_map/all_gather | solution.py:277
  651.6 7.6 fusion.360
  659.2 85.5 %all-gather.27.cloned.1.call-done = bf16[2816,1024]{1,0:T(8,128)(2,1)} async-done(((bf16[352,1024]{1,0:T(8,128)(2,1)}), bf16[2816,1024]{1,0:T(8,128)(2,1)}) %all-gather.27.cloned.1.call-update) | async-done | bytes 5767184 | tf_op jit(solution)/shard_map/all_gather | solution.py:278
  744.7 11.2 multiply_convert_fusion
  755.9 7.3 fusion.361
  763.3 4.0 multiply_reduce_fusion.4
  771.0 4.0 multiply_reduce_fusion.5
  777.4 2.3 add_add_fusion.3
  779.7 133.8 %while.105 = (s32[]{:T(128)}, f32[8,128,128]{2,1,0:T(8,128)}, bf16[8,64,8,128]{3,1,2,0:T(8,128)(2,1)}, f32[8,64]{1,0:T(8,128)}, f32[8,64,8,128]{3,1,2,0:T(8,128)...) while((s32[]{:T(128)}, f32[8,128,128]{2,1,0:T(8,128)}, ...), condition=%wide.region_13.14_spmd.clone, body=%wide.region_12.13_spmd.clone.sunk | while | flops 421363968 | bytes 11095223 | solution.py:211
  794.6 2.2 convolution_add_fusion.69
  844.6 2.2 convolution_add_fusion.69
  861.3 2.2 convolution_add_fusion.69
  878.0 2.2 convolution_add_fusion.69
  894.6 2.2 convolution_add_fusion.69
  911.3 2.2 convolution_add_fusion.69
  915.4 4.6 convolution_convert_fusion.4
  921.2 4.0 convolution_convert_fusion.5
  926.4 6.9 convolution_convert_fusion.2
  933.3 6.9 convolution_convert_fusion.1
  940.3 7.7 convolution_convert_fusion
  948.1 14.9 all-gather.35.cloned.1.call-done
  963.0 12.7 while.106
  980.9 325.7 %while.101 = (s32[]{:T(128)}, f32[8,128,128]{2,1,0:T(8,128)S(1)}, f32[8,64,8,128]{3,1,2,0:T(8,128)}, f32[8,64,8,128]{3,2,1,0:T(8,128)}, f32[8,64,8,128]{3,2,1,0:...) while((s32[]{:T(128)}, f32[8,128,128]{2,1,0:T(8,128)S(1)}, ...), condition=%wide.region_20.21_spmd, body=%wide.region_16.20_spmd.sunk | while | flops 1373404928 | bytes 52687284 | solution.py:173
  1306.6 3.0 multiply_reduce_fusion.6
  1314.7 3.8 add_add_fusion.2
  1318.7 7.5 multiply_reduce_fusion.3
  1326.2 5.9 multiply_multiply_fusion.3
  1332.1 6.3 pad_add_fusion
  1339.7 4.9 collective-permute-done.2
  1344.7 5.8 convolution_convert_fusion.3
  1351.9 4.7 fusion.363
  1356.6 6.8 add_convert_fusion
  1368.1 74.3 %reduce-scatter.23.cloned.1.call-done = bf16[352,1024]{1,0:T(8,128)(2,1)} async-done(((bf16[2816,1024]{1,0:T(8,128)(2,1)}), bf16[352,1024]{1,0:T(8,128)(2,1)}) %reduce-scatter.23.cloned.1.call-update) | async-done | bytes 720912 | tf_op jit(solution)/shard_map/reduce_scatter | solution.py:449
  1442.4 121.3 %reduce-scatter.13.cloned.1.call-done = bf16[128,3072]{1,0:T(8,128)(2,1)} async-done(((bf16[1024,3072]{1,0:T(8,128)(2,1)}), bf16[128,3072]{1,0:T(8,128)(2,1)}) %reduce-scatter.13.cloned.1.call-update) | async-done | bytes 786448 | tf_op jit(solution)/shard_map/reduce_scatter | solution.py:422
  1563.7 11.1 fusion.261
  1574.9 19.8 %all-reduce.16 = (bf16[1024]{0:T(1024)(128)(2,1)S(1)}, bf16[128]{0:T(256)(128)(2,1)S(1)}, bf16[1024]{0:T(1024)(128)(2,1)S(1)}) all-reduce(bf16[1024]{0:T(1024)(128)(2,1)S(1)} %get-tuple-element.1324, bf16[128]{0:T(256)(128)(2,1)S(1)} %bitcast_reduce_fusion, ...), channel_id=6, replica_groups=mesh['rep'=4,'fsdp'=8] {'fsdp'}, use_global_device_ids=true, to_apply=%region_24.25.clone | all-reduce | flops 2176 | bytes 8704
  1595.0 3.1 fusion.267
  1598.1 29.7 %reduce-scatter.25.cloned.1.call-done = bf16[128,8]{1,0:T(8,128)(2,1)} async-done(((bf16[1024,8]{1,0:T(8,128)(2,1)}), bf16[128,8]{1,0:T(8,128)(2,1)}) %reduce-scatter.25.cloned.1.call-update) | async-done | bytes 2064
  1628.6 64.4 %reduce-scatter.27.cloned.1.call-done = bf16[384,4]{1,0:T(8,128)(2,1)} async-done(((bf16[3072,4]{1,0:T(8,128)(2,1)}), bf16[384,4]{1,0:T(8,128)(2,1)}) %reduce-scatter.27.cloned.1.call-update) | async-done | bytes 3088
  1694.0 5.8 all-reduce.17
  1702.5 67.2 %all-reduce.21.cloned.1.call-done = (bf16[128,3072]{1,0:T(8,128)(2,1)}, bf16[128,1024]{1,0:T(8,128)(2,1)}, bf16[128,1024]{1,0:T(8,128)(2,1)}, bf16[128,2816]{1,0...) async-done(((bf16[128,3072]{1,0:T(8,128)(2,1)}, bf16[128,1024]{1,0:T(8,128)(2,1)}, bf16[128,1024]{1,0:T(8,128)(2,1)}, bf16[128,2816]{1,0:T(8,128)(2,1)}, ...) | async-done | bytes 3473424 | tf_op jit(solution)/shard_map/psum | solution.py:455
  1769.7 2.5 convert_element_type.758
  (1761 shorter events, 744.8 us)
Async XLA Ops:
  7.2 56.5 %copy-start.81 = (bf16[4,384]{1,0:T(4,128)(2,1)S(1)}, bf16[4,384]{1,0:T(4,128)(2,1)}, u32[]{:S(2)}) copy-start(bf16[4,384]{1,0:T(4,128)(2,1)} %param.32) | copy-start | bytes 9220
  7.2 105.5 %copy-start.31 = (bf16[512,1024]{1,0:T(8,128)(2,1)S(1)}, bf16[512,1024]{1,0:T(8,128)(2,1)}, u32[]{:S(2)}) copy-start(bf16[512,1024]{1,0:T(8,128)(2,1)} %param.26) | copy-start | bytes 3145732
  7.2 105.5 %all-gather.17.cloned.1.call-start = ((), (), s32[]{:S(2)}) async-start(), calls=%async_computation.8 | async-start | bytes 7077888 | tf_op jit(solution)/shard_map/all_gather | solution.py:269
  7.9 307.1 %all-gather.29.cloned.1.call-start = ((), (), s32[]{:S(2)}) async-start(), calls=%async_computation.20 | async-start | bytes 2359296 | tf_op jit(solution)/shard_map/all_gather | solution.py:24
  8.7 85.7 %collective-permute-start = (bf16[3]{0:T(256)(128)(2,1)S(1)}, bf16[3]{0:T(256)(128)(2,1)S(1)}, u32[]{:S(2)}, u32[]{:S(2)}) collective-permute-start(bf16[3]{0:T(256)(128)(2,1)S(1)} %slice.126), channel_id=1, source_target_pairs={{0,1},{1,2},{2,3},{3,4},{4,5},{5,6},{6,7},{8,9},{9,10},{10,11},{11... | collective-permute-start | bytes 26 | tf_op jit(solution)/shard_map/ppermute | solution.py:18
  32.5 887.5 %copy-start.75 = (f32[8,1,128]{2,1,0:T(1,128)}, f32[8,1,128]{2,1,0:T(1,128)S(1)}, u32[]{:S(2)}) copy-start(f32[8,1,128]{2,1,0:T(1,128)S(1)} %convert_element_type.791) | copy-start | bytes 12292
  60.7 859.4 %copy-start.77 = (f32[512]{0:T(512)}, f32[512]{0:T(512)S(1)}, u32[]{:S(2)}) copy-start(f32[512]{0:T(512)S(1)} %fusion.288) | copy-start | bytes 6148
  62.9 55.5 %copy-start.63 = (f32[512,8]{0,1:T(8,128)}, f32[512,8]{0,1:T(8,128)S(1)}, u32[]{:S(2)}) copy-start(f32[512,8]{0,1:T(8,128)S(1)} %fusion.274) | copy-start | bytes 49156
  94.4 30.6 %copy-start.53 = (f32[1,3072]{1,0:T(1,128)}, f32[1,3072]{1,0:T(1,128)S(1)}, u32[]{:S(2)}) copy-start(f32[1,3072]{1,0:T(1,128)S(1)} %get-tuple-element.1492) | copy-start | bytes 36868
  94.4 30.6 %copy-start.55 = (f32[1,3072]{1,0:T(1,128)}, f32[1,3072]{1,0:T(1,128)S(1)}, u32[]{:S(2)}) copy-start(f32[1,3072]{1,0:T(1,128)S(1)} %get-tuple-element.1493) | copy-start | bytes 36868
  94.4 30.6 %copy-start.57 = (f32[1,3072]{1,0:T(1,128)}, f32[1,3072]{1,0:T(1,128)S(1)}, u32[]{:S(2)}) copy-start(f32[1,3072]{1,0:T(1,128)S(1)} %get-tuple-element.1494) | copy-start | bytes 36868
  94.5 30.6 %copy-start.59 = (f32[1,3072]{1,0:T(1,128)}, f32[1,3072]{1,0:T(1,128)S(1)}, u32[]{:S(2)}) copy-start(f32[1,3072]{1,0:T(1,128)S(1)} %get-tuple-element.1495) | copy-start | bytes 36868
  94.6 29.1 %copy-start.79 = (s32[512]{0:T(512)S(1)}, s32[512]{0:T(512)}, u32[]{:S(2)}) copy-start(s32[512]{0:T(512)} %param.27) | copy-start | bytes 6148
  121.0 3.9 collective-permute-start.1
  123.7 16.9 copy-start.65
  123.7 16.9 copy-start.67
  123.7 16.9 copy-start.69
  123.7 16.9 copy-start.71
  125.0 15.7 copy-start.46
  264.6 26.2 %copy-start.84 = (bf16[128]{0:T(256)(128)(2,1)S(1)}, bf16[128]{0:T(256)(128)(2,1)}, u32[]{:S(2)}) copy-start(bf16[128]{0:T(256)(128)(2,1)} %param.35) | copy-start | bytes 772
  264.6 100.9 %all-gather.31.cloned.1.call-start = ((), (), s32[]{:S(2)}) async-start(), calls=%async_computation.21 | async-start | bytes 2359296 | tf_op jit(solution)/shard_map/all_gather | solution.py:24
  265.4 241.5 %all-gather.19.cloned.1.call-start = ((), (), s32[]{:S(2)}) async-start(), calls=%async_computation.9 | async-start | bytes 2359296 | tf_op jit(solution)/shard_map/all_gather | solution.py:271
  266.0 248.6 %all-gather.21.cloned.1.call-start = ((), (), s32[]{:S(2)}) async-start(), calls=%async_computation.10 | async-start | bytes 2359296 | tf_op jit(solution)/shard_map/all_gather | solution.py:274
  266.6 292.0 %all-gather.23.cloned.1.call-start = ((), (), s32[]{:S(2)}) async-start(), calls=%async_computation.11 | async-start | bytes 6488064 | tf_op jit(solution)/shard_map/all_gather | solution.py:276
  267.2 384.5 %all-gather.25.cloned.1.call-start = ((), (), s32[]{:S(2)}) async-start(), calls=%async_computation.12 | async-start | bytes 6488064 | tf_op jit(solution)/shard_map/all_gather | solution.py:277
  267.9 476.7 %all-gather.27.cloned.1.call-start = ((), (), s32[]{:S(2)}) async-start(), calls=%async_computation.13 | async-start | bytes 6488064 | tf_op jit(solution)/shard_map/all_gather | solution.py:278
  268.7 679.4 %all-gather.33.cloned.1.call-start = ((), (), s32[]{:S(2)}) async-start(), calls=%async_computation.22 | async-start | bytes 2359296 | tf_op jit(solution)/shard_map/all_gather | solution.py:24
  310.8 652.2 %all-gather.35.cloned.1.call-start = ((), (), s32[]{:S(2)}) async-start(), calls=%async_computation.23 | async-start | bytes 2359296 | tf_op jit(solution)/shard_map/all_gather | solution.py:24
  519.4 132.2 %copy-start.40 = (bf16[512,1024]{1,0:T(8,128)(2,1)}, bf16[512,1024]{1,0:T(8,128)(2,1)S(1)}, u32[]{:S(2)}) copy-start(bf16[512,1024]{1,0:T(8,128)(2,1)S(1)} %multiply_convert_fusion.2) | copy-start | bytes 3145732
  915.3 452.8 %reduce-scatter.17.cloned.1.call-start = ((), (), s32[]{:S(2)}) async-start(), calls=%async_computation.16 | async-start | bytes 2359296 | tf_op jit(solution)/shard_map/reduce_scatter | solution.py:437
  920.0 448.1 %reduce-scatter.15.cloned.1.call-start = ((), (), s32[]{:S(2)}) async-start(), calls=%async_computation.15 | async-start | bytes 2359296 | tf_op jit(solution)/shard_map/reduce_scatter | solution.py:428
  925.2 442.9 %reduce-scatter.19.cloned.1.call-start = ((), (), s32[]{:S(2)}) async-start(), calls=%async_computation.17 | async-start | bytes 6488064 | tf_op jit(solution)/shard_map/reduce_scatter | solution.py:443
  933.3 434.8 %reduce-scatter.21.cloned.1.call-start = ((), (), s32[]{:S(2)}) async-start(), calls=%async_computation.18 | async-start | bytes 6488064 | tf_op jit(solution)/shard_map/reduce_scatter | solution.py:446
  940.2 502.2 %reduce-scatter.23.cloned.1.call-start = ((), (), s32[]{:S(2)}) async-start(), calls=%async_computation.19 | async-start | bytes 6488064 | tf_op jit(solution)/shard_map/reduce_scatter | solution.py:449
  948.0 615.7 %reduce-scatter.13.cloned.1.call-start = ((), (), s32[]{:S(2)}) async-start(), calls=%async_computation.14 | async-start | bytes 7077888 | tf_op jit(solution)/shard_map/reduce_scatter | solution.py:422
  983.2 25.7 %copy-start.7 = (f32[64,8,128]{2,0,1:T(8,128)}, f32[64,8,128]{2,0,1:T(8,128)S(1)}, u32[]{:S(2)}) copy-start(f32[64,8,128]{2,0,1:T(8,128)S(1)} %dynamic-slice_bitcast_fusion.21) | copy-start | bytes 786436 | tf_op jit(solution)/shard_map/transpose(jvp())/while
  989.3 19.6 %copy-start.2 = (f32[8,64,128]{2,1,0:T(8,128)}, f32[8,64,128]{2,1,0:T(8,128)S(1)}, u32[]{:S(2)}) copy-start(f32[8,64,128]{2,1,0:T(8,128)S(1)} %convolution_add_fusion.50) | copy-start | bytes 786436 | tf_op jit(solution)/shard_map/transpose(jvp())/while
  1023.8 25.7 %copy-start.7 = (f32[64,8,128]{2,0,1:T(8,128)}, f32[64,8,128]{2,0,1:T(8,128)S(1)}, u32[]{:S(2)}) copy-start(f32[64,8,128]{2,0,1:T(8,128)S(1)} %dynamic-slice_bitcast_fusion.21) | copy-start | bytes 786436 | tf_op jit(solution)/shard_map/transpose(jvp())/while
  1029.9 19.6 %copy-start.2 = (f32[8,64,128]{2,1,0:T(8,128)}, f32[8,64,128]{2,1,0:T(8,128)S(1)}, u32[]{:S(2)}) copy-start(f32[8,64,128]{2,1,0:T(8,128)S(1)} %convolution_add_fusion.50) | copy-start | bytes 786436 | tf_op jit(solution)/shard_map/transpose(jvp())/while
  1064.4 25.7 %copy-start.7 = (f32[64,8,128]{2,0,1:T(8,128)}, f32[64,8,128]{2,0,1:T(8,128)S(1)}, u32[]{:S(2)}) copy-start(f32[64,8,128]{2,0,1:T(8,128)S(1)} %dynamic-slice_bitcast_fusion.21) | copy-start | bytes 786436 | tf_op jit(solution)/shard_map/transpose(jvp())/while
  1070.5 19.6 %copy-start.2 = (f32[8,64,128]{2,1,0:T(8,128)}, f32[8,64,128]{2,1,0:T(8,128)S(1)}, u32[]{:S(2)}) copy-start(f32[8,64,128]{2,1,0:T(8,128)S(1)} %convolution_add_fusion.50) | copy-start | bytes 786436 | tf_op jit(solution)/shard_map/transpose(jvp())/while
  1105.1 25.7 %copy-start.7 = (f32[64,8,128]{2,0,1:T(8,128)}, f32[64,8,128]{2,0,1:T(8,128)S(1)}, u32[]{:S(2)}) copy-start(f32[64,8,128]{2,0,1:T(8,128)S(1)} %dynamic-slice_bitcast_fusion.21) | copy-start | bytes 786436 | tf_op jit(solution)/shard_map/transpose(jvp())/while
  1111.1 19.6 %copy-start.2 = (f32[8,64,128]{2,1,0:T(8,128)}, f32[8,64,128]{2,1,0:T(8,128)S(1)}, u32[]{:S(2)}) copy-start(f32[8,64,128]{2,1,0:T(8,128)S(1)} %convolution_add_fusion.50) | copy-start | bytes 786436 | tf_op jit(solution)/shard_map/transpose(jvp())/while
  1145.7 25.7 %copy-start.7 = (f32[64,8,128]{2,0,1:T(8,128)}, f32[64,8,128]{2,0,1:T(8,128)S(1)}, u32[]{:S(2)}) copy-start(f32[64,8,128]{2,0,1:T(8,128)S(1)} %dynamic-slice_bitcast_fusion.21) | copy-start | bytes 786436 | tf_op jit(solution)/shard_map/transpose(jvp())/while
  1151.8 19.6 %copy-start.2 = (f32[8,64,128]{2,1,0:T(8,128)}, f32[8,64,128]{2,1,0:T(8,128)S(1)}, u32[]{:S(2)}) copy-start(f32[8,64,128]{2,1,0:T(8,128)S(1)} %convolution_add_fusion.50) | copy-start | bytes 786436 | tf_op jit(solution)/shard_map/transpose(jvp())/while
  1186.3 25.7 %copy-start.7 = (f32[64,8,128]{2,0,1:T(8,128)}, f32[64,8,128]{2,0,1:T(8,128)S(1)}, u32[]{:S(2)}) copy-start(f32[64,8,128]{2,0,1:T(8,128)S(1)} %dynamic-slice_bitcast_fusion.21) | copy-start | bytes 786436 | tf_op jit(solution)/shard_map/transpose(jvp())/while
  1192.4 19.6 %copy-start.2 = (f32[8,64,128]{2,1,0:T(8,128)}, f32[8,64,128]{2,1,0:T(8,128)S(1)}, u32[]{:S(2)}) copy-start(f32[8,64,128]{2,1,0:T(8,128)S(1)} %convolution_add_fusion.50) | copy-start | bytes 786436 | tf_op jit(solution)/shard_map/transpose(jvp())/while
  1227.0 25.7 %copy-start.7 = (f32[64,8,128]{2,0,1:T(8,128)}, f32[64,8,128]{2,0,1:T(8,128)S(1)}, u32[]{:S(2)}) copy-start(f32[64,8,128]{2,0,1:T(8,128)S(1)} %dynamic-slice_bitcast_fusion.21) | copy-start | bytes 786436 | tf_op jit(solution)/shard_map/transpose(jvp())/while
  1233.1 19.6 %copy-start.2 = (f32[8,64,128]{2,1,0:T(8,128)}, f32[8,64,128]{2,1,0:T(8,128)S(1)}, u32[]{:S(2)}) copy-start(f32[8,64,128]{2,1,0:T(8,128)S(1)} %convolution_add_fusion.50) | copy-start | bytes 786436 | tf_op jit(solution)/shard_map/transpose(jvp())/while
  1267.7 25.7 %copy-start.7 = (f32[64,8,128]{2,0,1:T(8,128)}, f32[64,8,128]{2,0,1:T(8,128)S(1)}, u32[]{:S(2)}) copy-start(f32[64,8,128]{2,0,1:T(8,128)S(1)} %dynamic-slice_bitcast_fusion.21) | copy-start | bytes 786436 | tf_op jit(solution)/shard_map/transpose(jvp())/while
  1273.8 19.6 %copy-start.2 = (f32[8,64,128]{2,1,0:T(8,128)}, f32[8,64,128]{2,1,0:T(8,128)S(1)}, u32[]{:S(2)}) copy-start(f32[8,64,128]{2,1,0:T(8,128)S(1)} %convolution_add_fusion.50) | copy-start | bytes 786436 | tf_op jit(solution)/shard_map/transpose(jvp())/while
  1309.9 8.6 slice-start.2
  1318.6 7.6 copy-start.54
  1318.6 7.6 copy-start.56
  1332.1 12.5 copy-start.34
  1332.1 12.5 copy-start.76
  1332.1 12.6 copy-start.78
  1338.4 6.2 collective-permute-start.2
  1350.5 277.3 %reduce-scatter.25.cloned.1.call-start = ((), (), s32[]{:S(2)}) async-start(), calls=%async_computation.24 | async-start | bytes 294912
  1364.9 328.2 %reduce-scatter.27.cloned.1.call-start = ((), (), s32[]{:S(2)}) async-start(), calls=%async_computation.25 | async-start | bytes 884736
  1366.2 403.5 %all-reduce.21.cloned.1.call-start = ((), (), s32[]{:S(2)}) async-start(), calls=%async_computation.26 | async-start | bytes 6946816 | tf_op jit(solution)/shard_map/psum | solution.py:455
  1563.7 11.2 copy-start.83
  1563.7 31.2 %copy-start.74 = (f32[512]{0:T(512)S(1)}, f32[512]{0:T(512)}, u32[]{:S(2)}) copy-start(f32[512]{0:T(512)} %copy-done.73) | copy-start | bytes 6148
  1563.7 31.2 %copy-start.22 = (f32[512,1024]{1,0:T(8,128)S(1)}, f32[512,1024]{1,0:T(8,128)}, u32[]{:S(2)}) copy-start(f32[512,1024]{1,0:T(8,128)} %copy-done.21) | copy-start | bytes 6291460
  (166 other events, 494.9 us)
Sparse Core Ops, SparseCore 0:
  10.2 102.4 all-gather.16
  264.7 50.2 all-gather.28
  317.7 47.7 all-gather.30
  367.5 47.9 all-gather.18
  417.5 47.7 all-gather.20
  467.3 91.2 all-gather.22
  560.8 90.8 all-gather.24
  653.8 90.8 all-gather.26
  747.4 47.4 all-gather.32
  915.4 47.4 all-gather.34
  966.5 66.4 reduce-scatter.16
  1036.4 66.6 reduce-scatter.14
  1106.8 109.0 reduce-scatter.18
  1219.3 110.5 reduce-scatter.20
  1333.4 109.0 reduce-scatter.22
  1445.8 117.7 reduce-scatter.12
  1567.4 60.3 reduce-scatter.24
  1631.6 61.4 reduce-scatter.26
  1696.0 73.6 all-reduce.20
where the time goes:
time: 1800 us; the launch traced here: 1780 us
  matrix products  665 us (37%)
  waiting for transfers between devices  664 us (37%)
  local copies, waits for them, and re-layouts  181 us (10%)
  blocking collectives  139 us (8%)
  other arithmetic  77.9 us (4%)
  loops' own time  30.9 us (2%)
    dot_general x664, matrix products, hi_einsum(): jnp.einsum(form, left, right, precision=HIGH, preferred_element_type=jnp....  383 us
    dot_general x192, matrix products, short_einsum(): return jnp.einsum(form, left, right, preferred_element_type=jnp.float32)  162 us
    reduce_scatter x1, waiting for transfers between devices, on_device(): lax.psum_scatter(qkv_grad.astype(jnp.bfloat16), 'fsdp', scatter_dimension...  121 us
    unnamed x21, waiting for transfers between devices  97.6 us
    all_gather x1, waiting for transfers between devices, on_device(): lax.all_gather(ffn_down, 'fsdp', axis=0, tiled=True)  85.5 us
    all_gather x1, waiting for transfers between devices, on_device(): lax.all_gather(ffn_up, 'fsdp', axis=0, tiled=True)  85.4 us
    dot_general x14, matrix products, contract(): lax.dot_general(left, right, (((left_dim,), (right_dim,)), ((), ())), pre...  80.5 us
    reduce_scatter x1, waiting for transfers between devices, on_device(): lax.psum_scatter(down_grad.astype(jnp.bfloat16), 'fsdp', scatter_dimensio...  74.3 us
  transfers between devices with their start and end apart: 22, of which 14 were waited for; matrix products, arithmetic and copies ran while one was open for 43% of the time, Pallas kernels for 0%

commit v1 on v0

v1 whole, which is shorter than its diff:
```python
from functools import partial

import jax
import jax.numpy as jnp
from jax import lax
from jax.experimental import pallas as pl
from jax.experimental.pallas import tpu as pltpu
from jax.sharding import PartitionSpec as P

SPAN = 64
EPSILON = 1e-06
BF = jnp.bfloat16
F32 = jnp.float32


def nn(a, b):
    return lax.dot_general(a, b, (((1,), (0,)), ((), ())), preferred_element_type=F32)


def nt(a, b):
    return lax.dot_general(a, b, (((1,), (1,)), ((), ())), preferred_element_type=F32)


def tn(a, b):
    return lax.dot_general(a, b, (((0,), (0,)), ((), ())), preferred_element_type=F32)


def block_masks(cols_ref, rows_ref, heads):
    n = SPAN
    row = lax.broadcasted_iota(jnp.int32, (n, n), 0)
    col = lax.broadcasted_iota(jnp.int32, (n, n), 1)
    ids = cols_ref[:, heads : heads + 1]
    ids_row = rows_ref[0, heads : heads + 1, :]
    before = rows_ref[0, heads + 1 : heads + 2, :]
    end = ids_row[:, n - 1 : n]
    same = ids == ids_row
    first = (ids == before[:, :1]).astype(F32)
    last = (ids == end).astype(F32)
    keep = (end == before[:, :1]).astype(F32)
    return row, col, same, first, last, keep


def summary_kernel(heads, q_dim, k_ref, v_ref, cols_ref, rows_ref, w_ref, u_ref, a_ref, x_ref, state):
    n, d = SPAN, q_dim
    block = pl.program_id(0)

    @pl.when(block == 0)
    def _():
        r = lax.broadcasted_iota(jnp.int32, (d, 2 * d), 0)
        c = lax.broadcasted_iota(jnp.int32, (d, 2 * d), 1)
        unit = (r + d == c).astype(F32)
        for h in range(heads):
            state[h] = unit

    row, col, same, first, last, keep = block_masks(cols_ref, rows_ref, heads)
    lower = jnp.logical_and(same, row > col)
    unit = (row == col).astype(F32)
    pair = jnp.logical_and(row == col + 1, (row & 1) == 1)
    keys = [k_ref[:, h * d : (h + 1) * d] for h in range(heads)]
    mixing = []
    inverse = []
    for h in range(heads):
        m = jnp.where(lower, nt(keys[h], keys[h]) * cols_ref[:, h : h + 1], 0.0)
        mixing.append(m)
        inverse.append((unit - jnp.where(pair, m, 0.0)).astype(BF))
    size = 2
    while size < n:
        level = jnp.logical_and(
            (row // (2 * size)) == (col // (2 * size)),
            jnp.logical_and(((row // size) & 1) == 1, ((col // size) & 1) == 0),
        )
        inner = [nn(jnp.where(level, mixing[h], 0.0).astype(BF), inverse[h]).astype(BF) for h in range(heads)]
        for h in range(heads):
            inverse[h] = inverse[h] - jnp.where(level, nn(inverse[h], inner[h]), 0.0).astype(BF)
        size *= 2
    first_low = first
    for h in range(heads):
        cut = slice(h * d, (h + 1) * d)
        a_ref[h] = inverse[h]
        scaled = (inverse[h].astype(F32) * rows_ref[0, h : h + 1, :]).astype(BF)
        both = nn(scaled, jnp.concatenate([keys[h], v_ref[:, cut]], axis=1))
        w = both[:, :d].astype(BF)
        u = both[:, d:].astype(BF)
        w_ref[:, cut] = w
        u_ref[:, cut] = u
        held = state[h]
        moved = nn(w, held.astype(BF)) * first_low
        fresh = (jnp.concatenate([u.astype(F32), jnp.zeros((n, d), F32)], axis=1) - moved).astype(BF)
        key_last = (keys[h].astype(F32) * last).astype(BF)
        state[h] = keep * held + tn(key_last, fresh)

    @pl.when(block == pl.num_programs(0) - 1)
    def _():
        x_ref[...] = state[...].astype(BF)


def forward_kernel(
    heads, d, q_ref, k_ref, w_ref, u_ref, cols_ref, rows_ref, s_ref, gate_ref, gain_ref,
    y_ref, o_ref, e_ref, kept_ref, state,
):
    n = SPAN
    block = pl.program_id(0)

    @pl.when(block == 0)
    def _():
        state[...] = s_ref[...].astype(F32)

    row, col, same, first, last, keep = block_masks(cols_ref, rows_ref, heads)
    visible = jnp.logical_and(same, row >= col)
    for h in range(heads):
        cut = slice(h * d, (h + 1) * d)
        q, k, w = q_ref[:, cut], k_ref[:, cut], w_ref[:, cut]
        held = state[h]
        held_low = held.astype(BF)
        kept_ref[0, h] = held_low
        both = nn(jnp.concatenate([w, q], axis=0), held_low)
        fresh = (u_ref[:, cut].astype(F32) - first * both[:n]).astype(BF)
        e_ref[:, cut] = fresh
        scores = jnp.where(visible, nt(q, k), 0.0).astype(BF)
        out = first * both[n:] + nn(scores, fresh)
        key_last = (k.astype(F32) * last).astype(BF)
        state[h] = keep * held + tn(key_last, fresh)
        o_ref[:, cut] = out
        g = gate_ref[:, cut]
        root = lax.rsqrt(jnp.mean(out * out, axis=1, keepdims=True) + EPSILON)
        y_ref[:, cut] = (out * root * gain_ref[...] * (g / (1.0 + jnp.exp(-g)))).astype(BF)


def adjoint_kernel(
    heads, d, q_ref, k_ref, w_ref, cols_ref, rows_ref, dy_ref, o_ref, gate_ref, gain_ref,
    do_ref, dgate_ref, dgain_ref, ds_ref, state,
):
    n = SPAN
    step = pl.program_id(0)

    @pl.when(step == 0)
    def _():
        state[...] = jnp.zeros_like(state)
        dgain_ref[...] = jnp.zeros_like(dgain_ref)

    row, col, same, first, last, keep = block_masks(cols_ref, rows_ref, heads)
    visible = jnp.logical_and(same, row >= col)
    gain = gain_ref[...]
    gain_sum = jnp.zeros((1, d), F32)
    for h in range(heads):
        cut = slice(h * d, (h + 1) * d)
        q, k, w = q_ref[:, cut], k_ref[:, cut], w_ref[:, cut]
        o, g, dy = o_ref[:, cut], gate_ref[:, cut], dy_ref[:, cut]
        root = lax.rsqrt(jnp.mean(o * o, axis=1, keepdims=True) + EPSILON)
        unit = o * root
        sig = 1.0 / (1.0 + jnp.exp(-g))
        m = g * sig
        t = dy * m
        gain_sum = gain_sum + jnp.sum(t * unit, axis=0, keepdims=True)
        tg = t * gain
        do = root * (tg - unit * jnp.mean(tg * unit, axis=1, keepdims=True))
        dgate_ref[:, cut] = (dy * gain * unit * (sig * (1.0 + g * (1.0 - sig)))).astype(BF)
        do_low = do.astype(BF)
        do_ref[:, cut] = do_low
        scores = jnp.where(visible, nt(q, k), 0.0).astype(BF)
        later = state[h]
        de = last * nn(k, later.astype(BF)) + tn(scores, do_low)
        left = jnp.concatenate([q.astype(F32) * first, w.astype(F32) * (-first)], axis=0).astype(BF)
        right = jnp.concatenate([do_low, de.astype(BF)], axis=0)
        state[h] = keep * later + tn(left, right)
    dgain_ref[...] += gain_sum

    @pl.when(step == pl.num_programs(0) - 1)
    def _():
        ds_ref[...] = state[...].astype(BF)


def backward_kernel(
    heads, d, q_ref, k_ref, v_ref, w_ref, u_ref, a_ref, e_ref, kept_ref, do_ref, cols_ref, rows_ref, s_ref,
    dq_ref, dk_ref, dv_ref, dr_ref, state,
):
    n = SPAN
    step = pl.program_id(0)

    @pl.when(step == 0)
    def _():
        state[...] = s_ref[...].astype(F32)

    row, col, same, first, last, keep = block_masks(cols_ref, rows_ref, heads)
    visible = jnp.logical_and(same, row >= col)
    lower = jnp.logical_and(same, row > col)
    lane = lax.broadcasted_iota(jnp.int32, (n, d), 1)
    rate_grads = jnp.zeros((n, d), F32)
    for h in range(heads):
        cut = slice(h * d, (h + 1) * d)
        q, k, v, w, u = q_ref[:, cut], k_ref[:, cut], v_ref[:, cut], w_ref[:, cut], u_ref[:, cut]
        do, e, held = do_ref[:, cut], e_ref[:, cut], kept_ref[0, h]
        rate = cols_ref[:, h : h + 1]
        later = state[h]
        later_low = later.astype(BF)
        scores = jnp.where(visible, nt(q, k), 0.0).astype(BF)
        de = last * nn(k, later_low) + tn(scores, do)
        de_low = de.astype(BF)
        dscores = jnp.where(visible, nt(do, e), 0.0).astype(BF)
        both = nt(jnp.concatenate([do, de_low], axis=0), held)
        dq_ref[:, cut] = first * both[:n] + nn(dscores, k)
        dw = -first * both[n:]
        dk = tn(dscores, q) + last * nt(e, later_low)
        pg = tn(a_ref[h], jnp.concatenate([dw.astype(BF), de_low], axis=1))
        p, g = pg[:, :d], pg[:, d:]
        dmix = jnp.where(lower, -nt(pg.astype(BF), jnp.concatenate([w, u], axis=1)), 0.0).astype(BF)
        kf = k.astype(F32)
        drk = p + nn(dmix, k)
        dk_ref[:, cut] = dk + tn(dmix, (kf * rate).astype(BF)) + rate * drk
        dv_ref[:, cut] = rate * g
        dr = jnp.sum(drk * kf + g * v.astype(F32), axis=1, keepdims=True)
        rate_grads = jnp.where(lane == h, dr, rate_grads)
        left = jnp.concatenate([q.astype(F32) * first, w.astype(F32) * (-first)], axis=0).astype(BF)
        right = jnp.concatenate([do, de_low], axis=0)
        state[h] = keep * later + tn(left, right)
    dr_ref[...] = rate_grads


def prefix_kernel(peers, x_ref, out_ref):
    cols = out_ref.shape[2]
    held = jnp.zeros(out_ref.shape[1:], F32)
    for i in range(peers):
        out_ref[i] = held.astype(BF)
        held = nn(x_ref[i, :, cols:], held.astype(BF)) + x_ref[i, :, :cols].astype(F32)


def suffix_kernel(peers, t_ref, g_ref, out_ref):
    held = jnp.zeros(out_ref.shape[1:], F32)
    cols = out_ref.shape[2]
    for i in reversed(range(peers)):
        out_ref[i] = held.astype(BF)
        held = tn(t_ref[i, :, cols:], held.astype(BF)) + g_ref[i].astype(F32)


VMEM_LIMIT = 48 * 1024 * 1024


def params():
    return pltpu.CompilerParams(dimension_semantics=("arbitrary",), vmem_limit_bytes=VMEM_LIMIT)


def specs(blocks, heads, d, flip):
    at = (lambda b: blocks - 1 - b) if flip else (lambda b: b)
    wide = pl.BlockSpec((SPAN, heads * d), lambda b: (at(b), 0))
    cols = pl.BlockSpec((SPAN, 2 * heads), lambda b: (at(b), 0))
    rows = pl.BlockSpec((1, 2 * heads, SPAN), lambda b: (at(b), 0, 0))
    state = pl.BlockSpec((heads, d, d), lambda b: (0, 0, 0))
    mix = pl.BlockSpec((heads, SPAN, SPAN), lambda b: (0, at(b), 0))
    kept = pl.BlockSpec((1, heads, d, d), lambda b: (at(b), 0, 0, 0))
    gain = pl.BlockSpec((1, d), lambda b: (0, 0))
    return wide, cols, rows, state, mix, kept, gain


def shape(dims, kind):
    return jax.ShapeDtypeStruct(dims, kind)


def delta_summary(k, v, cols, rows, heads):
    count, width = k.shape
    d, blocks = width // heads, count // SPAN
    wide, c, r, state, mix, kept, gain = specs(blocks, heads, d, False)
    return pl.pallas_call(
        partial(summary_kernel, heads, d),
        grid=(blocks,),
        in_specs=[wide, wide, c, r],
        out_specs=[wide, wide, mix, pl.BlockSpec((heads, d, 2 * d), lambda b: (0, 0, 0))],
        out_shape=[
            shape((count, width), BF),
            shape((count, width), BF),
            shape((heads, count, SPAN), BF),
            shape((heads, d, 2 * d), BF),
        ],
        scratch_shapes=[pltpu.VMEM((heads, d, 2 * d), F32)],
        compiler_params=params(),
        name="delta_summary",
    )(k, v, cols, rows)


def delta_forward(q, k, w, u, cols, rows, entry, gate, gain_full, heads):
    count, width = k.shape
    d, blocks = width // heads, count // SPAN
    wide, c, r, state, mix, kept, gain = specs(blocks, heads, d, False)
    return pl.pallas_call(
        partial(forward_kernel, heads, d),
        grid=(blocks,),
        in_specs=[wide, wide, wide, wide, c, r, state, wide, gain],
        out_specs=[wide, wide, wide, kept],
        out_shape=[
            shape((count, width), BF),
            shape((count, width), F32),
            shape((count, width), BF),
            shape((blocks, heads, d, d), BF),
        ],
        scratch_shapes=[pltpu.VMEM((heads, d, d), F32)],
        compiler_params=params(),
        name="delta_forward",
    )(q, k, w, u, cols, rows, entry, gate, gain_full)


def delta_adjoint(q, k, w, cols, rows, dy, o, gate, gain_full, heads):
    count, width = k.shape
    d, blocks = width // heads, count // SPAN
    wide, c, r, state, mix, kept, gain = specs(blocks, heads, d, True)
    return pl.pallas_call(
        partial(adjoint_kernel, heads, d),
        grid=(blocks,),
        in_specs=[wide, wide, wide, c, r, wide, wide, wide, gain],
        out_specs=[wide, wide, gain, state],
        out_shape=[
            shape((count, width), BF),
            shape((count, width), BF),
            shape((1, d), F32),
            shape((heads, d, d), BF),
        ],
        scratch_shapes=[pltpu.VMEM((heads, d, d), F32)],
        compiler_params=params(),
        name="delta_adjoint",
    )(q, k, w, cols, rows, dy, o, gate, gain_full)


def delta_backward(q, k, v, w, u, a, e, kept_states, do, cols, rows, later, heads):
    count, width = k.shape
    d, blocks = width // heads, count // SPAN
    wide, c, r, state, mix, kept, gain = specs(blocks, heads, d, True)
    return pl.pallas_call(
        partial(backward_kernel, heads, d),
        grid=(blocks,),
        in_specs=[wide, wide, wide, wide, wide, mix, wide, kept, wide, c, r, state],
        out_specs=[wide, wide, wide, pl.BlockSpec((SPAN, d), lambda b: (blocks - 1 - b, 0))],
        out_shape=[
            shape((count, width), F32),
            shape((count, width), F32),
            shape((count, width), F32),
            shape((count, d), F32),
        ],
        scratch_shapes=[pltpu.VMEM((heads, d, d), F32)],
        compiler_params=params(),
        name="delta_backward",
    )(q, k, v, w, u, a, e, kept_states, do, cols, rows, later)


def scan_states(x):
    peers, d, width = x.shape
    return pl.pallas_call(
        partial(prefix_kernel, peers),
        out_shape=shape((peers, d, width - d), BF),
        name="state_prefix",
    )(x)


def scan_grads(x, g):
    peers, d, width = g.shape
    return pl.pallas_call(
        partial(suffix_kernel, peers),
        out_shape=shape((peers, d, width), BF),
        name="state_suffix",
    )(x, g)


class Place:
    def __init__(self):
        self.nf, self.nr = lax.axis_size("fsdp"), lax.axis_size("rep")
        self.ny = 2 if self.nf <= 8 else self.nf // 4
        self.nz = self.nf // self.ny
        self.nc = 2 if self.nr % 2 == 0 else 1
        self.nx = self.nr // self.nc
        self.f, self.r = lax.axis_index("fsdp"), lax.axis_index("rep")
        self.z, self.y = self.f // self.ny, self.f % self.ny
        self.x, self.c = self.r // self.nc, self.r % self.nc

    def send(self, value, way, steps):
        if way == "z":
            pairs = [
                (z * self.ny + y, (z + steps) % self.nz * self.ny + y)
                for z in range(self.nz)
                for y in range(self.ny)
            ]
            return lax.ppermute(value, "fsdp", pairs)
        if way == "y":
            pairs = [
                (z * self.ny + y, z * self.ny + (y + steps) % self.ny)
                for z in range(self.nz)
                for y in range(self.ny)
            ]
            return lax.ppermute(value, "fsdp", pairs)
        if way == "x":
            pairs = [
                (x * self.nc + c, (x + steps) % self.nx * self.nc + c)
                for x in range(self.nx)
                for c in range(self.nc)
            ]
            return lax.ppermute(value, "rep", pairs)
        pairs = [
            (x * self.nc + c, x * self.nc + (c + steps) % self.nc)
            for x in range(self.nx)
            for c in range(self.nc)
        ]
        return lax.ppermute(value, "rep", pairs)

    def size(self, way):
        return {"z": self.nz, "y": self.ny, "x": self.nx, "c": self.nc}[way]

    def at(self, way):
        return {"z": self.z, "y": self.y, "x": self.x, "c": self.c}[way]


def place_kernel(count, rows, each, by_rows, widths, offs_ref, own_ref, *refs):
    stacks, outs, sems = refs[: len(count)], refs[len(count) : -1], refs[-1]
    copies = []

    def put(src, row, height, col, width_of):
        start = 0
        for out, width in zip(outs, widths):
            copy = pltpu.make_async_copy(
                src(start, width), out.at[pl.ds(row, height), col(width)], sems.at[len(copies)]
            )
            copy.start()
            copies.append(copy)
            start += width

    top = pl.multiple_of(offs_ref[0], rows)
    put(lambda s, w: own_ref.at[:, pl.ds(s, w)], top, rows, lambda w: pl.ds(0, w), None)
    at = 1
    for stack, number in zip(stacks, count):
        for j in range(number):
            if by_rows:
                row = pl.multiple_of(offs_ref[at], each)
                put(lambda s, w, j=j: stack.at[j, :, pl.ds(s, w)], row, each, lambda w: pl.ds(0, w), None)
            else:
                row = pl.multiple_of(offs_ref[at], rows)
                column = pl.multiple_of(offs_ref[at + 1], each)
                put(lambda s, w, j=j: stack.at[j], row, rows, lambda w: pl.ds(column, each), None)
            at += 1 if by_rows else 2
    for copy in copies:
        copy.wait()


def gather_weights(here, shard, widths, deep, by_rows=True):
    rows, total = shard.shape
    parts = here.nr if deep else here.nc
    extent = rows if by_rows else total
    each = extent // parts
    if extent % parts or each % (32 if by_rows else 128) or rows % 32:
        whole = lax.all_gather(shard, "fsdp", axis=0, tiled=True)
        starts = [sum(widths[:i]) for i in range(len(widths))]
        return [whole[:, s : s + w] for s, w in zip(starts, widths)]
    part = here.r if deep else here.c
    piece = lax.dynamic_slice_in_dim(shard, part * each, each, 0 if by_rows else 1)
    near = [(s, 0, here.send(piece, "z", s)) for s in range(1, here.nz)]
    far = [(0, s, here.send(piece, "y", s)) for s in range(1, here.ny)]
    far += [(sz, s, here.send(a, "y", s)) for sz, zero, a in near for s in range(1, here.ny)]
    pieces = near + far
    stack = jnp.stack([a for sz, sy, a in pieces])
    stacks = [(0, 0, stack)]
    if deep:
        stacks += [(s, 0, here.send(stack, "x", s)) for s in range(1, here.nx)]
    stacks += [(sx, s, here.send(a, "c", s)) for sx, zero, a in stacks for s in range(1, here.nc)]
    offsets = [here.f * rows]
    for sx, sc, a in stacks:
        x, c = (here.x - sx) % here.nx, (here.c - sc) % here.nc
        inside = (x * here.nc + c if deep else c) * each
        for sz, sy, unused in pieces:
            source = (here.z - sz) % here.nz * here.ny + (here.y - sy) % here.ny
            if by_rows:
                offsets.append(source * rows + inside)
            else:
                offsets += [source * rows, inside]
    offsets = jnp.stack(offsets).astype(jnp.int32)
    count = [len(pieces)] * len(stacks)
    any_space = pl.BlockSpec(memory_space=pl.ANY)
    outs = pl.pallas_call(
        partial(place_kernel, count, rows, each, by_rows, widths),
        grid_spec=pltpu.PrefetchScalarGridSpec(
            num_scalar_prefetch=1,
            grid=(1,),
            in_specs=[any_space] * (1 + len(stacks)),
            out_specs=[pl.BlockSpec((here.nf * rows, w), lambda i, o: (0, 0)) for w in widths],
            scratch_shapes=[pltpu.SemaphoreType.DMA(((1 + sum(count)) * len(widths),))],
        ),
        out_shape=[jax.ShapeDtypeStruct((here.nf * rows, w), shard.dtype) for w in widths],
        compiler_params=pltpu.CompilerParams(vmem_limit_bytes=VMEM_LIMIT),
        name="place_weights",
    )(offsets, shard, *[a for sx, sc, a in stacks])
    return outs


def scatter_way(here, array, way, axis):
    number, mine = here.size(way), here.at(way)
    total = lax.dynamic_index_in_dim(array, mine, axis, keepdims=False).astype(F32)
    for s in range(1, number):
        out = lax.dynamic_index_in_dim(array, (mine + s) % number, axis, keepdims=False)
        total = total + here.send(out, way, s).astype(F32)
    return total.astype(BF)


def join_way(here, array, way, axis):
    number, mine = here.size(way), here.at(way)
    got = [array] + [here.send(array, way, s) for s in range(1, number)]
    if number == 2:
        ahead = jnp.concatenate(got, axis=axis)
        behind = jnp.concatenate(got[::-1], axis=axis)
        return jnp.where(mine == 0, ahead, behind)
    stack = jnp.stack(got)
    order = (mine - jnp.arange(number)) % number
    stack = jnp.take(stack, order, axis=0)
    return jnp.concatenate([stack[i] for i in range(number)], axis=axis)


def reduce_grad(here, left, right, order):
    width = right.shape[1]
    half = width // here.nc
    if here.nc == 2:
        theirs = lax.dynamic_slice_in_dim(right, (1 - here.c) * half, half, 1)
        mine = lax.dynamic_slice_in_dim(right, here.c * half, half, 1)
        away = contract(left, theirs, 0, 0).astype(BF)
        came = here.send(away, "c", 1)
        part = (contract(left, mine, 0, 0) + came.astype(F32)).astype(BF)
    else:
        part = contract(left, right, 0, 0).astype(BF)
    rows = part.shape[0] // here.nf
    part = part.reshape(here.nz, here.ny, rows, half)
    split = False
    have = {"z": 0, "y": 1}
    for way in order:
        if way == "x":
            if len(have) == 2:
                lead = part.shape[:2]
                part = part.reshape(lead + (here.nx, rows // here.nx, half))
                part = scatter_way(here, part, "x", 2)
                split = True
            elif len(have) == 0:
                total = part.astype(F32)
                for s in range(1, here.nx):
                    total = total + here.send(part, "x", s).astype(F32)
                part = total.astype(BF)
            else:
                part = part.reshape((part.shape[0], here.nx, rows // here.nx, half))
                part = scatter_way(here, part, "x", 1)
                split = True
        else:
            axis = 1 if (way == "y" and "z" in have) else 0
            part = scatter_way(here, part, way, axis)
            have.pop(way)
    if split:
        part = join_way(here, part, "x", 0)
    if here.nc == 2:
        part = join_way(here, part, "c", 1)
    return part.astype(F32)


def sum_all(here, array):
    for way in ("c", "x", "y", "z"):
        low = array.astype(BF)
        total = low.astype(F32)
        got = [here.send(low, way, s).astype(F32) for s in range(1, here.size(way))]
        array = total
        for g in got:
            array = array + g
    return array


def contract(left, right, left_dim, right_dim):
    return lax.dot_general(
        left, right, (((left_dim,), (right_dim,)), ((), ())), preferred_element_type=F32
    )


def rms_norm(values, gain):
    return values * lax.rsqrt(jnp.mean(values * values, axis=-1, keepdims=True) + EPSILON) * gain


def make_features(extended, taps, beta_pre, masks, head_count):
    row_count = beta_pre.shape[0]
    lead = extended.shape[0] - row_count
    mixed = taps[0] * extended[lead:] * masks[0]
    for offset in range(1, 4):
        mixed = mixed + taps[offset] * extended[lead - offset : lead - offset + row_count] * masks[offset]
    active = jax.nn.silu(mixed)
    model_width = active.shape[1] // 3
    head_dim = model_width // head_count
    queries = active[:, :model_width] * head_dim ** (-0.5)
    key_raw = active[:, model_width : 2 * model_width].reshape(row_count, head_count, head_dim)
    key_unit = key_raw * lax.rsqrt(jnp.sum(key_raw * key_raw, axis=-1, keepdims=True) + EPSILON)
    values = active[:, 2 * model_width :]
    return (queries, key_unit.reshape(row_count, model_width), values, jax.nn.sigmoid(beta_pre))


def swiglu(up_gate, up_lin):
    return jax.nn.silu(up_gate) * up_lin


def from_behind(value, steps):
    count = lax.axis_size("fsdp")
    first, last = (max(0, -steps), min(count, count - steps))
    return lax.ppermute(value, "fsdp", [(source, source + steps) for source in range(first, last)])


def to_owners(parts, fanout):
    heads, d, width = parts.shape
    cut = parts.reshape(heads, d, fanout, width // fanout)
    return jnp.swapaxes(cut, 1, 2).reshape(heads * fanout, d, width // fanout)


def to_heads(parts, fanout):
    owners, d, width = parts.shape
    cut = parts.reshape(owners // fanout, fanout, d, width)
    return jnp.swapaxes(cut, 1, 2).reshape(owners // fanout, d, width * fanout)


def swap(value):
    return lax.all_to_all(value, "fsdp", 0, 0, tiled=True)


def gather_small(here, arrays):
    flat = jnp.concatenate([a.reshape(-1) for a in arrays])
    near = [(s, 0, here.send(flat, "z", s)) for s in range(1, here.nz)]
    far = [(sz, s, here.send(a, "y", s)) for sz, zero, a in [(0, 0, flat)] + near for s in range(1, here.ny)]
    pieces = [(0, 0, flat)] + near + far
    stack = jnp.stack([a for sz, sy, a in pieces])
    source = jnp.stack(
        [(here.z - sz) % here.nz * here.ny + (here.y - sy) % here.ny for sz, sy, a in pieces]
    )
    pick = (lax.broadcasted_iota(jnp.int32, (here.nf, here.nf), 0) == source[None, :]).astype(BF)
    whole = contract(pick, stack, 1, 0)
    outs, at = [], 0
    for a in arrays:
        outs.append(whole[:, at : at + a.size].reshape((here.nf,) + a.shape))
        at += a.size
    return outs


def on_device(
    hidden_in,
    seg_ids,
    attn_gain,
    qkv_weight,
    beta_weight,
    gate_weight,
    conv_taps,
    out_gain,
    out_weight,
    ffn_gain,
    ffn_gate,
    ffn_up,
    ffn_down,
    cotangent,
):
    here = Place()
    row_count, width = hidden_in.shape
    heads = beta_weight.shape[1]
    head_dim = width // heads
    blocks = row_count // SPAN
    rim = 8

    rim_rows = from_behind(hidden_in[row_count - rim :], 1)
    numbers = seg_ids + 1
    rim_ids = from_behind(numbers[row_count - rim :], 1)
    attn_s, outgain_s, ffngain_s, taps_s = gather_small(
        here, (attn_gain, out_gain, ffn_gain, conv_taps)
    )
    attn_scale = attn_s.reshape(-1)
    outgain_scale = outgain_s.reshape(1, -1)
    ffngain_scale = ffngain_s.reshape(-1)
    taps_scale = jnp.swapaxes(taps_s, 0, 1).reshape(conv_taps.shape[0], -1)

    (qkv_full,) = gather_weights(here, qkv_weight, [3 * width], True)
    lanes = 128
    beta_wide = jnp.pad(beta_weight, ((0, 0), (0, lanes - heads)))
    gate_full, outw_full, beta_full = gather_weights(
        here,
        jnp.concatenate([gate_weight, out_weight, beta_wide], axis=1),
        [width, width, lanes],
        False,
    )
    hidden_units = ffn_gate.shape[1]
    hidgate_full, hidup_full = gather_weights(
        here, jnp.concatenate([ffn_gate, ffn_up], axis=1), [hidden_units, hidden_units], True
    )
    (down_full,) = gather_weights(here, ffn_down, [width], False, by_rows=False)

    residual = hidden_in.astype(F32)
    extended_in = jnp.concatenate([rim_rows, hidden_in]).astype(F32)
    normed_ext = rms_norm(extended_in, attn_scale).astype(BF)
    normed_low = normed_ext[rim:]
    mixed_pre = jnp.dot(normed_ext, qkv_full, preferred_element_type=F32)
    beta_pre = jnp.dot(normed_low, beta_full, preferred_element_type=F32)[:, :heads]
    gate_pre = jnp.dot(normed_low, gate_full, preferred_element_type=F32)
    ids = jnp.concatenate([rim_ids, numbers]).astype(F32)
    masks = jnp.stack(
        [
            (ids[rim - offset : rim - offset + row_count] == ids[rim:]).astype(F32)
            for offset in range(4)
        ]
    )[:, :, None]
    features, feature_back = jax.vjp(
        partial(make_features, masks=masks, head_count=heads), mixed_pre, taps_scale, beta_pre
    )
    queries, key_unit, values, rates = features
    query_low, key_low, value_low = queries.astype(BF), key_unit.astype(BF), values.astype(BF)
    own_ids = ids[rim:]
    before = ids[rim - 1 : rim - 1 + row_count : SPAN]
    cols = jnp.concatenate([rates, own_ids[:, None], jnp.zeros((row_count, heads - 1), F32)], 1)
    rows = jnp.concatenate(
        [
            jnp.swapaxes(rates.reshape(blocks, SPAN, heads), 1, 2),
            own_ids.reshape(blocks, 1, SPAN),
            jnp.broadcast_to(before[:, None, None], (blocks, 1, SPAN)),
            jnp.zeros((blocks, heads - 2, SPAN), F32),
        ],
        1,
    )
    w, u, a, moves = delta_summary(key_low, value_low, cols, rows, heads)
    fanout = here.nf // heads
    if fanout > 1:
        moves = jnp.concatenate(
            [
                to_owners(moves[:, :, :head_dim], fanout),
                jnp.repeat(moves[:, :, head_dim:], fanout, axis=0),
            ],
            axis=2,
        )
    owned = swap(moves)
    entry = swap(scan_states(owned))
    if fanout > 1:
        entry = to_heads(entry, fanout)
    gated_low, attn_heads, fresh, kept = delta_forward(
        query_low, key_low, w, u, cols, rows, entry, gate_pre, outgain_scale, heads
    )
    middle = residual + jnp.dot(gated_low, outw_full, preferred_element_type=F32)
    normed_two, norm_two_back = jax.vjp(rms_norm, middle, ffngain_scale)
    normed_two_low = normed_two.astype(BF)
    up_gate = jnp.dot(normed_two_low, hidgate_full, preferred_element_type=F32)
    up_lin = jnp.dot(normed_two_low, hidup_full, preferred_element_type=F32)
    hidden_ff, swiglu_back = jax.vjp(swiglu, up_gate, up_lin)
    hidden_low = hidden_ff.astype(BF)
    output = (middle + jnp.dot(hidden_low, down_full, preferred_element_type=F32)).astype(BF)

    top_grad = cotangent.astype(F32)
    down_total = reduce_grad(here, hidden_low, cotangent, "yzx")
    hidden_grad = contract(cotangent, down_full, 1, 1)
    upgate_grad, uplin_grad = swiglu_back(hidden_grad)
    upgate_low, uplin_low = upgate_grad.astype(BF), uplin_grad.astype(BF)
    hidgate_total = reduce_grad(here, normed_two_low, upgate_low, "xyz")
    hidup_total = reduce_grad(here, normed_two_low, uplin_low, "xyz")
    normed_two_grad = contract(upgate_low, hidgate_full, 1, 1) + contract(uplin_low, hidup_full, 1, 1)
    middle_back, ffngain_grad = norm_two_back(normed_two_grad)
    middle_grad = top_grad + middle_back
    middle_low = middle_grad.astype(BF)
    outproj_total = reduce_grad(here, gated_low, middle_low, "yzx")
    gated_grad = contract(middle_low, outw_full, 1, 1)
    heads_grad, gatepre_low, outgain_grad, local_later = delta_adjoint(
        query_low, key_low, w, cols, rows, gated_grad, attn_heads, gate_pre, outgain_scale, heads
    )
    if fanout > 1:
        local_later = to_owners(local_later, fanout)
    later = swap(scan_grads(owned, swap(local_later)))
    if fanout > 1:
        later = to_heads(later, fanout)
    gate_total = reduce_grad(here, normed_low, gatepre_low, "yzx")
    query_grad, key_grad, value_grad, rate_grad = delta_backward(
        query_low, key_low, value_low, w, u, a, fresh, kept, heads_grad, cols, rows, later, heads
    )
    ext_grad, taps_grad, betapre_grad = feature_back(
        (query_grad, key_grad, value_grad, rate_grad[:, :heads])
    )
    mixed_low = ext_grad.astype(BF)
    betapre_low = betapre_grad.astype(BF)
    parts = [
        reduce_grad(here, normed_ext, mixed_low[:, i * width : (i + 1) * width], order)
        for i, order in enumerate(("xyz", "yzx", "zyx"))
    ]
    qkv_total = jnp.concatenate(parts, axis=1)
    beta_grad = contract(normed_low, betapre_low, 0, 0)
    wide_grad = contract(mixed_low, qkv_full, 1, 1)
    rim_grad = from_behind(wide_grad[:rim].astype(BF), -1).astype(F32)
    normed_grad = (
        wide_grad[rim:]
        + jnp.pad(rim_grad, ((row_count - rim, 0), (0, 0)))
        + contract(betapre_low, beta_full[:, :heads], 1, 1)
        + contract(gatepre_low, gate_full, 1, 1)
    )
    input_back, attngain_grad = jax.vjp(rms_norm, residual, attn_scale)[1](normed_grad)
    input_grad = (middle_grad + input_back).astype(BF)

    small = (
        attngain_grad.reshape(here.nf, -1),
        beta_grad.reshape(here.nf, -1),
        jnp.swapaxes(taps_grad.reshape(taps_grad.shape[0], here.nf, -1), 0, 1).reshape(here.nf, -1),
        outgain_grad.reshape(here.nf, -1),
        ffngain_grad.reshape(here.nf, -1),
    )
    summed = sum_all(here, jnp.concatenate(small, axis=1))
    mine = lax.dynamic_index_in_dim(summed, here.f, 0, keepdims=False)
    ends = [0]
    for s in small:
        ends.append(ends[-1] + s.shape[1])
    cut = [mine[ends[i] : ends[i + 1]] for i in range(len(small))]
    return (
        output,
        input_grad,
        cut[0],
        qkv_total,
        cut[1].reshape(-1, heads),
        gate_total,
        cut[2].reshape(conv_taps.shape),
        cut[3],
        outproj_total,
        cut[4],
        hidgate_total,
        hidup_total,
        down_total,
    )


def solution(mesh):
    placed = (
        P(("rep", "fsdp"), None),
        P(("rep", "fsdp")),
        P("fsdp"),
        P("fsdp", None),
        P("fsdp", None),
        P("fsdp", None),
        P(None, "fsdp"),
        P("fsdp"),
        P("fsdp", None),
        P("fsdp"),
        P("fsdp", None),
        P("fsdp", None),
        P("fsdp", None),
        P(("rep", "fsdp"), None),
    )
    return jax.shard_map(
        on_device,
        mesh=mesh,
        in_specs=placed,
        out_specs=(
            P(("rep", "fsdp"), None),
            P(("rep", "fsdp"), None),
            P("fsdp"),
            P("fsdp", None),
            P("fsdp", None),
            P("fsdp", None),
            P(None, "fsdp"),
            P("fsdp"),
            P("fsdp", None),
            P("fsdp"),
            P("fsdp", None),
            P("fsdp", None),
            P("fsdp", None),
        ),
        check_vma=False,
    )
```

time: 1800 us -> 836 us (0.46)
  matrix products: 665 us -> 112 us
  waiting for transfers between devices: 664 us -> 280 us
  starting transfers between devices: 9.91 us -> 170 us
  blocking collectives: 139 us -> 0 us
  Pallas kernels: 0 us -> 135 us
  local copies, waits for them, and re-layouts: 181 us -> 63.6 us
  loops' own time: 30.9 us -> 0 us
    dot_general x871 -> x7, matrix products: 584 us -> 36.7 us  [the longest x1 11 us: on_device(): up_gate = jnp.dot(normed_two_low, hidgate_full, preferred_element_type=F32)]
    all_gather x10 -> x0, waiting for transfers between devices: 298 us -> none  [the longest x1 85.5 us: on_device(): lax.all_gather(ffn_down, 'fsdp', axis=0, tiled=True)]
    ppermute x3 -> x111, waiting for transfers between devices: 5.47 us -> 278 us  [the longest x71 233 us: send(): return lax.ppermute(value, 'fsdp', pairs)]
    reduce_scatter x6 -> x0, waiting for transfers between devices: 196 us -> none  [the longest x1 121 us: on_device(): lax.psum_scatter(qkv_grad.astype(jnp.bfloat16), 'fsdp', scatter_dimension...]
    ppermute x3 -> x111, starting transfers between devices: 8.74 us -> 146 us  [the longest x71 118 us: send(): return lax.ppermute(value, 'fsdp', pairs)]
    pallas_call x0 -> x10, Pallas kernels: none -> 135 us  [the longest x1 50.6 us: delta_backward(): pl.pallas_call(partial(backward_kernel, heads, d), grid=(blocks,), in_spe...]
    unnamed x21 -> x0, waiting for transfers between devices: 97.6 us -> none
    all_gather x4 -> x0, blocking collectives: 92.5 us -> none  [the longest x1 30.7 us: on_device(): lax.all_gather(conv_taps, 'fsdp', axis=1, tiled=True)]
  transfers between devices with their start and end apart: 22 -> 115, of which waited for: 14 -> 55; matrix products, arithmetic and copies ran while one was open for 43% -> 21% of each run, Pallas kernels for 0% -> 13%
where the time goes in v1:
time: 836 us; the launch traced here: 831 us
  waiting for transfers between devices  280 us (33%)
  starting transfers between devices  170 us (20%)
  Pallas kernels  135 us (16%)
  matrix products  112 us (13%)
  other arithmetic  67 us (8%)
  local copies, waits for them, and re-layouts  63.6 us (8%)
    ppermute x71, waiting for transfers between devices, send(): return lax.ppermute(value, 'fsdp', pairs)  233 us
    ppermute x71, starting transfers between devices, send(): return lax.ppermute(value, 'fsdp', pairs)  118 us
    dot_general x25, matrix products, contract(): lax.dot_general(left, right, (((left_dim,), (right_dim,)), ((), ())), pre...  74.8 us
    pallas_call x1, Pallas kernels, delta_backward(): pl.pallas_call(partial(backward_kernel, heads, d), grid=(blocks,), in_spe...  50.6 us
    unnamed x236, local copies, waits for them, and re-layouts  40 us
    ppermute x37, waiting for transfers between devices, send(): return lax.ppermute(value, 'rep', pairs)  39.6 us
    pallas_call x4, Pallas kernels, gather_weights(): pl.pallas_call(partial(place_kernel, count, rows, each, by_rows, widths),...  26.4 us
    all_to_all x4, starting transfers between devices, swap(): return lax.all_to_all(value, 'fsdp', 0, 0, tiled=True)  24.6 us
  transfers between devices with their start and end apart: 115, of which 55 were waited for; matrix products, arithmetic and copies ran while one was open for 21% of the time, Pallas kernels for 13%

profile of v1, /device:TPU:0, one launch (start us, length us, event | category | flops | bytes accessed | tf_op | source)
XLA Modules:
  0.0 830.9 jit_solution(6678263861105721278)
XLA Ops:
  40.6 11.0 %collective-permute-start.8 = (bf16[32,3072]{1,0:T(8,128)(2,1)}, bf16[32,3072]{1,0:T(8,128)(2,1)S(1)}, u32[]{:S(2)}, u32[]{:S(2)}) collective-permute-start(bf16[32,3072]{1,0:T(8,128)(2,1)} %constant_dynamic-slice_fusion.13), channel_id=1, source_target_pairs={{0,2},{1,3},{2,4},{3,5},{4,6},{5,7},{6,0},{7,1},{8,10},{9,11},{10,... | collective-permute-start | bytes 589832 | tf_op jit(solution)/shard_map/ppermute | solution.py:378
  55.9 10.3 %collective-permute-start.9 = (bf16[32,3072]{1,0:T(8,128)(2,1)}, bf16[32,3072]{1,0:T(8,128)(2,1)S(1)}, u32[]{:S(2)}, u32[]{:S(2)}) collective-permute-start(bf16[32,3072]{1,0:T(8,128)(2,1)} %constant_dynamic-slice_fusion.13), channel_id=1, source_target_pairs={{0,4},{1,5},{2,6},{3,7},{4,0},{5,1},{6,2},{7,3},{8,12},{9,13},{10,... | collective-permute-start | bytes 589832 | tf_op jit(solution)/shard_map/ppermute | solution.py:378
  66.3 6.7 collective-permute-done.9
  75.0 3.9 collective-permute-done.10
  80.6 4.4 collective-permute-done.11
  85.1 9.5 %collective-permute-done.19 = bf16[64,2176]{1,0:T(8,128)(2,1)S(1)} collective-permute-done((bf16[64,2176]{1,0:T(8,128)(2,1)S(1)}, bf16[64,2176]{1,0:T(8,128)(2,1)S(1)}, u32[]{:S(2)}, u32[]{:S(2)}) %collective-permute-start.19) | collective-permute-done | bytes 278560 | tf_op jit(solution)/shard_map/ppermute | solution.py:378
  95.0 12.0 %collective-permute-done.20 = bf16[64,2176]{1,0:T(8,128)(2,1)S(1)} collective-permute-done((bf16[64,2176]{1,0:T(8,128)(2,1)S(1)}, bf16[64,2176]{1,0:T(8,128)(2,1)S(1)}, u32[]{:S(2)}, u32[]{:S(2)}) %collective-permute-start.20) | collective-permute-done | bytes 278560 | tf_op jit(solution)/shard_map/ppermute | solution.py:378
  107.0 6.5 collective-permute-done.21
  115.9 6.0 collective-permute-done.22
  137.9 10.3 %collective-permute-done.38 = bf16[352,512]{1,0:T(8,128)(2,1)S(1)} collective-permute-done((bf16[352,512]{1,0:T(8,128)(2,1)S(1)}, bf16[352,512]{1,0:T(8,128)(2,1)S(1)}, u32[]{:S(2)}, u32[]{:S(2)}) %collective-permute-start.38) | collective-permute-done | bytes 360480 | tf_op jit(solution)/shard_map/ppermute | solution.py:378
  157.5 4.5 collective-permute-done.23
  163.5 4.5 collective-permute-done.24
  169.5 4.5 collective-permute-done.25
  175.4 6.2 collective-permute-done.31
  183.9 5.5 collective-permute-done.32
  191.7 5.5 collective-permute-done.33
  197.9 6.9 collective-permute-done.41
  204.9 11.2 %collective-permute-done.15.refs_1_ = bf16[7,32,3072]{2,1,0:T(8,128)(2,1)} collective-permute-done((bf16[7,32,3072]{2,1,0:T(8,128)(2,1)S(1)}, bf16[7,32,3072]{2,1,0:T(8,128)(2,1)}, u32[]{:S(2)}, u32[]{:S(2)}) %collective-permute-start.15) | collective-permute-done | bytes 1376288 | tf_op jit(solution)/shard_map/ppermute | solution.py:392
  225.5 7.6 place_weights.4
  233.1 5.6 fusion.153
  238.7 6.8 fusion.2
  256.1 23.6 %delta_summary.1 = (bf16[512,1024]{1,0:T(8,128)(2,1)S(1)}, bf16[512,1024]{1,0:T(8,128)(2,1)S(1)}, bf16[8,512,64]{2,1,0:T(8,128)(2,1)S(1)}, bf16[8,128,256]{2,1,0:T(8,128)(2,1)S(1)}) custom-call(bf16[512,1024]{1,0:T(8,128)(2,1)S(1)} %get-tuple-element.139.k_ref, bf16[512,1024]{1,0:T(8,128)(2,1)S(1)} %slice.263.v_ref, ...), custom_call_target="tpu_custom_call" | custom-call | tf_op jit(solution)/shard_map/delta_summary/pallas_call | solution.py:262
  283.4 7.4 all-to-all-start
  295.0 4.6 fusion.56.gate_ref
  299.5 5.8 place_weights.7
  308.5 5.6 all-to-all-start.1
  314.0 8.6 %fusion.155 = f32[2816,512]{0,1:T(8,128)} fusion(bf16[2816,1024]{1,0:T(8,128)(2,1)} %place_weights.7, bf16[512,1024]{1,0:T(8,128)(2,1)} %param.27), kind=kOutput, calls=%fused_computation.350 | convolution fusion | flops 2952790016 | bytes 12582912 | tf_op jit(solution)/shard_map/dot_general | solution.py:563
  324.6 14.0 %delta_forward.1 = (bf16[512,1024]{1,0:T(8,128)(2,1)S(1)}, f32[512,1024]{1,0:T(8,128)}, bf16[512,1024]{1,0:T(8,128)(2,1)S(1)}, bf16[8,8,128,128]{3,2,1,0:T(8,128)(2,1)}) custom-call(bf16[512,1024]{1,0:T(8,128)(2,1)S(1)} %get-tuple-element.140.q_ref, bf16[512,1024]{1,0:T(8,128)(2,1)S(1)} %get-tuple-element.139.k_ref, bf16[512,1024]{1,0:T(8,128)(2,1)S(1)} %copy-done.1, ...), custom_call_target="tpu_custom_call" | custom-call | tf_op jit(solution)/shard_map/delta_forward/pallas_call | solution.py:283
  344.3 9.3 %place_weights.6 = (bf16[1024,2816]{1,0:T(8,128)(2,1)}, bf16[1024,2816]{1,0:T(8,128)(2,1)}) custom-call(s32[29]{0:T(128)S(1)} %stack.420.offs_ref, bf16[128,5632]{1,0:T(8,128)(2,1)S(1)} %copy-done.5, bf16[7,32,5632]{2,1,0:T(8,128)(2,1)} %bitcast_dynamic-update-slice_fusion.7.refs_0_, bf16[7,32,5632]{2,1,0:T(8,128)(2,1)} %collective-permute-done.34.refs_1_, ...), custom_call_target="tpu_custom_call" | custom-call | tf_op jit(solution)/shard_map/place_weights/pallas_call | solution.py:471
  353.6 7.7 fusion.154
  361.3 11.0 %fusion.5 = (bf16[512,2816]{1,0:T(8,128)(2,1)}, bf16[512,2816]{1,0:T(8,128)(2,1)}, bf16[512,2816]{1,0:T(8,128)(2,1)}) fusion(f32[512,2816]{1,0:T(8,128)} %fusion.154, f32[2816,512]{0,1:T(8,128)} %fusion.155, bf16[512,1024]{1,0:T(8,128)(2,1)S(1)} %multiply_convert_fusion.1, bf16[1024,2816]{1,0:T(8,128)(2,1)S(1)} %copy-done.82), kind=kOutput, calls=%fused_computation.18 | convolution fusion | flops 2975858688 | bytes 27000832 | tf_op jit(solution)/shard_map/dot_general | solution.py:732
  372.4 6.1 add_convert_fusion.9
  393.5 14.9 %delta_adjoint.1 = (bf16[512,1024]{1,0:T(8,128)(2,1)S(1)}, bf16[512,1024]{1,0:T(8,128)(2,1)S(1)}, f32[1,128]{1,0:T(1,128)S(1)}, bf16[8,128,128]{2,1,0:T(8,128)(2,1)S(1)}) custom-call(bf16[512,1024]{1,0:T(8,128)(2,1)S(1)} %get-tuple-element.140.q_ref, bf16[512,1024]{1,0:T(8,128)(2,1)S(1)} %get-tuple-element.139.k_ref, bf16[512,1024]{1,0:T(8,128)(2,1)S(1)} %copy-done.2, ...), custom_call_target="tpu_custom_call" | custom-call | tf_op jit(solution)/shard_map/delta_adjoint/pallas_call | solution.py:304
  411.1 5.3 all-to-all-start.2
  420.0 4.8 convolution_convert_fusion.1
  427.9 6.3 all-to-all-start.3
  437.5 5.1 convolution_convert_fusion.2
  445.8 50.6 %delta_backward.1 = (f32[512,1024]{1,0:T(8,128)}, f32[512,1024]{1,0:T(8,128)}, f32[512,1024]{1,0:T(8,128)}, f32[512,128]{1,0:T(8,128)S(1)}) custom-call(bf16[512,1024]{1,0:T(8,128)(2,1)S(1)} %get-tuple-element.140.q_ref, bf16[512,1024]{1,0:T(8,128)(2,1)S(1)} %get-tuple-element.139.k_ref, bf16[512,1024]{1,0:T(8,128)(2,1)S(1)} %slice.263.v_ref, ...), custom_call_target="tpu_custom_call" | custom-call | tf_op jit(solution)/shard_map/delta_backward/pallas_call | solution.py:325
  505.2 5.1 add_add_fusion.1
  510.5 7.5 multiply_reduce_fusion.3
  518.0 7.2 multiply_multiply_fusion.3
  525.2 6.5 add_convert_fusion
  532.2 6.8 fusion.158
  549.2 3.8 collective-permute-done.45
  553.0 6.2 fusion.20
  561.2 5.0 fusion.16
  585.1 10.5 %collective-permute-done.82 = bf16[4,128,512]{2,1,0:T(8,128)(2,1)S(1)} collective-permute-done((bf16[4,128,512]{2,1,0:T(8,128)(2,1)}, bf16[4,128,512]{2,1,0:T(8,128)(2,1)S(1)}, u32[]{:S(2)}, u32[]{:S(2)}) %collective-permute-start.82) | collective-permute-done | bytes 524320 | tf_op jit(solution)/shard_map/ppermute | solution.py:385
  598.3 6.2 collective-permute-done.75
  607.4 6.5 collective-permute-done.85
  614.1 4.1 collective-permute-done.77
  637.9 4.9 collective-permute-done.68
  642.8 10.8 %collective-permute-done.69 = bf16[2,128,512]{2,1,0:T(8,128)(2,1)S(1)} collective-permute-done((bf16[2,128,512]{2,1,0:T(8,128)(2,1)S(1)}, bf16[2,128,512]{2,1,0:T(8,128)(2,1)S(1)}, u32[]{:S(2)}, u32[]{:S(2)}) %collective-permute-start.69) | collective-permute-done | bytes 262176 | tf_op jit(solution)/shard_map/ppermute | solution.py:378
  659.1 11.6 %collective-permute-done.71 = bf16[128,512]{1,0:T(8,128)(2,1)S(1)} collective-permute-done((bf16[128,512]{1,0:T(8,128)(2,1)S(1)}, bf16[128,512]{1,0:T(8,128)(2,1)S(1)}, u32[]{:S(2)}, u32[]{:S(2)}) %collective-permute-start.71) | collective-permute-done | bytes 131104 | tf_op jit(solution)/shard_map/ppermute | solution.py:385
  672.5 5.6 collective-permute-start.62
  683.0 3.8 collective-permute-done.63
  693.6 4.6 collective-permute-done.65
  719.6 23.2 %collective-permute-done.105 = bf16[4,352,512]{2,1,0:T(8,128)(2,1)S(1)} collective-permute-done((bf16[4,352,512]{2,1,0:T(8,128)(2,1)S(1)}, bf16[4,352,512]{2,1,0:T(8,128)(2,1)S(1)}, u32[]{:S(2)}, u32[]{:S(2)}) %collective-permute-start.105) | collective-permute-done | bytes 1441824 | tf_op jit(solution)/shard_map/ppermute | solution.py:385
  748.7 8.0 collective-permute-done.106
  756.7 13.7 %collective-permute-done.107 = bf16[352,512]{1,0:T(8,128)(2,1)S(1)} collective-permute-done((bf16[352,512]{1,0:T(8,128)(2,1)S(1)}, bf16[352,512]{1,0:T(8,128)(2,1)S(1)}, u32[]{:S(2)}, u32[]{:S(2)}) %collective-permute-start.107) | collective-permute-done | bytes 360480 | tf_op jit(solution)/shard_map/ppermute | solution.py:378
  772.1 5.9 collective-permute-done.89
  779.6 5.3 collective-permute-done.109
  795.1 3.8 collective-permute-start.91
  799.4 5.8 collective-permute-start.93
  809.1 8.2 collective-permute-done.92
  (606 shorter events, 297.2 us)
Async XLA Ops:
  3.5 22.6 %collective-permute-start = (bf16[1808]{0:T(1024)(128)(2,1)S(1)}, bf16[1808]{0:T(1024)(128)(2,1)S(1)}, u32[]{:S(2)}, u32[]{:S(2)}) collective-permute-start(bf16[1808]{0:T(1024)(128)(2,1)S(1)} %concatenate.97), channel_id=1, source_target_pairs={{0,2},{1,3},{2,4},{3,5},{4,6},{5,7},{6,0},{7,1},{8,10},{9,11},{10,... | collective-permute-start | bytes 10856 | tf_op jit(solution)/shard_map/ppermute | solution.py:378
  6.5 20.8 %collective-permute-start.1 = (bf16[1808]{0:T(1024)(128)(2,1)S(1)}, bf16[1808]{0:T(1024)(128)(2,1)S(1)}, u32[]{:S(2)}, u32[]{:S(2)}) collective-permute-start(bf16[1808]{0:T(1024)(128)(2,1)S(1)} %concatenate.97), channel_id=1, source_target_pairs={{0,4},{1,5},{2,6},{3,7},{4,0},{5,1},{6,2},{7,3},{8,12},{9,13},{10,... | collective-permute-start | bytes 10856 | tf_op jit(solution)/shard_map/ppermute | solution.py:378
  9.1 19.0 %collective-permute-start.2 = (bf16[1808]{0:T(1024)(128)(2,1)S(1)}, bf16[1808]{0:T(1024)(128)(2,1)S(1)}, u32[]{:S(2)}, u32[]{:S(2)}) collective-permute-start(bf16[1808]{0:T(1024)(128)(2,1)S(1)} %concatenate.97), channel_id=1, source_target_pairs={{0,6},{1,7},{2,0},{3,1},{4,2},{5,3},{6,4},{7,5},{8,14},{9,15},{10,... | collective-permute-start | bytes 10856 | tf_op jit(solution)/shard_map/ppermute | solution.py:378
  10.5 20.5 %collective-permute-start.3 = (bf16[1808]{0:T(1024)(128)(2,1)S(1)}, bf16[1808]{0:T(1024)(128)(2,1)S(1)}, u32[]{:S(2)}, u32[]{:S(2)}) collective-permute-start(bf16[1808]{0:T(1024)(128)(2,1)S(1)} %concatenate.97), channel_id=1, source_target_pairs={{0,1},{1,0},{2,3},{3,2},{4,5},{5,4},{6,7},{7,6},{8,9},{9,8},{10,11... | collective-permute-start | bytes 10856 | tf_op jit(solution)/shard_map/ppermute | solution.py:385
  25.3 96.6 %collective-permute-start.27 = (bf16[32,5632]{1,0:T(8,128)(2,1)}, bf16[32,5632]{1,0:T(8,128)(2,1)}, u32[]{:S(2)}, u32[]{:S(2)}) collective-permute-start(bf16[32,5632]{1,0:T(8,128)(2,1)} %constant_dynamic-slice_fusion.11), channel_id=1, source_target_pairs={{0,2},{1,3},{2,4},{3,5},{4,6},{5,7},{6,0},{7,1},{8,10},{9,11},{10,... | collective-permute-start | bytes 1081352 | tf_op jit(solution)/shard_map/ppermute | solution.py:378
  31.0 95.4 %collective-permute-start.28 = (bf16[32,5632]{1,0:T(8,128)(2,1)}, bf16[32,5632]{1,0:T(8,128)(2,1)}, u32[]{:S(2)}, u32[]{:S(2)}) collective-permute-start(bf16[32,5632]{1,0:T(8,128)(2,1)} %constant_dynamic-slice_fusion.11), channel_id=1, source_target_pairs={{0,4},{1,5},{2,6},{3,7},{4,0},{5,1},{6,2},{7,3},{8,12},{9,13},{10,... | collective-permute-start | bytes 1081352 | tf_op jit(solution)/shard_map/ppermute | solution.py:378
  31.2 98.6 %collective-permute-start.29 = (bf16[32,5632]{1,0:T(8,128)(2,1)}, bf16[32,5632]{1,0:T(8,128)(2,1)}, u32[]{:S(2)}, u32[]{:S(2)}) collective-permute-start(bf16[32,5632]{1,0:T(8,128)(2,1)} %constant_dynamic-slice_fusion.11), channel_id=1, source_target_pairs={{0,6},{1,7},{2,0},{3,1},{4,2},{5,3},{6,4},{7,5},{8,14},{9,15},{10,... | collective-permute-start | bytes 1081352 | tf_op jit(solution)/shard_map/ppermute | solution.py:378
  34.7 98.6 %collective-permute-start.30 = (bf16[32,5632]{1,0:T(8,128)(2,1)}, bf16[32,5632]{1,0:T(8,128)(2,1)}, u32[]{:S(2)}, u32[]{:S(2)}) collective-permute-start(bf16[32,5632]{1,0:T(8,128)(2,1)} %constant_dynamic-slice_fusion.11), channel_id=1, source_target_pairs={{0,1},{1,0},{2,3},{3,2},{4,5},{5,4},{6,7},{7,6},{8,9},{9,8},{10,11... | collective-permute-start | bytes 1081352 | tf_op jit(solution)/shard_map/ppermute | solution.py:385
  40.6 15.3 %collective-permute-start.8 = (bf16[32,3072]{1,0:T(8,128)(2,1)}, bf16[32,3072]{1,0:T(8,128)(2,1)S(1)}, u32[]{:S(2)}, u32[]{:S(2)}) collective-permute-start(bf16[32,3072]{1,0:T(8,128)(2,1)} %constant_dynamic-slice_fusion.13), channel_id=1, source_target_pairs={{0,2},{1,3},{2,4},{3,5},{4,6},{5,7},{6,0},{7,1},{8,10},{9,11},{10,... | collective-permute-start | bytes 589832 | tf_op jit(solution)/shard_map/ppermute | solution.py:378
  55.9 17.1 %collective-permute-start.9 = (bf16[32,3072]{1,0:T(8,128)(2,1)}, bf16[32,3072]{1,0:T(8,128)(2,1)S(1)}, u32[]{:S(2)}, u32[]{:S(2)}) collective-permute-start(bf16[32,3072]{1,0:T(8,128)(2,1)} %constant_dynamic-slice_fusion.13), channel_id=1, source_target_pairs={{0,4},{1,5},{2,6},{3,7},{4,0},{5,1},{6,2},{7,3},{8,12},{9,13},{10,... | collective-permute-start | bytes 589832 | tf_op jit(solution)/shard_map/ppermute | solution.py:378
  122.0 26.3 %collective-permute-start.38 = (bf16[352,512]{1,0:T(8,128)(2,1)S(1)}, bf16[352,512]{1,0:T(8,128)(2,1)S(1)}, u32[]{:S(2)}, u32[]{:S(2)}) collective-permute-start(bf16[352,512]{1,0:T(8,128)(2,1)S(1)} %copy-done.54), channel_id=1, source_target_pairs={{0,4},{1,5},{2,6},{3,7},{4,0},{5,1},{6,2},{7,3},{8,12},{9,13},{10,... | collective-permute-start | bytes 1081352 | tf_op jit(solution)/shard_map/ppermute | solution.py:378
  126.4 24.1 %collective-permute-start.39 = (bf16[352,512]{1,0:T(8,128)(2,1)S(1)}, bf16[352,512]{1,0:T(8,128)(2,1)S(1)}, u32[]{:S(2)}, u32[]{:S(2)}) collective-permute-start(bf16[352,512]{1,0:T(8,128)(2,1)S(1)} %copy-done.54), channel_id=1, source_target_pairs={{0,6},{1,7},{2,0},{3,1},{4,2},{5,3},{6,4},{7,5},{8,14},{9,15},{10,... | collective-permute-start | bytes 1081352 | tf_op jit(solution)/shard_map/ppermute | solution.py:378
  129.8 22.0 %collective-permute-start.40 = (bf16[352,512]{1,0:T(8,128)(2,1)S(1)}, bf16[352,512]{1,0:T(8,128)(2,1)S(1)}, u32[]{:S(2)}, u32[]{:S(2)}) collective-permute-start(bf16[352,512]{1,0:T(8,128)(2,1)S(1)} %copy-done.54), channel_id=1, source_target_pairs={{0,1},{1,0},{2,3},{3,2},{4,5},{5,4},{6,7},{7,6},{8,9},{9,8},{10,11... | collective-permute-start | bytes 1081352 | tf_op jit(solution)/shard_map/ppermute | solution.py:385
  133.3 20.7 %collective-permute-start.12 = (bf16[32,3072]{1,0:T(8,128)(2,1)S(1)}, bf16[32,3072]{1,0:T(8,128)(2,1)S(1)}, u32[]{:S(2)}, u32[]{:S(2)}) collective-permute-start(bf16[32,3072]{1,0:T(8,128)(2,1)S(1)} %collective-permute-done.8), channel_id=1, source_target_pairs={{0,1},{1,0},{2,3},{3,2},{4,5},{5,4},{6,7},{7,6},{8,9},{9,8},{10,11... | collective-permute-start | bytes 589832 | tf_op jit(solution)/shard_map/ppermute | solution.py:385
  135.3 19.2 %collective-permute-start.13 = (bf16[32,3072]{1,0:T(8,128)(2,1)S(1)}, bf16[32,3072]{1,0:T(8,128)(2,1)S(1)}, u32[]{:S(2)}, u32[]{:S(2)}) collective-permute-start(bf16[32,3072]{1,0:T(8,128)(2,1)S(1)} %collective-permute-done.9), channel_id=1, source_target_pairs={{0,1},{1,0},{2,3},{3,2},{4,5},{5,4},{6,7},{7,6},{8,9},{9,8},{10,11... | collective-permute-start | bytes 589832 | tf_op jit(solution)/shard_map/ppermute | solution.py:385
  151.8 16.2 %collective-permute-start.24 = (bf16[64,2176]{1,0:T(8,128)(2,1)S(1)}, bf16[64,2176]{1,0:T(8,128)(2,1)S(1)}, u32[]{:S(2)}, u32[]{:S(2)}) collective-permute-start(bf16[64,2176]{1,0:T(8,128)(2,1)S(1)} %collective-permute-done.20), channel_id=1, source_target_pairs={{0,1},{1,0},{2,3},{3,2},{4,5},{5,4},{6,7},{7,6},{8,9},{9,8},{10,11... | collective-permute-start | bytes 835592 | tf_op jit(solution)/shard_map/ppermute | solution.py:385
  154.0 20.0 %collective-permute-start.25 = (bf16[64,2176]{1,0:T(8,128)(2,1)S(1)}, bf16[64,2176]{1,0:T(8,128)(2,1)S(1)}, u32[]{:S(2)}, u32[]{:S(2)}) collective-permute-start(bf16[64,2176]{1,0:T(8,128)(2,1)S(1)} %collective-permute-done.21), channel_id=1, source_target_pairs={{0,1},{1,0},{2,3},{3,2},{4,5},{5,4},{6,7},{7,6},{8,9},{9,8},{10,11... | collective-permute-start | bytes 835592 | tf_op jit(solution)/shard_map/ppermute | solution.py:385
  154.6 27.1 %collective-permute-start.31 = (bf16[32,5632]{1,0:T(8,128)(2,1)}, bf16[32,5632]{1,0:T(8,128)(2,1)S(1)}, u32[]{:S(2)}, u32[]{:S(2)}) collective-permute-start(bf16[32,5632]{1,0:T(8,128)(2,1)} %collective-permute-done.27), channel_id=1, source_target_pairs={{0,1},{1,0},{2,3},{3,2},{4,5},{5,4},{6,7},{7,6},{8,9},{9,8},{10,11... | collective-permute-start | bytes 1081352 | tf_op jit(solution)/shard_map/ppermute | solution.py:385
  156.1 33.3 %collective-permute-start.32 = (bf16[32,5632]{1,0:T(8,128)(2,1)}, bf16[32,5632]{1,0:T(8,128)(2,1)S(1)}, u32[]{:S(2)}, u32[]{:S(2)}) collective-permute-start(bf16[32,5632]{1,0:T(8,128)(2,1)} %collective-permute-done.28), channel_id=1, source_target_pairs={{0,1},{1,0},{2,3},{3,2},{4,5},{5,4},{6,7},{7,6},{8,9},{9,8},{10,11... | collective-permute-start | bytes 1081352 | tf_op jit(solution)/shard_map/ppermute | solution.py:385
  162.0 35.1 %collective-permute-start.33 = (bf16[32,5632]{1,0:T(8,128)(2,1)}, bf16[32,5632]{1,0:T(8,128)(2,1)S(1)}, u32[]{:S(2)}, u32[]{:S(2)}) collective-permute-start(bf16[32,5632]{1,0:T(8,128)(2,1)} %collective-permute-done.29), channel_id=1, source_target_pairs={{0,1},{1,0},{2,3},{3,2},{4,5},{5,4},{6,7},{7,6},{8,9},{9,8},{10,11... | collective-permute-start | bytes 1081352 | tf_op jit(solution)/shard_map/ppermute | solution.py:385
  168.0 36.9 %collective-permute-start.41 = (bf16[352,512]{1,0:T(8,128)(2,1)S(1)}, bf16[352,512]{1,0:T(8,128)(2,1)S(1)}, u32[]{:S(2)}, u32[]{:S(2)}) collective-permute-start(bf16[352,512]{1,0:T(8,128)(2,1)S(1)} %collective-permute-done.37), channel_id=1, source_target_pairs={{0,1},{1,0},{2,3},{3,2},{4,5},{5,4},{6,7},{7,6},{8,9},{9,8},{10,11... | collective-permute-start | bytes 1081352 | tf_op jit(solution)/shard_map/ppermute | solution.py:385
  174.0 42.9 %collective-permute-start.42 = (bf16[352,512]{1,0:T(8,128)(2,1)S(1)}, bf16[352,512]{1,0:T(8,128)(2,1)S(1)}, u32[]{:S(2)}, u32[]{:S(2)}) collective-permute-start(bf16[352,512]{1,0:T(8,128)(2,1)S(1)} %collective-permute-done.38), channel_id=1, source_target_pairs={{0,1},{1,0},{2,3},{3,2},{4,5},{5,4},{6,7},{7,6},{8,9},{9,8},{10,11... | collective-permute-start | bytes 1081352 | tf_op jit(solution)/shard_map/ppermute | solution.py:385
  181.7 37.4 %collective-permute-start.43 = (bf16[352,512]{1,0:T(8,128)(2,1)S(1)}, bf16[352,512]{1,0:T(8,128)(2,1)S(1)}, u32[]{:S(2)}, u32[]{:S(2)}) collective-permute-start(bf16[352,512]{1,0:T(8,128)(2,1)S(1)} %collective-permute-done.39), channel_id=1, source_target_pairs={{0,1},{1,0},{2,3},{3,2},{4,5},{5,4},{6,7},{7,6},{8,9},{9,8},{10,11... | collective-permute-start | bytes 1081352 | tf_op jit(solution)/shard_map/ppermute | solution.py:385
  189.4 26.6 %collective-permute-start.15 = (bf16[7,32,3072]{2,1,0:T(8,128)(2,1)S(1)}, bf16[7,32,3072]{2,1,0:T(8,128)(2,1)}, u32[]{:S(2)}, u32[]{:S(2)}) collective-permute-start(bf16[7,32,3072]{2,1,0:T(8,128)(2,1)S(1)} %bitcast_dynamic-update-slice_fusion.21.refs_0_), channel_id=1, source_target_pairs={{0,16},{8,24},{16,0},{24,8},{1,17},{9,25},{17,1},{25,9},{2,18},{10... | collective-permute-start | bytes 4128776 | tf_op jit(solution)/shard_map/ppermute | solution.py:392
  197.1 22.9 %collective-permute-start.26 = (bf16[7,64,2176]{2,1,0:T(8,128)(2,1)S(1)}, bf16[7,64,2176]{2,1,0:T(8,128)(2,1)S(1)}, u32[]{:S(2)}, u32[]{:S(2)}) collective-permute-start(bf16[7,64,2176]{2,1,0:T(8,128)(2,1)S(1)} %bitcast_dynamic-update-slice_fusion.14.refs_0_), channel_id=1, source_target_pairs={{0,8},{8,0},{16,24},{24,16},{1,9},{9,1},{17,25},{25,17},{2,10},{10... | collective-permute-start | bytes 5849096 | tf_op jit(solution)/shard_map/ppermute | solution.py:398
  204.9 20.6 %collective-permute-start.16 = (bf16[7,32,3072]{2,1,0:T(8,128)(2,1)S(1)}, bf16[7,32,3072]{2,1,0:T(8,128)(2,1)}, u32[]{:S(2)}, u32[]{:S(2)}) collective-permute-start(bf16[7,32,3072]{2,1,0:T(8,128)(2,1)S(1)} %bitcast_dynamic-update-slice_fusion.21.refs_0_), channel_id=1, source_target_pairs={{0,8},{8,0},{16,24},{24,16},{1,9},{9,1},{17,25},{25,17},{2,10},{10... | collective-permute-start | bytes 4128776 | tf_op jit(solution)/shard_map/ppermute | solution.py:398
  216.8 74.1 %collective-permute-start.34 = (bf16[7,32,5632]{2,1,0:T(8,128)(2,1)}, bf16[7,32,5632]{2,1,0:T(8,128)(2,1)}, u32[]{:S(2)}, u32[]{:S(2)}) collective-permute-start(bf16[7,32,5632]{2,1,0:T(8,128)(2,1)} %bitcast_dynamic-update-slice_fusion.7.refs_0_), channel_id=1, source_target_pairs={{0,16},{8,24},{16,0},{24,8},{1,17},{9,25},{17,1},{25,9},{2,18},{10... | collective-permute-start | bytes 7569416 | tf_op jit(solution)/shard_map/ppermute | solution.py:392
  219.8 79.7 %collective-permute-start.44 = (bf16[7,352,512]{2,1,0:T(8,128)(2,1)}, bf16[7,352,512]{2,1,0:T(8,128)(2,1)}, u32[]{:S(2)}, u32[]{:S(2)}) collective-permute-start(bf16[7,352,512]{2,1,0:T(8,128)(2,1)} %bitcast_dynamic-update-slice_fusion.refs_0_), channel_id=1, source_target_pairs={{0,8},{8,0},{16,24},{24,16},{1,9},{9,1},{17,25},{25,17},{2,10},{10... | collective-permute-start | bytes 7569416 | tf_op jit(solution)/shard_map/ppermute | solution.py:398
  283.4 22.4 %all-to-all-start = ((bf16[8,128,256]{2,1,0:T(8,128)(2,1)}), bf16[8,128,256]{2,1,0:T(8,128)(2,1)}, u32[]{:S(2)}, u32[]{:S(2)}) async-start(bf16[8,128,256]{2,1,0:T(8,128)(2,1)} %copy-done.14), calls=%async_computation | async-start | bytes 1048576 | tf_op jit(solution)/shard_map/all_to_all | solution.py:611
  290.8 51.4 %collective-permute-start.35 = (bf16[7,32,5632]{2,1,0:T(8,128)(2,1)}, bf16[7,32,5632]{2,1,0:T(8,128)(2,1)}, u32[]{:S(2)}, u32[]{:S(2)}) collective-permute-start(bf16[7,32,5632]{2,1,0:T(8,128)(2,1)} %bitcast_dynamic-update-slice_fusion.7.refs_0_), channel_id=1, source_target_pairs={{0,8},{8,0},{16,24},{24,16},{1,9},{9,1},{17,25},{25,17},{2,10},{10... | collective-permute-start | bytes 7569416 | tf_op jit(solution)/shard_map/ppermute | solution.py:398
  290.9 51.3 %collective-permute-start.36 = (bf16[7,32,5632]{2,1,0:T(8,128)(2,1)}, bf16[7,32,5632]{2,1,0:T(8,128)(2,1)}, u32[]{:S(2)}, u32[]{:S(2)}) collective-permute-start(bf16[7,32,5632]{2,1,0:T(8,128)(2,1)} %collective-permute-done.34.refs_1_), channel_id=1, source_target_pairs={{0,8},{8,0},{16,24},{24,16},{1,9},{9,1},{17,25},{25,17},{2,10},{10... | collective-permute-start | bytes 7569416 | tf_op jit(solution)/shard_map/ppermute | solution.py:398
  308.5 14.9 %all-to-all-start.1 = ((bf16[8,128,128]{2,1,0:T(8,128)(2,1)}), bf16[8,128,128]{2,1,0:T(8,128)(2,1)}, u32[]{:S(2)}, u32[]{:S(2)}) async-start(bf16[8,128,128]{2,1,0:T(8,128)(2,1)} %state_prefix.1), calls=%async_computation.1 | async-start | bytes 524288 | tf_op jit(solution)/shard_map/all_to_all | solution.py:611
  411.1 14.0 %all-to-all-start.2 = ((bf16[8,128,128]{2,1,0:T(8,128)(2,1)}), bf16[8,128,128]{2,1,0:T(8,128)(2,1)}, u32[]{:S(2)}, u32[]{:S(2)}) async-start(bf16[8,128,128]{2,1,0:T(8,128)(2,1)} %copy-done.19), calls=%async_computation.2 | async-start | bytes 524288 | tf_op jit(solution)/shard_map/all_to_all | solution.py:611
  419.5 285.9 %collective-permute-start.104 = (bf16[2816,512]{1,0:T(8,128)(2,1)}, bf16[2816,512]{1,0:T(8,128)(2,1)}, u32[]{:S(2)}, u32[]{:S(2)}) collective-permute-start(bf16[2816,512]{1,0:T(8,128)(2,1)} %convolution_convert_fusion), channel_id=1, source_target_pairs={{0,8},{8,0},{16,24},{24,16},{1,9},{9,1},{17,25},{25,17},{2,10},{10... | collective-permute-start | bytes 8650760 | tf_op jit(solution)/shard_map/ppermute | solution.py:398
  419.5 149.3 %collective-permute-start.81 = (bf16[1024,512]{1,0:T(8,128)(2,1)}, bf16[1024,512]{1,0:T(8,128)(2,1)}, u32[]{:S(2)}, u32[]{:S(2)}) collective-permute-start(bf16[1024,512]{1,0:T(8,128)(2,1)} %convolution_convert_fusion.3), channel_id=1, source_target_pairs={{0,8},{8,0},{16,24},{24,16},{1,9},{9,1},{17,25},{25,17},{2,10},{10... | collective-permute-start | bytes 3145736 | tf_op jit(solution)/shard_map/ppermute | solution.py:398
  427.9 15.5 %all-to-all-start.3 = ((bf16[8,128,128]{2,1,0:T(8,128)(2,1)}), bf16[8,128,128]{2,1,0:T(8,128)(2,1)}, u32[]{:S(2)}, u32[]{:S(2)}) async-start(bf16[8,128,128]{2,1,0:T(8,128)(2,1)} %state_suffix.1), calls=%async_computation.3 | async-start | bytes 524288 | tf_op jit(solution)/shard_map/all_to_all | solution.py:611
  437.3 133.5 %collective-permute-start.74 = (bf16[1024,512]{1,0:T(8,128)(2,1)}, bf16[1024,512]{1,0:T(8,128)(2,1)}, u32[]{:S(2)}, u32[]{:S(2)}) collective-permute-start(bf16[1024,512]{1,0:T(8,128)(2,1)} %convolution_convert_fusion.4), channel_id=1, source_target_pairs={{0,8},{8,0},{16,24},{24,16},{1,9},{9,1},{17,25},{25,17},{2,10},{10... | collective-permute-start | bytes 3145736 | tf_op jit(solution)/shard_map/ppermute | solution.py:398
  547.4 81.8 %collective-permute-start.67 = (bf16[1024,512]{1,0:T(8,128)(2,1)}, bf16[1024,512]{1,0:T(8,128)(2,1)}, u32[]{:S(2)}, u32[]{:S(2)}) collective-permute-start(bf16[1024,512]{1,0:T(8,128)(2,1)} %convolution_convert_fusion.5), channel_id=1, source_target_pairs={{0,8},{8,0},{16,24},{24,16},{1,9},{9,1},{17,25},{25,17},{2,10},{10... | collective-permute-start | bytes 3145736 | tf_op jit(solution)/shard_map/ppermute | solution.py:398
  580.5 15.1 %collective-permute-start.82 = (bf16[4,128,512]{2,1,0:T(8,128)(2,1)}, bf16[4,128,512]{2,1,0:T(8,128)(2,1)S(1)}, u32[]{:S(2)}, u32[]{:S(2)}) collective-permute-start(bf16[4,128,512]{2,1,0:T(8,128)(2,1)} %dynamic-slice_bitcast_fusion.3), channel_id=1, source_target_pairs={{0,1},{1,0},{2,3},{3,2},{4,5},{5,4},{6,7},{7,6},{8,9},{9,8},{10,11... | collective-permute-start | bytes 1572872 | tf_op jit(solution)/shard_map/ppermute | solution.py:385
  581.9 22.6 %collective-permute-start.75 = (bf16[4,128,512]{2,1,0:T(8,128)(2,1)}, bf16[4,128,512]{2,1,0:T(8,128)(2,1)S(1)}, u32[]{:S(2)}, u32[]{:S(2)}) collective-permute-start(bf16[4,128,512]{2,1,0:T(8,128)(2,1)} %dynamic-slice_bitcast_fusion.4), channel_id=1, source_target_pairs={{0,1},{1,0},{2,3},{3,2},{4,5},{5,4},{6,7},{7,6},{8,9},{9,8},{10,11... | collective-permute-start | bytes 1572872 | tf_op jit(solution)/shard_map/ppermute | solution.py:385
  614.0 18.9 %collective-permute-start.52 = (bf16[1024,512]{1,0:T(8,128)(2,1)S(1)}, bf16[1024,512]{1,0:T(8,128)(2,1)S(1)}, u32[]{:S(2)}, u32[]{:S(2)}) collective-permute-start(bf16[1024,512]{1,0:T(8,128)(2,1)S(1)} %copy-done.88), channel_id=1, source_target_pairs={{0,8},{8,0},{16,24},{24,16},{1,9},{9,1},{17,25},{25,17},{2,10},{10... | collective-permute-start | bytes 3145736 | tf_op jit(solution)/shard_map/ppermute | solution.py:398
  618.2 18.4 %collective-permute-start.60 = (bf16[1024,512]{1,0:T(8,128)(2,1)S(1)}, bf16[1024,512]{1,0:T(8,128)(2,1)S(1)}, u32[]{:S(2)}, u32[]{:S(2)}) collective-permute-start(bf16[1024,512]{1,0:T(8,128)(2,1)S(1)} %copy-done.87), channel_id=1, source_target_pairs={{0,8},{8,0},{16,24},{24,16},{1,9},{9,1},{17,25},{25,17},{2,10},{10... | collective-permute-start | bytes 3145736 | tf_op jit(solution)/shard_map/ppermute | solution.py:398
  629.1 80.7 %collective-permute-start.96 = (bf16[1024,1408]{1,0:T(8,128)(2,1)S(1)}, bf16[1024,1408]{1,0:T(8,128)(2,1)S(1)}, u32[]{:S(2)}, u32[]{:S(2)}) collective-permute-start(bf16[1024,1408]{1,0:T(8,128)(2,1)S(1)} %copy-done.84), channel_id=1, source_target_pairs={{0,8},{8,0},{16,24},{24,16},{1,9},{9,1},{17,25},{25,17},{2,10},{10... | collective-permute-start | bytes 8650760 | tf_op jit(solution)/shard_map/ppermute | solution.py:398
  632.9 20.7 %collective-permute-start.69 = (bf16[2,128,512]{2,1,0:T(8,128)(2,1)S(1)}, bf16[2,128,512]{2,1,0:T(8,128)(2,1)S(1)}, u32[]{:S(2)}, u32[]{:S(2)}) collective-permute-start(bf16[2,128,512]{2,1,0:T(8,128)(2,1)S(1)} %get-tuple-element.155), channel_id=1, source_target_pairs={{0,4},{1,5},{2,6},{3,7},{4,0},{5,1},{6,2},{7,3},{8,12},{9,13},{10,... | collective-permute-start | bytes 786440 | tf_op jit(solution)/shard_map/ppermute | solution.py:378
  636.5 17.1 %collective-permute-start.70 = (bf16[2,128,512]{2,1,0:T(8,128)(2,1)S(1)}, bf16[2,128,512]{2,1,0:T(8,128)(2,1)S(1)}, u32[]{:S(2)}, u32[]{:S(2)}) collective-permute-start(bf16[2,128,512]{2,1,0:T(8,128)(2,1)S(1)} %get-tuple-element.154), channel_id=1, source_target_pairs={{0,6},{1,7},{2,0},{3,1},{4,2},{5,3},{6,4},{7,5},{8,14},{9,15},{10,... | collective-permute-start | bytes 786440 | tf_op jit(solution)/shard_map/ppermute | solution.py:378
  653.6 18.7 %collective-permute-start.61 = (bf16[4,128,512]{2,1,0:T(8,128)(2,1)S(1)}, bf16[4,128,512]{2,1,0:T(8,128)(2,1)S(1)}, u32[]{:S(2)}, u32[]{:S(2)}) collective-permute-start(bf16[4,128,512]{2,1,0:T(8,128)(2,1)S(1)} %dynamic-slice_bitcast_fusion.5), channel_id=1, source_target_pairs={{0,1},{1,0},{2,3},{3,2},{4,5},{5,4},{6,7},{7,6},{8,9},{9,8},{10,11... | collective-permute-start | bytes 1572872 | tf_op jit(solution)/shard_map/ppermute | solution.py:385
  654.2 16.5 %collective-permute-start.71 = (bf16[128,512]{1,0:T(8,128)(2,1)S(1)}, bf16[128,512]{1,0:T(8,128)(2,1)S(1)}, u32[]{:S(2)}, u32[]{:S(2)}) collective-permute-start(bf16[128,512]{1,0:T(8,128)(2,1)S(1)} %dynamic-slice_bitcast_fusion.25), channel_id=1, source_target_pairs={{0,1},{1,0},{2,3},{3,2},{4,5},{5,4},{6,7},{7,6},{8,9},{9,8},{10,11... | collective-permute-start | bytes 393224 | tf_op jit(solution)/shard_map/ppermute | solution.py:385
  656.8 21.3 %collective-permute-start.53 = (bf16[4,2,64,512]{3,2,0,1:T(8,128)(2,1)S(1)}, bf16[4,2,64,512]{3,2,0,1:T(8,128)(2,1)S(1)}, u32[]{:S(2)}, u32[]{:S(2)}) collective-permute-start(bf16[4,2,64,512]{3,2,0,1:T(8,128)(2,1)S(1)} %bitcast.395), channel_id=1, source_target_pairs={{0,16},{8,24},{16,0},{24,8},{1,17},{9,25},{17,1},{25,9},{2,18},{10... | collective-permute-start | bytes 1572872 | tf_op jit(solution)/shard_map/ppermute | solution.py:392
  678.8 35.5 %collective-permute-start.88 = (bf16[1024,1408]{1,0:T(8,128)(2,1)S(1)}, bf16[1024,1408]{1,0:T(8,128)(2,1)S(1)}, u32[]{:S(2)}, u32[]{:S(2)}) collective-permute-start(bf16[1024,1408]{1,0:T(8,128)(2,1)S(1)} %copy-done.83), channel_id=1, source_target_pairs={{0,8},{8,0},{16,24},{24,16},{1,9},{9,1},{17,25},{25,17},{2,10},{10... | collective-permute-start | bytes 8650760 | tf_op jit(solution)/shard_map/ppermute | solution.py:398
  704.5 13.7 %collective-permute-start.66 = (bf16[128,512]{1,0:T(8,128)(2,1)S(1)}, bf16[128,512]{1,0:T(8,128)(2,1)S(1)}, u32[]{:S(2)}, u32[]{:S(2)}) collective-permute-start(bf16[128,512]{1,0:T(8,128)(2,1)S(1)} %add_convert_fusion.14), channel_id=1, source_target_pairs={{0,8},{8,0},{16,24},{24,16},{1,9},{9,1},{17,25},{25,17},{2,10},{10... | collective-permute-start | bytes 393224 | tf_op jit(solution)/shard_map/ppermute | solution.py:398
  709.2 33.6 %collective-permute-start.105 = (bf16[4,352,512]{2,1,0:T(8,128)(2,1)S(1)}, bf16[4,352,512]{2,1,0:T(8,128)(2,1)S(1)}, u32[]{:S(2)}, u32[]{:S(2)}) collective-permute-start(bf16[4,352,512]{2,1,0:T(8,128)(2,1)S(1)} %dynamic-slice_bitcast_fusion), channel_id=1, source_target_pairs={{0,1},{1,0},{2,3},{3,2},{4,5},{5,4},{6,7},{7,6},{8,9},{9,8},{10,11... | collective-permute-start | bytes 4325384 | tf_op jit(solution)/shard_map/ppermute | solution.py:385
  712.7 34.7 %collective-permute-start.97 = (bf16[4,2,64,1408]{3,2,0,1:T(8,128)(2,1)S(1)}, bf16[4,2,64,1408]{3,2,0,1:T(8,128)(2,1)S(1)}, u32[]{:S(2)}, u32[]{:S(2)}) collective-permute-start(bf16[4,2,64,1408]{3,2,0,1:T(8,128)(2,1)S(1)} %bitcast.385), channel_id=1, source_target_pairs={{0,16},{8,24},{16,0},{24,8},{1,17},{9,25},{17,1},{25,9},{2,18},{10... | collective-permute-start | bytes 4325384 | tf_op jit(solution)/shard_map/ppermute | solution.py:392
  716.6 61.4 %collective-permute-start.89 = (bf16[4,2,64,1408]{3,2,0,1:T(8,128)(2,1)S(1)}, bf16[4,2,64,1408]{3,2,0,1:T(8,128)(2,1)S(1)}, u32[]{:S(2)}, u32[]{:S(2)}) collective-permute-start(bf16[4,2,64,1408]{3,2,0,1:T(8,128)(2,1)S(1)} %bitcast.384), channel_id=1, source_target_pairs={{0,16},{8,24},{16,0},{24,8},{1,17},{9,25},{17,1},{25,9},{2,18},{10... | collective-permute-start | bytes 4325384 | tf_op jit(solution)/shard_map/ppermute | solution.py:392
  743.8 26.6 %collective-permute-start.107 = (bf16[352,512]{1,0:T(8,128)(2,1)S(1)}, bf16[352,512]{1,0:T(8,128)(2,1)S(1)}, u32[]{:S(2)}, u32[]{:S(2)}) collective-permute-start(bf16[352,512]{1,0:T(8,128)(2,1)S(1)} %get-tuple-element.150), channel_id=1, source_target_pairs={{0,4},{1,5},{2,6},{3,7},{4,0},{5,1},{6,2},{7,3},{8,12},{9,13},{10,... | collective-permute-start | bytes 1081352 | tf_op jit(solution)/shard_map/ppermute | solution.py:378
  747.4 23.0 %collective-permute-start.108 = (bf16[352,512]{1,0:T(8,128)(2,1)S(1)}, bf16[352,512]{1,0:T(8,128)(2,1)S(1)}, u32[]{:S(2)}, u32[]{:S(2)}) collective-permute-start(bf16[352,512]{1,0:T(8,128)(2,1)S(1)} %get-tuple-element.149), channel_id=1, source_target_pairs={{0,6},{1,7},{2,0},{3,1},{4,2},{5,3},{6,4},{7,5},{8,14},{9,15},{10,... | collective-permute-start | bytes 1081352 | tf_op jit(solution)/shard_map/ppermute | solution.py:378
  747.8 37.2 %collective-permute-start.98 = (bf16[4,64,1408]{2,1,0:T(8,128)(2,1)S(1)}, bf16[4,64,1408]{2,1,0:T(8,128)(2,1)S(1)}, u32[]{:S(2)}, u32[]{:S(2)}) collective-permute-start(bf16[4,64,1408]{2,1,0:T(8,128)(2,1)S(1)} %dynamic-slice_bitcast_fusion.1), channel_id=1, source_target_pairs={{0,1},{1,0},{2,3},{3,2},{4,5},{5,4},{6,7},{7,6},{8,9},{9,8},{10,11... | collective-permute-start | bytes 2162696 | tf_op jit(solution)/shard_map/ppermute | solution.py:385
  770.6 14.3 %collective-permute-start.109 = (bf16[352,512]{1,0:T(8,128)(2,1)S(1)}, bf16[352,512]{1,0:T(8,128)(2,1)S(1)}, u32[]{:S(2)}, u32[]{:S(2)}) collective-permute-start(bf16[352,512]{1,0:T(8,128)(2,1)S(1)} %fusion.50), channel_id=1, source_target_pairs={{0,16},{8,24},{16,0},{24,8},{1,17},{9,25},{17,1},{25,9},{2,18},{10... | collective-permute-start | bytes 1081352 | tf_op jit(solution)/shard_map/ppermute | solution.py:392
  778.5 16.4 %collective-permute-start.90 = (bf16[4,64,1408]{2,1,0:T(8,128)(2,1)S(1)}, bf16[4,64,1408]{2,1,0:T(8,128)(2,1)S(1)}, u32[]{:S(2)}, u32[]{:S(2)}) collective-permute-start(bf16[4,64,1408]{2,1,0:T(8,128)(2,1)S(1)} %dynamic-slice_bitcast_fusion.2), channel_id=1, source_target_pairs={{0,1},{1,0},{2,3},{3,2},{4,5},{5,4},{6,7},{7,6},{8,9},{9,8},{10,11... | collective-permute-start | bytes 2162696 | tf_op jit(solution)/shard_map/ppermute | solution.py:385
  785.0 37.8 %collective-permute-start.110 = (bf16[352,512]{1,0:T(8,128)(2,1)S(1)}, bf16[352,512]{1,0:T(8,128)(2,1)S(1)}, u32[]{:S(2)}, u32[]{:S(2)}) collective-permute-start(bf16[352,512]{1,0:T(8,128)(2,1)S(1)} %add_convert_fusion.10), channel_id=1, source_target_pairs={{0,8},{8,0},{16,24},{24,16},{1,9},{9,1},{17,25},{25,17},{2,10},{10... | collective-permute-start | bytes 1081352 | tf_op jit(solution)/shard_map/ppermute | solution.py:398
  785.3 13.6 %collective-permute-start.100 = (bf16[64,1408]{1,0:T(8,128)(2,1)S(1)}, bf16[64,1408]{1,0:T(8,128)(2,1)S(1)}, u32[]{:S(2)}, u32[]{:S(2)}) collective-permute-start(bf16[64,1408]{1,0:T(8,128)(2,1)S(1)} %get-tuple-element.158), channel_id=1, source_target_pairs={{0,4},{1,5},{2,6},{3,7},{4,0},{5,1},{6,2},{7,3},{8,12},{9,13},{10,... | collective-permute-start | bytes 540680 | tf_op jit(solution)/shard_map/ppermute | solution.py:378
  795.1 14.0 %collective-permute-start.91 = (bf16[64,1408]{1,0:T(8,128)(2,1)S(1)}, bf16[64,1408]{1,0:T(8,128)(2,1)S(1)}, u32[]{:S(2)}, u32[]{:S(2)}) collective-permute-start(bf16[64,1408]{1,0:T(8,128)(2,1)S(1)} %get-tuple-element.159), channel_id=1, source_target_pairs={{0,2},{1,3},{2,4},{3,5},{4,6},{5,7},{6,0},{7,1},{8,10},{9,11},{10,... | collective-permute-start | bytes 540680 | tf_op jit(solution)/shard_map/ppermute | solution.py:378
  798.9 18.4 %collective-permute-start.92 = (bf16[64,1408]{1,0:T(8,128)(2,1)S(1)}, bf16[64,1408]{1,0:T(8,128)(2,1)S(1)}, u32[]{:S(2)}, u32[]{:S(2)}) collective-permute-start(bf16[64,1408]{1,0:T(8,128)(2,1)S(1)} %get-tuple-element.161), channel_id=1, source_target_pairs={{0,4},{1,5},{2,6},{3,7},{4,0},{5,1},{6,2},{7,3},{8,12},{9,13},{10,... | collective-permute-start | bytes 540680 | tf_op jit(solution)/shard_map/ppermute | solution.py:378
  799.4 21.5 %collective-permute-start.93 = (bf16[64,1408]{1,0:T(8,128)(2,1)S(1)}, bf16[64,1408]{1,0:T(8,128)(2,1)S(1)}, u32[]{:S(2)}, u32[]{:S(2)}) collective-permute-start(bf16[64,1408]{1,0:T(8,128)(2,1)S(1)} %get-tuple-element.160), channel_id=1, source_target_pairs={{0,6},{1,7},{2,0},{3,1},{4,2},{5,3},{6,4},{7,5},{8,14},{9,15},{10,... | collective-permute-start | bytes 540680 | tf_op jit(solution)/shard_map/ppermute | solution.py:378
  805.3 17.2 %collective-permute-start.102 = (bf16[64,1408]{1,0:T(8,128)(2,1)S(1)}, bf16[64,1408]{1,0:T(8,128)(2,1)S(1)}, u32[]{:S(2)}, u32[]{:S(2)}) collective-permute-start(bf16[64,1408]{1,0:T(8,128)(2,1)S(1)} %fusion.94), channel_id=1, source_target_pairs={{0,16},{8,24},{16,0},{24,8},{1,17},{9,25},{17,1},{25,9},{2,18},{10... | collective-permute-start | bytes 540680 | tf_op jit(solution)/shard_map/ppermute | solution.py:392
  (154 other events, 2869.9 us)

commit v2 on v1

v2 whole, which is shorter than its diff:
```python
from functools import partial

import jax
import jax.numpy as jnp
from jax import lax
from jax.experimental import pallas as pl
from jax.experimental.pallas import tpu as pltpu
from jax.sharding import PartitionSpec as P

SPAN = 64
EPSILON = 1e-06
BF = jnp.bfloat16
F32 = jnp.float32


def nn(a, b):
    return lax.dot_general(a, b, (((1,), (0,)), ((), ())), preferred_element_type=F32)


def nt(a, b):
    return lax.dot_general(a, b, (((1,), (1,)), ((), ())), preferred_element_type=F32)


def tn(a, b):
    return lax.dot_general(a, b, (((0,), (0,)), ((), ())), preferred_element_type=F32)


def block_masks(cols_ref, rows_ref, heads):
    n = SPAN
    row = lax.broadcasted_iota(jnp.int32, (n, n), 0)
    col = lax.broadcasted_iota(jnp.int32, (n, n), 1)
    ids = cols_ref[:, heads : heads + 1]
    ids_row = rows_ref[0, heads : heads + 1, :]
    before = rows_ref[0, heads + 1 : heads + 2, :]
    end = ids_row[:, n - 1 : n]
    same = ids == ids_row
    first = (ids == before[:, :1]).astype(F32)
    last = (ids == end).astype(F32)
    keep = (end == before[:, :1]).astype(F32)
    return row, col, same, first, last, keep


def sigmoid(z):
    return 0.5 * jnp.tanh(0.5 * z) + 0.5


def shifted_rows(x, prev, masks):
    both = jnp.concatenate([prev, x], axis=0)
    lead = prev.shape[0]
    return [x] + [both[lead - j : lead - j + x.shape[0]] * masks[j - 1] for j in (1, 2, 3)]


def mix_rows(rows, taps):
    mixed = rows[0] * taps[0:1]
    for j in (1, 2, 3):
        mixed = mixed + rows[j] * taps[j : j + 1]
    return mixed


def lag_masks(cols_ref, heads):
    return [cols_ref[:, heads + j : heads + j + 1] for j in (1, 2, 3)]


def kv_at(heads, d, h):
    half = heads // 2
    start = (h // half) * 2 * half * d + (h % half) * d
    return slice(start, start + d), slice(start + half * d, start + half * d + d)


def summary_kernel(
    heads, d, pre_ref, prev_ref, taps_ref, cols_ref, rows_ref,
    k_ref, v_ref, w_ref, u_ref, a_ref, x_ref, state,
):
    n = SPAN
    block = pl.program_id(0)

    @pl.when(block == 0)
    def _():
        r = lax.broadcasted_iota(jnp.int32, (d, 2 * d), 0)
        c = lax.broadcasted_iota(jnp.int32, (d, 2 * d), 1)
        unit = (r + d == c).astype(F32)
        for h in range(heads):
            state[h] = unit

    row, col, same, first, last, keep = block_masks(cols_ref, rows_ref, heads)
    lower = jnp.logical_and(same, row > col)
    unit = (row == col).astype(F32)
    pair = jnp.logical_and(row == col + 1, (row & 1) == 1)
    masks = lag_masks(cols_ref, heads)
    keys = []
    mixing = []
    inverse = []
    for h in range(heads):
        cut = slice(h * d, (h + 1) * d)
        at_k, at_v = kv_at(heads, d, h)
        z = mix_rows(shifted_rows(pre_ref[:, at_k], prev_ref[:, at_k], masks), taps_ref[:, at_k])
        act = z * sigmoid(z)
        root = lax.rsqrt(jnp.sum(act * act, axis=1, keepdims=True) + EPSILON)
        keys.append((act * root).astype(BF))
        k_ref[:, cut] = keys[h]
        z = mix_rows(shifted_rows(pre_ref[:, at_v], prev_ref[:, at_v], masks), taps_ref[:, at_v])
        v_ref[:, cut] = (z * sigmoid(z)).astype(BF)
        m = jnp.where(lower, nt(keys[h], keys[h]) * cols_ref[:, h : h + 1], 0.0)
        mixing.append(m)
        inverse.append((unit - jnp.where(pair, m, 0.0)).astype(BF))
    size = 2
    while size < n:
        level = jnp.logical_and(
            (row // (2 * size)) == (col // (2 * size)),
            jnp.logical_and(((row // size) & 1) == 1, ((col // size) & 1) == 0),
        )
        inner = [nn(jnp.where(level, mixing[h], 0.0).astype(BF), inverse[h]).astype(BF) for h in range(heads)]
        for h in range(heads):
            inverse[h] = inverse[h] - jnp.where(level, nn(inverse[h], inner[h]), 0.0).astype(BF)
        size *= 2
    for h in range(heads):
        cut = slice(h * d, (h + 1) * d)
        a_ref[h] = inverse[h]
        scaled = (inverse[h].astype(F32) * rows_ref[0, h : h + 1, :]).astype(BF)
        both = nn(scaled, jnp.concatenate([keys[h], v_ref[:, cut]], axis=1))
        w = both[:, :d].astype(BF)
        u = both[:, d:].astype(BF)
        w_ref[:, cut] = w
        u_ref[:, cut] = u
        held = state[h]
        moved = nn(w, held.astype(BF)) * first
        fresh = (jnp.concatenate([u.astype(F32), jnp.zeros((n, d), F32)], axis=1) - moved).astype(BF)
        key_last = (keys[h].astype(F32) * last).astype(BF)
        state[h] = keep * held + tn(key_last, fresh)

    @pl.when(block == pl.num_programs(0) - 1)
    def _():
        x_ref[...] = state[...].astype(BF)


def forward_kernel(
    heads, d, pre_ref, prev_ref, taps_ref, k_ref, w_ref, u_ref, cols_ref, rows_ref, s_ref, gate_ref, gain_ref,
    q_ref, y_ref, o_ref, e_ref, kept_ref, state,
):
    n = SPAN
    block = pl.program_id(0)

    @pl.when(block == 0)
    def _():
        state[...] = s_ref[...].astype(F32)

    row, col, same, first, last, keep = block_masks(cols_ref, rows_ref, heads)
    visible = jnp.logical_and(same, row >= col)
    masks = lag_masks(cols_ref, heads)
    for h in range(heads):
        cut = slice(h * d, (h + 1) * d)
        z = mix_rows(shifted_rows(pre_ref[:, cut], prev_ref[:, cut], masks), taps_ref[:, cut])
        q = (z * sigmoid(z) * d ** (-0.5)).astype(BF)
        q_ref[:, cut] = q
        k, w = k_ref[:, cut], w_ref[:, cut]
        held = state[h]
        held_low = held.astype(BF)
        kept_ref[0, h] = held_low
        both = nn(jnp.concatenate([w, q], axis=0), held_low)
        fresh = (u_ref[:, cut].astype(F32) - first * both[:n]).astype(BF)
        e_ref[:, cut] = fresh
        scores = jnp.where(visible, nt(q, k), 0.0).astype(BF)
        out = first * both[n:] + nn(scores, fresh)
        key_last = (k.astype(F32) * last).astype(BF)
        state[h] = keep * held + tn(key_last, fresh)
        o_ref[:, cut] = out
        g = gate_ref[:, cut]
        root = lax.rsqrt(jnp.mean(out * out, axis=1, keepdims=True) + EPSILON)
        y_ref[:, cut] = (out * root * gain_ref[...] * (g * sigmoid(g))).astype(BF)


def adjoint_kernel(
    heads, d, q_ref, k_ref, w_ref, cols_ref, rows_ref, dy_ref, o_ref, gate_ref, gain_ref,
    do_ref, dgate_ref, dgain_ref, ds_ref, state,
):
    n = SPAN
    step = pl.program_id(0)

    @pl.when(step == 0)
    def _():
        state[...] = jnp.zeros_like(state)
        dgain_ref[...] = jnp.zeros_like(dgain_ref)

    row, col, same, first, last, keep = block_masks(cols_ref, rows_ref, heads)
    visible = jnp.logical_and(same, row >= col)
    gain = gain_ref[...]
    gain_sum = jnp.zeros((1, d), F32)
    for h in range(heads):
        cut = slice(h * d, (h + 1) * d)
        q, k, w = q_ref[:, cut], k_ref[:, cut], w_ref[:, cut]
        o, g, dy = o_ref[:, cut], gate_ref[:, cut], dy_ref[:, cut]
        root = lax.rsqrt(jnp.mean(o * o, axis=1, keepdims=True) + EPSILON)
        unit = o * root
        sig = sigmoid(g)
        m = g * sig
        t = dy * m
        gain_sum = gain_sum + jnp.sum(t * unit, axis=0, keepdims=True)
        tg = t * gain
        do = root * (tg - unit * jnp.mean(tg * unit, axis=1, keepdims=True))
        dgate_ref[:, cut] = (dy * gain * unit * (sig * (1.0 + g * (1.0 - sig)))).astype(BF)
        do_low = do.astype(BF)
        do_ref[:, cut] = do_low
        scores = jnp.where(visible, nt(q, k), 0.0).astype(BF)
        later = state[h]
        de = last * nn(k, later.astype(BF)) + tn(scores, do_low)
        left = jnp.concatenate([q.astype(F32) * first, w.astype(F32) * (-first)], axis=0).astype(BF)
        right = jnp.concatenate([do_low, de.astype(BF)], axis=0)
        state[h] = keep * later + tn(left, right)
    dgain_ref[...] += gain_sum

    @pl.when(step == pl.num_programs(0) - 1)
    def _():
        ds_ref[...] = state[...].astype(BF)


def backward_kernel(
    heads, part, d, q_ref, k_ref, v_ref, w_ref, u_ref, a_ref, e_ref, kept_ref, do_ref, cols_ref, rows_ref, s_ref,
    qpre_ref, qprev_ref, qtaps_ref, kvpre_ref, kvprev_ref, kvtaps_ref,
    dpre_ref, dbeta_ref, dtaps_ref, state, carry,
):
    n = SPAN
    step = pl.program_id(0)
    number = heads // 2

    @pl.when(step == 0)
    def _():
        state[...] = s_ref[...].astype(F32)
        carry[...] = jnp.zeros_like(carry)
        dtaps_ref[...] = jnp.zeros_like(dtaps_ref)

    @pl.when(step < pl.num_programs(0) - 1)
    def _():
        row, col, same, first, last, keep = block_masks(cols_ref, rows_ref, heads)
        visible = jnp.logical_and(same, row >= col)
        lower = jnp.logical_and(same, row > col)
        lane = lax.broadcasted_iota(jnp.int32, (n, d), 1)
        masks = lag_masks(cols_ref, heads)
        rate_grads = jnp.zeros((n, d), F32)

        def conv_back(dact, z, sig, rows, taps, at):
            dconv = dact * (sig * (1.0 + z * (1.0 - sig)))
            here = slice(at, at + d)
            dtaps_ref[:, here] += jnp.concatenate(
                [jnp.sum(dconv * r, axis=0, keepdims=True) for r in rows], axis=0
            )
            dpre = dconv * taps[0:1]
            for j in (1, 2, 3):
                masked = dconv * masks[j - 1]
                both = jnp.concatenate([masked, carry[j - 1, :, here]], axis=0)
                dpre = dpre + both[j : n + j] * taps[j : j + 1]
                carry[j - 1, :, here] = masked[:8]
            dpre_ref[:, here] = dpre.astype(BF)

        for h in range(number):
            cut = slice(h * d, (h + 1) * d)
            cut_v = slice((number + h) * d, (number + h + 1) * d)
            q, k, v, w, u = q_ref[:, cut], k_ref[:, cut], v_ref[:, cut], w_ref[:, cut], u_ref[:, cut]
            do, e, held = do_ref[:, cut], e_ref[:, cut], kept_ref[0, h]
            at = part * number + h
            rate = cols_ref[:, at : at + 1]
            later = state[h]
            later_low = later.astype(BF)
            scores = jnp.where(visible, nt(q, k), 0.0).astype(BF)
            de = last * nn(k, later_low) + tn(scores, do)
            de_low = de.astype(BF)
            dscores = jnp.where(visible, nt(do, e), 0.0).astype(BF)
            both = nt(jnp.concatenate([do, de_low], axis=0), held)
            dq = first * both[:n] + nn(dscores, k)
            dw = -first * both[n:]
            dk = tn(dscores, q) + last * nt(e, later_low)
            pg = tn(a_ref[h], jnp.concatenate([dw.astype(BF), de_low], axis=1))
            p, g = pg[:, :d], pg[:, d:]
            dmix = jnp.where(lower, -nt(pg.astype(BF), jnp.concatenate([w, u], axis=1)), 0.0).astype(BF)
            kf = k.astype(F32)
            drk = p + nn(dmix, k)
            dk = dk + tn(dmix, (kf * rate).astype(BF)) + rate * drk
            dr = jnp.sum(drk * kf + g * v.astype(F32), axis=1, keepdims=True)
            rate_grads = jnp.where(lane == at, dr * rate * (1.0 - rate), rate_grads)
            left = jnp.concatenate([q.astype(F32) * first, w.astype(F32) * (-first)], axis=0).astype(BF)
            right = jnp.concatenate([do, de_low], axis=0)
            state[h] = keep * later + tn(left, right)

            taps = qtaps_ref[:, cut]
            rows = shifted_rows(qpre_ref[:, cut], qprev_ref[:, cut], masks)
            z = mix_rows(rows, taps)
            conv_back(dq * d ** (-0.5), z, sigmoid(z), rows, taps, h * d)
            taps = kvtaps_ref[:, cut]
            rows = shifted_rows(kvpre_ref[:, cut], kvprev_ref[:, cut], masks)
            z = mix_rows(rows, taps)
            sig = sigmoid(z)
            act = z * sig
            root = lax.rsqrt(jnp.sum(act * act, axis=1, keepdims=True) + EPSILON)
            unit = act * root
            dact = root * (dk - unit * jnp.sum(unit * dk, axis=1, keepdims=True))
            conv_back(dact, z, sig, rows, taps, (number + h) * d)
            taps = kvtaps_ref[:, cut_v]
            rows = shifted_rows(kvpre_ref[:, cut_v], kvprev_ref[:, cut_v], masks)
            z = mix_rows(rows, taps)
            conv_back(rate * g, z, sigmoid(z), rows, taps, (2 * number + h) * d)
        dbeta_ref[...] = rate_grads

    @pl.when(step == pl.num_programs(0) - 1)
    def _():
        wide = number * d
        for i, taps_ref, at in ((0, qtaps_ref, 0), (1, kvtaps_ref, 0), (2, kvtaps_ref, wide)):
            here = slice(i * wide, (i + 1) * wide)
            dpre = jnp.zeros((8, wide), F32)
            for j in (1, 2, 3):
                held = carry[j - 1, :, here]
                both = jnp.concatenate([jnp.zeros_like(held), held], axis=0)
                dpre = dpre + both[j : 8 + j] * taps_ref[j : j + 1, at : at + wide]
            dpre_ref[0:8, here] = dpre.astype(BF)


def prefix_kernel(peers, x_ref, out_ref):
    cols = out_ref.shape[2]
    held = jnp.zeros(out_ref.shape[1:], F32)
    for i in range(peers):
        out_ref[i] = held.astype(BF)
        held = nn(x_ref[i, :, cols:], held.astype(BF)) + x_ref[i, :, :cols].astype(F32)


def suffix_kernel(peers, t_ref, g_ref, out_ref):
    held = jnp.zeros(out_ref.shape[1:], F32)
    cols = out_ref.shape[2]
    for i in reversed(range(peers)):
        out_ref[i] = held.astype(BF)
        held = tn(t_ref[i, :, cols:], held.astype(BF)) + g_ref[i].astype(F32)


VMEM_LIMIT = 16 * 1024 * 1024


def params():
    return pltpu.CompilerParams(dimension_semantics=("arbitrary",), vmem_limit_bytes=VMEM_LIMIT)


def cost(microseconds):
    return pl.CostEstimate(
        flops=int(microseconds * 1e9), bytes_accessed=int(microseconds * 3e6), transcendentals=0
    )


def specs(blocks, heads, d, flip):
    at = (lambda b: blocks - 1 - b) if flip else (lambda b: b)
    wide = pl.BlockSpec((SPAN, heads * d), lambda b: (at(b), 0))
    cols = pl.BlockSpec((SPAN, 2 * heads), lambda b: (at(b), 0))
    rows = pl.BlockSpec((1, 2 * heads, SPAN), lambda b: (at(b), 0, 0))
    state = pl.BlockSpec((heads, d, d), lambda b: (0, 0, 0))
    mix = pl.BlockSpec((heads, SPAN, SPAN), lambda b: (0, at(b), 0))
    kept = pl.BlockSpec((1, heads, d, d), lambda b: (at(b), 0, 0, 0))
    gain = pl.BlockSpec((1, d), lambda b: (0, 0))
    return wide, cols, rows, state, mix, kept, gain


def shape(dims, kind):
    return jax.ShapeDtypeStruct(dims, kind)


def before_block(blocks, rim, flip, size, column):
    def index(step):
        b = blocks - 1 - jnp.minimum(step, blocks - 1) if flip else step
        per = SPAN // rim
        return jnp.where(b == 0, blocks * per, b * per - 1), column

    return pl.BlockSpec((rim, size), index)


def delta_summary(pre, taps, cols, rows, heads):
    count, width = cols.shape[0], pre.shape[1] // 2
    d, blocks = width // heads, count // SPAN
    rim = pre.shape[0] - count
    wide, c, r, state, mix, kept, gain = specs(blocks, heads, d, False)
    return pl.pallas_call(
        partial(summary_kernel, heads, d),
        grid=(blocks,),
        in_specs=[
            pl.BlockSpec((SPAN, 2 * width), lambda b: (b, 0)),
            before_block(blocks, rim, False, 2 * width, 0),
            pl.BlockSpec((4, 2 * width), lambda b: (0, 0)),
            c,
            r,
        ],
        out_specs=[wide, wide, wide, wide, mix, pl.BlockSpec((heads, d, 2 * d), lambda b: (0, 0, 0))],
        out_shape=[
            shape((count, width), BF),
            shape((count, width), BF),
            shape((count, width), BF),
            shape((count, width), BF),
            shape((heads, count, SPAN), BF),
            shape((heads, d, 2 * d), BF),
        ],
        scratch_shapes=[pltpu.VMEM((heads, d, 2 * d), F32)],
        compiler_params=params(),
        cost_estimate=cost(24),
        name="delta_summary",
    )(pre, pre, taps, cols, rows)


def delta_forward(pre, taps, k, w, u, cols, rows, entry, gain_full, heads):
    count, width = k.shape
    d, blocks = width // heads, count // SPAN
    rim = pre.shape[0] - count
    wide, c, r, state, mix, kept, gain = specs(blocks, heads, d, False)
    return pl.pallas_call(
        partial(forward_kernel, heads, d),
        grid=(blocks,),
        in_specs=[
            wide,
            before_block(blocks, rim, False, width, 0),
            pl.BlockSpec((4, width), lambda b: (0, 0)),
            wide,
            wide,
            wide,
            c,
            r,
            state,
            pl.BlockSpec((SPAN, width), lambda b: (b, 1)),
            gain,
        ],
        out_specs=[wide, wide, wide, wide, kept],
        out_shape=[
            shape((count, width), BF),
            shape((count, width), BF),
            shape((count, width), F32),
            shape((count, width), BF),
            shape((blocks, heads, d, d), BF),
        ],
        scratch_shapes=[pltpu.VMEM((heads, d, d), F32)],
        compiler_params=params(),
        cost_estimate=cost(16),
        name="delta_forward",
    )(pre, pre, taps, k, w, u, cols, rows, entry, pre, gain_full)


def delta_adjoint(q, k, w, cols, rows, dy, o, gate, gain_full, heads):
    count, width = k.shape
    d, blocks = width // heads, count // SPAN
    wide, c, r, state, mix, kept, gain = specs(blocks, heads, d, True)
    return pl.pallas_call(
        partial(adjoint_kernel, heads, d),
        grid=(blocks,),
        in_specs=[
            wide,
            wide,
            wide,
            c,
            r,
            wide,
            wide,
            pl.BlockSpec((SPAN, width), lambda b: (blocks - 1 - b, 1)),
            gain,
        ],
        out_specs=[wide, wide, gain, state],
        out_shape=[
            shape((count, width), BF),
            shape((count, width), BF),
            shape((1, d), F32),
            shape((heads, d, d), BF),
        ],
        scratch_shapes=[pltpu.VMEM((heads, d, d), F32)],
        compiler_params=params(),
        cost_estimate=cost(15),
        name="delta_adjoint",
    )(q, k, w, cols, rows, dy, o, gate, gain_full)


def delta_backward(part, q, k, v, w, u, a, e, kept_states, do, cols, rows, later, qg_pre, qtaps, kv_pre, kvtaps, heads):
    count, width = k.shape
    d, blocks = width // heads, count // SPAN
    rim = kv_pre.shape[0] - count
    number = heads // 2
    size = number * d

    def at(step):
        return blocks - 1 - jnp.minimum(step, blocks - 1)

    wide = pl.BlockSpec((SPAN, size), lambda b: (at(b), part))
    in_specs = [
        wide,
        wide,
        wide,
        wide,
        wide,
        pl.BlockSpec((number, SPAN, SPAN), lambda b: (part, at(b), 0)),
        wide,
        pl.BlockSpec((1, number, d, d), lambda b: (at(b), part, 0, 0)),
        wide,
        pl.BlockSpec((SPAN, 2 * heads), lambda b: (at(b), 0)),
        pl.BlockSpec((1, 2 * heads, SPAN), lambda b: (at(b), 0, 0)),
        pl.BlockSpec((number, d, d), lambda b: (part, 0, 0)),
        wide,
        before_block(blocks, rim, True, size, part),
        pl.BlockSpec((4, size), lambda b: (0, part)),
        pl.BlockSpec((SPAN, 2 * size), lambda b: (at(b), part)),
        before_block(blocks, rim, True, 2 * size, part),
        pl.BlockSpec((4, 2 * size), lambda b: (0, part)),
    ]
    return pl.pallas_call(
        partial(backward_kernel, heads, part, d),
        grid=(blocks + 1,),
        in_specs=in_specs,
        out_specs=[
            pl.BlockSpec((SPAN, 3 * size), lambda b: (jnp.where(b < blocks, blocks - 1 - b, blocks), 0)),
            pl.BlockSpec((SPAN, d), lambda b: (at(b), 0)),
            pl.BlockSpec((4, 3 * size), lambda b: (0, 0)),
        ],
        out_shape=[
            shape((count + rim, 3 * size), BF),
            shape((count, d), F32),
            shape((4, 3 * size), F32),
        ],
        scratch_shapes=[pltpu.VMEM((number, d, d), F32), pltpu.VMEM((3, rim, 3 * size), F32)],
        compiler_params=params(),
        cost_estimate=cost(32),
        name="delta_backward",
    )(q, k, v, w, u, a, e, kept_states, do, cols, rows, later, qg_pre, qg_pre, qtaps, kv_pre, kv_pre, kvtaps)


def scan_states(x):
    peers, d, width = x.shape
    return pl.pallas_call(
        partial(prefix_kernel, peers),
        out_shape=shape((peers, d, width - d), BF),
        cost_estimate=cost(3),
        name="state_prefix",
    )(x)


def scan_grads(x, g):
    peers, d, width = g.shape
    return pl.pallas_call(
        partial(suffix_kernel, peers),
        out_shape=shape((peers, d, width), BF),
        cost_estimate=cost(3),
        name="state_suffix",
    )(x, g)


def hold(value, *after):
    return lax.optimization_barrier((value, after))[0]


class Place:
    def __init__(self):
        self.nf, self.nr = lax.axis_size("fsdp"), lax.axis_size("rep")
        self.ny = self.nf // 4
        self.nx = self.nr // 2
        self.f, self.r = lax.axis_index("fsdp"), lax.axis_index("rep")
        z = self.f // self.ny
        self.mine = {"v": z // 2, "w": z % 2, "y": self.f % self.ny, "x": self.r // 2, "c": self.r % 2}
        self.number = {"v": 2, "w": 2, "y": self.ny, "x": self.nx, "c": 2}
        self.stride = {"v": 2 * self.ny, "w": self.ny, "y": 1, "x": 2, "c": 1}

    def send(self, value, way, steps=1):
        axis = "rep" if way in "xc" else "fsdp"
        total = self.nr if way in "xc" else self.nf
        number, stride = self.number[way], self.stride[way]
        pairs = []
        for i in range(total):
            at = i // stride % number
            pairs.append((i, i + ((at + steps) % number - at) * stride))
        return lax.ppermute(value, axis, pairs)


def place_kernel(count, rows, each, by_rows, widths, offs_ref, own_ref, *refs):
    stacks, outs, sems = refs[: len(count)], refs[len(count) : -1], refs[-1]
    copies = []

    def put(src, row, height, column, out):
        copy = pltpu.make_async_copy(src, out.at[pl.ds(row, height), column], sems.at[len(copies)])
        copy.start()
        copies.append(copy)

    starts = [sum(widths[:i]) for i in range(len(widths))]
    top = pl.multiple_of(offs_ref[0], rows)
    for start, width, out in zip(starts, widths, outs):
        put(own_ref.at[:, pl.ds(start, width)], top, rows, pl.ds(0, width), out)
    at = 1
    for stack, number in zip(stacks, count):
        for j in range(number):
            row = pl.multiple_of(offs_ref[at], each if by_rows else rows)
            if by_rows:
                for start, width, out in zip(starts, widths, outs):
                    put(stack.at[j, :, pl.ds(start, width)], row, each, pl.ds(0, width), out)
                at += 1
            else:
                column = pl.multiple_of(offs_ref[at + 1], each)
                put(stack.at[j], row, rows, pl.ds(column, each), outs[0])
                at += 2
    for copy in copies:
        copy.wait()


class Gather:
    def __init__(self, here, shard, widths, deep, by_rows=True):
        self.here, self.shard, self.widths, self.deep, self.by_rows = here, shard, widths, deep, by_rows
        rows, total = shard.shape
        parts = here.nr if deep else 2
        extent = rows if by_rows else total
        self.each = extent // parts
        self.plain = bool(extent % parts or self.each % (32 if by_rows else 128) or rows % 32)
        self.plain = self.plain or here.ny != 2 or here.nx != 2
        self.have = {}
        if self.plain:
            return
        part = here.r if deep else here.mine["c"]
        self.have[""] = lax.dynamic_slice_in_dim(shard, part * self.each, self.each, 0 if by_rows else 1)

    def got(self, *names):
        return [] if self.plain else [self.have[name] for name in names]

    def move(self, *names, after=()):
        if not self.plain:
            for name in names:
                self.have[name] = self.here.send(hold(self.have[name[:-1]], *after), name[-1])

    def pile(self):
        if not self.plain:
            self.have["z"] = jnp.stack([self.have[name] for name in ("", "w", "v", "vw")])

    def place(self):
        here, shard, widths = self.here, self.shard, self.widths
        rows, each = shard.shape[0], self.each
        if self.plain:
            whole = lax.all_gather(shard, "fsdp", axis=0, tiled=True)
            starts = [sum(widths[:i]) for i in range(len(widths))]
            return [whole[:, s : s + w] for s, w in zip(starts, widths)]
        mine = here.mine
        offsets = [here.f * rows]
        names = [name for name in self.have if name.startswith("z")]
        for name in names:
            x, c, y = ((mine[way] + (way in name)) % 2 for way in "xcy")
            inside = (x * 2 + c if self.deep else c) * each
            for j in range(4):
                v = (mine["v"] + j // 2) % 2
                w = (mine["w"] + j % 2) % 2
                source = (v * 2 + w) * here.ny + y
                offsets += [source * rows + inside] if self.by_rows else [source * rows, inside]
        offsets = jnp.stack(offsets).astype(jnp.int32)
        stacks = [self.have[name] for name in names]
        count = [4] * len(stacks)
        any_space = pl.BlockSpec(memory_space=pl.ANY)
        size = here.nf * rows
        return pl.pallas_call(
            partial(place_kernel, count, rows, each, self.by_rows, widths),
            grid_spec=pltpu.PrefetchScalarGridSpec(
                num_scalar_prefetch=1,
                grid=(1,),
                in_specs=[any_space] * (1 + len(stacks)),
                out_specs=[pl.BlockSpec((size, w), lambda i, o: (0, 0)) for w in widths],
                scratch_shapes=[pltpu.SemaphoreType.DMA(((1 + sum(count)) * len(widths),))],
            ),
            out_shape=[jax.ShapeDtypeStruct((size, w), shard.dtype) for w in widths],
            compiler_params=pltpu.CompilerParams(
                vmem_limit_bytes=2 * size * sum(widths) * 2 + (1 << 20)
            ),
            cost_estimate=cost(6),
            name="place_weights",
        )(offsets, shard, *stacks)


class Reduce:
    def __init__(self, here):
        self.here = here
        self.split = False

    def swap(self, away):
        self.came = self.here.send(away.astype(BF), "c")

    def take(self, part):
        self.begin(part + self.came.astype(F32))

    def begin(self, part):
        part = part.astype(BF)
        here = self.here
        rows = part.shape[0] // here.nf
        self.part = part.reshape(2, 2, here.ny, rows, part.shape[1])
        self.axes = ["v", "w", "y"]

    def step(self, way, *after):
        here = self.here
        part = hold(self.part, *after)
        number, mine = here.number[way], here.mine[way]
        if way in "xc" and not self.axes:
            total = part.astype(F32)
            for s in range(1, number):
                total = total + here.send(part, way, s).astype(F32)
            self.part = total.astype(BF)
            return
        if way == "x":
            axis = len(self.axes)
            shape = part.shape
            part = part.reshape(shape[:axis] + (number, shape[axis] // number) + shape[axis + 1 :])
            self.split = True
        else:
            axis = self.axes.index(way)
            self.axes.pop(axis)
        total = lax.dynamic_index_in_dim(part, mine, axis, keepdims=False).astype(F32)
        for s in range(1, number):
            out = lax.dynamic_index_in_dim(part, (mine + s) % number, axis, keepdims=False)
            total = total + here.send(out, way, s).astype(F32)
        self.part = total.astype(BF)

    def rows(self):
        if self.split:
            self.part = join_way(self.here, self.part, "x", 0)

    def other(self):
        return self.here.send(self.part, "c")


def join_way(here, array, way, axis):
    number, mine = here.number[way], here.mine[way]
    got = [array] + [here.send(array, way, s) for s in range(1, number)]
    if number == 2:
        ahead = jnp.concatenate(got, axis=axis)
        behind = jnp.concatenate(got[::-1], axis=axis)
        return jnp.where(mine == 0, ahead, behind)
    stack = jnp.stack(got)
    order = (mine - jnp.arange(number)) % number
    stack = jnp.take(stack, order, axis=0)
    return jnp.concatenate([stack[i] for i in range(number)], axis=axis)


def contract(left, right, left_dim, right_dim):
    return lax.dot_general(
        left, right, (((left_dim,), (right_dim,)), ((), ())), preferred_element_type=F32
    )


def rms_norm(values, gain):
    return values * lax.rsqrt(jnp.mean(values * values, axis=-1, keepdims=True) + EPSILON) * gain


def swiglu(pair):
    half = pair.shape[1] // 2
    return jax.nn.silu(pair[:, :half]) * pair[:, half:]


def kv_order(array):
    half = array.shape[1] // 6
    return [array[:, i * half : (i + 1) * half] for i in (2, 4, 3, 5)]


def from_behind(value, steps):
    count = lax.axis_size("fsdp")
    first, last = (max(0, -steps), min(count, count - steps))
    return lax.ppermute(value, "fsdp", [(source, source + steps) for source in range(first, last)])


def to_owners(parts, fanout):
    heads, d, width = parts.shape
    cut = parts.reshape(heads, d, fanout, width // fanout)
    return jnp.swapaxes(cut, 1, 2).reshape(heads * fanout, d, width // fanout)


def to_heads(parts, fanout):
    owners, d, width = parts.shape
    cut = parts.reshape(owners // fanout, fanout, d, width)
    return jnp.swapaxes(cut, 1, 2).reshape(owners // fanout, d, width * fanout)


def swap(value):
    return lax.all_to_all(value, "fsdp", 0, 0, tiled=True)


def by_core(here, for_zero, for_one):
    return jnp.where(here.mine["c"] == 0, for_zero, for_one)


def on_device(
    hidden_in,
    seg_ids,
    attn_gain,
    qkv_weight,
    beta_weight,
    gate_weight,
    conv_taps,
    out_gain,
    out_weight,
    ffn_gain,
    ffn_gate,
    ffn_up,
    ffn_down,
    cotangent,
):
    here = Place()
    row_count, width = hidden_in.shape
    heads = beta_weight.shape[1]
    head_dim = width // heads
    blocks = row_count // SPAN
    rim = 8
    lanes = 128
    hidden_units = ffn_gate.shape[1]

    rim_rows = from_behind(hidden_in[row_count - rim :], 1)
    numbers = seg_ids + 1
    rim_ids = from_behind(numbers[row_count - rim :], 1)

    small = [attn_gain, out_gain, ffn_gain, conv_taps]
    shard_rows = qkv_weight.shape[0]
    flat = jnp.concatenate([a.reshape(-1) for a in small])
    columns = -(-flat.size // shard_rows)
    flat = jnp.pad(flat, (0, columns * shard_rows - flat.size)).reshape(shard_rows, columns)
    extra = jnp.concatenate(
        [beta_weight, flat, jnp.zeros((shard_rows, lanes - heads - columns), BF)], axis=1
    )
    first = Gather(
        here,
        jnp.concatenate(kv_order(qkv_weight) + [extra], axis=1),
        [2 * width, lanes],
        True,
    )
    second = Gather(
        here,
        jnp.concatenate([qkv_weight[:, :width], gate_weight, out_weight], axis=1),
        [2 * width, width],
        False,
    )
    third = Gather(here, jnp.concatenate([ffn_gate, ffn_up], axis=1), [2 * hidden_units], True)
    fourth = Gather(here, ffn_down, [width], False, by_rows=False)
    first.move("v", "w")
    first.move("vw")
    first.pile()
    first.move("zy", "zx", "zc")
    first.move("zyx", "zyc", "zxc")
    second.move("v", "w", after=first.got("vw"))
    first.move("zyxc", after=second.got("v", "w"))
    second.move("vw")
    second.pile()
    kv_full, extra_full = first.place()

    small_full = extra_full[:, heads : heads + columns].reshape(here.nf, -1)
    cuts, at = [], 0
    for array in small:
        cuts.append(small_full[:, at : at + array.size].astype(F32))
        at += array.size
    attn_scale = cuts[0].reshape(-1)
    outgain_scale = cuts[1].reshape(1, -1)
    ffngain_scale = cuts[2].reshape(-1)
    taps_count = conv_taps.shape[0]
    taps_scale = jnp.swapaxes(cuts[3].reshape(here.nf, taps_count, -1), 0, 1).reshape(taps_count, -1)
    query_taps = taps_scale[:, :width]
    kv_taps = jnp.concatenate(kv_order(taps_scale), axis=1)
    residual = hidden_in.astype(F32)
    extended_in = jnp.concatenate([hidden_in, rim_rows]).astype(F32)
    normed_ext = rms_norm(extended_in, attn_scale).astype(BF)
    normed_low = normed_ext[:row_count]
    second.move("zy")
    kv_full = hold(kv_full, second.got("z"))
    kv_pre = jnp.dot(normed_ext, kv_full, preferred_element_type=F32)
    third.move("v", "w", after=[kv_pre])
    beta_pre = jnp.dot(normed_low, extra_full, preferred_element_type=F32)[:, :heads]
    rates = jax.nn.sigmoid(beta_pre)
    ids = jnp.concatenate([rim_ids, numbers]).astype(F32)
    own_ids = numbers.astype(F32)
    before = ids[rim - 1 : rim - 1 + row_count : SPAN]
    cols = jnp.concatenate(
        [rates, own_ids[:, None]]
        + [(ids[rim - j : rim - j + row_count] == own_ids).astype(F32)[:, None] for j in (1, 2, 3)]
        + [jnp.zeros((row_count, heads - 4), F32)],
        1,
    )
    rows = jnp.concatenate(
        [
            jnp.swapaxes(rates.reshape(blocks, SPAN, heads), 1, 2),
            own_ids.reshape(blocks, 1, SPAN),
            jnp.broadcast_to(before[:, None, None], (blocks, 1, SPAN)),
            jnp.zeros((blocks, heads - 2, SPAN), F32),
        ],
        1,
    )
    second.move("zc", after=[cols])
    key_low, value_low, w, u, a, moves = delta_summary(kv_pre, kv_taps, cols, rows, heads)
    moves = hold(moves, second.got("zy"), third.got("v", "w"))
    second.move("zyc", after=[moves])
    third.move("vw", after=[moves])
    fourth.move("v", "w", after=[moves])
    third.pile()
    third.move("zy", "zx")
    fanout = here.nf // heads
    if fanout > 1:
        moves = jnp.concatenate(
            [
                to_owners(moves[:, :, :head_dim], fanout),
                jnp.repeat(moves[:, :, head_dim:], fanout, axis=0),
            ],
            axis=2,
        )
    owned = swap(moves)
    qg_full, outw_full = second.place()
    qg_pre = jnp.dot(normed_ext, qg_full, preferred_element_type=F32)
    fourth.move("vw", after=[owned])
    fourth.pile()
    third.move("zyx", after=[owned])
    third.move("zc", "zxc", "zyc", after=[owned])
    entry = swap(scan_states(owned))
    if fanout > 1:
        entry = to_heads(entry, fanout)
    fourth.move("zy", after=[entry] + third.got("zy"))
    fourth.move("zc", after=[entry])
    query_low, gated_low, attn_heads, fresh, kept = delta_forward(
        qg_pre, query_taps, key_low, w, u, cols, rows, entry, outgain_scale, heads
    )
    third.move("zyxc", after=[gated_low])
    fourth.move("zyc", after=[gated_low])
    middle = residual + jnp.dot(gated_low, outw_full, preferred_element_type=F32)
    normed_two, norm_two_back = jax.vjp(rms_norm, middle, ffngain_scale)
    normed_two_low = normed_two.astype(BF)
    (pair_full,) = third.place()
    pair_pre = jnp.dot(normed_two_low, pair_full, preferred_element_type=F32)
    hidden_ff, swiglu_back = jax.vjp(swiglu, pair_pre)
    hidden_low = hidden_ff.astype(BF)
    (down_full,) = fourth.place()

    c = here.mine["c"]

    def shares(array, start, size):
        half = size // 2
        cut = [lax.dynamic_slice_in_dim(array, start + at * half, half, 1) for at in (1 - c, c)]
        return cut

    hidden_grad = contract(cotangent, down_full, 1, 1)
    theirs, ours = shares(cotangent, 0, width)
    down_sum = Reduce(here)
    down_sum.swap(contract(hidden_low, theirs, 0, 0))
    (pair_grad,) = swiglu_back(hidden_grad)
    pair_low = pair_grad.astype(BF)
    hidden_sums = [Reduce(here), Reduce(here)]
    quarter = hidden_units // 2
    nears = []
    for i, one in enumerate(hidden_sums):
        away = lax.dynamic_slice_in_dim(pair_low, (1 - c) * hidden_units + i * quarter, quarter, 1)
        nears.append(lax.dynamic_slice_in_dim(pair_low, c * hidden_units + i * quarter, quarter, 1))
        one.swap(contract(normed_two_low, away, 0, 0))
    hidden_a, hidden_b = hidden_sums
    down_sum.take(contract(hidden_low, hold(ours, pair_low), 0, 0))
    top_grad = cotangent.astype(F32)
    normed_two_grad = contract(pair_low, pair_full, 1, 1)
    middle_back, ffngain_grad = norm_two_back(normed_two_grad)
    middle_grad = top_grad + middle_back
    middle_low = middle_grad.astype(BF)
    gated_grad = contract(middle_low, outw_full, 1, 1)
    gated_grad = hold(gated_grad, down_sum.part, hidden_a.came, hidden_b.came)
    down_sum.step("y")
    heads_grad, gatepre_low, outgain_grad, local_later = delta_adjoint(
        query_low, key_low, w, cols, rows, gated_grad, attn_heads, qg_pre, outgain_scale, heads
    )
    local_later = hold(local_later, down_sum.part)
    if fanout > 1:
        local_later = to_owners(local_later, fanout)
    came_later = swap(local_later)

    near_a, near_b = hold(tuple(nears), local_later)
    hidden_a.take(contract(normed_two_low, near_a, 0, 0))
    hidden_b.take(contract(normed_two_low, near_b, 0, 0))
    down_sum.step("w", local_later)
    came_later = hold(came_later, hidden_a.part, hidden_b.part)
    hidden_a.step("x")
    hidden_b.step("y")
    later = swap(scan_grads(owned, came_later))
    if fanout > 1:
        later = to_heads(later, fanout)
    hidden_held, middle_held, gatepre_held = hold((hidden_low, middle_low, gatepre_low), came_later)
    output = (middle + jnp.dot(hidden_held, down_full, preferred_element_type=F32)).astype(BF)
    out_grad = contract(gated_low, middle_held, 0, 0)
    gate_grad = contract(normed_low, gatepre_held, 0, 0)
    other_sum = Reduce(here)
    other_sum.swap(by_core(here, gate_grad, out_grad))
    later = hold(later, down_sum.part, output, hidden_a.part, hidden_b.part, other_sum.came)
    other_sum.take(by_core(here, out_grad, gate_grad))
    later = hold(later, other_sum.part)
    down_sum.step("v")
    hidden_a.step("y")
    hidden_b.step("w")
    other_sum.step("x")
    state = (query_low, key_low, value_low, w, u, a, fresh, kept, heads_grad, cols, rows)
    mixed_a, beta_a, taps_a = delta_backward(
        0, *state, later, qg_pre, query_taps, kv_pre, kv_taps, heads
    )
    mixed_a = hold(mixed_a, down_sum.part, hidden_a.part, hidden_b.part, other_sum.part)
    a_sum = Reduce(here)
    size = 3 * width // 2
    theirs, ours = shares(mixed_a, 0, size)
    a_sum.swap(contract(normed_ext, theirs, 0, 0))
    a_sum.take(contract(normed_ext, ours, 0, 0))
    later = hold(later, a_sum.part)
    a_sum.step("x")
    hidden_a.step("w", mixed_a)
    hidden_b.step("v", mixed_a)
    other_sum.step("y", mixed_a)
    mixed_b, beta_b, taps_b = delta_backward(
        1, *state, later, qg_pre, query_taps, kv_pre, kv_taps, heads
    )
    mixed_b = hold(mixed_b, hidden_a.part, hidden_b.part, other_sum.part, a_sum.part)
    b_sum = Reduce(here)
    theirs, ours = shares(mixed_b, 0, size)
    b_sum.swap(contract(normed_ext, theirs, 0, 0))
    b_sum.take(contract(normed_ext, ours, 0, 0))
    mixed_b = hold(mixed_b, b_sum.part)
    b_sum.step("x")
    a_sum.step("y", mixed_b)
    hidden_a.step("v", mixed_b)
    other_sum.step("w", mixed_b)
    betapre_low = (beta_a + beta_b).astype(BF)
    beta_grad = contract(normed_low, betapre_low, 0, 0)[:, :heads]
    eighth = width // 2
    wide_grad = (
        contract(mixed_a[:, eighth:], kv_full[:, :width], 1, 1)
        + contract(mixed_b[:, eighth:], kv_full[:, width:], 1, 1)
        + contract(mixed_a[:, :eighth], qg_full[:, :eighth], 1, 1)
        + contract(mixed_b[:, :eighth], qg_full[:, eighth:width], 1, 1)
    )
    rim_grad = from_behind(wide_grad[row_count:].astype(BF), -1).astype(F32)
    normed_grad = hold(
        wide_grad[:row_count]
        + jnp.pad(rim_grad, ((row_count - rim, 0), (0, 0)))
        + contract(betapre_low, extra_full, 1, 1)
        + contract(gatepre_low, qg_full[:, width:], 1, 1),
        a_sum.part,
    )
    input_back, attngain_grad = jax.vjp(rms_norm, residual, attn_scale)[1](normed_grad)
    input_grad = (middle_grad + input_back).astype(BF)

    def by_kind(first_heads, other_heads):
        cut = [slice(i * eighth, (i + 1) * eighth) for i in range(3)]
        both = [array[:, s] for s in cut for array in (first_heads, other_heads)]
        return jnp.concatenate(both, axis=1)

    taps_grad = by_kind(taps_a, taps_b)
    parts = (
        attngain_grad.reshape(here.nf, -1),
        outgain_grad.reshape(here.nf, -1),
        ffngain_grad.reshape(here.nf, -1),
        jnp.swapaxes(taps_grad.reshape(taps_count, here.nf, -1), 0, 1).reshape(here.nf, -1),
    )
    flat = jnp.concatenate(parts, axis=1)
    flat = jnp.pad(flat, ((0, 0), (0, columns * shard_rows - flat.shape[1])))
    extra = jnp.concatenate(
        [
            beta_grad,
            flat.reshape(width, columns),
            jnp.zeros((width, lanes - heads - columns), F32),
        ],
        axis=1,
    )
    small_sum = Reduce(here)
    small_sum.begin(extra)
    first_tail = (b_sum.part, hidden_a.part, other_sum.part, a_sum.part)
    b_sum.step("y", *first_tail)
    a_sum.step("w", *first_tail)
    other_sum.step("v", *first_tail)
    down_sum.step("x", *first_tail)
    small_sum.step("y", b_sum.part)
    second_tail = (b_sum.part, a_sum.part, other_sum.part, down_sum.part)
    b_sum.step("w", *second_tail)
    a_sum.step("v", *second_tail)
    hidden_b.step("x", *second_tail)
    small_sum.step("w", b_sum.part)
    b_sum.step("v", a_sum.part, hidden_b.part)
    small_sum.step("v", b_sum.part)
    small_sum.step("x")
    small_sum.step("c")
    for done in (hidden_a, other_sum, a_sum, b_sum):
        done.rows()
    hidden = jnp.concatenate([hidden_a.part, hidden_b.part], axis=1)
    other = here.send(hidden, "c")
    hidgate_total = by_core(here, hidden, other).astype(F32)
    hidup_total = by_core(here, other, hidden).astype(F32)
    other = other_sum.other()
    outproj_total = by_core(here, other_sum.part, other).astype(F32)
    gate_total = by_core(here, other, other_sum.part).astype(F32)
    down_total = join_way(here, down_sum.part, "c", 1).astype(F32)
    qkv_total = by_kind(
        join_way(here, a_sum.part, "c", 1), join_way(here, b_sum.part, "c", 1)
    ).astype(F32)
    extra = small_sum.part.astype(F32)
    flat = extra[:, heads : heads + columns].reshape(-1)
    cut, at = [], 0
    for part in parts:
        cut.append(flat[at : at + part.shape[1]])
        at += part.shape[1]
    return (
        output,
        input_grad,
        cut[0],
        qkv_total,
        extra[:, :heads],
        gate_total,
        cut[3].reshape(conv_taps.shape),
        cut[1],
        outproj_total,
        cut[2],
        hidgate_total,
        hidup_total,
        down_total,
    )


def solution(mesh):
    placed = (
        P(("rep", "fsdp"), None),
        P(("rep", "fsdp")),
        P("fsdp"),
        P("fsdp", None),
        P("fsdp", None),
        P("fsdp", None),
        P(None, "fsdp"),
        P("fsdp"),
        P("fsdp", None),
        P("fsdp"),
        P("fsdp", None),
        P("fsdp", None),
        P("fsdp", None),
        P(("rep", "fsdp"), None),
    )
    return jax.shard_map(
        on_device,
        mesh=mesh,
        in_specs=placed,
        out_specs=(
            P(("rep", "fsdp"), None),
            P(("rep", "fsdp"), None),
            P("fsdp"),
            P("fsdp", None),
            P("fsdp", None),
            P("fsdp", None),
            P(None, "fsdp"),
            P("fsdp"),
            P("fsdp", None),
            P("fsdp"),
            P("fsdp", None),
            P("fsdp", None),
            P("fsdp", None),
        ),
        check_vma=False,
    )
```

time: 836 us -> 667 us (0.80)
  waiting for transfers between devices: 280 us -> 193 us
  starting transfers between devices: 170 us -> 92.9 us
  matrix products: 112 us -> 96.6 us
  local copies, waits for them, and re-layouts: 63.6 us -> 75.3 us
  other arithmetic: 67 us -> 56.6 us
    ppermute x108 -> x76, waiting for transfers between devices: 273 us -> 192 us  [send(): return lax.ppermute(value, axis, pairs)]
    ppermute x108 -> x76, starting transfers between devices: 139 us -> 67.6 us  [send(): return lax.ppermute(value, axis, pairs)]
    mul x3 -> x1, other arithmetic: 14 us -> 0.07 us  [rms_norm(): values * lax.rsqrt(jnp.mean(values * values, axis=-1, keepdims=True) + EP...]
    convert_element_type x36, other arithmetic: 20.3 us -> 33.8 us  [the longest x28 18.1 us: step(): self.part = total.astype(BF)]
    dot_general x25 -> x22, matrix products: 74.8 us -> 64.5 us  [contract(): lax.dot_general(left, right, (((left_dim,), (right_dim,)), ((), ())), pre...]
    reduce_sum x3 -> x1, other arithmetic: 11 us -> 1.3 us  [rms_norm(): values * lax.rsqrt(jnp.mean(values * values, axis=-1, keepdims=True) + EP...]
    dot_general x6 -> x5, matrix products: 35.4 us -> 30.8 us  [the longest x1 10.9 us: on_device(): pair_pre = jnp.dot(normed_two_low, pair_full, preferred_element_type=F32)]
    pallas_call x5 -> x6, Pallas kernels: 77 us -> 79.8 us  [the longest x2 66.2 us: delta_backward(): pl.pallas_call(partial(backward_kernel, heads, part, d), grid=(blocks + 1...]
  transfers between devices with their start and end apart: 115 -> 83, of which waited for: 55 -> 29; matrix products, arithmetic and copies ran while one was open for 21% -> 23% of each run, Pallas kernels for 13% -> 21%
where the time goes in v2:
time: 667 us; the launch traced here: 657 us
  waiting for transfers between devices  193 us (29%)
  Pallas kernels  140 us (21%)
  matrix products  96.6 us (14%)
  starting transfers between devices  92.9 us (14%)
  local copies, waits for them, and re-layouts  75.3 us (11%)
  other arithmetic  56.6 us (8%)
    ppermute x76, waiting for transfers between devices, send(): return lax.ppermute(value, axis, pairs)  192 us
    ppermute x76, starting transfers between devices, send(): return lax.ppermute(value, axis, pairs)  67.6 us
    pallas_call x2, Pallas kernels, delta_backward(): pl.pallas_call(partial(backward_kernel, heads, part, d), grid=(blocks + 1...  66.2 us
    dot_general x22, matrix products, contract(): lax.dot_general(left, right, (((left_dim,), (right_dim,)), ((), ())), pre...  64.5 us
    unnamed x244, local copies, waits for them, and re-layouts  40 us
    pallas_call x1, Pallas kernels, delta_summary(): pl.pallas_call(partial(summary_kernel, heads, d), grid=(blocks,), in_spec...  26 us
    convert_element_type x28, other arithmetic, step(): self.part = total.astype(BF)  18.1 us
    all_to_all x4, starting transfers between devices, swap(): return lax.all_to_all(value, 'fsdp', 0, 0, tiled=True)  18 us
  transfers between devices with their start and end apart: 83, of which 29 were waited for; matrix products, arithmetic and copies ran while one was open for 23% of the time, Pallas kernels for 21%

profile of v2, /device:TPU:0, one launch (start us, length us, event | category | flops | bytes accessed | tf_op | source)
XLA Modules:
  0.0 657.4 jit_solution(11172411920205199133)
XLA Ops:
  6.0 4.1 collective-permute-start.2
  12.4 3.4 collective-permute-start
  15.9 2.3 collective-permute-start.15
  21.9 4.6 collective-permute-done.3
  31.8 8.1 %collective-permute-done.4.refs_1_ = bf16[4,32,2176]{2,1,0:T(8,128)(2,1)} collective-permute-done((bf16[4,32,2176]{2,1,0:T(8,128)(2,1)S(1)}, bf16[4,32,2176]{2,1,0:T(8,128)(2,1)}, u32[]{:S(2)}, u32[]{:S(2)}) %collective-permute-start.4) | collective-permute-done | bytes 557088 | tf_op jit(solution)/shard_map/ppermute | solution.py:563
  43.7 5.4 collective-permute-done.10
  51.4 6.0 collective-permute-done.11
  57.9 7.9 %collective-permute-done.13 = bf16[64,3072]{1,0:T(8,128)(2,1)} collective-permute-done((bf16[64,3072]{1,0:T(8,128)(2,1)}, bf16[64,3072]{1,0:T(8,128)(2,1)}, u32[]{:S(2)}, u32[]{:S(2)}) %collective-permute-start.13) | collective-permute-done | bytes 393248 | tf_op jit(solution)/shard_map/ppermute | solution.py:563
  65.8 2.6 pad_maximum_fusion.refs_0_
  68.9 3.0 place_weights.4
  76.5 6.7 %fusion.101.pre_ref.prev_ref.kvpre_ref.kvprev_ref = f32[520,2048]{1,0:T(8,128)} fusion(bf16[520,1024]{1,0:T(8,128)(2,1)S(1)} %fusion.8, bf16[1024,2048]{1,0:T(8,128)(2,1)} %copy-done.18), kind=kOutput, calls=%fused_computation.255 | convolution fusion | flops 2181038080 | bytes 9519104 | tf_op jit(solution)/shard_map/dot_general | solution.py:852
  84.7 2.2 copy-done.20
  86.9 26.0 %delta_summary.1 = (bf16[512,1024]{1,0:T(8,128)(2,1)S(1)}, bf16[512,1024]{1,0:T(8,128)(2,1)S(1)}, bf16[512,1024]{1,0:T(8,128)(2,1)S(1)}, bf16[512,1024]{1,0:T(8,...) custom-call(f32[520,2048]{1,0:T(8,128)S(1)} %copy-done.20, f32[520,2048]{1,0:T(8,128)S(1)} %copy-done.20, ...), custom_call_target="tpu_custom_call" | custom-call | flops 24000000000 | bytes 72000000 | tf_op jit(solution)/shard_map/delta_summary/pallas_call | solution.py:374
  117.9 5.9 all-to-all-start
  123.8 2.9 collective-permute-start.29
  131.4 23.2 %collective-permute-done.29 = bf16[352,512]{1,0:T(8,128)(2,1)} collective-permute-done((bf16[352,512]{1,0:T(8,128)(2,1)}, bf16[352,512]{1,0:T(8,128)(2,1)}, u32[]{:S(2)}, u32[]{:S(2)}) %collective-permute-start.29) | collective-permute-done | bytes 360480 | tf_op jit(solution)/shard_map/ppermute | solution.py:563
  158.4 2.7 state_prefix.1
  161.1 3.6 all-to-all-start.1
  166.2 2.6 pad_maximum_fusion.2.refs_0_
  168.9 3.7 place_weights.5
  173.9 4.4 fusion.102.pre_ref.prev_ref.gate_ref.qpre_ref.qprev_ref
  178.3 14.1 %collective-permute-done.21.refs_1_ = bf16[4,32,5632]{2,1,0:T(8,128)(2,1)} collective-permute-done((bf16[4,32,5632]{2,1,0:T(8,128)(2,1)S(1)}, bf16[4,32,5632]{2,1,0:T(8,128)(2,1)}, u32[]{:S(2)}, u32[]{:S(2)}) %collective-permute-start.21) | collective-permute-done | bytes 1441824 | tf_op jit(solution)/shard_map/ppermute | solution.py:563
  198.8 13.1 %delta_forward.1 = (bf16[512,1024]{1,0:T(8,128)(2,1)S(1)}, bf16[512,1024]{1,0:T(8,128)(2,1)S(1)}, f32[512,1024]{1,0:T(8,128)S(1)}, bf16[512,1024]{1,0:T(8,128)(2,1)S(1)}, bf16[8,8,128,128]{3,2,1,0:T(8,128)(2,1)S(1)}) custom-call(f32[520,2048]{1,0:T(8,128)S(1)} %copy-done.22, f32[520,2048]{1,0:T(8,128)S(1)} %copy-done.22, ...), custom_call_target="tpu_custom_call" | custom-call | flops 16000000000 | bytes 48000000 | tf_op jit(solution)/shard_map/delta_forward/pallas_call | solution.py:405
  214.7 13.6 %collective-permute-done.23.refs_3_ = bf16[4,32,5632]{2,1,0:T(8,128)(2,1)} collective-permute-done((bf16[4,32,5632]{2,1,0:T(8,128)(2,1)}, bf16[4,32,5632]{2,1,0:T(8,128)(2,1)}, u32[]{:S(2)}, u32[]{:S(2)}) %collective-permute-start.23) | collective-permute-done | bytes 1441824 | tf_op jit(solution)/shard_map/ppermute | solution.py:563
  233.0 14.0 %collective-permute-done.31.refs_1_ = bf16[4,352,512]{2,1,0:T(8,128)(2,1)S(1)} collective-permute-done((bf16[4,352,512]{2,1,0:T(8,128)(2,1)S(1)}, bf16[4,352,512]{2,1,0:T(8,128)(2,1)S(1)}, u32[]{:S(2)}, u32[]{:S(2)}) %collective-permute-start.31) | collective-permute-done | bytes 1441824 | tf_op jit(solution)/shard_map/ppermute | solution.py:563
  247.6 4.3 place_weights.6
  251.9 10.9 %fusion.103 = f32[512,5632]{1,0:T(8,128)} fusion(bf16[512,1024]{1,0:T(8,128)(2,1)} %multiply_convert_fusion.1, bf16[1024,5632]{1,0:T(8,128)(2,1)S(1)} %place_weights.6), kind=kOutput, calls=%fused_computation.257 | convolution fusion | flops 5905580032 | bytes 24117248 | tf_op jit(solution)/shard_map/dot_general | solution.py:912
  262.9 2.7 place_weights.7
  265.6 13.0 %bitcast_multiply_fusion.1 = (f32[512,2816]{1,0:T(8,128)}, f32[512,2816]{1,0:T(8,128)}, bf16[512,2816]{1,0:T(8,128)(2,1)S(1)}) fusion(f32[512,5632]{1,0:T(8,128)} %fusion.103, bf16[2816,1024]{1,0:T(8,128)(2,1)S(1)} %place_weights.7, bf16[512,1024]{1,0:T(8,128)(2,1)S(1)} %copy-done.65), kind=kOutput, calls=%fused_computation.5 | convolution fusion | flops 2972975104 | bytes 32768000 | tf_op jit(solution)/shard_map/dot_general | solution.py:727
  278.6 3.3 convolution_convert_fusion
  282.0 7.4 %add_convert_fusion = bf16[512,5632]{1,0:T(8,128)(2,1)} fusion(f32[512,2816]{1,0:T(8,128)} %get-tuple-element.170, f32[512,2816]{1,0:T(8,128)} %get-tuple-element.169), kind=kLoop, calls=%fused_computation | loop fusion | flops 5767168 | bytes 17301504 | tf_op jit(solution)/shard_map/convert_element_type | solution.py:929
  289.4 4.9 convolution_convert_fusion.1
  294.8 3.4 convolution_convert_fusion.2
  298.2 9.9 %multiply_reduce_fusion = (bf16[1024]{0:T(1024)(128)(2,1)}, f32[512]{0:T(512)S(1)}, f32[512,1024]{1,0:T(8,128)S(1)}) fusion(f32[512,1024]{1,0:T(8,128)S(1)} %copy-done.56, f32[512]{0:T(512)S(1)} %fusion.94, f32[1024]{0:T(1024)S(1)} %get-tuple-element.192, bf16[512,5632]{1,0:T(8,128)(2,1)S(1)} %copy-done.59, bf16[1024,5632]{1,0:T(8,128)(2,1)} %copy-done), kind=kOutput, calls=%fused_computation.50 | convolution fusion | flops 5908724224 | bytes 21506048 | tf_op jit(solution)/shard_map/dot_general | solution.py:727
  314.4 3.8 add_convert_fusion.3
  322.3 15.2 %delta_adjoint.1 = (bf16[512,1024]{1,0:T(8,128)(2,1)S(1)}, bf16[512,1024]{1,0:T(8,128)(2,1)S(1)}, f32[1,128]{1,0:T(1,128)S(1)}, bf16[8,128,128]{2,1,0:T(8,128)(2,1)}) custom-call(bf16[512,1024]{1,0:T(8,128)(2,1)S(1)} %copy-done.41, bf16[512,1024]{1,0:T(8,128)(2,1)S(1)} %copy-done.31, bf16[512,1024]{1,0:T(8,128)(2,1)S(1)} %copy-done.35, ...), custom_call_target="tpu_custom_call" | custom-call | flops 15000000512 | bytes 45000000 | tf_op jit(solution)/shard_map/delta_adjoint/pallas_call | solution.py:440
  339.2 15.9 %collective-permute-done.37 = bf16[2,2,352,512]{3,2,0,1:T(8,128)(2,1)} collective-permute-done((bf16[2,2,352,512]{3,2,0,1:T(8,128)(2,1)}, bf16[2,2,352,512]{3,2,0,1:T(8,128)(2,1)}, u32[]{:S(2)}, u32[]{:S(2)}) %collective-permute-start.37) | collective-permute-done | bytes 1441824 | tf_op jit(solution)/shard_map/ppermute | solution.py:563
  355.0 3.4 fusion.5
  358.4 4.3 all-to-all-start.2
  362.7 4.1 add_convert_fusion.1
  378.5 2.6 fusion.105
  381.2 4.0 select_convert_fusion
  385.2 2.8 state_suffix.1
  388.0 4.2 all-to-all-start.3
  392.2 8.3 %add_convert_fusion.7 = bf16[512,1024]{1,0:T(8,128)(2,1)} fusion(f32[512,1024]{1,0:T(8,128)} %copy-done.55, bf16[512,2816]{1,0:T(8,128)(2,1)} %copy-done.109, bf16[2816,1024]{1,0:T(8,128)(2,1)} %copy-done.24), kind=kOutput, calls=%fused_computation.57 | convolution fusion | flops 2953838592 | bytes 11796480 | tf_op jit(solution)/shard_map/dot_general | solution.py:966
  402.0 3.0 collective-permute-start.42
  412.3 9.0 %collective-permute-done.42 = bf16[352,512]{1,0:T(8,128)(2,1)S(1)} collective-permute-done((bf16[352,512]{1,0:T(8,128)(2,1)S(1)}, bf16[352,512]{1,0:T(8,128)(2,1)S(1)}, u32[]{:S(2)}, u32[]{:S(2)}) %collective-permute-start.42) | collective-permute-done | bytes 360480 | tf_op jit(solution)/shard_map/ppermute | solution.py:563
  422.2 9.0 %collective-permute-done.44 = bf16[2,128,1408]{2,1,0:T(8,128)(2,1)S(1)} collective-permute-done((bf16[2,128,1408]{2,1,0:T(8,128)(2,1)S(1)}, bf16[2,128,1408]{2,1,0:T(8,128)(2,1)S(1)}, u32[]{:S(2)}, u32[]{:S(2)}) %collective-permute-start.44) | collective-permute-done | bytes 720928 | tf_op jit(solution)/shard_map/ppermute | solution.py:563
  433.3 2.9 add_convert_fusion.4
  453.6 33.1 %delta_backward.2 = (bf16[520,1536]{1,0:T(8,128)(2,1)S(1)}, f32[512,128]{1,0:T(8,128)S(1)}, f32[4,1536]{1,0:T(4,128)S(1)}) custom-call(bf16[512,1024]{1,0:T(8,128)(2,1)S(1)} %copy-done.42, bf16[512,1024]{1,0:T(8,128)(2,1)S(1)} %copy-done.32, bf16[512,1024]{1,0:T(8,128)(2,1)S(1)} %copy-done.48, bf16[512,1024]{1,0:T(8,128)(2,1)S(1)} %copy-done.36, ...), custom_call_target="tpu_custom_call" | custom-call | flops 32000000000 | bytes 96000000 | tf_op jit(solution)/shard_map/delta_backward/pallas_call | solution.py:499
  494.3 2.5 collective-permute-start.47
  498.1 14.2 %collective-permute-done.48 = bf16[128,1408]{1,0:T(8,128)(2,1)S(1)} collective-permute-done((bf16[128,1408]{1,0:T(8,128)(2,1)S(1)}, bf16[128,1408]{1,0:T(8,128)(2,1)S(1)}, u32[]{:S(2)}, u32[]{:S(2)}) %collective-permute-start.48) | collective-permute-done | bytes 360480 | tf_op jit(solution)/shard_map/ppermute | solution.py:563
  515.9 33.1 %delta_backward.3 = (bf16[520,1536]{1,0:T(8,128)(2,1)S(1)}, f32[512,128]{1,0:T(8,128)S(1)}, f32[4,1536]{1,0:T(4,128)S(1)}) custom-call(bf16[512,1024]{1,0:T(8,128)(2,1)S(1)} %copy-done.42, bf16[512,1024]{1,0:T(8,128)(2,1)S(1)} %copy-done.32, bf16[512,1024]{1,0:T(8,128)(2,1)S(1)} %copy-done.48, bf16[512,1024]{1,0:T(8,128)(2,1)S(1)} %copy-done.36, ...), custom_call_target="tpu_custom_call" | custom-call | flops 32000000000 | bytes 96000000 | tf_op jit(solution)/shard_map/delta_backward/pallas_call | solution.py:499
  557.2 2.4 collective-permute-start.55
  565.6 2.7 collective-permute-start.53
  572.5 12.1 %collective-permute-done.76 = bf16[64,1408]{1,0:T(8,128)(2,1)S(1)} collective-permute-done((bf16[64,1408]{1,0:T(8,128)(2,1)S(1)}, bf16[64,1408]{1,0:T(8,128)(2,1)S(1)}, u32[]{:S(2)}, u32[]{:S(2)}) %collective-permute-start.76) | collective-permute-done | bytes 180256 | tf_op jit(solution)/shard_map/ppermute | solution.py:563
  592.9 4.6 fusion.11
  603.4 4.8 collective-permute-done.60
  609.4 3.9 collective-permute-done.74
  617.5 4.2 collective-permute-done.64
  627.4 4.1 collective-permute-done.63
  633.7 4.1 collective-permute-done.66
  638.9 3.7 collective-permute-done.67
  644.4 2.3 collective-permute-done.68
  (548 shorter events, 183.9 us)
Async XLA Ops:
  6.0 15.5 %collective-permute-start.2 = (bf16[32,2176]{1,0:T(8,128)(2,1)S(1)}, bf16[32,2176]{1,0:T(8,128)(2,1)S(1)}, u32[]{:S(2)}, u32[]{:S(2)}) collective-permute-start(bf16[32,2176]{1,0:T(8,128)(2,1)S(1)} %constant_dynamic-slice_fusion.12), channel_id=1, source_target_pairs={{0,4},{1,5},{2,6},{3,7},{4,0},{5,1},{6,2},{7,3},{8,12},{9,13},{10,... | collective-permute-start | bytes 417800 | tf_op jit(solution)/shard_map/ppermute | solution.py:563
  10.1 11.8 %collective-permute-start.1 = (bf16[32,2176]{1,0:T(8,128)(2,1)S(1)}, bf16[32,2176]{1,0:T(8,128)(2,1)S(1)}, u32[]{:S(2)}, u32[]{:S(2)}) collective-permute-start(bf16[32,2176]{1,0:T(8,128)(2,1)S(1)} %constant_dynamic-slice_fusion.12), channel_id=1, source_target_pairs={{0,2},{1,3},{2,0},{3,1},{4,6},{5,7},{6,4},{7,5},{8,10},{9,11},{10,... | collective-permute-start | bytes 417800 | tf_op jit(solution)/shard_map/ppermute | solution.py:563
  12.4 36.9 %collective-permute-start = (bf16[8,1024]{1,0:T(8,128)(2,1)S(1)}, bf16[8,1024]{1,0:T(8,128)(2,1)S(1)}, u32[]{:S(2)}, u32[]{:S(2)}) collective-permute-start(bf16[8,1024]{1,0:T(8,128)(2,1)S(1)} %slice.173), channel_id=1, source_target_pairs={{0,1},{1,2},{2,3},{3,4},{4,5},{5,6},{6,7},{8,9},{9,10},{10,11},{11... | collective-permute-start | bytes 49160 | tf_op jit(solution)/shard_map/ppermute | solution.py:749
  15.9 27.3 %collective-permute-start.15 = (s32[8]{0:T(128)S(1)}, s32[8]{0:T(128)S(1)}, u32[]{:S(2)}, u32[]{:S(2)}) collective-permute-start(s32[8]{0:T(128)S(1)} %slice.183), channel_id=1, source_target_pairs={{0,1},{1,2},{2,3},{3,4},{4,5},{5,6},{6,7},{8,9},{9,10},{10,11},{11... | collective-permute-start | bytes 104 | tf_op jit(solution)/shard_map/ppermute | solution.py:749
  27.6 12.3 %collective-permute-start.4 = (bf16[4,32,2176]{2,1,0:T(8,128)(2,1)S(1)}, bf16[4,32,2176]{2,1,0:T(8,128)(2,1)}, u32[]{:S(2)}, u32[]{:S(2)}) collective-permute-start(bf16[4,32,2176]{2,1,0:T(8,128)(2,1)S(1)} %pad_maximum_fusion.6.refs_0_), channel_id=1, source_target_pairs={{0,1},{1,0},{2,3},{3,2},{4,5},{5,4},{6,7},{7,6},{8,9},{9,8},{10,11... | collective-permute-start | bytes 1671176 | tf_op jit(solution)/shard_map/ppermute | solution.py:563
  29.9 20.9 %collective-permute-start.5 = (bf16[4,32,2176]{2,1,0:T(8,128)(2,1)S(1)}, bf16[4,32,2176]{2,1,0:T(8,128)(2,1)}, u32[]{:S(2)}, u32[]{:S(2)}) collective-permute-start(bf16[4,32,2176]{2,1,0:T(8,128)(2,1)S(1)} %pad_maximum_fusion.6.refs_0_), channel_id=1, source_target_pairs={{0,16},{8,24},{16,0},{24,8},{1,17},{9,25},{17,1},{25,9},{2,18},{10... | collective-permute-start | bytes 1671176 | tf_op jit(solution)/shard_map/ppermute | solution.py:563
  31.4 17.7 %collective-permute-start.10 = (bf16[64,3072]{1,0:T(8,128)(2,1)}, bf16[64,3072]{1,0:T(8,128)(2,1)}, u32[]{:S(2)}, u32[]{:S(2)}) collective-permute-start(bf16[64,3072]{1,0:T(8,128)(2,1)} %constant_dynamic-slice_fusion.11), channel_id=1, source_target_pairs={{0,4},{1,5},{2,6},{3,7},{4,0},{5,1},{6,2},{7,3},{8,12},{9,13},{10,... | collective-permute-start | bytes 1179656 | tf_op jit(solution)/shard_map/ppermute | solution.py:563
  39.8 17.6 %collective-permute-start.7 = (bf16[4,32,2176]{2,1,0:T(8,128)(2,1)}, bf16[4,32,2176]{2,1,0:T(8,128)(2,1)}, u32[]{:S(2)}, u32[]{:S(2)}) collective-permute-start(bf16[4,32,2176]{2,1,0:T(8,128)(2,1)} %collective-permute-done.4.refs_1_), channel_id=1, source_target_pairs={{0,16},{8,24},{16,0},{24,8},{1,17},{9,25},{17,1},{25,9},{2,18},{10... | collective-permute-start | bytes 1671176 | tf_op jit(solution)/shard_map/ppermute | solution.py:563
  43.2 14.2 %collective-permute-start.11 = (bf16[64,3072]{1,0:T(8,128)(2,1)}, bf16[64,3072]{1,0:T(8,128)(2,1)S(1)}, u32[]{:S(2)}, u32[]{:S(2)}) collective-permute-start(bf16[64,3072]{1,0:T(8,128)(2,1)} %constant_dynamic-slice_fusion.11), channel_id=1, source_target_pairs={{0,2},{1,3},{2,0},{3,1},{4,6},{5,7},{6,4},{7,5},{8,10},{9,11},{10,... | collective-permute-start | bytes 1179656 | tf_op jit(solution)/shard_map/ppermute | solution.py:563
  49.1 16.7 %collective-permute-start.13 = (bf16[64,3072]{1,0:T(8,128)(2,1)}, bf16[64,3072]{1,0:T(8,128)(2,1)}, u32[]{:S(2)}, u32[]{:S(2)}) collective-permute-start(bf16[64,3072]{1,0:T(8,128)(2,1)} %collective-permute-done.10), channel_id=1, source_target_pairs={{0,2},{1,3},{2,0},{3,1},{4,6},{5,7},{6,4},{7,5},{8,10},{9,11},{10,... | collective-permute-start | bytes 1179656 | tf_op jit(solution)/shard_map/ppermute | solution.py:563
  50.8 18.1 %collective-permute-start.6 = (bf16[4,32,2176]{2,1,0:T(8,128)(2,1)S(1)}, bf16[4,32,2176]{2,1,0:T(8,128)(2,1)S(1)}, u32[]{:S(2)}, u32[]{:S(2)}) collective-permute-start(bf16[4,32,2176]{2,1,0:T(8,128)(2,1)S(1)} %pad_maximum_fusion.6.refs_0_), channel_id=1, source_target_pairs={{0,8},{8,0},{16,24},{24,16},{1,9},{9,1},{17,25},{25,17},{2,10},{10... | collective-permute-start | bytes 1671176 | tf_op jit(solution)/shard_map/ppermute | solution.py:563
  50.9 18.1 %collective-permute-start.8 = (bf16[4,32,2176]{2,1,0:T(8,128)(2,1)}, bf16[4,32,2176]{2,1,0:T(8,128)(2,1)S(1)}, u32[]{:S(2)}, u32[]{:S(2)}) collective-permute-start(bf16[4,32,2176]{2,1,0:T(8,128)(2,1)} %collective-permute-done.4.refs_1_), channel_id=1, source_target_pairs={{0,8},{8,0},{16,24},{24,16},{1,9},{9,1},{17,25},{25,17},{2,10},{10... | collective-permute-start | bytes 1671176 | tf_op jit(solution)/shard_map/ppermute | solution.py:563
  57.4 11.5 %collective-permute-start.9 = (bf16[4,32,2176]{2,1,0:T(8,128)(2,1)}, bf16[4,32,2176]{2,1,0:T(8,128)(2,1)S(1)}, u32[]{:S(2)}, u32[]{:S(2)}) collective-permute-start(bf16[4,32,2176]{2,1,0:T(8,128)(2,1)} %collective-permute-done.5.refs_2_), channel_id=1, source_target_pairs={{0,8},{8,0},{16,24},{24,16},{1,9},{9,1},{17,25},{25,17},{2,10},{10... | collective-permute-start | bytes 1671176 | tf_op jit(solution)/shard_map/ppermute | solution.py:563
  68.4 49.5 %collective-permute-start.14 = (bf16[4,64,3072]{2,1,0:T(8,128)(2,1)}, bf16[4,64,3072]{2,1,0:T(8,128)(2,1)}, u32[]{:S(2)}, u32[]{:S(2)}) collective-permute-start(bf16[4,64,3072]{2,1,0:T(8,128)(2,1)} %pad_maximum_fusion.refs_0_), channel_id=1, source_target_pairs={{0,1},{1,0},{2,3},{3,2},{4,5},{5,4},{6,7},{7,6},{8,9},{9,8},{10,11... | collective-permute-start | bytes 4718600 | tf_op jit(solution)/shard_map/ppermute | solution.py:563
  83.3 34.6 %collective-permute-start.17 = (bf16[32,5632]{1,0:T(8,128)(2,1)S(1)}, bf16[32,5632]{1,0:T(8,128)(2,1)}, u32[]{:S(2)}, u32[]{:S(2)}) collective-permute-start(bf16[32,5632]{1,0:T(8,128)(2,1)S(1)} %copy-done.88), channel_id=1, source_target_pairs={{0,4},{1,5},{2,6},{3,7},{4,0},{5,1},{6,2},{7,3},{8,12},{9,13},{10,... | collective-permute-start | bytes 1081352 | tf_op jit(solution)/shard_map/ppermute | solution.py:563
  83.3 34.5 %collective-permute-start.18 = (bf16[32,5632]{1,0:T(8,128)(2,1)S(1)}, bf16[32,5632]{1,0:T(8,128)(2,1)}, u32[]{:S(2)}, u32[]{:S(2)}) collective-permute-start(bf16[32,5632]{1,0:T(8,128)(2,1)S(1)} %copy-done.88), channel_id=1, source_target_pairs={{0,2},{1,3},{2,0},{3,1},{4,6},{5,7},{6,4},{7,5},{8,10},{9,11},{10,... | collective-permute-start | bytes 1081352 | tf_op jit(solution)/shard_map/ppermute | solution.py:563
  84.5 84.4 %collective-permute-start.16 = (bf16[4,64,3072]{2,1,0:T(8,128)(2,1)}, bf16[4,64,3072]{2,1,0:T(8,128)(2,1)}, u32[]{:S(2)}, u32[]{:S(2)}) collective-permute-start(bf16[4,64,3072]{2,1,0:T(8,128)(2,1)} %pad_maximum_fusion.refs_0_), channel_id=1, source_target_pairs={{0,8},{8,0},{16,24},{24,16},{1,9},{9,1},{17,25},{25,17},{2,10},{10... | collective-permute-start | bytes 4718600 | tf_op jit(solution)/shard_map/ppermute | solution.py:563
  117.9 36.7 %all-to-all-start = ((bf16[8,128,256]{2,1,0:T(8,128)(2,1)}), bf16[8,128,256]{2,1,0:T(8,128)(2,1)S(1)}, u32[]{:S(2)}, u32[]{:S(2)}) async-start(bf16[8,128,256]{2,1,0:T(8,128)(2,1)} %get-tuple-element.97), calls=%async_computation | async-start | bytes 1048576 | tf_op jit(solution)/shard_map/all_to_all | solution.py:765
  123.8 30.8 %collective-permute-start.29 = (bf16[352,512]{1,0:T(8,128)(2,1)}, bf16[352,512]{1,0:T(8,128)(2,1)}, u32[]{:S(2)}, u32[]{:S(2)}) collective-permute-start(bf16[352,512]{1,0:T(8,128)(2,1)} %constant_dynamic-slice_fusion.9), channel_id=1, source_target_pairs={{0,4},{1,5},{2,6},{3,7},{4,0},{5,1},{6,2},{7,3},{8,12},{9,13},{10,... | collective-permute-start | bytes 1081352 | tf_op jit(solution)/shard_map/ppermute | solution.py:563
  126.7 27.9 %collective-permute-start.20 = (bf16[32,5632]{1,0:T(8,128)(2,1)}, bf16[32,5632]{1,0:T(8,128)(2,1)}, u32[]{:S(2)}, u32[]{:S(2)}) collective-permute-start(bf16[32,5632]{1,0:T(8,128)(2,1)} %collective-permute-done.17), channel_id=1, source_target_pairs={{0,2},{1,3},{2,0},{3,1},{4,6},{5,7},{6,4},{7,5},{8,10},{9,11},{10,... | collective-permute-start | bytes 1081352 | tf_op jit(solution)/shard_map/ppermute | solution.py:563
  128.2 40.7 %collective-permute-start.19 = (bf16[4,64,3072]{2,1,0:T(8,128)(2,1)}, bf16[4,64,3072]{2,1,0:T(8,128)(2,1)}, u32[]{:S(2)}, u32[]{:S(2)}) collective-permute-start(bf16[4,64,3072]{2,1,0:T(8,128)(2,1)} %collective-permute-done.14.refs_1_), channel_id=1, source_target_pairs={{0,8},{8,0},{16,24},{24,16},{1,9},{9,1},{17,25},{25,17},{2,10},{10... | collective-permute-start | bytes 4718600 | tf_op jit(solution)/shard_map/ppermute | solution.py:563
  130.9 33.9 %collective-permute-start.28 = (bf16[352,512]{1,0:T(8,128)(2,1)}, bf16[352,512]{1,0:T(8,128)(2,1)}, u32[]{:S(2)}, u32[]{:S(2)}) collective-permute-start(bf16[352,512]{1,0:T(8,128)(2,1)} %constant_dynamic-slice_fusion.9), channel_id=1, source_target_pairs={{0,2},{1,3},{2,0},{3,1},{4,6},{5,7},{6,4},{7,5},{8,10},{9,11},{10,... | collective-permute-start | bytes 1081352 | tf_op jit(solution)/shard_map/ppermute | solution.py:563
  154.6 11.6 %collective-permute-start.30 = (bf16[352,512]{1,0:T(8,128)(2,1)}, bf16[352,512]{1,0:T(8,128)(2,1)}, u32[]{:S(2)}, u32[]{:S(2)}) collective-permute-start(bf16[352,512]{1,0:T(8,128)(2,1)} %collective-permute-done.29), channel_id=1, source_target_pairs={{0,2},{1,3},{2,0},{3,1},{4,6},{5,7},{6,4},{7,5},{8,10},{9,11},{10,... | collective-permute-start | bytes 1081352 | tf_op jit(solution)/shard_map/ppermute | solution.py:563
  156.9 35.5 %collective-permute-start.21 = (bf16[4,32,5632]{2,1,0:T(8,128)(2,1)S(1)}, bf16[4,32,5632]{2,1,0:T(8,128)(2,1)}, u32[]{:S(2)}, u32[]{:S(2)}) collective-permute-start(bf16[4,32,5632]{2,1,0:T(8,128)(2,1)S(1)} %pad_maximum_fusion.1.refs_0_), channel_id=1, source_target_pairs={{0,1},{1,0},{2,3},{3,2},{4,5},{5,4},{6,7},{7,6},{8,9},{9,8},{10,11... | collective-permute-start | bytes 4325384 | tf_op jit(solution)/shard_map/ppermute | solution.py:563
  161.1 31.8 %all-to-all-start.1 = ((bf16[8,128,128]{2,1,0:T(8,128)(2,1)}), bf16[8,128,128]{2,1,0:T(8,128)(2,1)S(1)}, u32[]{:S(2)}, u32[]{:S(2)}) async-start(bf16[8,128,128]{2,1,0:T(8,128)(2,1)} %state_prefix.1), calls=%async_computation.1 | async-start | bytes 524288 | tf_op jit(solution)/shard_map/all_to_all | solution.py:765
  164.7 49.8 %collective-permute-start.22 = (bf16[4,32,5632]{2,1,0:T(8,128)(2,1)S(1)}, bf16[4,32,5632]{2,1,0:T(8,128)(2,1)}, u32[]{:S(2)}, u32[]{:S(2)}) collective-permute-start(bf16[4,32,5632]{2,1,0:T(8,128)(2,1)S(1)} %pad_maximum_fusion.1.refs_0_), channel_id=1, source_target_pairs={{0,16},{8,24},{16,0},{24,8},{1,17},{9,25},{17,1},{25,9},{2,18},{10... | collective-permute-start | bytes 4325384 | tf_op jit(solution)/shard_map/ppermute | solution.py:563
  166.2 80.8 %collective-permute-start.24 = (bf16[4,32,5632]{2,1,0:T(8,128)(2,1)S(1)}, bf16[4,32,5632]{2,1,0:T(8,128)(2,1)}, u32[]{:S(2)}, u32[]{:S(2)}) collective-permute-start(bf16[4,32,5632]{2,1,0:T(8,128)(2,1)S(1)} %pad_maximum_fusion.1.refs_0_), channel_id=1, source_target_pairs={{0,8},{8,0},{16,24},{24,16},{1,9},{9,1},{17,25},{25,17},{2,10},{10... | collective-permute-start | bytes 4325384 | tf_op jit(solution)/shard_map/ppermute | solution.py:563
  192.4 36.0 %collective-permute-start.23 = (bf16[4,32,5632]{2,1,0:T(8,128)(2,1)}, bf16[4,32,5632]{2,1,0:T(8,128)(2,1)}, u32[]{:S(2)}, u32[]{:S(2)}) collective-permute-start(bf16[4,32,5632]{2,1,0:T(8,128)(2,1)} %collective-permute-done.21.refs_1_), channel_id=1, source_target_pairs={{0,16},{8,24},{16,0},{24,8},{1,17},{9,25},{17,1},{25,9},{2,18},{10... | collective-permute-start | bytes 4325384 | tf_op jit(solution)/shard_map/ppermute | solution.py:563
  212.9 34.6 %collective-permute-start.26 = (bf16[4,32,5632]{2,1,0:T(8,128)(2,1)}, bf16[4,32,5632]{2,1,0:T(8,128)(2,1)S(1)}, u32[]{:S(2)}, u32[]{:S(2)}) collective-permute-start(bf16[4,32,5632]{2,1,0:T(8,128)(2,1)} %collective-permute-done.21.refs_1_), channel_id=1, source_target_pairs={{0,8},{8,0},{16,24},{24,16},{1,9},{9,1},{17,25},{25,17},{2,10},{10... | collective-permute-start | bytes 4325384 | tf_op jit(solution)/shard_map/ppermute | solution.py:563
  213.0 34.0 %collective-permute-start.31 = (bf16[4,352,512]{2,1,0:T(8,128)(2,1)S(1)}, bf16[4,352,512]{2,1,0:T(8,128)(2,1)S(1)}, u32[]{:S(2)}, u32[]{:S(2)}) collective-permute-start(bf16[4,352,512]{2,1,0:T(8,128)(2,1)S(1)} %copy-done.5), channel_id=1, source_target_pairs={{0,1},{1,0},{2,3},{3,2},{4,5},{5,4},{6,7},{7,6},{8,9},{9,8},{10,11... | collective-permute-start | bytes 4325384 | tf_op jit(solution)/shard_map/ppermute | solution.py:563
  214.5 33.0 %collective-permute-start.25 = (bf16[4,32,5632]{2,1,0:T(8,128)(2,1)}, bf16[4,32,5632]{2,1,0:T(8,128)(2,1)S(1)}, u32[]{:S(2)}, u32[]{:S(2)}) collective-permute-start(bf16[4,32,5632]{2,1,0:T(8,128)(2,1)} %collective-permute-done.22.refs_2_), channel_id=1, source_target_pairs={{0,8},{8,0},{16,24},{24,16},{1,9},{9,1},{17,25},{25,17},{2,10},{10... | collective-permute-start | bytes 4325384 | tf_op jit(solution)/shard_map/ppermute | solution.py:563
  228.3 19.2 %collective-permute-start.27 = (bf16[4,32,5632]{2,1,0:T(8,128)(2,1)}, bf16[4,32,5632]{2,1,0:T(8,128)(2,1)S(1)}, u32[]{:S(2)}, u32[]{:S(2)}) collective-permute-start(bf16[4,32,5632]{2,1,0:T(8,128)(2,1)} %collective-permute-done.23.refs_3_), channel_id=1, source_target_pairs={{0,8},{8,0},{16,24},{24,16},{1,9},{9,1},{17,25},{25,17},{2,10},{10... | collective-permute-start | bytes 4325384 | tf_op jit(solution)/shard_map/ppermute | solution.py:563
  247.0 15.9 %collective-permute-start.32 = (bf16[4,352,512]{2,1,0:T(8,128)(2,1)S(1)}, bf16[4,352,512]{2,1,0:T(8,128)(2,1)S(1)}, u32[]{:S(2)}, u32[]{:S(2)}) collective-permute-start(bf16[4,352,512]{2,1,0:T(8,128)(2,1)S(1)} %copy-done.5), channel_id=1, source_target_pairs={{0,8},{8,0},{16,24},{24,16},{1,9},{9,1},{17,25},{25,17},{2,10},{10... | collective-permute-start | bytes 4325384 | tf_op jit(solution)/shard_map/ppermute | solution.py:563
  247.0 15.9 %collective-permute-start.33 = (bf16[4,352,512]{2,1,0:T(8,128)(2,1)S(1)}, bf16[4,352,512]{2,1,0:T(8,128)(2,1)}, u32[]{:S(2)}, u32[]{:S(2)}) collective-permute-start(bf16[4,352,512]{2,1,0:T(8,128)(2,1)S(1)} %collective-permute-done.31.refs_1_), channel_id=1, source_target_pairs={{0,8},{8,0},{16,24},{24,16},{1,9},{9,1},{17,25},{25,17},{2,10},{10... | collective-permute-start | bytes 4325384 | tf_op jit(solution)/shard_map/ppermute | solution.py:563
  282.0 31.4 %collective-permute-start.34 = (bf16[2816,512]{1,0:T(8,128)(2,1)}, bf16[2816,512]{1,0:T(8,128)(2,1)}, u32[]{:S(2)}, u32[]{:S(2)}) collective-permute-start(bf16[2816,512]{1,0:T(8,128)(2,1)} %convolution_convert_fusion), channel_id=1, source_target_pairs={{0,8},{8,0},{16,24},{24,16},{1,9},{9,1},{17,25},{25,17},{2,10},{10... | collective-permute-start | bytes 8650760 | tf_op jit(solution)/shard_map/ppermute | solution.py:563
  294.3 27.9 %collective-permute-start.36 = (bf16[1024,1408]{1,0:T(8,128)(2,1)}, bf16[1024,1408]{1,0:T(8,128)(2,1)S(1)}, u32[]{:S(2)}, u32[]{:S(2)}) collective-permute-start(bf16[1024,1408]{1,0:T(8,128)(2,1)} %convolution_convert_fusion.1), channel_id=1, source_target_pairs={{0,8},{8,0},{16,24},{24,16},{1,9},{9,1},{17,25},{25,17},{2,10},{10... | collective-permute-start | bytes 8650760 | tf_op jit(solution)/shard_map/ppermute | solution.py:563
  298.2 24.0 %collective-permute-start.35 = (bf16[1024,1408]{1,0:T(8,128)(2,1)}, bf16[1024,1408]{1,0:T(8,128)(2,1)S(1)}, u32[]{:S(2)}, u32[]{:S(2)}) collective-permute-start(bf16[1024,1408]{1,0:T(8,128)(2,1)} %convolution_convert_fusion.2), channel_id=1, source_target_pairs={{0,8},{8,0},{16,24},{24,16},{1,9},{9,1},{17,25},{25,17},{2,10},{10... | collective-permute-start | bytes 8650760 | tf_op jit(solution)/shard_map/ppermute | solution.py:563
  320.7 34.3 %collective-permute-start.37 = (bf16[2,2,352,512]{3,2,0,1:T(8,128)(2,1)}, bf16[2,2,352,512]{3,2,0,1:T(8,128)(2,1)}, u32[]{:S(2)}, u32[]{:S(2)}) collective-permute-start(bf16[2,2,352,512]{3,2,0,1:T(8,128)(2,1)} %bitcast.300), channel_id=1, source_target_pairs={{0,1},{1,0},{2,3},{3,2},{4,5},{5,4},{6,7},{7,6},{8,9},{9,8},{10,11... | collective-permute-start | bytes 4325384 | tf_op jit(solution)/shard_map/ppermute | solution.py:563
  358.4 20.0 %all-to-all-start.2 = ((bf16[8,128,128]{2,1,0:T(8,128)(2,1)}), bf16[8,128,128]{2,1,0:T(8,128)(2,1)S(1)}, u32[]{:S(2)}, u32[]{:S(2)}) async-start(bf16[8,128,128]{2,1,0:T(8,128)(2,1)} %get-tuple-element.121), calls=%async_computation.2 | async-start | bytes 524288 | tf_op jit(solution)/shard_map/all_to_all | solution.py:765
  369.4 35.7 %collective-permute-start.40 = (bf16[2,2,128,1408]{3,2,0,1:T(8,128)(2,1)}, bf16[2,2,128,1408]{3,2,0,1:T(8,128)(2,1)}, u32[]{:S(2)}, u32[]{:S(2)}) collective-permute-start(bf16[2,2,128,1408]{3,2,0,1:T(8,128)(2,1)} %bitcast.299), channel_id=1, source_target_pairs={{0,1},{1,0},{2,3},{3,2},{4,5},{5,4},{6,7},{7,6},{8,9},{9,8},{10,11... | collective-permute-start | bytes 4325384 | tf_op jit(solution)/shard_map/ppermute | solution.py:563
  374.6 34.2 %collective-permute-start.39 = (bf16[2,2,2,64,1408]{4,3,2,1,0:T(8,128)(2,1)}, bf16[2,2,2,64,1408]{4,3,2,1,0:T(8,128)(2,1)}, u32[]{:S(2)}, u32[]{:S(2)}) collective-permute-start(bf16[2,2,2,64,1408]{4,3,2,1,0:T(8,128)(2,1)} %dynamic-slice_bitcast_fusion), channel_id=1, source_target_pairs={{0,16},{8,24},{16,0},{24,8},{1,17},{9,25},{17,1},{25,9},{2,18},{10... | collective-permute-start | bytes 4325384 | tf_op jit(solution)/shard_map/ppermute | solution.py:563
  377.0 23.5 %collective-permute-start.38 = (bf16[2,352,512]{2,1,0:T(8,128)(2,1)}, bf16[2,352,512]{2,1,0:T(8,128)(2,1)}, u32[]{:S(2)}, u32[]{:S(2)}) collective-permute-start(bf16[2,352,512]{2,1,0:T(8,128)(2,1)} %dynamic-slice_bitcast_fusion.5), channel_id=1, source_target_pairs={{0,2},{1,3},{2,0},{3,1},{4,6},{5,7},{6,4},{7,5},{8,10},{9,11},{10,... | collective-permute-start | bytes 2162696 | tf_op jit(solution)/shard_map/ppermute | solution.py:563
  385.2 48.1 %collective-permute-start.41 = (bf16[1024,1024]{1,0:T(8,128)(2,1)}, bf16[1024,1024]{1,0:T(8,128)(2,1)}, u32[]{:S(2)}, u32[]{:S(2)}) collective-permute-start(bf16[1024,1024]{1,0:T(8,128)(2,1)} %get-tuple-element.204), channel_id=1, source_target_pairs={{0,8},{8,0},{16,24},{24,16},{1,9},{9,1},{17,25},{25,17},{2,10},{10... | collective-permute-start | bytes 6291464 | tf_op jit(solution)/shard_map/ppermute | solution.py:563
  388.0 51.0 %all-to-all-start.3 = ((bf16[8,128,128]{2,1,0:T(8,128)(2,1)}), bf16[8,128,128]{2,1,0:T(8,128)(2,1)S(1)}, u32[]{:S(2)}, u32[]{:S(2)}) async-start(bf16[8,128,128]{2,1,0:T(8,128)(2,1)} %state_suffix.1), calls=%async_computation.3 | async-start | bytes 524288 | tf_op jit(solution)/shard_map/all_to_all | solution.py:765
  402.0 19.3 %collective-permute-start.42 = (bf16[352,512]{1,0:T(8,128)(2,1)S(1)}, bf16[352,512]{1,0:T(8,128)(2,1)S(1)}, u32[]{:S(2)}, u32[]{:S(2)}) collective-permute-start(bf16[352,512]{1,0:T(8,128)(2,1)S(1)} %dynamic-slice_bitcast_fusion.11), channel_id=1, source_target_pairs={{0,4},{1,5},{2,6},{3,7},{4,0},{5,1},{6,2},{7,3},{8,12},{9,13},{10,... | collective-permute-start | bytes 1081352 | tf_op jit(solution)/shard_map/ppermute | solution.py:563
  407.0 24.1 %collective-permute-start.44 = (bf16[2,128,1408]{2,1,0:T(8,128)(2,1)S(1)}, bf16[2,128,1408]{2,1,0:T(8,128)(2,1)S(1)}, u32[]{:S(2)}, u32[]{:S(2)}) collective-permute-start(bf16[2,128,1408]{2,1,0:T(8,128)(2,1)S(1)} %dynamic-slice_bitcast_fusion.3), channel_id=1, source_target_pairs={{0,2},{1,3},{2,0},{3,1},{4,6},{5,7},{6,4},{7,5},{8,10},{9,11},{10,... | collective-permute-start | bytes 2162696 | tf_op jit(solution)/shard_map/ppermute | solution.py:563
  410.8 21.4 %collective-permute-start.43 = (bf16[2,2,64,1408]{3,2,1,0:T(8,128)(2,1)S(1)}, bf16[2,2,64,1408]{3,2,1,0:T(8,128)(2,1)S(1)}, u32[]{:S(2)}, u32[]{:S(2)}) collective-permute-start(bf16[2,2,64,1408]{3,2,1,0:T(8,128)(2,1)S(1)} %dynamic-slice_bitcast_fusion.4), channel_id=1, source_target_pairs={{0,1},{1,0},{2,3},{3,2},{4,5},{5,4},{6,7},{7,6},{8,9},{9,8},{10,11... | collective-permute-start | bytes 2162696 | tf_op jit(solution)/shard_map/ppermute | solution.py:563
  437.8 48.9 %collective-permute-start.45 = (bf16[2,2,2,64,1024]{4,3,2,1,0:T(8,128)(2,1)}, bf16[2,2,2,64,1024]{4,3,2,1,0:T(8,128)(2,1)}, u32[]{:S(2)}, u32[]{:S(2)}) collective-permute-start(bf16[2,2,2,64,1024]{4,3,2,1,0:T(8,128)(2,1)} %dynamic-slice_bitcast_fusion.1), channel_id=1, source_target_pairs={{0,16},{8,24},{16,0},{24,8},{1,17},{9,25},{17,1},{25,9},{2,18},{10... | collective-permute-start | bytes 3145736 | tf_op jit(solution)/shard_map/ppermute | solution.py:563
  491.0 22.5 %collective-permute-start.46 = (bf16[1024,768]{1,0:T(8,128)(2,1)S(1)}, bf16[1024,768]{1,0:T(8,128)(2,1)S(1)}, u32[]{:S(2)}, u32[]{:S(2)}) collective-permute-start(bf16[1024,768]{1,0:T(8,128)(2,1)S(1)} %convolution_convert_fusion.4), channel_id=1, source_target_pairs={{0,8},{8,0},{16,24},{24,16},{1,9},{9,1},{17,25},{25,17},{2,10},{10... | collective-permute-start | bytes 4718600 | tf_op jit(solution)/shard_map/ppermute | solution.py:563
  491.1 22.1 %collective-permute-start.49 = (bf16[2,2,64,1024]{3,2,1,0:T(8,128)(2,1)S(1)}, bf16[2,2,64,1024]{3,2,1,0:T(8,128)(2,1)S(1)}, u32[]{:S(2)}, u32[]{:S(2)}) collective-permute-start(bf16[2,2,64,1024]{3,2,1,0:T(8,128)(2,1)S(1)} %dynamic-slice_bitcast_fusion.6), channel_id=1, source_target_pairs={{0,1},{1,0},{2,3},{3,2},{4,5},{5,4},{6,7},{7,6},{8,9},{9,8},{10,11... | collective-permute-start | bytes 1572872 | tf_op jit(solution)/shard_map/ppermute | solution.py:563
  493.0 19.3 %collective-permute-start.48 = (bf16[128,1408]{1,0:T(8,128)(2,1)S(1)}, bf16[128,1408]{1,0:T(8,128)(2,1)S(1)}, u32[]{:S(2)}, u32[]{:S(2)}) collective-permute-start(bf16[128,1408]{1,0:T(8,128)(2,1)S(1)} %dynamic-slice_bitcast_fusion.9), channel_id=1, source_target_pairs={{0,4},{1,5},{2,6},{3,7},{4,0},{5,1},{6,2},{7,3},{8,12},{9,13},{10,... | collective-permute-start | bytes 1081352 | tf_op jit(solution)/shard_map/ppermute | solution.py:563
  494.3 18.8 %collective-permute-start.47 = (bf16[2,64,1408]{2,1,0:T(8,128)(2,1)S(1)}, bf16[2,64,1408]{2,1,0:T(8,128)(2,1)S(1)}, u32[]{:S(2)}, u32[]{:S(2)}) collective-permute-start(bf16[2,64,1408]{2,1,0:T(8,128)(2,1)S(1)} %dynamic-slice_bitcast_fusion.10), channel_id=1, source_target_pairs={{0,2},{1,3},{2,0},{3,1},{4,6},{5,7},{6,4},{7,5},{8,10},{9,11},{10,... | collective-permute-start | bytes 1081352 | tf_op jit(solution)/shard_map/ppermute | solution.py:563
  515.0 34.1 %collective-permute-start.50 = (bf16[2,2,2,64,768]{4,3,2,1,0:T(8,128)(2,1)S(1)}, bf16[2,2,2,64,768]{4,3,2,1,0:T(8,128)(2,1)S(1)}, u32[]{:S(2)}, u32[]{:S(2)}) collective-permute-start(bf16[2,2,2,64,768]{4,3,2,1,0:T(8,128)(2,1)S(1)} %dynamic-slice_bitcast_fusion.2), channel_id=1, source_target_pairs={{0,16},{8,24},{16,0},{24,8},{1,17},{9,25},{17,1},{25,9},{2,18},{10... | collective-permute-start | bytes 2359304 | tf_op jit(solution)/shard_map/ppermute | solution.py:563
  557.1 14.7 %collective-permute-start.56 = (bf16[2,64,1024]{2,1,0:T(8,128)(2,1)S(1)}, bf16[2,64,1024]{2,1,0:T(8,128)(2,1)S(1)}, u32[]{:S(2)}, u32[]{:S(2)}) collective-permute-start(bf16[2,64,1024]{2,1,0:T(8,128)(2,1)S(1)} %dynamic-slice_bitcast_fusion.12), channel_id=1, source_target_pairs={{0,2},{1,3},{2,0},{3,1},{4,6},{5,7},{6,4},{7,5},{8,10},{9,11},{10,... | collective-permute-start | bytes 786440 | tf_op jit(solution)/shard_map/ppermute | solution.py:563
  557.2 13.9 %collective-permute-start.55 = (bf16[64,1408]{1,0:T(8,128)(2,1)S(1)}, bf16[64,1408]{1,0:T(8,128)(2,1)S(1)}, u32[]{:S(2)}, u32[]{:S(2)}) collective-permute-start(bf16[64,1408]{1,0:T(8,128)(2,1)S(1)} %dynamic-slice_bitcast_fusion.15), channel_id=1, source_target_pairs={{0,4},{1,5},{2,6},{3,7},{4,0},{5,1},{6,2},{7,3},{8,12},{9,13},{10,... | collective-permute-start | bytes 540680 | tf_op jit(solution)/shard_map/ppermute | solution.py:563
  561.5 36.0 %collective-permute-start.54 = (bf16[2,2,2,64,768]{4,3,0,1,2:T(8,128)(2,1)}, bf16[2,2,2,64,768]{4,3,0,1,2:T(8,128)(2,1)}, u32[]{:S(2)}, u32[]{:S(2)}) collective-permute-start(bf16[2,2,2,64,768]{4,3,0,1,2:T(8,128)(2,1)} %bitcast.301), channel_id=1, source_target_pairs={{0,16},{8,24},{16,0},{24,8},{1,17},{9,25},{17,1},{25,9},{2,18},{10... | collective-permute-start | bytes 2359304 | tf_op jit(solution)/shard_map/ppermute | solution.py:563
  565.6 19.2 %collective-permute-start.53 = (bf16[2,2,64,768]{3,2,1,0:T(8,128)(2,1)S(1)}, bf16[2,2,64,768]{3,2,1,0:T(8,128)(2,1)S(1)}, u32[]{:S(2)}, u32[]{:S(2)}) collective-permute-start(bf16[2,2,64,768]{3,2,1,0:T(8,128)(2,1)S(1)} %dynamic-slice_bitcast_fusion.8), channel_id=1, source_target_pairs={{0,1},{1,0},{2,3},{3,2},{4,5},{5,4},{6,7},{7,6},{8,9},{9,8},{10,11... | collective-permute-start | bytes 1179656 | tf_op jit(solution)/shard_map/ppermute | solution.py:563
  571.2 13.5 %collective-permute-start.76 = (bf16[64,1408]{1,0:T(8,128)(2,1)S(1)}, bf16[64,1408]{1,0:T(8,128)(2,1)S(1)}, u32[]{:S(2)}, u32[]{:S(2)}) collective-permute-start(bf16[64,1408]{1,0:T(8,128)(2,1)S(1)} %fusion.73), channel_id=1, source_target_pairs={{0,16},{8,24},{16,0},{24,8},{1,17},{9,25},{17,1},{25,9},{2,18},{10... | collective-permute-start | bytes 540680 | tf_op jit(solution)/shard_map/ppermute | solution.py:563
  598.9 14.4 %collective-permute-start.61 = (bf16[352,512]{1,0:T(8,128)(2,1)S(1)}, bf16[352,512]{1,0:T(8,128)(2,1)S(1)}, u32[]{:S(2)}, u32[]{:S(2)}) collective-permute-start(bf16[352,512]{1,0:T(8,128)(2,1)S(1)} %copy-done.81), channel_id=1, source_target_pairs={{0,16},{8,24},{16,0},{24,8},{1,17},{9,25},{17,1},{25,9},{2,18},{10... | collective-permute-start | bytes 1081352 | tf_op jit(solution)/shard_map/ppermute | solution.py:563
  613.5 18.9 %collective-permute-start.78 = (bf16[352,512]{1,0:T(8,128)(2,1)S(1)}, bf16[352,512]{1,0:T(8,128)(2,1)S(1)}, u32[]{:S(2)}, u32[]{:S(2)}) collective-permute-start(bf16[352,512]{1,0:T(8,128)(2,1)S(1)} %add_convert_fusion.9), channel_id=1, source_target_pairs={{0,8},{8,0},{16,24},{24,16},{1,9},{9,1},{17,25},{25,17},{2,10},{10... | collective-permute-start | bytes 1081352 | tf_op jit(solution)/shard_map/ppermute | solution.py:563
  614.1 17.4 %collective-permute-start.65 = (bf16[128,1408]{1,0:T(8,128)(2,1)S(1)}, bf16[128,1408]{1,0:T(8,128)(2,1)S(1)}, u32[]{:S(2)}, u32[]{:S(2)}) collective-permute-start(bf16[128,1408]{1,0:T(8,128)(2,1)S(1)} %copy-done.80), channel_id=1, source_target_pairs={{0,16},{8,24},{16,0},{24,8},{1,17},{9,25},{17,1},{25,9},{2,18},{10... | collective-permute-start | bytes 1081352 | tf_op jit(solution)/shard_map/ppermute | solution.py:563
  615.4 11.7 %collective-permute-start.62 = (bf16[2,64,768]{2,1,0:T(8,128)(2,1)S(1)}, bf16[2,64,768]{2,1,0:T(8,128)(2,1)S(1)}, u32[]{:S(2)}, u32[]{:S(2)}) collective-permute-start(bf16[2,64,768]{2,1,0:T(8,128)(2,1)S(1)} %dynamic-slice_bitcast_fusion.13), channel_id=1, source_target_pairs={{0,2},{1,3},{2,0},{3,1},{4,6},{5,7},{6,4},{7,5},{8,10},{9,11},{10,... | collective-permute-start | bytes 589832 | tf_op jit(solution)/shard_map/ppermute | solution.py:563
  627.3 17.0 %collective-permute-start.71 = (bf16[128,768]{1,0:T(8,128)(2,1)S(1)}, bf16[128,768]{1,0:T(8,128)(2,1)S(1)}, u32[]{:S(2)}, u32[]{:S(2)}) collective-permute-start(bf16[128,768]{1,0:T(8,128)(2,1)S(1)} %maximum_select_fusion.5), channel_id=1, source_target_pairs={{0,8},{8,0},{16,24},{24,16},{1,9},{9,1},{17,25},{25,17},{2,10},{10... | collective-permute-start | bytes 589832 | tf_op jit(solution)/shard_map/ppermute | solution.py:563
  638.9 16.2 %collective-permute-start.77 = (bf16[128,2816]{1,0:T(8,128)(2,1)}, bf16[128,2816]{1,0:T(8,128)(2,1)S(1)}, u32[]{:S(2)}, u32[]{:S(2)}) collective-permute-start(bf16[128,2816]{1,0:T(8,128)(2,1)} %pad_maximum_fusion.5), channel_id=1, source_target_pairs={{0,8},{8,0},{16,24},{24,16},{1,9},{9,1},{17,25},{25,17},{2,10},{10... | collective-permute-start | bytes 2162696 | tf_op jit(solution)/shard_map/ppermute | solution.py:563
  (135 other events, 1270.8 us)

commit v3 on v2

--- a/solution.py
+++ b/solution.py
@@ -331,6 +331,10 @@
 VMEM_LIMIT = 16 * 1024 * 1024
 
 
+def in_hbm(*arrays):
+    return [pltpu.with_memory_space_constraint(a, pltpu.HBM) for a in arrays]
+
+
 def params():
     return pltpu.CompilerParams(dimension_semantics=("arbitrary",), vmem_limit_bytes=VMEM_LIMIT)
 
@@ -394,7 +398,7 @@
         compiler_params=params(),
         cost_estimate=cost(24),
         name="delta_summary",
-    )(pre, pre, taps, cols, rows)
+    )(*in_hbm(pre, pre, taps, cols, rows))
 
 
 def delta_forward(pre, taps, k, w, u, cols, rows, entry, gain_full, heads):
@@ -430,7 +434,7 @@
         compiler_params=params(),
         cost_estimate=cost(16),
         name="delta_forward",
-    )(pre, pre, taps, k, w, u, cols, rows, entry, pre, gain_full)
+    )(*in_hbm(pre, pre, taps, k, w, u, cols, rows, entry, pre, gain_full))
 
 
 def delta_adjoint(q, k, w, cols, rows, dy, o, gate, gain_full, heads):
@@ -462,7 +466,7 @@
         compiler_params=params(),
         cost_estimate=cost(15),
         name="delta_adjoint",
-    )(q, k, w, cols, rows, dy, o, gate, gain_full)
+    )(*in_hbm(q, k, w, cols, rows, dy, o, gate, gain_full))
 
 
 def delta_backward(part, q, k, v, w, u, a, e, kept_states, do, cols, rows, later, qg_pre, qtaps, kv_pre, kvtaps, heads):
@@ -514,7 +518,7 @@
         compiler_params=params(),
         cost_estimate=cost(32),
         name="delta_backward",
-    )(q, k, v, w, u, a, e, kept_states, do, cols, rows, later, qg_pre, qg_pre, qtaps, kv_pre, kv_pre, kvtaps)
+    )(*in_hbm(q, k, v, w, u, a, e, kept_states, do, cols, rows, later, qg_pre, qg_pre, qtaps, kv_pre, kv_pre, kvtaps))
 
 
 def scan_states(x):
@@ -549,10 +553,12 @@
         self.f, self.r = lax.axis_index("fsdp"), lax.axis_index("rep")
         z = self.f // self.ny
         self.mine = {"v": z // 2, "w": z % 2, "y": self.f % self.ny, "x": self.r // 2, "c": self.r % 2}
-        self.number = {"v": 2, "w": 2, "y": self.ny, "x": self.nx, "c": 2}
+        self.number = {"v": 2, "w": 2, "u": 2, "y": self.ny, "x": self.nx, "c": 2}
         self.stride = {"v": 2 * self.ny, "w": self.ny, "y": 1, "x": 2, "c": 1}
 
     def send(self, value, way, steps=1):
+        if way == "u":
+            return lax.ppermute(value, "fsdp", [(i, i ^ 3 * self.ny) for i in range(self.nf)])
         axis = "rep" if way in "xc" else "fsdp"
         total = self.nr if way in "xc" else self.nf
         number, stride = self.number[way], self.stride[way]
@@ -666,7 +672,8 @@
         self.split = False
 
     def swap(self, away):
-        self.came = self.here.send(away.astype(BF), "c")
+        self.away = away.astype(BF)
+        self.came = self.here.send(self.away, "c")
 
     def take(self, part):
         self.begin(part + self.came.astype(F32))
@@ -678,15 +685,13 @@
         self.part = part.reshape(2, 2, here.ny, rows, part.shape[1])
         self.axes = ["v", "w", "y"]
 
-    def step(self, way, *after):
+    def go(self, way, *after):
         here = self.here
         part = hold(self.part, *after)
         number, mine = here.number[way], here.mine[way]
         if way in "xc" and not self.axes:
-            total = part.astype(F32)
-            for s in range(1, number):
-                total = total + here.send(part, way, s).astype(F32)
-            self.part = total.astype(BF)
+            self.total = part.astype(F32)
+            self.got = [here.send(part, way, s) for s in range(1, number)]
             return
         if way == "x":
             axis = len(self.axes)
@@ -696,11 +701,44 @@
         else:
             axis = self.axes.index(way)
             self.axes.pop(axis)
-        total = lax.dynamic_index_in_dim(part, mine, axis, keepdims=False).astype(F32)
-        for s in range(1, number):
-            out = lax.dynamic_index_in_dim(part, (mine + s) % number, axis, keepdims=False)
-            total = total + here.send(out, way, s).astype(F32)
+        self.total = lax.dynamic_index_in_dim(part, mine, axis, keepdims=False).astype(F32)
+        self.got = [
+            here.send(
+                lax.dynamic_index_in_dim(part, (mine + s) % number, axis, keepdims=False), way, s
+            )
+            for s in range(1, number)
+        ]
+
+    def begin_x(self, part, *after):
+        self.part, self.axes = part, []
+        self.go("x", *after)
+
+    def both(self):
+        self.total = self.part.astype(F32)
+        self.got = [self.here.send(self.part, "c")]
+
+    def end(self):
+        total = self.total
+        for came in self.got:
+            total = total + came.astype(F32)
         self.part = total.astype(BF)
+
+    def step(self, way, *after):
+        self.go(way, *after)
+        self.end()
+
+    def go_z(self, *after):
+        here = self.here
+        part = hold(self.part, *after)
+        v, w = here.mine["v"], here.mine["w"]
+
+        def at(dv, dw):
+            one = lax.dynamic_index_in_dim(part, (v + dv) % 2, 0, keepdims=False)
+            return lax.dynamic_index_in_dim(one, (w + dw) % 2, 0, keepdims=False)
+
+        self.total = at(0, 0).astype(F32)
+        self.got = [here.send(at(*d), way) for d, way in (((1, 0), "v"), ((1, 1), "u"), ((0, 1), "w"))]
+        self.axes = self.axes[2:]
 
     def rows(self):
         if self.split:
@@ -708,6 +746,14 @@
 
     def other(self):
         return self.here.send(self.part, "c")
+
+
+def meet(value, *sums):
+    value, came = lax.optimization_barrier((value, [one.got for one in sums]))
+    for one, got in zip(sums, came):
+        one.got = got
+        one.end()
+    return value
 
 
 def join_way(here, array, way, axis):
@@ -721,6 +767,24 @@
     order = (mine - jnp.arange(number)) % number
     stack = jnp.take(stack, order, axis=0)
     return jnp.concatenate([stack[i] for i in range(number)], axis=axis)
+
+
+def gather_apart(here, shard):
+    rows = shard.shape[0] // here.nr
+    piece = lax.dynamic_slice_in_dim(shard, here.r * rows, rows, 0)
+    return lax.all_gather(piece, ("fsdp", "rep"), axis=0, tiled=True)
+
+
+def scatter_owners(array):
+    return lax.psum_scatter(array, "fsdp", scatter_dimension=0, tiled=True)
+
+
+def sum_x(here, array, *after):
+    array = hold(array, *after)
+    total = array.astype(F32)
+    for s in range(1, here.nx):
+        total = total + here.send(array, "x", s).astype(F32)
+    return total.astype(BF)
 
 
 def contract(left, right, left_dim, right_dim):
@@ -794,9 +858,7 @@
     lanes = 128
     hidden_units = ffn_gate.shape[1]
 
-    rim_rows = from_behind(hidden_in[row_count - rim :], 1)
     numbers = seg_ids + 1
-    rim_ids = from_behind(numbers[row_count - rim :], 1)
 
     small = [attn_gain, out_gain, ffn_gain, conv_taps]
     shard_rows = qkv_weight.shape[0]
@@ -818,17 +880,21 @@
         [2 * width, width],
         False,
     )
-    third = Gather(here, jnp.concatenate([ffn_gate, ffn_up], axis=1), [2 * hidden_units], True)
-    fourth = Gather(here, ffn_down, [width], False, by_rows=False)
+    pair_full = gather_apart(here, jnp.concatenate([ffn_gate, ffn_up], axis=1))
+    down_full = gather_apart(here, ffn_down)
+    rim_rows = from_behind(hidden_in[row_count - rim :], 1)
+    rim_ids = from_behind(numbers[row_count - rim :], 1)
     first.move("v", "w")
     first.move("vw")
     first.pile()
-    first.move("zy", "zx", "zc")
-    first.move("zyx", "zyc", "zxc")
-    second.move("v", "w", after=first.got("vw"))
-    first.move("zyxc", after=second.got("v", "w"))
-    second.move("vw")
-    second.pile()
+    if not first.plain:
+        first.have["z"], rim_rows, rim_ids = lax.optimization_barrier((first.have["z"], rim_rows, rim_ids))
+    first.move("zy", "zx")
+    first.move("zc")
+    second.move("v", "w", after=first.got("z"))
+    first.move("zyx", after=first.got("zx", "zc"))
+    first.move("zyc", "zxc")
+    first.move("zyxc", after=first.got("zyc", "zxc"))
     kv_full, extra_full = first.place()
 
     small_full = extra_full[:, heads : heads + columns].reshape(here.nf, -1)
@@ -847,10 +913,10 @@
     extended_in = jnp.concatenate([hidden_in, rim_rows]).astype(F32)
     normed_ext = rms_norm(extended_in, attn_scale).astype(BF)
     normed_low = normed_ext[:row_count]
-    second.move("zy")
-    kv_full = hold(kv_full, second.got("z"))
     kv_pre = jnp.dot(normed_ext, kv_full, preferred_element_type=F32)
-    third.move("v", "w", after=[kv_pre])
+    second.move("vw", after=[kv_full])
+    second.pile()
+    second.move("zy", after=[kv_pre])
     beta_pre = jnp.dot(normed_low, extra_full, preferred_element_type=F32)[:, :heads]
     rates = jax.nn.sigmoid(beta_pre)
     ids = jnp.concatenate([rim_ids, numbers]).astype(F32)
@@ -871,14 +937,8 @@
         ],
         1,
     )
-    second.move("zc", after=[cols])
     key_low, value_low, w, u, a, moves = delta_summary(kv_pre, kv_taps, cols, rows, heads)
-    moves = hold(moves, second.got("zy"), third.got("v", "w"))
-    second.move("zyc", after=[moves])
-    third.move("vw", after=[moves])
-    fourth.move("v", "w", after=[moves])
-    third.pile()
-    third.move("zy", "zx")
+    second.move("zc", "zyc", after=[moves])
     fanout = here.nf // heads
     if fanout > 1:
         moves = jnp.concatenate(
@@ -891,28 +951,18 @@
     owned = swap(moves)
     qg_full, outw_full = second.place()
     qg_pre = jnp.dot(normed_ext, qg_full, preferred_element_type=F32)
-    fourth.move("vw", after=[owned])
-    fourth.pile()
-    third.move("zyx", after=[owned])
-    third.move("zc", "zxc", "zyc", after=[owned])
     entry = swap(scan_states(owned))
     if fanout > 1:
         entry = to_heads(entry, fanout)
-    fourth.move("zy", after=[entry] + third.got("zy"))
-    fourth.move("zc", after=[entry])
     query_low, gated_low, attn_heads, fresh, kept = delta_forward(
         qg_pre, query_taps, key_low, w, u, cols, rows, entry, outgain_scale, heads
     )
-    third.move("zyxc", after=[gated_low])
-    fourth.move("zyc", after=[gated_low])
     middle = residual + jnp.dot(gated_low, outw_full, preferred_element_type=F32)
-    normed_two, norm_two_back = jax.vjp(rms_norm, middle, ffngain_scale)
+    normed_two, norm_two_back = jax.vjp(partial(rms_norm, gain=ffngain_scale), middle)
     normed_two_low = normed_two.astype(BF)
-    (pair_full,) = third.place()
     pair_pre = jnp.dot(normed_two_low, pair_full, preferred_element_type=F32)
     hidden_ff, swiglu_back = jax.vjp(swiglu, pair_pre)
     hidden_low = hidden_ff.astype(BF)
-    (down_full,) = fourth.place()
 
     c = here.mine["c"]
 
@@ -921,91 +971,94 @@
         cut = [lax.dynamic_slice_in_dim(array, start + at * half, half, 1) for at in (1 - c, c)]
         return cut
 
-    hidden_grad = contract(cotangent, down_full, 1, 1)
     theirs, ours = shares(cotangent, 0, width)
     down_sum = Reduce(here)
     down_sum.swap(contract(hidden_low, theirs, 0, 0))
+    hidden_grad = contract(cotangent, down_full, 1, 1)
     (pair_grad,) = swiglu_back(hidden_grad)
     pair_low = pair_grad.astype(BF)
-    hidden_sums = [Reduce(here), Reduce(here)]
-    quarter = hidden_units // 2
-    nears = []
-    for i, one in enumerate(hidden_sums):
-        away = lax.dynamic_slice_in_dim(pair_low, (1 - c) * hidden_units + i * quarter, quarter, 1)
-        nears.append(lax.dynamic_slice_in_dim(pair_low, c * hidden_units + i * quarter, quarter, 1))
-        one.swap(contract(normed_two_low, away, 0, 0))
-    hidden_a, hidden_b = hidden_sums
-    down_sum.take(contract(hidden_low, hold(ours, pair_low), 0, 0))
+    down_half = (contract(hidden_low, hold(ours, pair_low), 0, 0) + down_sum.came.astype(F32)).astype(BF)
+    down_apart = scatter_owners(down_half)
     top_grad = cotangent.astype(F32)
     normed_two_grad = contract(pair_low, pair_full, 1, 1)
-    middle_back, ffngain_grad = norm_two_back(normed_two_grad)
+    (middle_back,) = norm_two_back(normed_two_grad)
     middle_grad = top_grad + middle_back
     middle_low = middle_grad.astype(BF)
     gated_grad = contract(middle_low, outw_full, 1, 1)
-    gated_grad = hold(gated_grad, down_sum.part, hidden_a.came, hidden_b.came)
-    down_sum.step("y")
+    theirs, ours = shares(pair_low, 0, 2 * hidden_units)
+    pair_sum = Reduce(here)
+    pair_sum.swap(contract(normed_two_low, theirs, 0, 0))
+    gated_grad = hold(gated_grad, down_half, pair_sum.away)
     heads_grad, gatepre_low, outgain_grad, local_later = delta_adjoint(
         query_low, key_low, w, cols, rows, gated_grad, attn_heads, qg_pre, outgain_scale, heads
     )
-    local_later = hold(local_later, down_sum.part)
     if fanout > 1:
         local_later = to_owners(local_later, fanout)
     came_later = swap(local_later)
 
-    near_a, near_b = hold(tuple(nears), local_later)
-    hidden_a.take(contract(normed_two_low, near_a, 0, 0))
-    hidden_b.take(contract(normed_two_low, near_b, 0, 0))
-    down_sum.step("w", local_later)
-    came_later = hold(came_later, hidden_a.part, hidden_b.part)
-    hidden_a.step("x")
-    hidden_b.step("y")
-    later = swap(scan_grads(owned, came_later))
+    ours = hold(ours, local_later)
+    pair_half = (contract(normed_two_low, ours, 0, 0) + pair_sum.came.astype(F32)).astype(BF)
+    pair_apart = scatter_owners(pair_half)
+    came_later = hold(came_later, pair_half)
+    summed_later = scan_grads(owned, came_later)
+    later = swap(summed_later)
     if fanout > 1:
         later = to_heads(later, fanout)
-    hidden_held, middle_held, gatepre_held = hold((hidden_low, middle_low, gatepre_low), came_later)
-    output = (middle + jnp.dot(hidden_held, down_full, preferred_element_type=F32)).astype(BF)
+    hidden_held, middle_held, gatepre_held = hold((hidden_low, middle_low, gatepre_low), summed_later)
     out_grad = contract(gated_low, middle_held, 0, 0)
     gate_grad = contract(normed_low, gatepre_held, 0, 0)
     other_sum = Reduce(here)
     other_sum.swap(by_core(here, gate_grad, out_grad))
-    later = hold(later, down_sum.part, output, hidden_a.part, hidden_b.part, other_sum.came)
-    other_sum.take(by_core(here, out_grad, gate_grad))
+    output = (middle + jnp.dot(hidden_held, down_full, preferred_element_type=F32)).astype(BF)
+    other_sum.take(hold(by_core(here, out_grad, gate_grad), output))
     later = hold(later, other_sum.part)
-    down_sum.step("v")
-    hidden_a.step("y")
-    hidden_b.step("w")
-    other_sum.step("x")
+    other_sum.go("x")
     state = (query_low, key_low, value_low, w, u, a, fresh, kept, heads_grad, cols, rows)
     mixed_a, beta_a, taps_a = delta_backward(
         0, *state, later, qg_pre, query_taps, kv_pre, kv_taps, heads
     )
-    mixed_a = hold(mixed_a, down_sum.part, hidden_a.part, hidden_b.part, other_sum.part)
+    mixed_a = meet(mixed_a, other_sum)
+    other_sum.go("y")
     a_sum = Reduce(here)
     size = 3 * width // 2
     theirs, ours = shares(mixed_a, 0, size)
     a_sum.swap(contract(normed_ext, theirs, 0, 0))
     a_sum.take(contract(normed_ext, ours, 0, 0))
     later = hold(later, a_sum.part)
-    a_sum.step("x")
-    hidden_a.step("w", mixed_a)
-    hidden_b.step("v", mixed_a)
-    other_sum.step("y", mixed_a)
+    a_sum.go("x")
     mixed_b, beta_b, taps_b = delta_backward(
         1, *state, later, qg_pre, query_taps, kv_pre, kv_taps, heads
     )
-    mixed_b = hold(mixed_b, hidden_a.part, hidden_b.part, other_sum.part, a_sum.part)
+    mixed_b = hold(meet(mixed_b, other_sum, a_sum), pair_apart)
+    a_sum.go("y")
+    other_sum.go("w")
+    eighth = width // 2
+
+    def by_kind(first_heads, other_heads):
+        cut = [slice(i * eighth, (i + 1) * eighth) for i in range(3)]
+        both = [array[:, s] for s in cut for array in (first_heads, other_heads)]
+        return jnp.concatenate(both, axis=1)
+
+    betapre_low = (beta_a + beta_b).astype(BF)
+    taps_grad = by_kind(taps_a, taps_b)
+    parts = (
+        outgain_grad.reshape(here.nf, -1),
+        jnp.swapaxes(taps_grad.reshape(taps_count, here.nf, -1), 0, 1).reshape(here.nf, -1),
+    )
+    flat = jnp.concatenate(parts, axis=1)
+    flat = jnp.pad(flat, ((0, 0), (0, columns * shard_rows - flat.shape[1])))
+    extra = jnp.pad(flat.reshape(width, columns), ((0, 0), (heads, lanes - heads - columns)))
+    small_sum = Reduce(here)
+    small_sum.begin(contract(normed_low, hold(betapre_low, mixed_b), 0, 0) + extra)
+    small_sum.both()
     b_sum = Reduce(here)
     theirs, ours = shares(mixed_b, 0, size)
     b_sum.swap(contract(normed_ext, theirs, 0, 0))
     b_sum.take(contract(normed_ext, ours, 0, 0))
-    mixed_b = hold(mixed_b, b_sum.part)
-    b_sum.step("x")
-    a_sum.step("y", mixed_b)
-    hidden_a.step("v", mixed_b)
-    other_sum.step("w", mixed_b)
-    betapre_low = (beta_a + beta_b).astype(BF)
-    beta_grad = contract(normed_low, betapre_low, 0, 0)[:, :heads]
-    eighth = width // 2
+    small_sum.end()
+    mixed_b = hold(mixed_b, b_sum.part, small_sum.part)
+    b_sum.go("x")
+    small_sum.go("x")
     wide_grad = (
         contract(mixed_a[:, eighth:], kv_full[:, :width], 1, 1)
         + contract(mixed_b[:, eighth:], kv_full[:, width:], 1, 1)
@@ -1013,69 +1066,63 @@
         + contract(mixed_b[:, :eighth], qg_full[:, eighth:width], 1, 1)
     )
     rim_grad = from_behind(wide_grad[row_count:].astype(BF), -1).astype(F32)
-    normed_grad = hold(
+    normed_grad = (
         wide_grad[:row_count]
         + jnp.pad(rim_grad, ((row_count - rim, 0), (0, 0)))
         + contract(betapre_low, extra_full, 1, 1)
-        + contract(gatepre_low, qg_full[:, width:], 1, 1),
-        a_sum.part,
-    )
-    input_back, attngain_grad = jax.vjp(rms_norm, residual, attn_scale)[1](normed_grad)
-    input_grad = (middle_grad + input_back).astype(BF)
-
-    def by_kind(first_heads, other_heads):
-        cut = [slice(i * eighth, (i + 1) * eighth) for i in range(3)]
-        both = [array[:, s] for s in cut for array in (first_heads, other_heads)]
-        return jnp.concatenate(both, axis=1)
-
-    taps_grad = by_kind(taps_a, taps_b)
-    parts = (
-        attngain_grad.reshape(here.nf, -1),
-        outgain_grad.reshape(here.nf, -1),
-        ffngain_grad.reshape(here.nf, -1),
-        jnp.swapaxes(taps_grad.reshape(taps_count, here.nf, -1), 0, 1).reshape(here.nf, -1),
-    )
-    flat = jnp.concatenate(parts, axis=1)
-    flat = jnp.pad(flat, ((0, 0), (0, columns * shard_rows - flat.shape[1])))
-    extra = jnp.concatenate(
-        [
-            beta_grad,
-            flat.reshape(width, columns),
-            jnp.zeros((width, lanes - heads - columns), F32),
-        ],
-        axis=1,
-    )
-    small_sum = Reduce(here)
-    small_sum.begin(extra)
-    first_tail = (b_sum.part, hidden_a.part, other_sum.part, a_sum.part)
-    b_sum.step("y", *first_tail)
-    a_sum.step("w", *first_tail)
-    other_sum.step("v", *first_tail)
-    down_sum.step("x", *first_tail)
-    small_sum.step("y", b_sum.part)
-    second_tail = (b_sum.part, a_sum.part, other_sum.part, down_sum.part)
-    b_sum.step("w", *second_tail)
-    a_sum.step("v", *second_tail)
-    hidden_b.step("x", *second_tail)
-    small_sum.step("w", b_sum.part)
-    b_sum.step("v", a_sum.part, hidden_b.part)
-    small_sum.step("v", b_sum.part)
-    small_sum.step("x")
-    small_sum.step("c")
-    for done in (hidden_a, other_sum, a_sum, b_sum):
-        done.rows()
-    hidden = jnp.concatenate([hidden_a.part, hidden_b.part], axis=1)
-    other = here.send(hidden, "c")
-    hidgate_total = by_core(here, hidden, other).astype(F32)
-    hidup_total = by_core(here, other, hidden).astype(F32)
-    other = other_sum.other()
-    outproj_total = by_core(here, other_sum.part, other).astype(F32)
-    gate_total = by_core(here, other, other_sum.part).astype(F32)
+        + contract(gatepre_low, qg_full[:, width:], 1, 1)
+    )
+    normed_grad = meet(normed_grad, b_sum, a_sum, other_sum, small_sum)
+    b_sum.go("y")
+    small_sum.go("y")
+    a_sum.go("w")
+    other_sum.go("v")
+    (input_back,) = jax.vjp(partial(rms_norm, gain=attn_scale), residual)[1](normed_grad)
+    input_grad = meet((middle_grad + input_back).astype(BF), b_sum, a_sum, other_sum, small_sum)
+    b_sum.go("w", input_grad)
+    a_sum.go("v", input_grad)
+    small_sum.go("w", input_grad)
+    pair_sum.begin_x(pair_apart, input_grad)
+    for one in (b_sum, a_sum, small_sum):
+        one.end()
+    b_sum.go("v", a_sum.part)
+    small_sum.go("v", a_sum.part)
+    held = meet(a_sum.part, b_sum, small_sum, pair_sum)
+    down_sum.begin_x(down_apart, held)
+    down_sum.end()
+    both = Reduce(here)
+    both.part = jnp.concatenate([b_sum.part, held, other_sum.part, small_sum.part], axis=1)
+    both.split = True
+    both.rows()
     down_total = join_way(here, down_sum.part, "c", 1).astype(F32)
+    other = here.send(pair_sum.part, "c")
+    hidgate_total = by_core(here, pair_sum.part, other).astype(F32)
+    hidup_total = by_core(here, other, pair_sum.part).astype(F32)
+    whole = both.other()
+    piece = size // 2
+    ends = [piece, 2 * piece, 2 * piece + width]
+
+    def joined(start, end):
+        mine, theirs = both.part[:, start:end], whole[:, start:end]
+        return by_core(here, mine, theirs), by_core(here, theirs, mine)
+
+    outproj_total, gate_total = [part.astype(F32) for part in joined(ends[1], ends[2])]
+    b_first, b_second = joined(0, ends[0])
+    a_first, a_second = joined(ends[0], ends[1])
     qkv_total = by_kind(
-        join_way(here, a_sum.part, "c", 1), join_way(here, b_sum.part, "c", 1)
+        jnp.concatenate([a_first, a_second], axis=1), jnp.concatenate([b_first, b_second], axis=1)
     ).astype(F32)
-    extra = small_sum.part.astype(F32)
+    extra = both.part[:, ends[2] :].astype(F32)
+    beta_total = extra[:, :heads]
+
+    def gain_grad(gain, pairs):
+        total = sum(jnp.sum(weight.astype(F32) * grad, axis=1) for weight, grad in pairs)
+        return total / gain.astype(F32)
+
+    attngain_total = gain_grad(
+        attn_gain, ((qkv_weight, qkv_total), (beta_weight, beta_total), (gate_weight, gate_total))
+    )
+    ffngain_total = gain_grad(ffn_gain, ((ffn_gate, hidgate_total), (ffn_up, hidup_total)))
     flat = extra[:, heads : heads + columns].reshape(-1)
     cut, at = [], 0
     for part in parts:
@@ -1084,14 +1131,14 @@
     return (
         output,
         input_grad,
+        attngain_total,
+        qkv_total,
+        beta_total,
+        gate_total,
+        cut[1].reshape(conv_taps.shape),
         cut[0],
-        qkv_total,
-        extra[:, :heads],
-        gate_total,
-        cut[3].reshape(conv_taps.shape),
-        cut[1],
         outproj_total,
-        cut[2],
+        ffngain_total,
         hidgate_total,
         hidup_total,
         down_total,

time: 667 us -> 574 us (0.86)
  waiting for transfers between devices: 193 us -> 132 us
  local copies, waits for them, and re-layouts: 75.3 us -> 41.7 us
  starting transfers between devices: 92.9 us -> 77.5 us
  matrix products: 96.6 us -> 110 us
  between operations: 3.19 us -> 16.1 us
  other arithmetic: 56.6 us -> 49.5 us
    ppermute x76 -> x44, waiting for transfers between devices: 192 us -> 86.3 us  [send(): return lax.ppermute(value, axis, pairs)]
    all_to_all x4, waiting for transfers between devices: 0.01 us -> 42.6 us  [swap(): return lax.all_to_all(value, 'fsdp', 0, 0, tiled=True)]
    ppermute x76 -> x44, starting transfers between devices: 67.6 us -> 45.8 us  [send(): return lax.ppermute(value, axis, pairs)]
    convert_element_type x33 -> x24, other arithmetic: 26.8 us -> 12.4 us  [the longest x19 4.71 us: end(): self.part = total.astype(BF)]
    unnamed x244 -> x190, local copies, waits for them, and re-layouts: 40 us -> 26 us
    dot_general x22 -> x20, matrix products: 64.5 us -> 74.7 us  [contract(): lax.dot_general(left, right, (((left_dim,), (right_dim,)), ((), ())), pre...]
    dynamic_slice x7, local copies, waits for them, and re-layouts: 8.99 us -> 1.98 us  [the longest x3 1.18 us: go(): lax.dynamic_index_in_dim(part, mine, axis, keepdims=False).astype(F32)]
    pallas_call x4 -> x2, Pallas kernels: 13.7 us -> 6.82 us  [place(): pl.pallas_call(partial(place_kernel, count, rows, each, self.by_rows, wid...]
  transfers between devices with their start and end apart: 83 -> 55, of which waited for: 29 -> 21; matrix products, arithmetic and copies ran while one was open for 23% -> 23% of each run, Pallas kernels for 21% -> 24%
where the time goes in v3:
time: 574 us; the launch traced here: 565 us
  Pallas kernels  138 us (24%)
  waiting for transfers between devices  132 us (23%)
  matrix products  110 us (19%)
  starting transfers between devices  77.5 us (14%)
  other arithmetic  49.5 us (9%)
  local copies, waits for them, and re-layouts  41.7 us (7%)
  between operations  16.1 us (3%)
    ppermute x44, waiting for transfers between devices, send(): return lax.ppermute(value, axis, pairs)  86.3 us
    dot_general x20, matrix products, contract(): lax.dot_general(left, right, (((left_dim,), (right_dim,)), ((), ())), pre...  74.7 us
    pallas_call x2, Pallas kernels, delta_backward(): pl.pallas_call(partial(backward_kernel, heads, part, d), grid=(blocks + 1...  68.2 us
    ppermute x44, starting transfers between devices, send(): return lax.ppermute(value, axis, pairs)  45.8 us
    all_to_all x4, waiting for transfers between devices, swap(): return lax.all_to_all(value, 'fsdp', 0, 0, tiled=True)  42.6 us
    pallas_call x1, Pallas kernels, delta_summary(): pl.pallas_call(partial(summary_kernel, heads, d), grid=(blocks,), in_spec...  27.3 us
    unnamed x190, local copies, waits for them, and re-layouts  26 us
    all_to_all x4, starting transfers between devices, swap(): return lax.all_to_all(value, 'fsdp', 0, 0, tiled=True)  24.1 us
  transfers between devices with their start and end apart: 55, of which 21 were waited for; matrix products, arithmetic and copies ran while one was open for 23% of the time, Pallas kernels for 24%

profile of v3, /device:TPU:0, one launch (start us, length us, event | category | flops | bytes accessed | tf_op | source)
XLA Modules:
  0.0 565.4 jit_solution(9363335872936288705)
XLA Ops:
  10.2 4.1 collective-permute-start.1
  16.0 3.4 collective-permute-start.4
  20.1 2.3 collective-permute-start.3
  23.0 6.9 %collective-permute-done.2 = bf16[32,2176]{1,0:T(8,128)(2,1)S(1)} collective-permute-done((bf16[32,2176]{1,0:T(8,128)(2,1)S(1)}, bf16[32,2176]{1,0:T(8,128)(2,1)S(1)}, u32[]{:S(2)}, u32[]{:S(2)}) %collective-permute-start.2) | collective-permute-done | bytes 139296 | tf_op jit(solution)/shard_map/ppermute | solution.py:569
  35.8 4.3 collective-permute-done.5.refs_1_
  40.1 3.9 collective-permute-done.6.refs_2_
  44.0 2.5 collective-permute-start.8
  48.5 2.9 collective-permute-start.13
  51.4 6.1 %collective-permute-start.12 = (bf16[64,3072]{1,0:T(8,128)(2,1)}, bf16[64,3072]{1,0:T(8,128)(2,1)}, u32[]{:S(2)}, u32[]{:S(2)}) collective-permute-start(bf16[64,3072]{1,0:T(8,128)(2,1)} %constant_dynamic-slice_fusion.9), channel_id=1, source_target_pairs={{0,2},{1,3},{2,0},{3,1},{4,6},{5,7},{6,4},{7,5},{8,10},{9,11},{10,... | collective-permute-start | bytes 1179656 | tf_op jit(solution)/shard_map/ppermute | solution.py:569
  57.5 6.3 %collective-permute-done.8.refs_4_ = bf16[4,32,2176]{2,1,0:T(8,128)(2,1)} collective-permute-done((bf16[4,32,2176]{2,1,0:T(8,128)(2,1)S(1)}, bf16[4,32,2176]{2,1,0:T(8,128)(2,1)}, u32[]{:S(2)}, u32[]{:S(2)}) %collective-permute-start.8) | collective-permute-done | bytes 557088 | tf_op jit(solution)/shard_map/ppermute | solution.py:569
  69.8 3.4 place_weights.2
  79.3 7.2 %fusion.87.pre_ref.prev_ref.kvpre_ref.kvprev_ref = f32[520,2048]{1,0:T(8,128)} fusion(bf16[520,1024]{1,0:T(8,128)(2,1)S(1)} %fusion.6, bf16[1024,2048]{1,0:T(8,128)(2,1)} %copy-done.16), kind=kOutput, calls=%fused_computation.222 | convolution fusion | flops 2181038080 | bytes 9519104 | tf_op jit(solution)/shard_map/dot_general | solution.py:916
  88.0 12.7 %collective-permute-done.14 = bf16[64,3072]{1,0:T(8,128)(2,1)S(1)} collective-permute-done((bf16[64,3072]{1,0:T(8,128)(2,1)}, bf16[64,3072]{1,0:T(8,128)(2,1)S(1)}, u32[]{:S(2)}, u32[]{:S(2)}) %collective-permute-start.14) | collective-permute-done | bytes 393248 | tf_op jit(solution)/shard_map/ppermute | solution.py:569
  102.0 27.3 %delta_summary.1 = (bf16[512,1024]{1,0:T(8,128)(2,1)S(1)}, bf16[512,1024]{1,0:T(8,128)(2,1)S(1)}, bf16[512,1024]{1,0:T(8,128)(2,1)S(1)}, bf16[512,1024]{1,0:T(8,...) custom-call(f32[520,2048]{1,0:T(8,128)} %fusion.87.pre_ref.prev_ref.kvpre_ref.kvprev_ref, ...), custom_call_target="tpu_custom_call" | custom-call | flops 24000000000 | bytes 72000000 | tf_op jit(solution)/shard_map/delta_summary/pallas_call | solution.py:378
  134.3 7.2 %collective-permute-done.15.refs_1_ = bf16[4,64,3072]{2,1,0:T(8,128)(2,1)} collective-permute-done((bf16[4,64,3072]{2,1,0:T(8,128)(2,1)S(1)}, bf16[4,64,3072]{2,1,0:T(8,128)(2,1)}, u32[]{:S(2)}, u32[]{:S(2)}) %collective-permute-start.15) | collective-permute-done | bytes 1572896 | tf_op jit(solution)/shard_map/ppermute | solution.py:569
  141.5 10.6 %all-to-all-start = ((bf16[8,128,256]{2,1,0:T(8,128)(2,1)}), bf16[8,128,256]{2,1,0:T(8,128)(2,1)}, u32[]{:S(2)}, u32[]{:S(2)}) async-start(bf16[8,128,256]{2,1,0:T(8,128)(2,1)} %get-tuple-element.97), calls=%async_computation | async-start | bytes 1048576 | tf_op jit(solution)/shard_map/all_to_all | solution.py:829
  153.4 21.3 %all-to-all-done.x_ref.t_ref = bf16[8,128,256]{2,1,0:T(8,128)(2,1)} async-done(((bf16[8,128,256]{2,1,0:T(8,128)(2,1)}), bf16[8,128,256]{2,1,0:T(8,128)(2,1)}, u32[]{:S(2)}, u32[]{:S(2)}) %all-to-all-start) | async-done | bytes 524320 | tf_op jit(solution)/shard_map/all_to_all | solution.py:829
  174.6 2.7 state_prefix.1
  177.3 4.0 all-to-all-start.1
  181.7 3.4 place_weights.3
  186.4 2.1 copy-done.4
  188.5 4.4 fusion.88.pre_ref.prev_ref.gate_ref.qpre_ref.qprev_ref
  192.9 5.2 all-to-all-done.1.s_ref
  198.1 14.4 %delta_forward.1 = (bf16[512,1024]{1,0:T(8,128)(2,1)S(1)}, bf16[512,1024]{1,0:T(8,128)(2,1)S(1)}, f32[512,1024]{1,0:T(8,128)S(1)}, bf16[512,1024]{1,0:T(8,128)(2,1)S(1)}, bf16[8,8,128,128]{3,2,1,0:T(8,128)(2,1)S(1)}) custom-call(f32[520,2048]{1,0:T(8,128)} %fusion.88.pre_ref.prev_ref.gate_ref.qpre_ref.qprev_ref, ...), custom_call_target="tpu_custom_call" | custom-call | flops 16000000000 | bytes 48000000 | tf_op jit(solution)/shard_map/delta_forward/pallas_call | solution.py:409
  213.5 2.9 multiply_reduce_fusion.1
  216.5 2.8 multiply_convert_fusion.1
  219.3 11.7 %fusion.89 = f32[512,5632]{1,0:T(8,128)} fusion(bf16[512,1024]{1,0:T(8,128)(2,1)} %multiply_convert_fusion.1, bf16[1024,5632]{1,0:T(8,128)(2,1)} %all-gather.3.cloned.1.call-done), kind=kOutput, calls=%fused_computation.224 | convolution fusion | flops 5905580032 | bytes 24117248 | tf_op jit(solution)/shard_map/dot_general | solution.py:963
  231.0 13.3 %bitcast_multiply_fusion.1 = (f32[512,2816]{1,0:T(8,128)}, f32[512,2816]{1,0:T(8,128)}, bf16[512,2816]{1,0:T(8,128)(2,1)}) fusion(f32[512,5632]{1,0:T(8,128)} %fusion.89, bf16[2816,1024]{1,0:T(8,128)(2,1)} %all-gather.5.cloned.1.call-done, bf16[512,1024]{1,0:T(8,128)(2,1)} %param.27), kind=kOutput, calls=%fused_computation.6 | convolution fusion | flops 2972975104 | bytes 32768000 | tf_op jit(solution)/shard_map/dot_general | solution.py:791
  244.3 7.5 %add_convert_fusion.1 = bf16[512,5632]{1,0:T(8,128)(2,1)} fusion(f32[512,2816]{1,0:T(8,128)} %get-tuple-element.211, f32[512,2816]{1,0:T(8,128)} %get-tuple-element.210), kind=kLoop, calls=%fused_computation.1 | loop fusion | flops 5767168 | bytes 17301504 | tf_op jit(solution)/shard_map/convert_element_type | solution.py:979
  251.8 7.8 %convolution_convert_fusion = bf16[1024,2816]{1,0:T(8,128)(2,1)} fusion(bf16[512,1024]{1,0:T(8,128)(2,1)} %multiply_convert_fusion.1, bf16[512,5632]{1,0:T(8,128)(2,1)} %add_convert_fusion.1, s32[]{:T(128)S(6)} %select_n.516), kind=kOutput, calls=%fused_computation.11 | convolution fusion | flops 2955673600 | bytes 9699332 | tf_op jit(solution)/shard_map/dot_general | solution.py:791
  260.9 3.8 convolution_convert_fusion.1
  265.3 9.4 %multiply_reduce_fusion = (f32[512]{0:T(512)S(1)}, f32[512,1024]{1,0:T(8,128)S(1)}) fusion(f32[512,1024]{1,0:T(8,128)} %get-tuple-element.245, f32[1024]{0:T(1024)S(1)} %get-tuple-element.235, bf16[512,5632]{1,0:T(8,128)(2,1)S(1)} %bitcast.227, bf16[1024,5632]{1,0:T(8,128)(2,1)} %all-gather.3.cloned.1.call-done), kind=kOutput, calls=%fused_computation.47 | convolution fusion | flops 5907152384 | bytes 21501952 | tf_op jit(solution)/shard_map/dot_general | solution.py:791
  274.8 2.9 fusion.83
  277.7 2.6 fusion.90.dy_ref
  283.2 3.4 add_convert_fusion.2
  286.6 16.1 %delta_adjoint.1 = (bf16[512,1024]{1,0:T(8,128)(2,1)S(1)}, bf16[512,1024]{1,0:T(8,128)(2,1)S(1)}, f32[1,128]{1,0:T(1,128)S(1)}, bf16[8,128,128]{2,1,0:T(8,128)(2,1)}) custom-call(bf16[512,1024]{1,0:T(8,128)(2,1)} %copy-done.24, bf16[512,1024]{1,0:T(8,128)(2,1)} %copy-done.21, bf16[512,1024]{1,0:T(8,128)(2,1)} %copy-done.22, f32[512,16]{1,0:T(8,128)} %copy.51.cols_ref, ...), custom_call_target="tpu_custom_call" | custom-call | flops 15000000512 | bytes 45000000 | tf_op jit(solution)/shard_map/delta_adjoint/pallas_call | solution.py:444
  303.7 7.1 %add_convert_fusion = bf16[1024,2816]{1,0:T(8,128)(2,1)} fusion(bf16[1024,2816]{1,0:T(8,128)(2,1)} %collective-permute-done.19, bf16[512,1024]{1,0:T(8,128)(2,1)S(1)} %copy-done.51, bf16[512,2816]{1,0:T(8,128)(2,1)S(1)} %copy-done.48), kind=kOutput, calls=%fused_computation | convolution fusion | flops 2961440768 | bytes 15466496 | tf_op jit(solution)/shard_map/dot_general | solution.py:791
  310.8 3.4 all-to-all-start.2
  314.3 14.5 %all-to-all-done.2.g_ref = bf16[8,128,128]{2,1,0:T(8,128)(2,1)S(1)} async-done(((bf16[8,128,128]{2,1,0:T(8,128)(2,1)}), bf16[8,128,128]{2,1,0:T(8,128)(2,1)S(1)}, u32[]{:S(2)}, u32[]{:S(2)}) %all-to-all-start.2) | async-done | bytes 262176 | tf_op jit(solution)/shard_map/all_to_all | solution.py:829
  329.4 2.8 state_suffix.1
  333.6 3.4 broadcast_select_fusion
  336.9 2.2 select_convert_fusion
  339.1 6.0 %all-to-all-start.3 = ((bf16[8,128,128]{2,1,0:T(8,128)(2,1)}), bf16[8,128,128]{2,1,0:T(8,128)(2,1)S(1)}, u32[]{:S(2)}, u32[]{:S(2)}) async-start(bf16[8,128,128]{2,1,0:T(8,128)(2,1)} %state_suffix.1), calls=%async_computation.3 | async-start | bytes 524288 | tf_op jit(solution)/shard_map/all_to_all | solution.py:829
  345.2 8.6 %add_convert_fusion.6 = bf16[512,1024]{1,0:T(8,128)(2,1)} fusion(f32[512,1024]{1,0:T(8,128)} %get-tuple-element.245, bf16[512,2816]{1,0:T(8,128)(2,1)} %get-tuple-element.114, bf16[2816,1024]{1,0:T(8,128)(2,1)} %all-gather.5.cloned.1.call-done), kind=kOutput, calls=%fused_computation.46 | convolution fusion | flops 2953838592 | bytes 11796480 | tf_op jit(solution)/shard_map/dot_general | solution.py:1012
  353.8 2.5 add_convert_fusion.3
  362.6 34.0 %delta_backward.2 = (bf16[520,1536]{1,0:T(8,128)(2,1)S(1)}, f32[512,128]{1,0:T(8,128)S(1)}, f32[4,1536]{1,0:T(4,128)S(1)}) custom-call(bf16[512,1024]{1,0:T(8,128)(2,1)} %copy-done.24, bf16[512,1024]{1,0:T(8,128)(2,1)} %copy-done.21, bf16[512,1024]{1,0:T(8,128)(2,1)} %copy-done.27, bf16[512,1024]{1,0:T(8,128)(2,1)} %copy-done.22, ...), custom_call_target="tpu_custom_call" | custom-call | flops 32000000000 | bytes 96000000 | tf_op jit(solution)/shard_map/delta_backward/pallas_call | solution.py:503
  396.7 2.6 convolution_convert_fusion.3
  400.7 2.1 fusion.14
  405.3 3.3 fusion.36
  408.6 2.6 fusion.19
  411.3 2.9 add_convert_fusion.5
  416.8 34.1 %delta_backward.3 = (bf16[520,1536]{1,0:T(8,128)(2,1)S(1)}, f32[512,128]{1,0:T(8,128)S(1)}, f32[4,1536]{1,0:T(4,128)S(1)}) custom-call(bf16[512,1024]{1,0:T(8,128)(2,1)} %copy-done.24, bf16[512,1024]{1,0:T(8,128)(2,1)} %copy-done.21, bf16[512,1024]{1,0:T(8,128)(2,1)} %copy-done.27, bf16[512,1024]{1,0:T(8,128)(2,1)} %copy-done.22, ...), custom_call_target="tpu_custom_call" | custom-call | flops 32000000000 | bytes 96000000 | tf_op jit(solution)/shard_map/delta_backward/pallas_call | solution.py:503
  453.0 3.8 convolution_convert_fusion.2
  462.3 3.0 add_convert_fusion.4
  472.5 3.3 collective-permute-done.27
  477.1 12.5 %collective-permute-done.31 = bf16[2,2,2,64,128]{4,3,0,1,2:T(8,128)(2,1)S(1)} collective-permute-done((bf16[2,2,2,64,128]{4,3,0,1,2:T(8,128)(2,1)S(1)}, bf16[2,2,2,64,128]{4,3,0,1,2:T(8,128)(2,1)S(1)}, u32[]{:S(2)}, u32[]{:S(2)}) %collective-permute-start.31) | collective-permute-done | bytes 131104 | tf_op jit(solution)/shard_map/ppermute | solution.py:569
  495.2 3.7 fusion.9
  498.9 5.1 collective-permute-done.33
  504.1 3.1 collective-permute-done.32
  512.3 4.3 collective-permute-done.39
  523.4 3.3 collective-permute-done.38
  529.2 13.1 %collective-permute-done.42 = bf16[64,2688]{1,0:T(8,128)(2,1)S(1)} collective-permute-done((bf16[64,2688]{1,0:T(8,128)(2,1)S(1)}, bf16[64,2688]{1,0:T(8,128)(2,1)S(1)}, u32[]{:S(2)}, u32[]{:S(2)}) %collective-permute-start.42) | collective-permute-done | bytes 344096 | tf_op jit(solution)/shard_map/ppermute | solution.py:569
  545.5 2.4 fusion.51
  547.9 3.2 multiply_reduce_fusion.3
  (404 shorter events, 103.6 us)
Async XLA Ops:
  7.2 25.8 %copy-start = (bf16[352,1024]{1,0:T(8,128)(2,1)S(1)}, bf16[352,1024]{1,0:T(8,128)(2,1)}, u32[]{:S(2)}) copy-start(bf16[352,1024]{1,0:T(8,128)(2,1)} %param.26) | copy-start | bytes 2162692
  7.3 212.0 %all-gather.3.cloned.1.call-start = ((), (), s32[]{:S(2)}) async-start(), calls=%async_computation.6 | async-start | bytes 11894784 | tf_op jit(solution)/shard_map/all_gather | solution.py:775
  9.3 221.7 %all-gather.5.cloned.1.call-start = ((), (), s32[]{:S(2)}) async-start(), calls=%async_computation.7 | async-start | bytes 5947392 | tf_op jit(solution)/shard_map/all_gather | solution.py:775
  9.9 24.9 %slice-start.2 = ((bf16[128,3072]{1,0:T(8,128)(2,1)}), bf16[128,1024]{1,0:T(8,128)(2,1)S(1)}, s32[]{:S(2)}) async-start(bf16[128,3072]{1,0:T(8,128)(2,1)} %param.17), calls=%async_computation.12 | async-start | bytes 524288 | tf_op jit(solution)/shard_map/slice | solution.py:879
  9.9 24.9 %copy-start.52 = (bf16[128,1024]{1,0:T(8,128)(2,1)S(1)}, bf16[128,1024]{1,0:T(8,128)(2,1)}, u32[]{:S(2)}) copy-start(bf16[128,1024]{1,0:T(8,128)(2,1)} %param.19) | copy-start | bytes 786436
  10.2 12.2 %collective-permute-start.1 = (bf16[32,2176]{1,0:T(8,128)(2,1)S(1)}, bf16[32,2176]{1,0:T(8,128)(2,1)S(1)}, u32[]{:S(2)}, u32[]{:S(2)}) collective-permute-start(bf16[32,2176]{1,0:T(8,128)(2,1)S(1)} %constant_dynamic-slice_fusion.10), channel_id=1, source_target_pairs={{0,4},{1,5},{2,6},{3,7},{4,0},{5,1},{6,2},{7,3},{8,12},{9,13},{10,... | collective-permute-start | bytes 417800 | tf_op jit(solution)/shard_map/ppermute | solution.py:569
  14.3 8.6 %collective-permute-start = (bf16[32,2176]{1,0:T(8,128)(2,1)S(1)}, bf16[32,2176]{1,0:T(8,128)(2,1)S(1)}, u32[]{:S(2)}, u32[]{:S(2)}) collective-permute-start(bf16[32,2176]{1,0:T(8,128)(2,1)S(1)} %constant_dynamic-slice_fusion.10), channel_id=1, source_target_pairs={{0,2},{1,3},{2,0},{3,1},{4,6},{5,7},{6,4},{7,5},{8,10},{9,11},{10,... | collective-permute-start | bytes 417800 | tf_op jit(solution)/shard_map/ppermute | solution.py:569
  16.0 14.0 %collective-permute-start.4 = (s32[8]{0:T(128)S(1)}, s32[8]{0:T(128)S(1)}, u32[]{:S(2)}, u32[]{:S(2)}) collective-permute-start(s32[8]{0:T(128)S(1)} %slice.183), channel_id=1, source_target_pairs={{0,1},{1,2},{2,3},{3,4},{4,5},{5,6},{6,7},{8,9},{9,10},{10,11},{11... | collective-permute-start | bytes 104 | tf_op jit(solution)/shard_map/ppermute | solution.py:813
  20.1 9.9 %collective-permute-start.3 = (bf16[8,1024]{1,0:T(8,128)(2,1)S(1)}, bf16[8,1024]{1,0:T(8,128)(2,1)S(1)}, u32[]{:S(2)}, u32[]{:S(2)}) collective-permute-start(bf16[8,1024]{1,0:T(8,128)(2,1)S(1)} %slice.182), channel_id=1, source_target_pairs={{0,1},{1,2},{2,3},{3,4},{4,5},{5,6},{6,7},{8,9},{9,10},{10,11},{11... | collective-permute-start | bytes 49160 | tf_op jit(solution)/shard_map/ppermute | solution.py:813
  22.4 7.4 %collective-permute-start.2 = (bf16[32,2176]{1,0:T(8,128)(2,1)S(1)}, bf16[32,2176]{1,0:T(8,128)(2,1)S(1)}, u32[]{:S(2)}, u32[]{:S(2)}) collective-permute-start(bf16[32,2176]{1,0:T(8,128)(2,1)S(1)} %collective-permute-done.1), channel_id=1, source_target_pairs={{0,2},{1,3},{2,0},{3,1},{4,6},{5,7},{6,4},{7,5},{8,10},{9,11},{10,... | collective-permute-start | bytes 417800 | tf_op jit(solution)/shard_map/ppermute | solution.py:569
  30.0 10.1 %collective-permute-start.5 = (bf16[4,32,2176]{2,1,0:T(8,128)(2,1)S(1)}, bf16[4,32,2176]{2,1,0:T(8,128)(2,1)S(1)}, u32[]{:S(2)}, u32[]{:S(2)}) collective-permute-start(bf16[4,32,2176]{2,1,0:T(8,128)(2,1)S(1)} %pad_maximum_fusion.3.refs_0_), channel_id=1, source_target_pairs={{0,1},{1,0},{2,3},{3,2},{4,5},{5,4},{6,7},{7,6},{8,9},{9,8},{10,11... | collective-permute-start | bytes 1671176 | tf_op jit(solution)/shard_map/ppermute | solution.py:569
  31.6 12.4 %collective-permute-start.6 = (bf16[4,32,2176]{2,1,0:T(8,128)(2,1)S(1)}, bf16[4,32,2176]{2,1,0:T(8,128)(2,1)S(1)}, u32[]{:S(2)}, u32[]{:S(2)}) collective-permute-start(bf16[4,32,2176]{2,1,0:T(8,128)(2,1)S(1)} %pad_maximum_fusion.3.refs_0_), channel_id=1, source_target_pairs={{0,16},{8,24},{16,0},{24,8},{1,17},{9,25},{17,1},{25,9},{2,18},{10... | collective-permute-start | bytes 1671176 | tf_op jit(solution)/shard_map/ppermute | solution.py:569
  33.0 11.0 %collective-permute-start.7 = (bf16[4,32,2176]{2,1,0:T(8,128)(2,1)S(1)}, bf16[4,32,2176]{2,1,0:T(8,128)(2,1)}, u32[]{:S(2)}, u32[]{:S(2)}) collective-permute-start(bf16[4,32,2176]{2,1,0:T(8,128)(2,1)S(1)} %pad_maximum_fusion.3.refs_0_), channel_id=1, source_target_pairs={{0,8},{8,0},{16,24},{24,16},{1,9},{9,1},{17,25},{25,17},{2,10},{10... | collective-permute-start | bytes 1671176 | tf_op jit(solution)/shard_map/ppermute | solution.py:569
  34.8 30.7 %copy-start.76 = (s32[512]{0:T(512)S(1)}, s32[512]{0:T(512)}, u32[]{:S(2)}) copy-start(s32[512]{0:T(512)} %copy-done.75) | copy-start | bytes 6148
  34.8 30.6 %copy-start.85 = (s32[8]{0:T(128)S(1)}, s32[8]{0:T(128)}, u32[]{:S(2)}) copy-start(s32[8]{0:T(128)} %copy-done.84) | copy-start | bytes 100
  44.0 19.8 %collective-permute-start.8 = (bf16[4,32,2176]{2,1,0:T(8,128)(2,1)S(1)}, bf16[4,32,2176]{2,1,0:T(8,128)(2,1)}, u32[]{:S(2)}, u32[]{:S(2)}) collective-permute-start(bf16[4,32,2176]{2,1,0:T(8,128)(2,1)S(1)} %collective-permute-done.5.refs_1_), channel_id=1, source_target_pairs={{0,16},{8,24},{16,0},{24,8},{1,17},{9,25},{17,1},{25,9},{2,18},{10... | collective-permute-start | bytes 1671176 | tf_op jit(solution)/shard_map/ppermute | solution.py:569
  46.5 17.3 %collective-permute-start.10 = (bf16[4,32,2176]{2,1,0:T(8,128)(2,1)S(1)}, bf16[4,32,2176]{2,1,0:T(8,128)(2,1)S(1)}, u32[]{:S(2)}, u32[]{:S(2)}) collective-permute-start(bf16[4,32,2176]{2,1,0:T(8,128)(2,1)S(1)} %collective-permute-done.6.refs_2_), channel_id=1, source_target_pairs={{0,8},{8,0},{16,24},{24,16},{1,9},{9,1},{17,25},{25,17},{2,10},{10... | collective-permute-start | bytes 1671176 | tf_op jit(solution)/shard_map/ppermute | solution.py:569
  46.5 18.1 %collective-permute-start.9 = (bf16[4,32,2176]{2,1,0:T(8,128)(2,1)S(1)}, bf16[4,32,2176]{2,1,0:T(8,128)(2,1)S(1)}, u32[]{:S(2)}, u32[]{:S(2)}) collective-permute-start(bf16[4,32,2176]{2,1,0:T(8,128)(2,1)S(1)} %collective-permute-done.5.refs_1_), channel_id=1, source_target_pairs={{0,8},{8,0},{16,24},{24,16},{1,9},{9,1},{17,25},{25,17},{2,10},{10... | collective-permute-start | bytes 1671176 | tf_op jit(solution)/shard_map/ppermute | solution.py:569
  48.5 30.3 %collective-permute-start.13 = (bf16[64,3072]{1,0:T(8,128)(2,1)}, bf16[64,3072]{1,0:T(8,128)(2,1)}, u32[]{:S(2)}, u32[]{:S(2)}) collective-permute-start(bf16[64,3072]{1,0:T(8,128)(2,1)} %constant_dynamic-slice_fusion.9), channel_id=1, source_target_pairs={{0,4},{1,5},{2,6},{3,7},{4,0},{5,1},{6,2},{7,3},{8,12},{9,13},{10,... | collective-permute-start | bytes 1179656 | tf_op jit(solution)/shard_map/ppermute | solution.py:569
  51.4 36.6 %collective-permute-start.12 = (bf16[64,3072]{1,0:T(8,128)(2,1)}, bf16[64,3072]{1,0:T(8,128)(2,1)}, u32[]{:S(2)}, u32[]{:S(2)}) collective-permute-start(bf16[64,3072]{1,0:T(8,128)(2,1)} %constant_dynamic-slice_fusion.9), channel_id=1, source_target_pairs={{0,2},{1,3},{2,0},{3,1},{4,6},{5,7},{6,4},{7,5},{8,10},{9,11},{10,... | collective-permute-start | bytes 1179656 | tf_op jit(solution)/shard_map/ppermute | solution.py:569
  65.4 2.3 collective-permute-start.11
  75.8 199.0 %copy-start.64 = (f32[1024]{0:T(1024)}, f32[1024]{0:T(1024)S(1)}, u32[]{:S(2)}) copy-start(f32[1024]{0:T(1024)S(1)} %get-tuple-element.235) | copy-start | bytes 12292
  77.4 109.0 %copy-start.38 = (bf16[520,1024]{1,0:T(8,128)(2,1)}, bf16[520,1024]{1,0:T(8,128)(2,1)S(1)}, u32[]{:S(2)}) copy-start(bf16[520,1024]{1,0:T(8,128)(2,1)S(1)} %fusion.6) | copy-start | bytes 3194884
  78.8 21.8 %collective-permute-start.14 = (bf16[64,3072]{1,0:T(8,128)(2,1)}, bf16[64,3072]{1,0:T(8,128)(2,1)S(1)}, u32[]{:S(2)}, u32[]{:S(2)}) collective-permute-start(bf16[64,3072]{1,0:T(8,128)(2,1)} %collective-permute-done.13), channel_id=1, source_target_pairs={{0,2},{1,3},{2,0},{3,1},{4,6},{5,7},{6,4},{7,5},{8,10},{9,11},{10,... | collective-permute-start | bytes 1179656 | tf_op jit(solution)/shard_map/ppermute | solution.py:569
  79.3 21.3 %copy-start.50 = (bf16[1,64,3072]{2,1,0:T(8,128)(2,1)S(1)}, bf16[1,64,3072]{2,1,0:T(8,128)(2,1)}, u32[]{:S(2)}) copy-start(bf16[1,64,3072]{2,1,0:T(8,128)(2,1)} %fusion.125) | copy-start | bytes 1179652
  101.9 39.6 %collective-permute-start.15 = (bf16[4,64,3072]{2,1,0:T(8,128)(2,1)S(1)}, bf16[4,64,3072]{2,1,0:T(8,128)(2,1)}, u32[]{:S(2)}, u32[]{:S(2)}) collective-permute-start(bf16[4,64,3072]{2,1,0:T(8,128)(2,1)S(1)} %pad_maximum_fusion.refs_0_), channel_id=1, source_target_pairs={{0,1},{1,0},{2,3},{3,2},{4,5},{5,4},{6,7},{7,6},{8,9},{9,8},{10,11... | collective-permute-start | bytes 4718600 | tf_op jit(solution)/shard_map/ppermute | solution.py:569
  134.3 47.3 %collective-permute-start.16 = (bf16[4,64,3072]{2,1,0:T(8,128)(2,1)S(1)}, bf16[4,64,3072]{2,1,0:T(8,128)(2,1)}, u32[]{:S(2)}, u32[]{:S(2)}) collective-permute-start(bf16[4,64,3072]{2,1,0:T(8,128)(2,1)S(1)} %pad_maximum_fusion.refs_0_), channel_id=1, source_target_pairs={{0,8},{8,0},{16,24},{24,16},{1,9},{9,1},{17,25},{25,17},{2,10},{10... | collective-permute-start | bytes 4718600 | tf_op jit(solution)/shard_map/ppermute | solution.py:569
  141.5 40.2 %collective-permute-start.17 = (bf16[4,64,3072]{2,1,0:T(8,128)(2,1)}, bf16[4,64,3072]{2,1,0:T(8,128)(2,1)}, u32[]{:S(2)}, u32[]{:S(2)}) collective-permute-start(bf16[4,64,3072]{2,1,0:T(8,128)(2,1)} %collective-permute-done.15.refs_1_), channel_id=1, source_target_pairs={{0,8},{8,0},{16,24},{24,16},{1,9},{9,1},{17,25},{25,17},{2,10},{10... | collective-permute-start | bytes 4718600 | tf_op jit(solution)/shard_map/ppermute | solution.py:569
  141.5 33.1 %all-to-all-start = ((bf16[8,128,256]{2,1,0:T(8,128)(2,1)}), bf16[8,128,256]{2,1,0:T(8,128)(2,1)}, u32[]{:S(2)}, u32[]{:S(2)}) async-start(bf16[8,128,256]{2,1,0:T(8,128)(2,1)} %get-tuple-element.97), calls=%async_computation | async-start | bytes 1048576 | tf_op jit(solution)/shard_map/all_to_all | solution.py:829
  177.3 20.8 %all-to-all-start.1 = ((bf16[8,128,128]{2,1,0:T(8,128)(2,1)}), bf16[8,128,128]{2,1,0:T(8,128)(2,1)}, u32[]{:S(2)}, u32[]{:S(2)}) async-start(bf16[8,128,128]{2,1,0:T(8,128)(2,1)} %state_prefix.1), calls=%async_computation.1 | async-start | bytes 524288 | tf_op jit(solution)/shard_map/all_to_all | solution.py:829
  181.4 271.6 %reduce-scatter.3.cloned.1.call-start = ((), (), s32[]{:S(2)}) async-start(), calls=%async_computation.8 | async-start | bytes 6488064 | tf_op jit(solution)/shard_map/reduce_scatter | solution.py:779
  216.4 58.3 %copy-start.68 = (f32[512]{0:T(512)}, f32[512]{0:T(512)S(1)}, u32[]{:S(2)}) copy-start(f32[512]{0:T(512)S(1)} %fusion.80) | copy-start | bytes 6148
  259.6 44.1 %collective-permute-start.19 = (bf16[1024,2816]{1,0:T(8,128)(2,1)}, bf16[1024,2816]{1,0:T(8,128)(2,1)}, u32[]{:S(2)}, u32[]{:S(2)}) collective-permute-start(bf16[1024,2816]{1,0:T(8,128)(2,1)} %convolution_convert_fusion), channel_id=1, source_target_pairs={{0,8},{8,0},{16,24},{24,16},{1,9},{9,1},{17,25},{25,17},{2,10},{10... | collective-permute-start | bytes 17301512 | tf_op jit(solution)/shard_map/ppermute | solution.py:569
  264.7 17.4 %collective-permute-start.18 = (bf16[2816,512]{1,0:T(8,128)(2,1)S(1)}, bf16[2816,512]{1,0:T(8,128)(2,1)S(1)}, u32[]{:S(2)}, u32[]{:S(2)}) collective-permute-start(bf16[2816,512]{1,0:T(8,128)(2,1)S(1)} %convolution_convert_fusion.1), channel_id=1, source_target_pairs={{0,8},{8,0},{16,24},{24,16},{1,9},{9,1},{17,25},{25,17},{2,10},{10... | collective-permute-start | bytes 8650760 | tf_op jit(solution)/shard_map/ppermute | solution.py:569
  310.8 17.9 %all-to-all-start.2 = ((bf16[8,128,128]{2,1,0:T(8,128)(2,1)}), bf16[8,128,128]{2,1,0:T(8,128)(2,1)S(1)}, u32[]{:S(2)}, u32[]{:S(2)}) async-start(bf16[8,128,128]{2,1,0:T(8,128)(2,1)} %get-tuple-element.111), calls=%async_computation.2 | async-start | bytes 524288 | tf_op jit(solution)/shard_map/all_to_all | solution.py:829
  339.1 14.7 %collective-permute-start.20 = (bf16[1024,1024]{1,0:T(8,128)(2,1)}, bf16[1024,1024]{1,0:T(8,128)(2,1)}, u32[]{:S(2)}, u32[]{:S(2)}) collective-permute-start(bf16[1024,1024]{1,0:T(8,128)(2,1)} %select_convert_fusion), channel_id=1, source_target_pairs={{0,8},{8,0},{16,24},{24,16},{1,9},{9,1},{17,25},{25,17},{2,10},{10... | collective-permute-start | bytes 6291464 | tf_op jit(solution)/shard_map/ppermute | solution.py:569
  339.1 22.8 %all-to-all-start.3 = ((bf16[8,128,128]{2,1,0:T(8,128)(2,1)}), bf16[8,128,128]{2,1,0:T(8,128)(2,1)S(1)}, u32[]{:S(2)}, u32[]{:S(2)}) async-start(bf16[8,128,128]{2,1,0:T(8,128)(2,1)} %state_suffix.1), calls=%async_computation.3 | async-start | bytes 524288 | tf_op jit(solution)/shard_map/all_to_all | solution.py:829
  345.1 181.6 %reduce-scatter.5.cloned.1.call-start = ((), (), s32[]{:S(2)}) async-start(), calls=%async_computation.9 | async-start | bytes 3244032 | tf_op jit(solution)/shard_map/reduce_scatter | solution.py:779
  358.6 38.0 %collective-permute-start.21 = (bf16[2,2,2,64,1024]{4,3,2,1,0:T(8,128)(2,1)}, bf16[2,2,2,64,1024]{4,3,2,1,0:T(8,128)(2,1)}, u32[]{:S(2)}, u32[]{:S(2)}) collective-permute-start(bf16[2,2,2,64,1024]{4,3,2,1,0:T(8,128)(2,1)} %dynamic-slice_bitcast_fusion), channel_id=1, source_target_pairs={{0,16},{8,24},{16,0},{24,8},{1,17},{9,25},{17,1},{25,9},{2,18},{10... | collective-permute-start | bytes 3145736 | tf_op jit(solution)/shard_map/ppermute | solution.py:569
  399.3 12.0 %collective-permute-start.22 = (bf16[1024,768]{1,0:T(8,128)(2,1)}, bf16[1024,768]{1,0:T(8,128)(2,1)}, u32[]{:S(2)}, u32[]{:S(2)}) collective-permute-start(bf16[1024,768]{1,0:T(8,128)(2,1)} %convolution_convert_fusion.3), channel_id=1, source_target_pairs={{0,8},{8,0},{16,24},{24,16},{1,9},{9,1},{17,25},{25,17},{2,10},{10... | collective-permute-start | bytes 4718600 | tf_op jit(solution)/shard_map/ppermute | solution.py:569
  403.8 47.3 %collective-permute-start.23 = (bf16[2,2,64,1024]{3,2,1,0:T(8,128)(2,1)S(1)}, bf16[2,2,64,1024]{3,2,1,0:T(8,128)(2,1)S(1)}, u32[]{:S(2)}, u32[]{:S(2)}) collective-permute-start(bf16[2,2,64,1024]{3,2,1,0:T(8,128)(2,1)S(1)} %dynamic-slice_bitcast_fusion.1), channel_id=1, source_target_pairs={{0,1},{1,0},{2,3},{3,2},{4,5},{5,4},{6,7},{7,6},{8,9},{9,8},{10,11... | collective-permute-start | bytes 1572872 | tf_op jit(solution)/shard_map/ppermute | solution.py:569
  415.2 35.9 %collective-permute-start.24 = (bf16[2,2,2,64,768]{4,3,0,1,2:T(8,128)(2,1)S(1)}, bf16[2,2,2,64,768]{4,3,0,1,2:T(8,128)(2,1)S(1)}, u32[]{:S(2)}, u32[]{:S(2)}) collective-permute-start(bf16[2,2,2,64,768]{4,3,0,1,2:T(8,128)(2,1)S(1)} %bitcast.234), channel_id=1, source_target_pairs={{0,16},{8,24},{16,0},{24,8},{1,17},{9,25},{17,1},{25,9},{2,18},{10... | collective-permute-start | bytes 2359304 | tf_op jit(solution)/shard_map/ppermute | solution.py:569
  456.8 5.5 collective-permute-start.25
  459.8 17.3 %collective-permute-start.30 = (bf16[2,64,1024]{2,1,0:T(8,128)(2,1)S(1)}, bf16[2,64,1024]{2,1,0:T(8,128)(2,1)S(1)}, u32[]{:S(2)}, u32[]{:S(2)}) collective-permute-start(bf16[2,64,1024]{2,1,0:T(8,128)(2,1)S(1)} %dynamic-slice_bitcast_fusion.4), channel_id=1, source_target_pairs={{0,2},{1,3},{2,0},{3,1},{4,6},{5,7},{6,4},{7,5},{8,10},{9,11},{10,... | collective-permute-start | bytes 786440 | tf_op jit(solution)/shard_map/ppermute | solution.py:569
  460.4 1.8 collective-permute-start.26
  461.2 15.9 %collective-permute-start.29 = (bf16[2,2,64,768]{3,2,0,1:T(8,128)(2,1)S(1)}, bf16[2,2,64,768]{3,2,0,1:T(8,128)(2,1)S(1)}, u32[]{:S(2)}, u32[]{:S(2)}) collective-permute-start(bf16[2,2,64,768]{3,2,0,1:T(8,128)(2,1)S(1)} %dynamic-slice_bitcast_fusion.3), channel_id=1, source_target_pairs={{0,1},{1,0},{2,3},{3,2},{4,5},{5,4},{6,7},{7,6},{8,9},{9,8},{10,11... | collective-permute-start | bytes 1179656 | tf_op jit(solution)/shard_map/ppermute | solution.py:569
  466.9 22.6 %collective-permute-start.28 = (bf16[2,2,2,64,768]{4,3,0,1,2:T(8,128)(2,1)S(1)}, bf16[2,2,2,64,768]{4,3,0,1,2:T(8,128)(2,1)S(1)}, u32[]{:S(2)}, u32[]{:S(2)}) collective-permute-start(bf16[2,2,2,64,768]{4,3,0,1,2:T(8,128)(2,1)S(1)} %bitcast.233), channel_id=1, source_target_pairs={{0,16},{8,24},{16,0},{24,8},{1,17},{9,25},{17,1},{25,9},{2,18},{10... | collective-permute-start | bytes 2359304 | tf_op jit(solution)/shard_map/ppermute | solution.py:569
  470.0 5.7 %collective-permute-start.27 = (bf16[8,1024]{1,0:T(8,128)(2,1)S(1)}, bf16[8,1024]{1,0:T(8,128)(2,1)S(1)}, u32[]{:S(2)}, u32[]{:S(2)}) collective-permute-start(bf16[8,1024]{1,0:T(8,128)(2,1)S(1)} %slice.351), channel_id=1, source_target_pairs={{1,0},{2,1},{3,2},{4,3},{5,4},{6,5},{7,6},{9,8},{10,9},{11,10},{12... | collective-permute-start | bytes 49160 | tf_op jit(solution)/shard_map/ppermute | solution.py:813
  471.7 17.9 %collective-permute-start.31 = (bf16[2,2,2,64,128]{4,3,0,1,2:T(8,128)(2,1)S(1)}, bf16[2,2,2,64,128]{4,3,0,1,2:T(8,128)(2,1)S(1)}, u32[]{:S(2)}, u32[]{:S(2)}) collective-permute-start(bf16[2,2,2,64,128]{4,3,0,1,2:T(8,128)(2,1)S(1)} %bitcast.244), channel_id=1, source_target_pairs={{0,16},{8,24},{16,0},{24,8},{1,17},{9,25},{17,1},{25,9},{2,18},{10... | collective-permute-start | bytes 393224 | tf_op jit(solution)/shard_map/ppermute | solution.py:569
  489.6 9.3 %collective-permute-start.35 = (bf16[2,2,64,128]{3,2,0,1:T(8,128)(2,1)S(1)}, bf16[2,2,64,128]{3,2,0,1:T(8,128)(2,1)S(1)}, u32[]{:S(2)}, u32[]{:S(2)}) collective-permute-start(bf16[2,2,64,128]{3,2,0,1:T(8,128)(2,1)S(1)} %dynamic-slice_bitcast_fusion.10), channel_id=1, source_target_pairs={{0,1},{1,0},{2,3},{3,2},{4,5},{5,4},{6,7},{7,6},{8,9},{9,8},{10,11... | collective-permute-start | bytes 196616 | tf_op jit(solution)/shard_map/ppermute | solution.py:569
  490.7 8.2 %collective-permute-start.34 = (bf16[64,1024]{1,0:T(8,128)(2,1)S(1)}, bf16[64,1024]{1,0:T(8,128)(2,1)S(1)}, u32[]{:S(2)}, u32[]{:S(2)}) collective-permute-start(bf16[64,1024]{1,0:T(8,128)(2,1)S(1)} %dynamic-slice_bitcast_fusion.7), channel_id=1, source_target_pairs={{0,4},{1,5},{2,6},{3,7},{4,0},{5,1},{6,2},{7,3},{8,12},{9,13},{10,... | collective-permute-start | bytes 393224 | tf_op jit(solution)/shard_map/ppermute | solution.py:569
  492.5 11.5 %collective-permute-start.33 = (bf16[2,64,768]{2,1,0:T(8,128)(2,1)S(1)}, bf16[2,64,768]{2,1,0:T(8,128)(2,1)S(1)}, u32[]{:S(2)}, u32[]{:S(2)}) collective-permute-start(bf16[2,64,768]{2,1,0:T(8,128)(2,1)S(1)} %dynamic-slice_bitcast_fusion.6), channel_id=1, source_target_pairs={{0,2},{1,3},{2,0},{3,1},{4,6},{5,7},{6,4},{7,5},{8,10},{9,11},{10,... | collective-permute-start | bytes 589832 | tf_op jit(solution)/shard_map/ppermute | solution.py:569
  493.4 13.7 %collective-permute-start.32 = (bf16[2,2,64,768]{3,2,0,1:T(8,128)(2,1)S(1)}, bf16[2,2,64,768]{3,2,0,1:T(8,128)(2,1)S(1)}, u32[]{:S(2)}, u32[]{:S(2)}) collective-permute-start(bf16[2,2,64,768]{3,2,0,1:T(8,128)(2,1)S(1)} %dynamic-slice_bitcast_fusion.2), channel_id=1, source_target_pairs={{0,1},{1,0},{2,3},{3,2},{4,5},{5,4},{6,7},{7,6},{8,9},{9,8},{10,11... | collective-permute-start | bytes 1179656 | tf_op jit(solution)/shard_map/ppermute | solution.py:569
  507.2 19.6 %collective-permute-start.41 = (bf16[128,2816]{1,0:T(8,128)(2,1)S(1)}, bf16[128,2816]{1,0:T(8,128)(2,1)S(1)}, u32[]{:S(2)}, u32[]{:S(2)}) collective-permute-start(bf16[128,2816]{1,0:T(8,128)(2,1)S(1)} %copy-done.56), channel_id=1, source_target_pairs={{0,16},{8,24},{16,0},{24,8},{1,17},{9,25},{17,1},{25,9},{2,18},{10... | collective-permute-start | bytes 2162696 | tf_op jit(solution)/shard_map/ppermute | solution.py:569
  508.8 7.8 %collective-permute-start.39 = (bf16[2,64,128]{2,1,0:T(8,128)(2,1)S(1)}, bf16[2,64,128]{2,1,0:T(8,128)(2,1)S(1)}, u32[]{:S(2)}, u32[]{:S(2)}) collective-permute-start(bf16[2,64,128]{2,1,0:T(8,128)(2,1)S(1)} %dynamic-slice_bitcast_fusion.11), channel_id=1, source_target_pairs={{0,2},{1,3},{2,0},{3,1},{4,6},{5,7},{6,4},{7,5},{8,10},{9,11},{10,... | collective-permute-start | bytes 98312 | tf_op jit(solution)/shard_map/ppermute | solution.py:569
  510.2 7.3 %collective-permute-start.37 = (bf16[64,768]{1,0:T(8,128)(2,1)S(1)}, bf16[64,768]{1,0:T(8,128)(2,1)S(1)}, u32[]{:S(2)}, u32[]{:S(2)}) collective-permute-start(bf16[64,768]{1,0:T(8,128)(2,1)S(1)} %dynamic-slice_bitcast_fusion.9), channel_id=1, source_target_pairs={{0,4},{1,5},{2,6},{3,7},{4,0},{5,1},{6,2},{7,3},{8,12},{9,13},{10,... | collective-permute-start | bytes 294920 | tf_op jit(solution)/shard_map/ppermute | solution.py:569
  511.0 9.0 %collective-permute-start.36 = (bf16[2,64,768]{2,1,0:T(8,128)(2,1)S(1)}, bf16[2,64,768]{2,1,0:T(8,128)(2,1)S(1)}, u32[]{:S(2)}, u32[]{:S(2)}) collective-permute-start(bf16[2,64,768]{2,1,0:T(8,128)(2,1)S(1)} %dynamic-slice_bitcast_fusion.5), channel_id=1, source_target_pairs={{0,2},{1,3},{2,0},{3,1},{4,6},{5,7},{6,4},{7,5},{8,10},{9,11},{10,... | collective-permute-start | bytes 589832 | tf_op jit(solution)/shard_map/ppermute | solution.py:569
  517.6 5.8 %collective-permute-start.40 = (bf16[64,128]{1,0:T(8,128)(2,1)S(1)}, bf16[64,128]{1,0:T(8,128)(2,1)S(1)}, u32[]{:S(2)}, u32[]{:S(2)}) collective-permute-start(bf16[64,128]{1,0:T(8,128)(2,1)S(1)} %dynamic-slice_bitcast_fusion.12), channel_id=1, source_target_pairs={{0,4},{1,5},{2,6},{3,7},{4,0},{5,1},{6,2},{7,3},{8,12},{9,13},{10,... | collective-permute-start | bytes 49160 | tf_op jit(solution)/shard_map/ppermute | solution.py:569
  520.1 6.6 %collective-permute-start.38 = (bf16[64,768]{1,0:T(8,128)(2,1)S(1)}, bf16[64,768]{1,0:T(8,128)(2,1)S(1)}, u32[]{:S(2)}, u32[]{:S(2)}) collective-permute-start(bf16[64,768]{1,0:T(8,128)(2,1)S(1)} %dynamic-slice_bitcast_fusion.8), channel_id=1, source_target_pairs={{0,4},{1,5},{2,6},{3,7},{4,0},{5,1},{6,2},{7,3},{8,12},{9,13},{10,... | collective-permute-start | bytes 294920 | tf_op jit(solution)/shard_map/ppermute | solution.py:569
  526.7 15.8 %collective-permute-start.45 = (bf16[352,512]{1,0:T(8,128)(2,1)}, bf16[352,512]{1,0:T(8,128)(2,1)S(1)}, u32[]{:S(2)}, u32[]{:S(2)}) collective-permute-start(bf16[352,512]{1,0:T(8,128)(2,1)} %reduce-scatter.5.cloned.1.call-done), channel_id=1, source_target_pairs={{0,16},{8,24},{16,0},{24,8},{1,17},{9,25},{17,1},{25,9},{2,18},{10... | collective-permute-start | bytes 1081352 | tf_op jit(solution)/shard_map/ppermute | solution.py:569
  528.0 14.3 %collective-permute-start.42 = (bf16[64,2688]{1,0:T(8,128)(2,1)S(1)}, bf16[64,2688]{1,0:T(8,128)(2,1)S(1)}, u32[]{:S(2)}, u32[]{:S(2)}) collective-permute-start(bf16[64,2688]{1,0:T(8,128)(2,1)S(1)} %pad_maximum_fusion.4), channel_id=1, source_target_pairs={{0,16},{8,24},{16,0},{24,8},{1,17},{9,25},{17,1},{25,9},{2,18},{10... | collective-permute-start | bytes 1032200 | tf_op jit(solution)/shard_map/ppermute | solution.py:569
  529.1 18.8 %collective-permute-start.44 = (bf16[128,2816]{1,0:T(8,128)(2,1)S(1)}, bf16[128,2816]{1,0:T(8,128)(2,1)}, u32[]{:S(2)}, u32[]{:S(2)}) collective-permute-start(bf16[128,2816]{1,0:T(8,128)(2,1)S(1)} %add_convert_fusion.7), channel_id=1, source_target_pairs={{0,8},{8,0},{16,24},{24,16},{1,9},{9,1},{17,25},{25,17},{2,10},{10... | collective-permute-start | bytes 2162696 | tf_op jit(solution)/shard_map/ppermute | solution.py:569
  542.4 9.1 %collective-permute-start.43 = (bf16[128,2688]{1,0:T(8,128)(2,1)S(1)}, bf16[128,2688]{1,0:T(8,128)(2,1)}, u32[]{:S(2)}, u32[]{:S(2)}) collective-permute-start(bf16[128,2688]{1,0:T(8,128)(2,1)S(1)} %maximum_select_fusion.1), channel_id=1, source_target_pairs={{0,8},{8,0},{16,24},{24,16},{1,9},{9,1},{17,25},{25,17},{2,10},{10... | collective-permute-start | bytes 2064392 | tf_op jit(solution)/shard_map/ppermute | solution.py:569
  542.6 2.8 collective-permute-start.46
  (81 other events, 336.7 us)
Sparse Core Ops, SparseCore 0:
  11.5 115.4 all-gather.2
  129.9 76.0 all-gather.4
  310.9 122.8 reduce-scatter.2
  437.3 80.9 reduce-scatter.4

commit v4 on v3

--- a/solution.py
+++ b/solution.py
@@ -8,6 +8,7 @@
 from jax.sharding import PartitionSpec as P
 
 SPAN = 64
+TOGETHER = 8
 EPSILON = 1e-06
 BF = jnp.bfloat16
 F32 = jnp.float32
@@ -23,6 +24,13 @@
 
 def tn(a, b):
     return lax.dot_general(a, b, (((0,), (0,)), ((), ())), preferred_element_type=F32)
+
+
+def in_turn(body, count, together):
+    for start in range(0, count, together):
+        running = [body(h) for h in range(start, min(start + together, count))]
+        while running:
+            running = [one for one in running if next(one, False)]
 
 
 def block_masks(cols_ref, rows_ref, heads):
@@ -47,7 +55,7 @@
 def shifted_rows(x, prev, masks):
     both = jnp.concatenate([prev, x], axis=0)
     lead = prev.shape[0]
-    return [x] + [both[lead - j : lead - j + x.shape[0]] * masks[j - 1] for j in (1, 2, 3)]
+    return [x] + [pltpu.roll(both, j, 0)[lead:] * masks[j - 1] for j in (1, 2, 3)]
 
 
 def mix_rows(rows, taps):
@@ -61,21 +69,35 @@
     return [cols_ref[:, heads + j : heads + j + 1] for j in (1, 2, 3)]
 
 
+def head_parts(heads):
+    return heads - heads // 4, heads // 4
+
+
 def kv_at(heads, d, h):
-    half = heads // 2
-    start = (h // half) * 2 * half * d + (h % half) * d
-    return slice(start, start + d), slice(start + half * d, start + half * d + d)
+    first, other = head_parts(heads)
+    number, start, inside = (first, 0, h) if h < first else (other, 2 * first, h - first)
+    at = (start + inside) * d
+    return slice(at, at + d), slice(at + number * d, at + number * d + d)
 
 
 def summary_kernel(
     heads, d, pre_ref, prev_ref, taps_ref, cols_ref, rows_ref,
-    k_ref, v_ref, w_ref, u_ref, a_ref, x_ref, state,
+    k_ref, v_ref, z_ref, w_ref, u_ref, a_ref, x_ref, state, levels,
 ):
     n = SPAN
     block = pl.program_id(0)
 
     @pl.when(block == 0)
     def _():
+        at = lax.broadcasted_iota(jnp.int32, (n, n), 0)
+        to = lax.broadcasted_iota(jnp.int32, (n, n), 1)
+        for i in range(levels.shape[0]):
+            size = 1 << i
+            level = jnp.logical_and(
+                (at // (2 * size)) == (to // (2 * size)),
+                jnp.logical_and(((at // size) & 1) == 1, ((to // size) & 1) == 0),
+            )
+            levels[i] = level.astype(F32).astype(BF)
         r = lax.broadcasted_iota(jnp.int32, (d, 2 * d), 0)
         c = lax.broadcasted_iota(jnp.int32, (d, 2 * d), 1)
         unit = (r + d == c).astype(F32)
@@ -84,49 +106,57 @@
 
     row, col, same, first, last, keep = block_masks(cols_ref, rows_ref, heads)
     lower = jnp.logical_and(same, row > col)
-    unit = (row == col).astype(F32)
-    pair = jnp.logical_and(row == col + 1, (row & 1) == 1)
+    unit = (row == col).astype(F32).astype(BF)
     masks = lag_masks(cols_ref, heads)
-    keys = []
-    mixing = []
-    inverse = []
-    for h in range(heads):
+    keys, mixing, inverse = ([None] * heads for i in range(3))
+    def features(h):
         cut = slice(h * d, (h + 1) * d)
         at_k, at_v = kv_at(heads, d, h)
         z = mix_rows(shifted_rows(pre_ref[:, at_k], prev_ref[:, at_k], masks), taps_ref[:, at_k])
+        z_ref[:, at_k] = z
+        yield True
         act = z * sigmoid(z)
         root = lax.rsqrt(jnp.sum(act * act, axis=1, keepdims=True) + EPSILON)
-        keys.append((act * root).astype(BF))
+        yield True
+        keys[h] = (act * root).astype(BF)
         k_ref[:, cut] = keys[h]
+        yield True
         z = mix_rows(shifted_rows(pre_ref[:, at_v], prev_ref[:, at_v], masks), taps_ref[:, at_v])
+        z_ref[:, at_v] = z
         v_ref[:, cut] = (z * sigmoid(z)).astype(BF)
-        m = jnp.where(lower, nt(keys[h], keys[h]) * cols_ref[:, h : h + 1], 0.0)
-        mixing.append(m)
-        inverse.append((unit - jnp.where(pair, m, 0.0)).astype(BF))
-    size = 2
-    while size < n:
-        level = jnp.logical_and(
-            (row // (2 * size)) == (col // (2 * size)),
-            jnp.logical_and(((row // size) & 1) == 1, ((col // size) & 1) == 0),
-        )
-        inner = [nn(jnp.where(level, mixing[h], 0.0).astype(BF), inverse[h]).astype(BF) for h in range(heads)]
+        m = jnp.where(lower, nt(keys[h], keys[h]) * cols_ref[:, h : h + 1], 0.0).astype(BF)
+        yield True
+        mixing[h] = m
+        inverse[h] = unit - m * levels[0]
+
+    in_turn(features, heads, TOGETHER)
+    for i in range(1, levels.shape[0]):
+        level = levels[i]
+        inner = [nn(mixing[h] * level, inverse[h]).astype(BF) for h in range(heads)]
         for h in range(heads):
-            inverse[h] = inverse[h] - jnp.where(level, nn(inverse[h], inner[h]), 0.0).astype(BF)
-        size *= 2
-    for h in range(heads):
+            inverse[h] = inverse[h] - nn(inverse[h], inner[h]).astype(BF) * level
+    def advance(h):
         cut = slice(h * d, (h + 1) * d)
         a_ref[h] = inverse[h]
         scaled = (inverse[h].astype(F32) * rows_ref[0, h : h + 1, :]).astype(BF)
+        yield True
         both = nn(scaled, jnp.concatenate([keys[h], v_ref[:, cut]], axis=1))
+        yield True
         w = both[:, :d].astype(BF)
         u = both[:, d:].astype(BF)
         w_ref[:, cut] = w
         u_ref[:, cut] = u
+        yield True
         held = state[h]
         moved = nn(w, held.astype(BF)) * first
+        yield True
         fresh = (jnp.concatenate([u.astype(F32), jnp.zeros((n, d), F32)], axis=1) - moved).astype(BF)
-        key_last = (keys[h].astype(F32) * last).astype(BF)
+        yield True
+        key_last = keys[h] * last.astype(BF)
+        yield True
         state[h] = keep * held + tn(key_last, fresh)
+
+    in_turn(advance, heads, TOGETHER)
 
     @pl.when(block == pl.num_programs(0) - 1)
     def _():
@@ -135,7 +165,7 @@
 
 def forward_kernel(
     heads, d, pre_ref, prev_ref, taps_ref, k_ref, w_ref, u_ref, cols_ref, rows_ref, s_ref, gate_ref, gain_ref,
-    q_ref, y_ref, o_ref, e_ref, kept_ref, state,
+    q_ref, z_ref, y_ref, o_ref, e_ref, kept_ref, state,
 ):
     n = SPAN
     block = pl.program_id(0)
@@ -147,26 +177,37 @@
     row, col, same, first, last, keep = block_masks(cols_ref, rows_ref, heads)
     visible = jnp.logical_and(same, row >= col)
     masks = lag_masks(cols_ref, heads)
-    for h in range(heads):
+    def one_head(h):
         cut = slice(h * d, (h + 1) * d)
         z = mix_rows(shifted_rows(pre_ref[:, cut], prev_ref[:, cut], masks), taps_ref[:, cut])
+        z_ref[:, cut] = z
         q = (z * sigmoid(z) * d ** (-0.5)).astype(BF)
         q_ref[:, cut] = q
+        yield True
         k, w = k_ref[:, cut], w_ref[:, cut]
         held = state[h]
         held_low = held.astype(BF)
         kept_ref[0, h] = held_low
         both = nn(jnp.concatenate([w, q], axis=0), held_low)
+        yield True
         fresh = (u_ref[:, cut].astype(F32) - first * both[:n]).astype(BF)
         e_ref[:, cut] = fresh
+        yield True
         scores = jnp.where(visible, nt(q, k), 0.0).astype(BF)
+        yield True
         out = first * both[n:] + nn(scores, fresh)
-        key_last = (k.astype(F32) * last).astype(BF)
+        yield True
+        key_last = k * last.astype(BF)
         state[h] = keep * held + tn(key_last, fresh)
+        yield True
         o_ref[:, cut] = out
+        yield True
         g = gate_ref[:, cut]
         root = lax.rsqrt(jnp.mean(out * out, axis=1, keepdims=True) + EPSILON)
+        yield True
         y_ref[:, cut] = (out * root * gain_ref[...] * (g * sigmoid(g))).astype(BF)
+
+    in_turn(one_head, heads, TOGETHER)
 
 
 def adjoint_kernel(
@@ -183,13 +224,16 @@
 
     row, col, same, first, last, keep = block_masks(cols_ref, rows_ref, heads)
     visible = jnp.logical_and(same, row >= col)
+    first_low = first.astype(BF)
     gain = gain_ref[...]
     gain_sum = jnp.zeros((1, d), F32)
-    for h in range(heads):
+    def one_head(h):
+        nonlocal gain_sum
         cut = slice(h * d, (h + 1) * d)
         q, k, w = q_ref[:, cut], k_ref[:, cut], w_ref[:, cut]
         o, g, dy = o_ref[:, cut], gate_ref[:, cut], dy_ref[:, cut]
         root = lax.rsqrt(jnp.mean(o * o, axis=1, keepdims=True) + EPSILON)
+        yield True
         unit = o * root
         sig = sigmoid(g)
         m = g * sig
@@ -197,15 +241,22 @@
         gain_sum = gain_sum + jnp.sum(t * unit, axis=0, keepdims=True)
         tg = t * gain
         do = root * (tg - unit * jnp.mean(tg * unit, axis=1, keepdims=True))
+        yield True
         dgate_ref[:, cut] = (dy * gain * unit * (sig * (1.0 + g * (1.0 - sig)))).astype(BF)
         do_low = do.astype(BF)
         do_ref[:, cut] = do_low
+        yield True
         scores = jnp.where(visible, nt(q, k), 0.0).astype(BF)
+        yield True
         later = state[h]
         de = last * nn(k, later.astype(BF)) + tn(scores, do_low)
-        left = jnp.concatenate([q.astype(F32) * first, w.astype(F32) * (-first)], axis=0).astype(BF)
+        yield True
+        left = jnp.concatenate([q * first_low, w * -first_low], axis=0)
         right = jnp.concatenate([do_low, de.astype(BF)], axis=0)
         state[h] = keep * later + tn(left, right)
+        yield True
+
+    in_turn(one_head, heads, TOGETHER)
     dgain_ref[...] += gain_sum
 
     @pl.when(step == pl.num_programs(0) - 1)
@@ -215,12 +266,13 @@
 
 def backward_kernel(
     heads, part, d, q_ref, k_ref, v_ref, w_ref, u_ref, a_ref, e_ref, kept_ref, do_ref, cols_ref, rows_ref, s_ref,
-    qpre_ref, qprev_ref, qtaps_ref, kvpre_ref, kvprev_ref, kvtaps_ref,
+    qz_ref, qpre_ref, qrim_ref, qtaps_ref, kvz_ref, kvpre_ref, kvrim_ref, kvtaps_ref,
     dpre_ref, dbeta_ref, dtaps_ref, state, carry,
 ):
     n = SPAN
     step = pl.program_id(0)
-    number = heads // 2
+    number = head_parts(heads)[part]
+    base = heads - number if part else 0
 
     @pl.when(step == 0)
     def _():
@@ -237,78 +289,98 @@
         masks = lag_masks(cols_ref, heads)
         rate_grads = jnp.zeros((n, d), F32)
 
-        def conv_back(dact, z, sig, rows, taps, at):
+        first_low = first.astype(BF)
+
+        def conv_back(dact, z, sig, pre, taps, at):
             dconv = dact * (sig * (1.0 + z * (1.0 - sig)))
             here = slice(at, at + d)
-            dtaps_ref[:, here] += jnp.concatenate(
-                [jnp.sum(dconv * r, axis=0, keepdims=True) for r in rows], axis=0
-            )
             dpre = dconv * taps[0:1]
+            sums = [jnp.sum(dconv * pre, axis=0, keepdims=True)]
             for j in (1, 2, 3):
                 masked = dconv * masks[j - 1]
                 both = jnp.concatenate([masked, carry[j - 1, :, here]], axis=0)
-                dpre = dpre + both[j : n + j] * taps[j : j + 1]
+                moved = pltpu.roll(both, both.shape[0] - j, 0)[:n]
+                dpre = dpre + moved * taps[j : j + 1]
+                sums.append(jnp.sum(moved * pre, axis=0, keepdims=True))
                 carry[j - 1, :, here] = masked[:8]
+            dtaps_ref[:, here] += jnp.concatenate(sums, axis=0)
             dpre_ref[:, here] = dpre.astype(BF)
 
-        for h in range(number):
+        def one_head(h):
+            nonlocal rate_grads
             cut = slice(h * d, (h + 1) * d)
             cut_v = slice((number + h) * d, (number + h + 1) * d)
             q, k, v, w, u = q_ref[:, cut], k_ref[:, cut], v_ref[:, cut], w_ref[:, cut], u_ref[:, cut]
             do, e, held = do_ref[:, cut], e_ref[:, cut], kept_ref[0, h]
-            at = part * number + h
+            at = base + h
             rate = cols_ref[:, at : at + 1]
             later = state[h]
             later_low = later.astype(BF)
             scores = jnp.where(visible, nt(q, k), 0.0).astype(BF)
+            yield True
             de = last * nn(k, later_low) + tn(scores, do)
+            yield True
             de_low = de.astype(BF)
             dscores = jnp.where(visible, nt(do, e), 0.0).astype(BF)
+            yield True
             both = nt(jnp.concatenate([do, de_low], axis=0), held)
+            yield True
             dq = first * both[:n] + nn(dscores, k)
             dw = -first * both[n:]
             dk = tn(dscores, q) + last * nt(e, later_low)
+            yield True
             pg = tn(a_ref[h], jnp.concatenate([dw.astype(BF), de_low], axis=1))
+            yield True
             p, g = pg[:, :d], pg[:, d:]
             dmix = jnp.where(lower, -nt(pg.astype(BF), jnp.concatenate([w, u], axis=1)), 0.0).astype(BF)
+            yield True
             kf = k.astype(F32)
             drk = p + nn(dmix, k)
             dk = dk + tn(dmix, (kf * rate).astype(BF)) + rate * drk
+            yield True
             dr = jnp.sum(drk * kf + g * v.astype(F32), axis=1, keepdims=True)
             rate_grads = jnp.where(lane == at, dr * rate * (1.0 - rate), rate_grads)
-            left = jnp.concatenate([q.astype(F32) * first, w.astype(F32) * (-first)], axis=0).astype(BF)
+            left = jnp.concatenate([q * first_low, w * -first_low], axis=0)
             right = jnp.concatenate([do, de_low], axis=0)
             state[h] = keep * later + tn(left, right)
-
-            taps = qtaps_ref[:, cut]
-            rows = shifted_rows(qpre_ref[:, cut], qprev_ref[:, cut], masks)
-            z = mix_rows(rows, taps)
-            conv_back(dq * d ** (-0.5), z, sigmoid(z), rows, taps, h * d)
-            taps = kvtaps_ref[:, cut]
-            rows = shifted_rows(kvpre_ref[:, cut], kvprev_ref[:, cut], masks)
-            z = mix_rows(rows, taps)
+            yield True
+
+            z = qz_ref[:, cut]
+            conv_back(dq * d ** (-0.5), z, sigmoid(z), qpre_ref[:, cut], qtaps_ref[:, cut], h * d)
+            yield True
+            z = kvz_ref[:, cut]
             sig = sigmoid(z)
             act = z * sig
             root = lax.rsqrt(jnp.sum(act * act, axis=1, keepdims=True) + EPSILON)
             unit = act * root
             dact = root * (dk - unit * jnp.sum(unit * dk, axis=1, keepdims=True))
-            conv_back(dact, z, sig, rows, taps, (number + h) * d)
-            taps = kvtaps_ref[:, cut_v]
-            rows = shifted_rows(kvpre_ref[:, cut_v], kvprev_ref[:, cut_v], masks)
-            z = mix_rows(rows, taps)
-            conv_back(rate * g, z, sigmoid(z), rows, taps, (2 * number + h) * d)
+            conv_back(dact, z, sig, kvpre_ref[:, cut], kvtaps_ref[:, cut], (number + h) * d)
+            yield True
+            z = kvz_ref[:, cut_v]
+            conv_back(
+                rate * g, z, sigmoid(z), kvpre_ref[:, cut_v], kvtaps_ref[:, cut_v], (2 * number + h) * d
+            )
+
+        in_turn(one_head, number, TOGETHER)
         dbeta_ref[...] = rate_grads
 
     @pl.when(step == pl.num_programs(0) - 1)
     def _():
         wide = number * d
-        for i, taps_ref, at in ((0, qtaps_ref, 0), (1, kvtaps_ref, 0), (2, kvtaps_ref, wide)):
-            here = slice(i * wide, (i + 1) * wide)
+        for i, taps_ref, rim_ref, at in (
+            (0, qtaps_ref, qrim_ref, 0),
+            (1, kvtaps_ref, kvrim_ref, 0),
+            (2, kvtaps_ref, kvrim_ref, wide),
+        ):
+            here, there = slice(i * wide, (i + 1) * wide), slice(at, at + wide)
             dpre = jnp.zeros((8, wide), F32)
+            sums = [jnp.zeros((1, wide), F32)]
             for j in (1, 2, 3):
                 held = carry[j - 1, :, here]
-                both = jnp.concatenate([jnp.zeros_like(held), held], axis=0)
-                dpre = dpre + both[j : 8 + j] * taps_ref[j : j + 1, at : at + wide]
+                moved = jnp.concatenate([jnp.zeros_like(held), held], axis=0)[j : 8 + j]
+                dpre = dpre + moved * taps_ref[j : j + 1, there]
+                sums.append(jnp.sum(moved * rim_ref[:, there], axis=0, keepdims=True))
+            dtaps_ref[:, here] += jnp.concatenate(sums, axis=0)
             dpre_ref[0:8, here] = dpre.astype(BF)
 
 
@@ -358,12 +430,15 @@
 
 
 def shape(dims, kind):
+    return pltpu.HBM(dims, kind)
+
+
+def near(dims, kind):
     return jax.ShapeDtypeStruct(dims, kind)
 
 
-def before_block(blocks, rim, flip, size, column):
-    def index(step):
-        b = blocks - 1 - jnp.minimum(step, blocks - 1) if flip else step
+def before_block(blocks, rim, size, column):
+    def index(b):
         per = SPAN // rim
         return jnp.where(b == 0, blocks * per, b * per - 1), column
 
@@ -380,23 +455,35 @@
         grid=(blocks,),
         in_specs=[
             pl.BlockSpec((SPAN, 2 * width), lambda b: (b, 0)),
-            before_block(blocks, rim, False, 2 * width, 0),
+            before_block(blocks, rim, 2 * width, 0),
             pl.BlockSpec((4, 2 * width), lambda b: (0, 0)),
             c,
             r,
         ],
-        out_specs=[wide, wide, wide, wide, mix, pl.BlockSpec((heads, d, 2 * d), lambda b: (0, 0, 0))],
+        out_specs=[
+            wide,
+            wide,
+            pl.BlockSpec((SPAN, 2 * width), lambda b: (b, 0)),
+            wide,
+            wide,
+            mix,
+            pl.BlockSpec((heads, d, 2 * d), lambda b: (0, 0, 0)),
+        ],
         out_shape=[
             shape((count, width), BF),
             shape((count, width), BF),
+            shape((count, 2 * width), F32),
             shape((count, width), BF),
             shape((count, width), BF),
             shape((heads, count, SPAN), BF),
             shape((heads, d, 2 * d), BF),
         ],
-        scratch_shapes=[pltpu.VMEM((heads, d, 2 * d), F32)],
+        scratch_shapes=[
+            pltpu.VMEM((heads, d, 2 * d), F32),
+            pltpu.VMEM((SPAN.bit_length() - 1, SPAN, SPAN), BF),
+        ],
         compiler_params=params(),
-        cost_estimate=cost(24),
+        cost_estimate=cost(21),
         name="delta_summary",
     )(*in_hbm(pre, pre, taps, cols, rows))
 
@@ -411,7 +498,7 @@
         grid=(blocks,),
         in_specs=[
             wide,
-            before_block(blocks, rim, False, width, 0),
+            before_block(blocks, rim, width, 0),
             pl.BlockSpec((4, width), lambda b: (0, 0)),
             wide,
             wide,
@@ -422,9 +509,10 @@
             pl.BlockSpec((SPAN, width), lambda b: (b, 1)),
             gain,
         ],
-        out_specs=[wide, wide, wide, wide, kept],
+        out_specs=[wide, wide, wide, wide, wide, kept],
         out_shape=[
             shape((count, width), BF),
+            shape((count, width), F32),
             shape((count, width), BF),
             shape((count, width), F32),
             shape((count, width), BF),
@@ -432,7 +520,7 @@
         ],
         scratch_shapes=[pltpu.VMEM((heads, d, d), F32)],
         compiler_params=params(),
-        cost_estimate=cost(16),
+        cost_estimate=cost(11),
         name="delta_forward",
     )(*in_hbm(pre, pre, taps, k, w, u, cols, rows, entry, pre, gain_full))
 
@@ -464,41 +552,44 @@
         ],
         scratch_shapes=[pltpu.VMEM((heads, d, d), F32)],
         compiler_params=params(),
-        cost_estimate=cost(15),
+        cost_estimate=cost(11),
         name="delta_adjoint",
     )(*in_hbm(q, k, w, cols, rows, dy, o, gate, gain_full))
 
 
-def delta_backward(part, q, k, v, w, u, a, e, kept_states, do, cols, rows, later, qg_pre, qtaps, kv_pre, kvtaps, heads):
+def delta_backward(part, q, k, v, w, u, a, e, kept_states, do, cols, rows, later, qz, qg_pre, qtaps, kvz, kv_pre, kvtaps, heads):
     count, width = k.shape
     d, blocks = width // heads, count // SPAN
     rim = kv_pre.shape[0] - count
-    number = heads // 2
+    number = head_parts(heads)[part]
+    part_at = (heads - number) // number if part else 0
     size = number * d
 
     def at(step):
         return blocks - 1 - jnp.minimum(step, blocks - 1)
 
-    wide = pl.BlockSpec((SPAN, size), lambda b: (at(b), part))
+    wide = pl.BlockSpec((SPAN, size), lambda b: (at(b), part_at))
     in_specs = [
         wide,
         wide,
         wide,
         wide,
         wide,
-        pl.BlockSpec((number, SPAN, SPAN), lambda b: (part, at(b), 0)),
+        pl.BlockSpec((number, SPAN, SPAN), lambda b: (part_at, at(b), 0)),
         wide,
-        pl.BlockSpec((1, number, d, d), lambda b: (at(b), part, 0, 0)),
+        pl.BlockSpec((1, number, d, d), lambda b: (at(b), part_at, 0, 0)),
         wide,
         pl.BlockSpec((SPAN, 2 * heads), lambda b: (at(b), 0)),
         pl.BlockSpec((1, 2 * heads, SPAN), lambda b: (at(b), 0, 0)),
-        pl.BlockSpec((number, d, d), lambda b: (part, 0, 0)),
+        pl.BlockSpec((number, d, d), lambda b: (part_at, 0, 0)),
         wide,
-        before_block(blocks, rim, True, size, part),
-        pl.BlockSpec((4, size), lambda b: (0, part)),
-        pl.BlockSpec((SPAN, 2 * size), lambda b: (at(b), part)),
-        before_block(blocks, rim, True, 2 * size, part),
-        pl.BlockSpec((4, 2 * size), lambda b: (0, part)),
+        wide,
+        pl.BlockSpec((rim, size), lambda b: (count // rim, part_at)),
+        pl.BlockSpec((4, size), lambda b: (0, part_at)),
+        pl.BlockSpec((SPAN, 2 * size), lambda b: (at(b), part_at)),
+        pl.BlockSpec((SPAN, 2 * size), lambda b: (at(b), part_at)),
+        pl.BlockSpec((rim, 2 * size), lambda b: (count // rim, part_at)),
+        pl.BlockSpec((4, 2 * size), lambda b: (0, part_at)),
     ]
     return pl.pallas_call(
         partial(backward_kernel, heads, part, d),
@@ -516,9 +607,9 @@
         ],
         scratch_shapes=[pltpu.VMEM((number, d, d), F32), pltpu.VMEM((3, rim, 3 * size), F32)],
         compiler_params=params(),
-        cost_estimate=cost(32),
+        cost_estimate=cost(8 + 2 * number),
         name="delta_backward",
-    )(*in_hbm(q, k, v, w, u, a, e, kept_states, do, cols, rows, later, qg_pre, qg_pre, qtaps, kv_pre, kv_pre, kvtaps))
+    )(*in_hbm(q, k, v, w, u, a, e, kept_states, do, cols, rows, later, qz, qg_pre, qg_pre, qtaps, kvz, kv_pre, kv_pre, kvtaps))
 
 
 def scan_states(x):
@@ -623,7 +714,8 @@
 
     def pile(self):
         if not self.plain:
-            self.have["z"] = jnp.stack([self.have[name] for name in ("", "w", "v", "vw")])
+            last = "u" if "u" in self.have else "vw"
+            self.have["z"] = jnp.stack([self.have[name] for name in ("", "w", "v", last)])
 
     def place(self):
         here, shard, widths = self.here, self.shard, self.widths
@@ -713,6 +805,16 @@
         self.part, self.axes = part, []
         self.go("x", *after)
 
+    def two(self, at):
+        first, second = Reduce(self.here), Reduce(self.here)
+        for one, cut in ((first, slice(0, at)), (second, slice(at, None))):
+            one.part, one.axes = self.part[..., cut], list(self.axes)
+        return first, second
+
+    def join(self, first, second):
+        self.part = jnp.concatenate([first.part, second.part], axis=-1)
+        self.axes, self.split = list(first.axes), True
+
     def both(self):
         self.total = self.part.astype(F32)
         self.got = [self.here.send(self.part, "c")]
@@ -803,8 +905,9 @@
 
 
 def kv_order(array):
-    half = array.shape[1] // 6
-    return [array[:, i * half : (i + 1) * half] for i in (2, 4, 3, 5)]
+    eighth = array.shape[1] // 24
+    starts, sizes = (8, 16, 14, 22), (6, 6, 2, 2)
+    return [array[:, i * eighth : (i + n) * eighth] for i, n in zip(starts, sizes)]
 
 
 def from_behind(value, steps):
@@ -878,7 +981,7 @@
         here,
         jnp.concatenate([qkv_weight[:, :width], gate_weight, out_weight], axis=1),
         [2 * width, width],
-        False,
+        True,
     )
     pair_full = gather_apart(here, jnp.concatenate([ffn_gate, ffn_up], axis=1))
     down_full = gather_apart(here, ffn_down)
@@ -916,7 +1019,7 @@
     kv_pre = jnp.dot(normed_ext, kv_full, preferred_element_type=F32)
     second.move("vw", after=[kv_full])
     second.pile()
-    second.move("zy", after=[kv_pre])
+    second.move("zy", "zx", after=[kv_pre])
     beta_pre = jnp.dot(normed_low, extra_full, preferred_element_type=F32)[:, :heads]
     rates = jax.nn.sigmoid(beta_pre)
     ids = jnp.concatenate([rim_ids, numbers]).astype(F32)
@@ -937,8 +1040,9 @@
         ],
         1,
     )
-    key_low, value_low, w, u, a, moves = delta_summary(kv_pre, kv_taps, cols, rows, heads)
-    second.move("zc", "zyc", after=[moves])
+    key_low, value_low, kv_mixed, w, u, a, moves = delta_summary(kv_pre, kv_taps, cols, rows, heads)
+    second.move("zyx", after=[moves] + second.got("zx"))
+    second.move("zc", "zyc", "zxc", after=[moves])
     fanout = here.nf // heads
     if fanout > 1:
         moves = jnp.concatenate(
@@ -949,12 +1053,13 @@
             axis=2,
         )
     owned = swap(moves)
+    second.move("zyxc", after=[owned])
     qg_full, outw_full = second.place()
     qg_pre = jnp.dot(normed_ext, qg_full, preferred_element_type=F32)
     entry = swap(scan_states(owned))
     if fanout > 1:
         entry = to_heads(entry, fanout)
-    query_low, gated_low, attn_heads, fresh, kept = delta_forward(
+    query_low, q_mixed, gated_low, attn_heads, fresh, kept = delta_forward(
         qg_pre, query_taps, key_low, w, u, cols, rows, entry, outgain_scale, heads
     )
     middle = residual + jnp.dot(gated_low, outw_full, preferred_element_type=F32)
@@ -988,7 +1093,9 @@
     theirs, ours = shares(pair_low, 0, 2 * hidden_units)
     pair_sum = Reduce(here)
     pair_sum.swap(contract(normed_two_low, theirs, 0, 0))
-    gated_grad = hold(gated_grad, down_half, pair_sum.away)
+    pair_half = (contract(normed_two_low, ours, 0, 0) + pair_sum.came.astype(F32)).astype(BF)
+    pair_apart = scatter_owners(pair_half)
+    gated_grad = hold(gated_grad, down_half, pair_half)
     heads_grad, gatepre_low, outgain_grad, local_later = delta_adjoint(
         query_low, key_low, w, cols, rows, gated_grad, attn_heads, qg_pre, outgain_scale, heads
     )
@@ -996,10 +1103,6 @@
         local_later = to_owners(local_later, fanout)
     came_later = swap(local_later)
 
-    ours = hold(ours, local_later)
-    pair_half = (contract(normed_two_low, ours, 0, 0) + pair_sum.came.astype(F32)).astype(BF)
-    pair_apart = scatter_owners(pair_half)
-    came_later = hold(came_later, pair_half)
     summed_later = scan_grads(owned, came_later)
     later = swap(summed_later)
     if fanout > 1:
@@ -1012,32 +1115,37 @@
     output = (middle + jnp.dot(hidden_held, down_full, preferred_element_type=F32)).astype(BF)
     other_sum.take(hold(by_core(here, out_grad, gate_grad), output))
     later = hold(later, other_sum.part)
-    other_sum.go("x")
+    other_x, other_y = other_sum.two(width // 2)
+    other_x.go("x", later)
+    other_y.go("y", later)
     state = (query_low, key_low, value_low, w, u, a, fresh, kept, heads_grad, cols, rows)
     mixed_a, beta_a, taps_a = delta_backward(
-        0, *state, later, qg_pre, query_taps, kv_pre, kv_taps, heads
-    )
-    mixed_a = meet(mixed_a, other_sum)
-    other_sum.go("y")
+        0, *state, later, q_mixed, qg_pre, query_taps, kv_mixed, kv_pre, kv_taps, heads
+    )
+    mixed_a = meet(mixed_a, other_x, other_y)
+    other_x.go("y")
+    other_y.go("x")
     a_sum = Reduce(here)
-    size = 3 * width // 2
-    theirs, ours = shares(mixed_a, 0, size)
+    cut = [number * head_dim for number in head_parts(heads)]
+    theirs, ours = shares(mixed_a, 0, 3 * cut[0])
     a_sum.swap(contract(normed_ext, theirs, 0, 0))
     a_sum.take(contract(normed_ext, ours, 0, 0))
-    later = hold(later, a_sum.part)
-    a_sum.go("x")
+    later = meet(hold(later, a_sum.part), other_x, other_y)
+    other_sum.join(other_x, other_y)
+    a_x, a_y = a_sum.two((a_sum.part.shape[-1] // lanes + 1) // 2 * lanes)
+    a_x.go("x", later)
+    a_y.go("y", later)
+    other_sum.go("w", later)
     mixed_b, beta_b, taps_b = delta_backward(
-        1, *state, later, qg_pre, query_taps, kv_pre, kv_taps, heads
-    )
-    mixed_b = hold(meet(mixed_b, other_sum, a_sum), pair_apart)
-    a_sum.go("y")
-    other_sum.go("w")
-    eighth = width // 2
-
+        1, *state, later, q_mixed, qg_pre, query_taps, kv_mixed, kv_pre, kv_taps, heads
+    )
+    mixed_b = hold(meet(mixed_b, other_sum, a_x, a_y), pair_apart)
     def by_kind(first_heads, other_heads):
-        cut = [slice(i * eighth, (i + 1) * eighth) for i in range(3)]
-        both = [array[:, s] for s in cut for array in (first_heads, other_heads)]
-        return jnp.concatenate(both, axis=1)
+        pieces = []
+        for i in range(3):
+            for array, wide in zip((first_heads, other_heads), cut):
+                pieces.append(array[:, i * wide : (i + 1) * wide])
+        return jnp.concatenate(pieces, axis=1)
 
     betapre_low = (beta_a + beta_b).astype(BF)
     taps_grad = by_kind(taps_a, taps_b)
@@ -1052,18 +1160,21 @@
     small_sum.begin(contract(normed_low, hold(betapre_low, mixed_b), 0, 0) + extra)
     small_sum.both()
     b_sum = Reduce(here)
-    theirs, ours = shares(mixed_b, 0, size)
+    theirs, ours = shares(mixed_b, 0, 3 * cut[1])
     b_sum.swap(contract(normed_ext, theirs, 0, 0))
     b_sum.take(contract(normed_ext, ours, 0, 0))
     small_sum.end()
     mixed_b = hold(mixed_b, b_sum.part, small_sum.part)
     b_sum.go("x")
+    a_x.go("y", mixed_b)
+    a_y.go("x", mixed_b)
+    other_sum.go("v", mixed_b)
     small_sum.go("x")
     wide_grad = (
-        contract(mixed_a[:, eighth:], kv_full[:, :width], 1, 1)
-        + contract(mixed_b[:, eighth:], kv_full[:, width:], 1, 1)
-        + contract(mixed_a[:, :eighth], qg_full[:, :eighth], 1, 1)
-        + contract(mixed_b[:, :eighth], qg_full[:, eighth:width], 1, 1)
+        contract(mixed_a[:, cut[0] :], kv_full[:, : 2 * cut[0]], 1, 1)
+        + contract(mixed_b[:, cut[1] :], kv_full[:, 2 * cut[0] :], 1, 1)
+        + contract(mixed_a[:, : cut[0]], qg_full[:, : cut[0]], 1, 1)
+        + contract(mixed_b[:, : cut[1]], qg_full[:, cut[0] : width], 1, 1)
     )
     rim_grad = from_behind(wide_grad[row_count:].astype(BF), -1).astype(F32)
     normed_grad = (
@@ -1072,47 +1183,48 @@
         + contract(betapre_low, extra_full, 1, 1)
         + contract(gatepre_low, qg_full[:, width:], 1, 1)
     )
-    normed_grad = meet(normed_grad, b_sum, a_sum, other_sum, small_sum)
+    normed_grad = meet(normed_grad, b_sum, a_x, a_y, other_sum, small_sum)
+    a_sum.join(a_x, a_y)
     b_sum.go("y")
     small_sum.go("y")
+    pair_sum.begin_x(pair_apart, normed_grad)
     a_sum.go("w")
-    other_sum.go("v")
     (input_back,) = jax.vjp(partial(rms_norm, gain=attn_scale), residual)[1](normed_grad)
-    input_grad = meet((middle_grad + input_back).astype(BF), b_sum, a_sum, other_sum, small_sum)
+    input_grad = meet(
+        (middle_grad + input_back).astype(BF), b_sum, a_sum, small_sum, pair_sum
+    )
     b_sum.go("w", input_grad)
     a_sum.go("v", input_grad)
     small_sum.go("w", input_grad)
-    pair_sum.begin_x(pair_apart, input_grad)
+    down_sum.begin_x(down_apart, input_grad)
     for one in (b_sum, a_sum, small_sum):
         one.end()
-    b_sum.go("v", a_sum.part)
+    down_sum.end()
+    b_sum.go("v", a_sum.part, down_sum.part)
     small_sum.go("v", a_sum.part)
-    held = meet(a_sum.part, b_sum, small_sum, pair_sum)
-    down_sum.begin_x(down_apart, held)
-    down_sum.end()
+    pair_part, down_part = hold((pair_sum.part, down_sum.part), a_sum.part)
+    other = here.send(pair_part, "c")
+    down_total = join_way(here, down_part, "c", 1).astype(F32)
+    held = meet(a_sum.part, b_sum, small_sum)
     both = Reduce(here)
     both.part = jnp.concatenate([b_sum.part, held, other_sum.part, small_sum.part], axis=1)
     both.split = True
     both.rows()
-    down_total = join_way(here, down_sum.part, "c", 1).astype(F32)
-    other = here.send(pair_sum.part, "c")
-    hidgate_total = by_core(here, pair_sum.part, other).astype(F32)
-    hidup_total = by_core(here, other, pair_sum.part).astype(F32)
+    hidgate_total = by_core(here, pair_part, other).astype(F32)
+    hidup_total = by_core(here, other, pair_part).astype(F32)
     whole = both.other()
-    piece = size // 2
-    ends = [piece, 2 * piece, 2 * piece + width]
+    ends = [0]
+    for one in (b_sum, a_sum, other_sum, small_sum):
+        ends.append(ends[-1] + one.part.shape[1])
 
     def joined(start, end):
         mine, theirs = both.part[:, start:end], whole[:, start:end]
         return by_core(here, mine, theirs), by_core(here, theirs, mine)
 
-    outproj_total, gate_total = [part.astype(F32) for part in joined(ends[1], ends[2])]
-    b_first, b_second = joined(0, ends[0])
-    a_first, a_second = joined(ends[0], ends[1])
-    qkv_total = by_kind(
-        jnp.concatenate([a_first, a_second], axis=1), jnp.concatenate([b_first, b_second], axis=1)
-    ).astype(F32)
-    extra = both.part[:, ends[2] :].astype(F32)
+    b_both, a_both, other_both = [joined(*pair) for pair in zip(ends[:3], ends[1:4])]
+    outproj_total, gate_total = [part.astype(F32) for part in other_both]
+    qkv_total = by_kind(jnp.concatenate(a_both, axis=1), jnp.concatenate(b_both, axis=1)).astype(F32)
+    extra = both.part[:, ends[3] :].astype(F32)
     beta_total = extra[:, :heads]
 
     def gain_grad(gain, pairs):

time: 574 us -> 512 us (0.89)
  Pallas kernels: 138 us -> 88.4 us
  waiting for transfers between devices: 132 us -> 110 us
  matrix products: 110 us -> 118 us
  local copies, waits for them, and re-layouts: 41.7 us -> 34.8 us
  starting transfers between devices: 77.5 us -> 84 us
    pallas_call x2, Pallas kernels: 68.2 us -> 32.3 us  [delta_backward(): pl.pallas_call(partial(backward_kernel, heads, part, d), grid=(blocks + 1...]
    ppermute x44 -> x52, waiting for transfers between devices: 86.3 us -> 72.8 us  [send(): return lax.ppermute(value, axis, pairs)]
    dot_general x20, matrix products: 74.7 us -> 84.4 us  [contract(): lax.dot_general(left, right, (((left_dim,), (right_dim,)), ((), ())), pre...]
    ppermute x44 -> x52, starting transfers between devices: 45.8 us -> 55.3 us  [send(): return lax.ppermute(value, axis, pairs)]
    all_to_all x4, waiting for transfers between devices: 42.6 us -> 33.1 us  [swap(): return lax.all_to_all(value, 'fsdp', 0, 0, tiled=True)]
    unnamed x190 -> x176, local copies, waits for them, and re-layouts: 26 us -> 17.6 us
    pallas_call x1, Pallas kernels: 27.3 us -> 21.5 us  [delta_summary(): pl.pallas_call(partial(summary_kernel, heads, d), grid=(blocks,), in_spec...]
  transfers between devices with their start and end apart: 55 -> 63, of which waited for: 21 -> 20; matrix products, arithmetic and copies ran while one was open for 23% -> 31% of each run, Pallas kernels for 24% -> 18%
where the time goes in v4:
time: 512 us; the launch traced here: 503 us
  matrix products  118 us (23%)
  waiting for transfers between devices  110 us (21%)
  Pallas kernels  88.4 us (17%)
  starting transfers between devices  84 us (16%)
  other arithmetic  51 us (10%)
  local copies, waits for them, and re-layouts  34.8 us (7%)
  between operations  16.1 us (3%)
    dot_general x20, matrix products, contract(): lax.dot_general(left, right, (((left_dim,), (right_dim,)), ((), ())), pre...  84.4 us
    ppermute x52, waiting for transfers between devices, send(): return lax.ppermute(value, axis, pairs)  72.8 us
    ppermute x52, starting transfers between devices, send(): return lax.ppermute(value, axis, pairs)  55.3 us
    all_to_all x4, waiting for transfers between devices, swap(): return lax.all_to_all(value, 'fsdp', 0, 0, tiled=True)  33.1 us
    pallas_call x2, Pallas kernels, delta_backward(): pl.pallas_call(partial(backward_kernel, heads, part, d), grid=(blocks + 1...  32.3 us
    pallas_call x1, Pallas kernels, delta_summary(): pl.pallas_call(partial(summary_kernel, heads, d), grid=(blocks,), in_spec...  21.5 us
    all_to_all x4, starting transfers between devices, swap(): return lax.all_to_all(value, 'fsdp', 0, 0, tiled=True)  20.9 us
    unnamed x176, local copies, waits for them, and re-layouts  17.6 us
  transfers between devices with their start and end apart: 63, of which 20 were waited for; matrix products, arithmetic and copies ran while one was open for 31% of the time, Pallas kernels for 18%

profile of v4, /device:TPU:0, one launch (start us, length us, event | category | flops | bytes accessed | tf_op | source)
XLA Modules:
  0.0 502.7 jit_solution(8104851498098340867)
XLA Ops:
  10.2 4.1 collective-permute-start.1
  16.0 3.4 collective-permute-start.4
  20.1 2.3 collective-permute-start.3
  23.0 6.9 %collective-permute-done.2 = bf16[32,2176]{1,0:T(8,128)(2,1)S(1)} collective-permute-done((bf16[32,2176]{1,0:T(8,128)(2,1)S(1)}, bf16[32,2176]{1,0:T(8,128)(2,1)S(1)}, u32[]{:S(2)}, u32[]{:S(2)}) %collective-permute-start.2) | collective-permute-done | bytes 139296 | tf_op jit(solution)/shard_map/ppermute | solution.py:660
  35.3 4.8 collective-permute-done.5.refs_1_
  40.1 4.2 collective-permute-done.6.refs_2_
  44.3 2.2 collective-permute-start.8
  47.8 2.7 collective-permute-start.13
  50.5 6.0 %collective-permute-start.12 = (bf16[32,3072]{1,0:T(8,128)(2,1)}, bf16[32,3072]{1,0:T(8,128)(2,1)}, u32[]{:S(2)}, u32[]{:S(2)}) collective-permute-start(bf16[32,3072]{1,0:T(8,128)(2,1)} %constant_dynamic-slice_fusion.6), channel_id=1, source_target_pairs={{0,2},{1,3},{2,0},{3,1},{4,6},{5,7},{6,4},{7,5},{8,10},{9,11},{10,... | collective-permute-start | bytes 589832 | tf_op jit(solution)/shard_map/ppermute | solution.py:660
  56.4 7.4 %collective-permute-done.8.refs_4_ = bf16[4,32,2176]{2,1,0:T(8,128)(2,1)} collective-permute-done((bf16[4,32,2176]{2,1,0:T(8,128)(2,1)S(1)}, bf16[4,32,2176]{2,1,0:T(8,128)(2,1)}, u32[]{:S(2)}, u32[]{:S(2)}) %collective-permute-start.8) | collective-permute-done | bytes 557088 | tf_op jit(solution)/shard_map/ppermute | solution.py:660
  69.8 3.4 place_weights.2
  73.2 2.1 copy-done.4
  80.2 6.6 %fusion.99.pre_ref.prev_ref.kvpre_ref.kvrim_ref = f32[520,2048]{1,0:T(8,128)} fusion(bf16[520,1024]{1,0:T(8,128)(2,1)S(1)} %fusion.12, bf16[1024,2048]{1,0:T(8,128)(2,1)} %copy-done.4), kind=kOutput, calls=%fused_computation.238 | convolution fusion | flops 2181038080 | bytes 9519104 | tf_op jit(solution)/shard_map/dot_general | solution.py:1019
  87.4 11.3 %collective-permute-done.14 = bf16[32,3072]{1,0:T(8,128)(2,1)S(1)} collective-permute-done((bf16[32,3072]{1,0:T(8,128)(2,1)}, bf16[32,3072]{1,0:T(8,128)(2,1)S(1)}, u32[]{:S(2)}, u32[]{:S(2)}) %collective-permute-start.14) | collective-permute-done | bytes 196640 | tf_op jit(solution)/shard_map/ppermute | solution.py:660
  100.5 2.4 collective-permute-start.16
  102.9 21.5 %delta_summary.1 = (bf16[512,1024]{1,0:T(8,128)(2,1)}, bf16[512,1024]{1,0:T(8,128)(2,1)}, f32[512,2048]{1,0:T(8,128)}, bf16[512,1024]{1,0:T(8,128)(2,1)}, bf16[5...) custom-call(f32[520,2048]{1,0:T(8,128)} %fusion.99.pre_ref.prev_ref.kvpre_ref.kvrim_ref, ...), custom_call_target="tpu_custom_call" | custom-call | flops 20999999488 | bytes 63000000 | tf_op jit(solution)/shard_map/delta_summary/pallas_call | solution.py:453
  124.4 5.4 %all-to-all-start = ((bf16[8,128,256]{2,1,0:T(8,128)(2,1)}), bf16[8,128,256]{2,1,0:T(8,128)(2,1)S(1)}, u32[]{:S(2)}, u32[]{:S(2)}) async-start(bf16[8,128,256]{2,1,0:T(8,128)(2,1)} %get-tuple-element.115), calls=%async_computation | async-start | bytes 1048576 | tf_op jit(solution)/shard_map/all_to_all | solution.py:932
  130.8 16.3 %all-to-all-done.x_ref.t_ref = bf16[8,128,256]{2,1,0:T(8,128)(2,1)S(1)} async-done(((bf16[8,128,256]{2,1,0:T(8,128)(2,1)}), bf16[8,128,256]{2,1,0:T(8,128)(2,1)S(1)}, u32[]{:S(2)}, u32[]{:S(2)}) %all-to-all-start) | async-done | bytes 524320 | tf_op jit(solution)/shard_map/all_to_all | solution.py:932
  150.3 2.7 state_prefix.1
  153.0 5.5 %all-to-all-start.1 = ((bf16[8,128,128]{2,1,0:T(8,128)(2,1)}), bf16[8,128,128]{2,1,0:T(8,128)(2,1)S(1)}, u32[]{:S(2)}, u32[]{:S(2)}) async-start(bf16[8,128,128]{2,1,0:T(8,128)(2,1)} %state_prefix.1), calls=%async_computation.1 | async-start | bytes 524288 | tf_op jit(solution)/shard_map/all_to_all | solution.py:932
  158.8 4.1 place_weights.3
  166.3 4.5 fusion.100.pre_ref.prev_ref.gate_ref.qpre_ref.qrim_ref
  171.6 10.8 %delta_forward.1 = (bf16[512,1024]{1,0:T(8,128)(2,1)}, f32[512,1024]{1,0:T(8,128)}, bf16[512,1024]{1,0:T(8,128)(2,1)}, f32[512,1024]{1,0:T(8,128)}, bf16[512,102...) custom-call(f32[520,2048]{1,0:T(8,128)} %fusion.100.pre_ref.prev_ref.gate_ref.qpre_ref.qrim_ref, ...), custom_call_target="tpu_custom_call" | custom-call | flops 11000000512 | bytes 33000000 | tf_op jit(solution)/shard_map/delta_forward/pallas_call | solution.py:496
  182.4 2.7 multiply_reduce_fusion.1
  187.6 11.9 %fusion.101 = f32[512,5632]{1,0:T(8,128)} fusion(bf16[512,1024]{1,0:T(8,128)(2,1)} %multiply_convert_fusion.1, bf16[1024,5632]{1,0:T(8,128)(2,1)} %all-gather.3.cloned.1.call-done), kind=kOutput, calls=%fused_computation.240 | convolution fusion | flops 5905580032 | bytes 24117248 | tf_op jit(solution)/shard_map/dot_general | solution.py:1068
  199.6 13.3 %bitcast_multiply_fusion.1 = (f32[512,2816]{1,0:T(8,128)}, f32[512,2816]{1,0:T(8,128)}, bf16[512,2816]{1,0:T(8,128)(2,1)}) fusion(f32[512,5632]{1,0:T(8,128)} %fusion.101, bf16[2816,1024]{1,0:T(8,128)(2,1)} %all-gather.5.cloned.1.call-done, bf16[512,1024]{1,0:T(8,128)(2,1)} %param.27), kind=kOutput, calls=%fused_computation.6 | convolution fusion | flops 2972975104 | bytes 32768000 | tf_op jit(solution)/shard_map/dot_general | solution.py:893
  212.9 7.4 %add_convert_fusion.1 = bf16[512,5632]{1,0:T(8,128)(2,1)} fusion(f32[512,2816]{1,0:T(8,128)} %get-tuple-element.247, f32[512,2816]{1,0:T(8,128)} %get-tuple-element.246), kind=kLoop, calls=%fused_computation.1 | loop fusion | flops 5767168 | bytes 17301504 | tf_op jit(solution)/shard_map/convert_element_type | solution.py:1084
  220.3 7.8 %convolution_convert_fusion = bf16[1024,2816]{1,0:T(8,128)(2,1)} fusion(bf16[512,1024]{1,0:T(8,128)(2,1)} %multiply_convert_fusion.1, bf16[512,5632]{1,0:T(8,128)(2,1)} %add_convert_fusion.1, s32[]{:T(128)S(6)} %select_n.639), kind=kOutput, calls=%fused_computation.11 | convolution fusion | flops 2955673600 | bytes 9699332 | tf_op jit(solution)/shard_map/dot_general | solution.py:893
  229.6 5.4 %convolution_convert_fusion.1 = bf16[2816,512]{1,0:T(8,128)(2,1)} fusion(bf16[512,2816]{1,0:T(8,128)(2,1)} %get-tuple-element.133, bf16[512,1024]{1,0:T(8,128)(2,1)} %param.27, s32[]{:T(128)S(6)} %select_n.637), kind=kOutput, calls=%fused_computation.13 | convolution fusion | flops 1477836800 | bytes 6291460 | tf_op jit(solution)/shard_map/dot_general | solution.py:893
  235.3 2.6 collective-permute-done.23
  237.9 6.8 %add_convert_fusion = bf16[1024,2816]{1,0:T(8,128)(2,1)} fusion(bf16[1024,2816]{1,0:T(8,128)(2,1)} %collective-permute-done.23, bf16[512,1024]{1,0:T(8,128)(2,1)S(1)} %copy-done.47, bf16[512,5632]{1,0:T(8,128)(2,1)S(1)} %bitcast.234, s32[]{:T(128)S(6)} %select_n.638), kind=kOutput, calls=%fused_computation | convolution fusion | flops 2961440768 | bytes 15466500 | tf_op jit(solution)/shard_map/dot_general | solution.py:893
  244.7 11.5 %multiply_reduce_fusion = (f32[512]{0:T(512)S(1)}, f32[512,1024]{1,0:T(8,128)S(1)}) fusion(f32[512,1024]{1,0:T(8,128)} %copy-done.14, f32[1024]{0:T(1024)S(1)} %get-tuple-element.271, bf16[512,5632]{1,0:T(8,128)(2,1)} %add_convert_fusion.1, bf16[1024,5632]{1,0:T(8,128)(2,1)} %all-gather.3.cloned.1.call-done), kind=kOutput, calls=%fused_computation.45 | convolution fusion | flops 5907152384 | bytes 21501952 | tf_op jit(solution)/shard_map/dot_general | solution.py:893
  257.5 2.6 fusion.102.dy_ref
  260.1 5.2 %add_convert_fusion.2 = bf16[2816,512]{1,0:T(8,128)(2,1)} fusion(bf16[2816,512]{1,0:T(8,128)(2,1)} %collective-permute-done.22, bf16[512,2816]{1,0:T(8,128)(2,1)S(1)} %copy-done.78, bf16[512,512]{1,0:T(8,128)(2,1)S(1)} %constant_dynamic-slice_fusion.4), kind=kOutput, calls=%fused_computation.7 | convolution fusion | flops 1480720384 | bytes 9175040 | tf_op jit(solution)/shard_map/dot_general | solution.py:893
  265.3 10.9 %delta_adjoint.1 = (bf16[512,1024]{1,0:T(8,128)(2,1)}, bf16[512,1024]{1,0:T(8,128)(2,1)}, f32[1,128]{1,0:T(1,128)}, bf16[8,128,128]{2,1,0:T(8,128)(2,1)}) custom-call(bf16[512,1024]{1,0:T(8,128)(2,1)} %get-tuple-element.127.q_ref, bf16[512,1024]{1,0:T(8,128)(2,1)} %get-tuple-element.122.k_ref, bf16[512,1024]{1,0:T(8,128)(2,1)} %get-tuple-element.123.w_ref, ...), custom_call_target="tpu_custom_call" | custom-call | flops 11000000512 | bytes 33000000 | tf_op jit(solution)/shard_map/delta_adjoint/pallas_call | solution.py:532
  276.2 5.9 %all-to-all-start.2 = ((bf16[8,128,128]{2,1,0:T(8,128)(2,1)}), bf16[8,128,128]{2,1,0:T(8,128)(2,1)S(1)}, u32[]{:S(2)}, u32[]{:S(2)}) async-start(bf16[8,128,128]{2,1,0:T(8,128)(2,1)} %get-tuple-element.132), calls=%async_computation.2 | async-start | bytes 524288 | tf_op jit(solution)/shard_map/all_to_all | solution.py:932
  282.1 16.8 %all-to-all-done.2.g_ref = bf16[8,128,128]{2,1,0:T(8,128)(2,1)S(1)} async-done(((bf16[8,128,128]{2,1,0:T(8,128)(2,1)}), bf16[8,128,128]{2,1,0:T(8,128)(2,1)S(1)}, u32[]{:S(2)}, u32[]{:S(2)}) %all-to-all-start.2) | async-done | bytes 262176 | tf_op jit(solution)/shard_map/all_to_all | solution.py:932
  299.6 2.8 state_suffix.1
  303.9 3.4 broadcast_select_fusion
  307.4 2.2 select_convert_fusion
  309.5 4.1 all-to-all-start.3
  313.7 7.9 %add_convert_fusion.5 = bf16[512,1024]{1,0:T(8,128)(2,1)} fusion(f32[512,1024]{1,0:T(8,128)S(1)} %copy-done.16, bf16[512,2816]{1,0:T(8,128)(2,1)} %get-tuple-element.133, bf16[2816,1024]{1,0:T(8,128)(2,1)} %all-gather.5.cloned.1.call-done), kind=kOutput, calls=%fused_computation.44 | convolution fusion | flops 2953838592 | bytes 11796480 | tf_op jit(solution)/shard_map/dot_general | solution.py:1115
  321.6 3.8 add_convert_fusion.4
  327.3 2.1 collective-permute-start.26
  329.6 19.1 %delta_backward.2 = (bf16[520,2304]{1,0:T(8,128)(2,1)}, f32[512,128]{1,0:T(8,128)}, f32[4,2304]{1,0:T(4,128)}) custom-call(bf16[512,1024]{1,0:T(8,128)(2,1)} %get-tuple-element.127.q_ref, bf16[512,1024]{1,0:T(8,128)(2,1)} %get-tuple-element.122.k_ref, bf16[512,1024]{1,0:T(8,128)(2,1)} %get-tuple-element.134.v_ref, ...), custom_call_target="tpu_custom_call" | custom-call | flops 20000000000 | bytes 60000000 | tf_op jit(solution)/shard_map/delta_backward/pallas_call | solution.py:594
  348.7 5.0 convolution_convert_fusion.2
  359.8 4.0 fusion.23
  363.7 3.2 fusion.3
  367.0 3.9 add_convert_fusion.3
  371.2 13.2 %delta_backward.3 = (bf16[520,768]{1,0:T(8,128)(2,1)}, f32[512,128]{1,0:T(8,128)}, f32[4,768]{1,0:T(4,128)}) custom-call(bf16[512,1024]{1,0:T(8,128)(2,1)} %get-tuple-element.127.q_ref, bf16[512,1024]{1,0:T(8,128)(2,1)} %get-tuple-element.122.k_ref, bf16[512,1024]{1,0:T(8,128)(2,1)} %get-tuple-element.134.v_ref, bf16[512,1024]{1,0:T(8,128)(2,1)} %get-tuple-element.123.w_ref, ...), custom_call_target="tpu_custom_call" | custom-call | flops 12000000000 | bytes 36000000 | tf_op jit(solution)/shard_map/delta_backward/pallas_call | solution.py:594
  395.0 10.6 %collective-permute-done.30 = bf16[2,64,1024]{2,1,0:T(8,128)(2,1)} collective-permute-done((bf16[2,64,1024]{2,1,0:T(8,128)(2,1)S(1)}, bf16[2,64,1024]{2,1,0:T(8,128)(2,1)}, u32[]{:S(2)}, u32[]{:S(2)}) %collective-permute-start.30) | collective-permute-done | bytes 262176 | tf_op jit(solution)/shard_map/ppermute | solution.py:660
  409.7 2.5 convolution_convert_fusion.3
  424.0 4.0 collective-permute-done.35
  430.6 6.8 %collective-permute-done.36 = bf16[2,2,2,64,384]{4,3,0,1,2:T(8,128)(2,1)S(1)} collective-permute-done((bf16[2,2,2,64,384]{4,3,0,1,2:T(8,128)(2,1)S(1)}, bf16[2,2,2,64,384]{4,3,0,1,2:T(8,128)(2,1)S(1)}, u32[]{:S(2)}, u32[]{:S(2)}) %collective-permute-start.36) | collective-permute-done | bytes 393248 | tf_op jit(solution)/shard_map/ppermute | solution.py:660
  444.3 2.1 fusion.15
  449.0 4.6 collective-permute-done.44
  455.8 2.6 collective-permute-start.46
  459.6 2.1 collective-permute-start.45
  462.5 2.1 collective-permute-done.45
  464.7 2.3 collective-permute-start.50
  469.4 2.8 collective-permute-done.48
  474.9 2.4 fusion.45
  477.4 3.5 collective-permute-done.51
  487.8 3.2 multiply_reduce_fusion.3
  (419 shorter events, 109.3 us)
Async XLA Ops:
  7.2 25.8 %copy-start = (bf16[352,1024]{1,0:T(8,128)(2,1)S(1)}, bf16[352,1024]{1,0:T(8,128)(2,1)}, u32[]{:S(2)}) copy-start(bf16[352,1024]{1,0:T(8,128)(2,1)} %param.26) | copy-start | bytes 2162692
  7.3 180.4 %all-gather.3.cloned.1.call-start = ((), (), s32[]{:S(2)}) async-start(), calls=%async_computation.6 | async-start | bytes 11894784 | tf_op jit(solution)/shard_map/all_gather | solution.py:877
  9.3 190.3 %all-gather.5.cloned.1.call-start = ((), (), s32[]{:S(2)}) async-start(), calls=%async_computation.7 | async-start | bytes 5947392 | tf_op jit(solution)/shard_map/all_gather | solution.py:877
  10.2 12.2 %collective-permute-start.1 = (bf16[32,2176]{1,0:T(8,128)(2,1)S(1)}, bf16[32,2176]{1,0:T(8,128)(2,1)S(1)}, u32[]{:S(2)}, u32[]{:S(2)}) collective-permute-start(bf16[32,2176]{1,0:T(8,128)(2,1)S(1)} %constant_dynamic-slice_fusion.7), channel_id=1, source_target_pairs={{0,4},{1,5},{2,6},{3,7},{4,0},{5,1},{6,2},{7,3},{8,12},{9,13},{10,... | collective-permute-start | bytes 417800 | tf_op jit(solution)/shard_map/ppermute | solution.py:660
  14.3 8.6 %collective-permute-start = (bf16[32,2176]{1,0:T(8,128)(2,1)S(1)}, bf16[32,2176]{1,0:T(8,128)(2,1)S(1)}, u32[]{:S(2)}, u32[]{:S(2)}) collective-permute-start(bf16[32,2176]{1,0:T(8,128)(2,1)S(1)} %constant_dynamic-slice_fusion.7), channel_id=1, source_target_pairs={{0,2},{1,3},{2,0},{3,1},{4,6},{5,7},{6,4},{7,5},{8,10},{9,11},{10,... | collective-permute-start | bytes 417800 | tf_op jit(solution)/shard_map/ppermute | solution.py:660
  16.0 14.0 %collective-permute-start.4 = (s32[8]{0:T(128)S(1)}, s32[8]{0:T(128)S(1)}, u32[]{:S(2)}, u32[]{:S(2)}) collective-permute-start(s32[8]{0:T(128)S(1)} %slice.195), channel_id=1, source_target_pairs={{0,1},{1,2},{2,3},{3,4},{4,5},{5,6},{6,7},{8,9},{9,10},{10,11},{11... | collective-permute-start | bytes 104 | tf_op jit(solution)/shard_map/ppermute | solution.py:916
  20.1 9.9 %collective-permute-start.3 = (bf16[8,1024]{1,0:T(8,128)(2,1)S(1)}, bf16[8,1024]{1,0:T(8,128)(2,1)S(1)}, u32[]{:S(2)}, u32[]{:S(2)}) collective-permute-start(bf16[8,1024]{1,0:T(8,128)(2,1)S(1)} %slice.194), channel_id=1, source_target_pairs={{0,1},{1,2},{2,3},{3,4},{4,5},{5,6},{6,7},{8,9},{9,10},{10,11},{11... | collective-permute-start | bytes 49160 | tf_op jit(solution)/shard_map/ppermute | solution.py:916
  22.4 7.4 %collective-permute-start.2 = (bf16[32,2176]{1,0:T(8,128)(2,1)S(1)}, bf16[32,2176]{1,0:T(8,128)(2,1)S(1)}, u32[]{:S(2)}, u32[]{:S(2)}) collective-permute-start(bf16[32,2176]{1,0:T(8,128)(2,1)S(1)} %collective-permute-done.1), channel_id=1, source_target_pairs={{0,2},{1,3},{2,0},{3,1},{4,6},{5,7},{6,4},{7,5},{8,10},{9,11},{10,... | collective-permute-start | bytes 417800 | tf_op jit(solution)/shard_map/ppermute | solution.py:660
  30.0 10.1 %collective-permute-start.5 = (bf16[4,32,2176]{2,1,0:T(8,128)(2,1)S(1)}, bf16[4,32,2176]{2,1,0:T(8,128)(2,1)S(1)}, u32[]{:S(2)}, u32[]{:S(2)}) collective-permute-start(bf16[4,32,2176]{2,1,0:T(8,128)(2,1)S(1)} %pad_maximum_fusion.4.refs_0_), channel_id=1, source_target_pairs={{0,1},{1,0},{2,3},{3,2},{4,5},{5,4},{6,7},{7,6},{8,9},{9,8},{10,11... | collective-permute-start | bytes 1671176 | tf_op jit(solution)/shard_map/ppermute | solution.py:660
  31.5 12.8 %collective-permute-start.6 = (bf16[4,32,2176]{2,1,0:T(8,128)(2,1)S(1)}, bf16[4,32,2176]{2,1,0:T(8,128)(2,1)}, u32[]{:S(2)}, u32[]{:S(2)}) collective-permute-start(bf16[4,32,2176]{2,1,0:T(8,128)(2,1)S(1)} %pad_maximum_fusion.4.refs_0_), channel_id=1, source_target_pairs={{0,16},{8,24},{16,0},{24,8},{1,17},{9,25},{17,1},{25,9},{2,18},{10... | collective-permute-start | bytes 1671176 | tf_op jit(solution)/shard_map/ppermute | solution.py:660
  33.0 11.3 %collective-permute-start.7 = (bf16[4,32,2176]{2,1,0:T(8,128)(2,1)S(1)}, bf16[4,32,2176]{2,1,0:T(8,128)(2,1)}, u32[]{:S(2)}, u32[]{:S(2)}) collective-permute-start(bf16[4,32,2176]{2,1,0:T(8,128)(2,1)S(1)} %pad_maximum_fusion.4.refs_0_), channel_id=1, source_target_pairs={{0,8},{8,0},{16,24},{24,16},{1,9},{9,1},{17,25},{25,17},{2,10},{10... | collective-permute-start | bytes 1671176 | tf_op jit(solution)/shard_map/ppermute | solution.py:660
  44.3 19.5 %collective-permute-start.8 = (bf16[4,32,2176]{2,1,0:T(8,128)(2,1)S(1)}, bf16[4,32,2176]{2,1,0:T(8,128)(2,1)}, u32[]{:S(2)}, u32[]{:S(2)}) collective-permute-start(bf16[4,32,2176]{2,1,0:T(8,128)(2,1)S(1)} %collective-permute-done.5.refs_1_), channel_id=1, source_target_pairs={{0,16},{8,24},{16,0},{24,8},{1,17},{9,25},{17,1},{25,9},{2,18},{10... | collective-permute-start | bytes 1671176 | tf_op jit(solution)/shard_map/ppermute | solution.py:660
  46.5 17.2 %collective-permute-start.10 = (bf16[4,32,2176]{2,1,0:T(8,128)(2,1)}, bf16[4,32,2176]{2,1,0:T(8,128)(2,1)S(1)}, u32[]{:S(2)}, u32[]{:S(2)}) collective-permute-start(bf16[4,32,2176]{2,1,0:T(8,128)(2,1)} %collective-permute-done.6.refs_2_), channel_id=1, source_target_pairs={{0,8},{8,0},{16,24},{24,16},{1,9},{9,1},{17,25},{25,17},{2,10},{10... | collective-permute-start | bytes 1671176 | tf_op jit(solution)/shard_map/ppermute | solution.py:660
  46.5 18.1 %collective-permute-start.9 = (bf16[4,32,2176]{2,1,0:T(8,128)(2,1)S(1)}, bf16[4,32,2176]{2,1,0:T(8,128)(2,1)S(1)}, u32[]{:S(2)}, u32[]{:S(2)}) collective-permute-start(bf16[4,32,2176]{2,1,0:T(8,128)(2,1)S(1)} %collective-permute-done.5.refs_1_), channel_id=1, source_target_pairs={{0,8},{8,0},{16,24},{24,16},{1,9},{9,1},{17,25},{25,17},{2,10},{10... | collective-permute-start | bytes 1671176 | tf_op jit(solution)/shard_map/ppermute | solution.py:660
  47.8 31.3 %collective-permute-start.13 = (bf16[32,3072]{1,0:T(8,128)(2,1)}, bf16[32,3072]{1,0:T(8,128)(2,1)}, u32[]{:S(2)}, u32[]{:S(2)}) collective-permute-start(bf16[32,3072]{1,0:T(8,128)(2,1)} %constant_dynamic-slice_fusion.6), channel_id=1, source_target_pairs={{0,4},{1,5},{2,6},{3,7},{4,0},{5,1},{6,2},{7,3},{8,12},{9,13},{10,... | collective-permute-start | bytes 589832 | tf_op jit(solution)/shard_map/ppermute | solution.py:660
  50.5 36.9 %collective-permute-start.12 = (bf16[32,3072]{1,0:T(8,128)(2,1)}, bf16[32,3072]{1,0:T(8,128)(2,1)}, u32[]{:S(2)}, u32[]{:S(2)}) collective-permute-start(bf16[32,3072]{1,0:T(8,128)(2,1)} %constant_dynamic-slice_fusion.6), channel_id=1, source_target_pairs={{0,2},{1,3},{2,0},{3,1},{4,6},{5,7},{6,4},{7,5},{8,10},{9,11},{10,... | collective-permute-start | bytes 589832 | tf_op jit(solution)/shard_map/ppermute | solution.py:660
  65.4 2.3 collective-permute-start.11
  79.1 19.7 %collective-permute-start.14 = (bf16[32,3072]{1,0:T(8,128)(2,1)}, bf16[32,3072]{1,0:T(8,128)(2,1)S(1)}, u32[]{:S(2)}, u32[]{:S(2)}) collective-permute-start(bf16[32,3072]{1,0:T(8,128)(2,1)} %collective-permute-done.13), channel_id=1, source_target_pairs={{0,2},{1,3},{2,0},{3,1},{4,6},{5,7},{6,4},{7,5},{8,10},{9,11},{10,... | collective-permute-start | bytes 589832 | tf_op jit(solution)/shard_map/ppermute | solution.py:660
  99.9 29.9 %collective-permute-start.15 = (bf16[4,32,3072]{2,1,0:T(8,128)(2,1)S(1)}, bf16[4,32,3072]{2,1,0:T(8,128)(2,1)S(1)}, u32[]{:S(2)}, u32[]{:S(2)}) collective-permute-start(bf16[4,32,3072]{2,1,0:T(8,128)(2,1)S(1)} %pad_maximum_fusion.2.refs_0_), channel_id=1, source_target_pairs={{0,1},{1,0},{2,3},{3,2},{4,5},{5,4},{6,7},{7,6},{8,9},{9,8},{10,11... | collective-permute-start | bytes 2359304 | tf_op jit(solution)/shard_map/ppermute | solution.py:660
  100.5 29.3 %collective-permute-start.16 = (bf16[4,32,3072]{2,1,0:T(8,128)(2,1)S(1)}, bf16[4,32,3072]{2,1,0:T(8,128)(2,1)}, u32[]{:S(2)}, u32[]{:S(2)}) collective-permute-start(bf16[4,32,3072]{2,1,0:T(8,128)(2,1)S(1)} %pad_maximum_fusion.2.refs_0_), channel_id=1, source_target_pairs={{0,16},{8,24},{16,0},{24,8},{1,17},{9,25},{17,1},{25,9},{2,18},{10... | collective-permute-start | bytes 2359304 | tf_op jit(solution)/shard_map/ppermute | solution.py:660
  124.4 22.7 %all-to-all-start = ((bf16[8,128,256]{2,1,0:T(8,128)(2,1)}), bf16[8,128,256]{2,1,0:T(8,128)(2,1)S(1)}, u32[]{:S(2)}, u32[]{:S(2)}) async-start(bf16[8,128,256]{2,1,0:T(8,128)(2,1)} %get-tuple-element.115), calls=%async_computation | async-start | bytes 1048576 | tf_op jit(solution)/shard_map/all_to_all | solution.py:932
  129.8 19.2 %collective-permute-start.17 = (bf16[4,32,3072]{2,1,0:T(8,128)(2,1)S(1)}, bf16[4,32,3072]{2,1,0:T(8,128)(2,1)}, u32[]{:S(2)}, u32[]{:S(2)}) collective-permute-start(bf16[4,32,3072]{2,1,0:T(8,128)(2,1)S(1)} %collective-permute-done.15.refs_1_), channel_id=1, source_target_pairs={{0,16},{8,24},{16,0},{24,8},{1,17},{9,25},{17,1},{25,9},{2,18},{10... | collective-permute-start | bytes 2359304 | tf_op jit(solution)/shard_map/ppermute | solution.py:660
  130.3 28.5 %collective-permute-start.18 = (bf16[4,32,3072]{2,1,0:T(8,128)(2,1)S(1)}, bf16[4,32,3072]{2,1,0:T(8,128)(2,1)}, u32[]{:S(2)}, u32[]{:S(2)}) collective-permute-start(bf16[4,32,3072]{2,1,0:T(8,128)(2,1)S(1)} %pad_maximum_fusion.2.refs_0_), channel_id=1, source_target_pairs={{0,8},{8,0},{16,24},{24,16},{1,9},{9,1},{17,25},{25,17},{2,10},{10... | collective-permute-start | bytes 2359304 | tf_op jit(solution)/shard_map/ppermute | solution.py:660
  130.3 28.5 %collective-permute-start.20 = (bf16[4,32,3072]{2,1,0:T(8,128)(2,1)}, bf16[4,32,3072]{2,1,0:T(8,128)(2,1)}, u32[]{:S(2)}, u32[]{:S(2)}) collective-permute-start(bf16[4,32,3072]{2,1,0:T(8,128)(2,1)} %collective-permute-done.16.refs_2_), channel_id=1, source_target_pairs={{0,8},{8,0},{16,24},{24,16},{1,9},{9,1},{17,25},{25,17},{2,10},{10... | collective-permute-start | bytes 2359304 | tf_op jit(solution)/shard_map/ppermute | solution.py:660
  130.8 28.0 %collective-permute-start.19 = (bf16[4,32,3072]{2,1,0:T(8,128)(2,1)S(1)}, bf16[4,32,3072]{2,1,0:T(8,128)(2,1)}, u32[]{:S(2)}, u32[]{:S(2)}) collective-permute-start(bf16[4,32,3072]{2,1,0:T(8,128)(2,1)S(1)} %collective-permute-done.15.refs_1_), channel_id=1, source_target_pairs={{0,8},{8,0},{16,24},{24,16},{1,9},{9,1},{17,25},{25,17},{2,10},{10... | collective-permute-start | bytes 2359304 | tf_op jit(solution)/shard_map/ppermute | solution.py:660
  149.0 9.8 %collective-permute-start.21 = (bf16[4,32,3072]{2,1,0:T(8,128)(2,1)}, bf16[4,32,3072]{2,1,0:T(8,128)(2,1)}, u32[]{:S(2)}, u32[]{:S(2)}) collective-permute-start(bf16[4,32,3072]{2,1,0:T(8,128)(2,1)} %collective-permute-done.17.refs_3_), channel_id=1, source_target_pairs={{0,8},{8,0},{16,24},{24,16},{1,9},{9,1},{17,25},{25,17},{2,10},{10... | collective-permute-start | bytes 2359304 | tf_op jit(solution)/shard_map/ppermute | solution.py:660
  153.0 17.9 %all-to-all-start.1 = ((bf16[8,128,128]{2,1,0:T(8,128)(2,1)}), bf16[8,128,128]{2,1,0:T(8,128)(2,1)S(1)}, u32[]{:S(2)}, u32[]{:S(2)}) async-start(bf16[8,128,128]{2,1,0:T(8,128)(2,1)} %state_prefix.1), calls=%async_computation.1 | async-start | bytes 524288 | tf_op jit(solution)/shard_map/all_to_all | solution.py:932
  158.5 249.2 %reduce-scatter.3.cloned.1.call-start = ((), (), s32[]{:S(2)}) async-start(), calls=%async_computation.8 | async-start | bytes 6488064 | tf_op jit(solution)/shard_map/reduce_scatter | solution.py:881
  228.1 9.8 %collective-permute-start.23 = (bf16[1024,2816]{1,0:T(8,128)(2,1)}, bf16[1024,2816]{1,0:T(8,128)(2,1)}, u32[]{:S(2)}, u32[]{:S(2)}) collective-permute-start(bf16[1024,2816]{1,0:T(8,128)(2,1)} %convolution_convert_fusion), channel_id=1, source_target_pairs={{0,8},{8,0},{16,24},{24,16},{1,9},{9,1},{17,25},{25,17},{2,10},{10... | collective-permute-start | bytes 17301512 | tf_op jit(solution)/shard_map/ppermute | solution.py:660
  235.1 25.1 %collective-permute-start.22 = (bf16[2816,512]{1,0:T(8,128)(2,1)}, bf16[2816,512]{1,0:T(8,128)(2,1)}, u32[]{:S(2)}, u32[]{:S(2)}) collective-permute-start(bf16[2816,512]{1,0:T(8,128)(2,1)} %convolution_convert_fusion.1), channel_id=1, source_target_pairs={{0,8},{8,0},{16,24},{24,16},{1,9},{9,1},{17,25},{25,17},{2,10},{10... | collective-permute-start | bytes 8650760 | tf_op jit(solution)/shard_map/ppermute | solution.py:660
  276.2 22.7 %all-to-all-start.2 = ((bf16[8,128,128]{2,1,0:T(8,128)(2,1)}), bf16[8,128,128]{2,1,0:T(8,128)(2,1)S(1)}, u32[]{:S(2)}, u32[]{:S(2)}) async-start(bf16[8,128,128]{2,1,0:T(8,128)(2,1)} %get-tuple-element.132), calls=%async_computation.2 | async-start | bytes 524288 | tf_op jit(solution)/shard_map/all_to_all | solution.py:932
  309.5 12.1 %collective-permute-start.24 = (bf16[1024,1024]{1,0:T(8,128)(2,1)}, bf16[1024,1024]{1,0:T(8,128)(2,1)}, u32[]{:S(2)}, u32[]{:S(2)}) collective-permute-start(bf16[1024,1024]{1,0:T(8,128)(2,1)} %select_convert_fusion), channel_id=1, source_target_pairs={{0,8},{8,0},{16,24},{24,16},{1,9},{9,1},{17,25},{25,17},{2,10},{10... | collective-permute-start | bytes 6291464 | tf_op jit(solution)/shard_map/ppermute | solution.py:660
  309.5 15.8 %all-to-all-start.3 = ((bf16[8,128,128]{2,1,0:T(8,128)(2,1)}), bf16[8,128,128]{2,1,0:T(8,128)(2,1)S(1)}, u32[]{:S(2)}, u32[]{:S(2)}) async-start(bf16[8,128,128]{2,1,0:T(8,128)(2,1)} %state_suffix.1), calls=%async_computation.3 | async-start | bytes 524288 | tf_op jit(solution)/shard_map/all_to_all | solution.py:932
  313.6 139.9 %reduce-scatter.5.cloned.1.call-start = ((), (), s32[]{:S(2)}) async-start(), calls=%async_computation.9 | async-start | bytes 3244032 | tf_op jit(solution)/shard_map/reduce_scatter | solution.py:881
  327.3 21.4 %collective-permute-start.26 = (bf16[2,2,128,512]{3,2,1,0:T(8,128)(2,1)S(1)}, bf16[2,2,128,512]{3,2,1,0:T(8,128)(2,1)S(1)}, u32[]{:S(2)}, u32[]{:S(2)}) collective-permute-start(bf16[2,2,128,512]{3,2,1,0:T(8,128)(2,1)S(1)} %dynamic-slice_bitcast_fusion.2), channel_id=1, source_target_pairs={{0,1},{1,0},{2,3},{3,2},{4,5},{5,4},{6,7},{7,6},{8,9},{9,8},{10,11... | collective-permute-start | bytes 1572872 | tf_op jit(solution)/shard_map/ppermute | solution.py:660
  329.5 19.2 %collective-permute-start.25 = (bf16[2,2,2,64,512]{4,3,2,1,0:T(8,128)(2,1)S(1)}, bf16[2,2,2,64,512]{4,3,2,1,0:T(8,128)(2,1)S(1)}, u32[]{:S(2)}, u32[]{:S(2)}) collective-permute-start(bf16[2,2,2,64,512]{4,3,2,1,0:T(8,128)(2,1)S(1)} %dynamic-slice_bitcast_fusion.3), channel_id=1, source_target_pairs={{0,16},{8,24},{16,0},{24,8},{1,17},{9,25},{17,1},{25,9},{2,18},{10... | collective-permute-start | bytes 1572872 | tf_op jit(solution)/shard_map/ppermute | solution.py:660
  353.7 13.3 %collective-permute-start.27 = (bf16[1024,1152]{1,0:T(8,128)(2,1)}, bf16[1024,1152]{1,0:T(8,128)(2,1)}, u32[]{:S(2)}, u32[]{:S(2)}) collective-permute-start(bf16[1024,1152]{1,0:T(8,128)(2,1)} %convolution_convert_fusion.2), channel_id=1, source_target_pairs={{0,8},{8,0},{16,24},{24,16},{1,9},{9,1},{17,25},{25,17},{2,10},{10... | collective-permute-start | bytes 7077896 | tf_op jit(solution)/shard_map/ppermute | solution.py:660
  356.5 14.7 %collective-permute-start.29 = (bf16[2,2,64,512]{3,2,1,0:T(8,128)(2,1)S(1)}, bf16[2,2,64,512]{3,2,1,0:T(8,128)(2,1)S(1)}, u32[]{:S(2)}, u32[]{:S(2)}) collective-permute-start(bf16[2,2,64,512]{3,2,1,0:T(8,128)(2,1)S(1)} %dynamic-slice_bitcast_fusion.8), channel_id=1, source_target_pairs={{0,16},{8,24},{16,0},{24,8},{1,17},{9,25},{17,1},{25,9},{2,18},{10... | collective-permute-start | bytes 786440 | tf_op jit(solution)/shard_map/ppermute | solution.py:660
  359.7 11.5 %collective-permute-start.28 = (bf16[2,2,64,512]{3,2,1,0:T(8,128)(2,1)S(1)}, bf16[2,2,64,512]{3,2,1,0:T(8,128)(2,1)S(1)}, u32[]{:S(2)}, u32[]{:S(2)}) collective-permute-start(bf16[2,2,64,512]{3,2,1,0:T(8,128)(2,1)S(1)} %dynamic-slice_bitcast_fusion.9), channel_id=1, source_target_pairs={{0,1},{1,0},{2,3},{3,2},{4,5},{5,4},{6,7},{7,6},{8,9},{9,8},{10,11... | collective-permute-start | bytes 786440 | tf_op jit(solution)/shard_map/ppermute | solution.py:660
  385.2 20.4 %collective-permute-start.32 = (bf16[2,2,128,512]{3,2,1,0:T(8,128)(2,1)}, bf16[2,2,128,512]{3,2,1,0:T(8,128)(2,1)}, u32[]{:S(2)}, u32[]{:S(2)}) collective-permute-start(bf16[2,2,128,512]{3,2,1,0:T(8,128)(2,1)} %dynamic-slice_bitcast_fusion.1), channel_id=1, source_target_pairs={{0,1},{1,0},{2,3},{3,2},{4,5},{5,4},{6,7},{7,6},{8,9},{9,8},{10,11... | collective-permute-start | bytes 1572872 | tf_op jit(solution)/shard_map/ppermute | solution.py:660
  388.0 17.6 %collective-permute-start.31 = (bf16[2,2,2,64,640]{4,3,2,1,0:T(8,128)(2,1)}, bf16[2,2,2,64,640]{4,3,2,1,0:T(8,128)(2,1)S(1)}, u32[]{:S(2)}, u32[]{:S(2)}) collective-permute-start(bf16[2,2,2,64,640]{4,3,2,1,0:T(8,128)(2,1)} %dynamic-slice_bitcast_fusion), channel_id=1, source_target_pairs={{0,16},{8,24},{16,0},{24,8},{1,17},{9,25},{17,1},{25,9},{2,18},{10... | collective-permute-start | bytes 1966088 | tf_op jit(solution)/shard_map/ppermute | solution.py:660
  389.2 16.3 %collective-permute-start.30 = (bf16[2,64,1024]{2,1,0:T(8,128)(2,1)S(1)}, bf16[2,64,1024]{2,1,0:T(8,128)(2,1)}, u32[]{:S(2)}, u32[]{:S(2)}) collective-permute-start(bf16[2,64,1024]{2,1,0:T(8,128)(2,1)S(1)} %dynamic-slice_bitcast_fusion.7), channel_id=1, source_target_pairs={{0,2},{1,3},{2,0},{3,1},{4,6},{5,7},{6,4},{7,5},{8,10},{9,11},{10,... | collective-permute-start | bytes 786440 | tf_op jit(solution)/shard_map/ppermute | solution.py:660
  409.7 4.4 collective-permute-start.34
  412.2 2.9 collective-permute-start.33
  414.2 16.4 %collective-permute-start.40 = (bf16[2,2,2,64,128]{4,3,0,1,2:T(8,128)(2,1)S(1)}, bf16[2,2,2,64,128]{4,3,0,1,2:T(8,128)(2,1)S(1)}, u32[]{:S(2)}, u32[]{:S(2)}) collective-permute-start(bf16[2,2,2,64,128]{4,3,0,1,2:T(8,128)(2,1)S(1)} %bitcast.258), channel_id=1, source_target_pairs={{0,16},{8,24},{16,0},{24,8},{1,17},{9,25},{17,1},{25,9},{2,18},{10... | collective-permute-start | bytes 393224 | tf_op jit(solution)/shard_map/ppermute | solution.py:660
  416.2 14.4 %collective-permute-start.39 = (bf16[64,1024]{1,0:T(8,128)(2,1)S(1)}, bf16[64,1024]{1,0:T(8,128)(2,1)S(1)}, u32[]{:S(2)}, u32[]{:S(2)}) collective-permute-start(bf16[64,1024]{1,0:T(8,128)(2,1)S(1)} %dynamic-slice_bitcast_fusion.12), channel_id=1, source_target_pairs={{0,4},{1,5},{2,6},{3,7},{4,0},{5,1},{6,2},{7,3},{8,12},{9,13},{10,... | collective-permute-start | bytes 393224 | tf_op jit(solution)/shard_map/ppermute | solution.py:660
  417.2 13.4 %collective-permute-start.38 = (bf16[2,2,64,512]{3,2,1,0:T(8,128)(2,1)S(1)}, bf16[2,2,64,512]{3,2,1,0:T(8,128)(2,1)S(1)}, u32[]{:S(2)}, u32[]{:S(2)}) collective-permute-start(bf16[2,2,64,512]{3,2,1,0:T(8,128)(2,1)S(1)} %dynamic-slice_bitcast_fusion.6), channel_id=1, source_target_pairs={{0,16},{8,24},{16,0},{24,8},{1,17},{9,25},{17,1},{25,9},{2,18},{10... | collective-permute-start | bytes 786440 | tf_op jit(solution)/shard_map/ppermute | solution.py:660
  418.7 12.0 %collective-permute-start.37 = (bf16[2,2,64,640]{3,2,1,0:T(8,128)(2,1)S(1)}, bf16[2,2,64,640]{3,2,1,0:T(8,128)(2,1)S(1)}, u32[]{:S(2)}, u32[]{:S(2)}) collective-permute-start(bf16[2,2,64,640]{3,2,1,0:T(8,128)(2,1)S(1)} %dynamic-slice_bitcast_fusion.4), channel_id=1, source_target_pairs={{0,1},{1,0},{2,3},{3,2},{4,5},{5,4},{6,7},{7,6},{8,9},{9,8},{10,11... | collective-permute-start | bytes 983048 | tf_op jit(solution)/shard_map/ppermute | solution.py:660
  422.1 5.9 %collective-permute-start.35 = (bf16[8,1024]{1,0:T(8,128)(2,1)S(1)}, bf16[8,1024]{1,0:T(8,128)(2,1)S(1)}, u32[]{:S(2)}, u32[]{:S(2)}) collective-permute-start(bf16[8,1024]{1,0:T(8,128)(2,1)S(1)} %slice.371), channel_id=1, source_target_pairs={{1,0},{2,1},{3,2},{4,3},{5,4},{6,5},{7,6},{9,8},{10,9},{11,10},{12... | collective-permute-start | bytes 49160 | tf_op jit(solution)/shard_map/ppermute | solution.py:916
  428.0 9.4 %collective-permute-start.36 = (bf16[2,2,2,64,384]{4,3,0,1,2:T(8,128)(2,1)S(1)}, bf16[2,2,2,64,384]{4,3,0,1,2:T(8,128)(2,1)S(1)}, u32[]{:S(2)}, u32[]{:S(2)}) collective-permute-start(bf16[2,2,2,64,384]{4,3,0,1,2:T(8,128)(2,1)S(1)} %bitcast.247), channel_id=1, source_target_pairs={{0,16},{8,24},{16,0},{24,8},{1,17},{9,25},{17,1},{25,9},{2,18},{10... | collective-permute-start | bytes 1179656 | tf_op jit(solution)/shard_map/ppermute | solution.py:660
  437.4 16.1 %collective-permute-start.44 = (bf16[128,2816]{1,0:T(8,128)(2,1)S(1)}, bf16[128,2816]{1,0:T(8,128)(2,1)}, u32[]{:S(2)}, u32[]{:S(2)}) collective-permute-start(bf16[128,2816]{1,0:T(8,128)(2,1)S(1)} %copy-done.52), channel_id=1, source_target_pairs={{0,16},{8,24},{16,0},{24,8},{1,17},{9,25},{17,1},{25,9},{2,18},{10... | collective-permute-start | bytes 2162696 | tf_op jit(solution)/shard_map/ppermute | solution.py:660
  438.7 7.7 %collective-permute-start.43 = (bf16[2,2,64,128]{3,2,0,1:T(8,128)(2,1)S(1)}, bf16[2,2,64,128]{3,2,0,1:T(8,128)(2,1)S(1)}, u32[]{:S(2)}, u32[]{:S(2)}) collective-permute-start(bf16[2,2,64,128]{3,2,0,1:T(8,128)(2,1)S(1)} %dynamic-slice_bitcast_fusion.14), channel_id=1, source_target_pairs={{0,1},{1,0},{2,3},{3,2},{4,5},{5,4},{6,7},{7,6},{8,9},{9,8},{10,11... | collective-permute-start | bytes 196616 | tf_op jit(solution)/shard_map/ppermute | solution.py:660
  440.7 7.6 %collective-permute-start.42 = (bf16[2,64,1152]{2,1,0:T(8,128)(2,1)S(1)}, bf16[2,64,1152]{2,1,0:T(8,128)(2,1)}, u32[]{:S(2)}, u32[]{:S(2)}) collective-permute-start(bf16[2,64,1152]{2,1,0:T(8,128)(2,1)S(1)} %dynamic-slice_bitcast_fusion.5), channel_id=1, source_target_pairs={{0,2},{1,3},{2,0},{3,1},{4,6},{5,7},{6,4},{7,5},{8,10},{9,11},{10,... | collective-permute-start | bytes 884744 | tf_op jit(solution)/shard_map/ppermute | solution.py:660
  442.5 5.7 %collective-permute-start.41 = (bf16[2,2,64,384]{3,2,0,1:T(8,128)(2,1)S(1)}, bf16[2,2,64,384]{3,2,0,1:T(8,128)(2,1)S(1)}, u32[]{:S(2)}, u32[]{:S(2)}) collective-permute-start(bf16[2,2,64,384]{3,2,0,1:T(8,128)(2,1)S(1)} %dynamic-slice_bitcast_fusion.10), channel_id=1, source_target_pairs={{0,1},{1,0},{2,3},{3,2},{4,5},{5,4},{6,7},{7,6},{8,9},{9,8},{10,11... | collective-permute-start | bytes 589832 | tf_op jit(solution)/shard_map/ppermute | solution.py:660
  453.5 13.5 %collective-permute-start.47 = (bf16[352,512]{1,0:T(8,128)(2,1)}, bf16[352,512]{1,0:T(8,128)(2,1)S(1)}, u32[]{:S(2)}, u32[]{:S(2)}) collective-permute-start(bf16[352,512]{1,0:T(8,128)(2,1)} %reduce-scatter.5.cloned.1.call-done), channel_id=1, source_target_pairs={{0,16},{8,24},{16,0},{24,8},{1,17},{9,25},{17,1},{25,9},{2,18},{10... | collective-permute-start | bytes 1081352 | tf_op jit(solution)/shard_map/ppermute | solution.py:660
  455.8 8.8 %collective-permute-start.46 = (bf16[64,1152]{1,0:T(8,128)(2,1)S(1)}, bf16[64,1152]{1,0:T(8,128)(2,1)S(1)}, u32[]{:S(2)}, u32[]{:S(2)}) collective-permute-start(bf16[64,1152]{1,0:T(8,128)(2,1)S(1)} %dynamic-slice_bitcast_fusion.11), channel_id=1, source_target_pairs={{0,4},{1,5},{2,6},{3,7},{4,0},{5,1},{6,2},{7,3},{8,12},{9,13},{10,... | collective-permute-start | bytes 442376 | tf_op jit(solution)/shard_map/ppermute | solution.py:660
  458.5 4.0 collective-permute-start.49
  459.6 5.0 collective-permute-start.45
  464.7 4.7 collective-permute-start.50
  467.2 5.1 %collective-permute-start.48 = (bf16[64,384]{1,0:T(8,128)(2,1)S(1)}, bf16[64,384]{1,0:T(8,128)(2,1)S(1)}, u32[]{:S(2)}, u32[]{:S(2)}) collective-permute-start(bf16[64,384]{1,0:T(8,128)(2,1)S(1)} %dynamic-slice_bitcast_fusion.15), channel_id=1, source_target_pairs={{0,4},{1,5},{2,6},{3,7},{4,0},{5,1},{6,2},{7,3},{8,12},{9,13},{10,... | collective-permute-start | bytes 147464 | tf_op jit(solution)/shard_map/ppermute | solution.py:660
  469.2 5.7 %collective-permute-start.54 = (bf16[352,512]{1,0:T(8,128)(2,1)S(1)}, bf16[352,512]{1,0:T(8,128)(2,1)}, u32[]{:S(2)}, u32[]{:S(2)}) collective-permute-start(bf16[352,512]{1,0:T(8,128)(2,1)S(1)} %add_convert_fusion.8), channel_id=1, source_target_pairs={{0,8},{8,0},{16,24},{24,16},{1,9},{9,1},{17,25},{25,17},{2,10},{10... | collective-permute-start | bytes 1081352 | tf_op jit(solution)/shard_map/ppermute | solution.py:660
  473.0 7.8 %collective-permute-start.51 = (bf16[64,2688]{1,0:T(8,128)(2,1)}, bf16[64,2688]{1,0:T(8,128)(2,1)}, u32[]{:S(2)}, u32[]{:S(2)}) collective-permute-start(bf16[64,2688]{1,0:T(8,128)(2,1)} %pad_maximum_fusion.6), channel_id=1, source_target_pairs={{0,16},{8,24},{16,0},{24,8},{1,17},{9,25},{17,1},{25,9},{2,18},{10... | collective-permute-start | bytes 1032200 | tf_op jit(solution)/shard_map/ppermute | solution.py:660
  474.9 12.9 %collective-permute-start.53 = (bf16[128,2816]{1,0:T(8,128)(2,1)S(1)}, bf16[128,2816]{1,0:T(8,128)(2,1)}, u32[]{:S(2)}, u32[]{:S(2)}) collective-permute-start(bf16[128,2816]{1,0:T(8,128)(2,1)S(1)} %add_convert_fusion.7), channel_id=1, source_target_pairs={{0,8},{8,0},{16,24},{24,16},{1,9},{9,1},{17,25},{25,17},{2,10},{10... | collective-permute-start | bytes 2162696 | tf_op jit(solution)/shard_map/ppermute | solution.py:660
  482.1 9.4 %collective-permute-start.52 = (bf16[128,2688]{1,0:T(8,128)(2,1)S(1)}, bf16[128,2688]{1,0:T(8,128)(2,1)S(1)}, u32[]{:S(2)}, u32[]{:S(2)}) collective-permute-start(bf16[128,2688]{1,0:T(8,128)(2,1)S(1)} %maximum_select_fusion.1), channel_id=1, source_target_pairs={{0,8},{8,0},{16,24},{24,16},{1,9},{9,1},{17,25},{25,17},{2,10},{10... | collective-permute-start | bytes 2064392 | tf_op jit(solution)/shard_map/ppermute | solution.py:660
  (82 other events, 461.9 us)
Sparse Core Ops, SparseCore 0:
  11.5 105.0 all-gather.2
  119.4 72.3 all-gather.4
  244.8 119.0 reduce-scatter.2
  367.3 75.6 reduce-scatter.4

commit v5 on v4

--- a/solution.py
+++ b/solution.py
@@ -612,6 +612,108 @@
     )(*in_hbm(q, k, v, w, u, a, e, kept_states, do, cols, rows, later, qz, qg_pre, qg_pre, qtaps, kvz, kv_pre, kv_pre, kvtaps))
 
 
+def feed_kernel(
+    n_ref, e_ref, mid_ref, g_ref, u_ref, d_ref, gb_ref, ub_ref, db_ref,
+    f_ref, pair_ref, out_ref, dn_ref, total, held,
+):
+    step = pl.program_id(0)
+    last = pl.num_programs(0) - 1
+    wide = g_ref.shape[1]
+
+    @pl.when(step == 0)
+    def _():
+        dn_ref[...] = jnp.zeros_like(dn_ref)
+        total[...] = mid_ref[...]
+
+    slot, other = step % 2, 1 - step % 2
+
+    def first(i):
+        gate = nn(n_ref[...], g_ref[...])
+        yield True
+        up = nn(n_ref[...], u_ref[...])
+        yield True
+        df = nt(e_ref[...], d_ref[...])
+        yield True
+        sig = sigmoid(gate)
+        act = gate * sig
+        f = (act * up).astype(BF)
+        dgate = (df * up * (sig * (1.0 + gate * (1.0 - sig)))).astype(BF)
+        dup = (df * act).astype(BF)
+        f_ref[...] = f
+        pair_ref[0] = dgate
+        pair_ref[1] = dup
+        held[slot, :, 0:wide] = f
+        held[slot, :, wide : 2 * wide] = dgate
+        held[slot, :, 2 * wide :] = dup
+        yield True
+
+    def second(i):
+        total[...] += nn(held[other, :, 0:wide], db_ref[...])
+        yield True
+        both_w = jnp.concatenate([gb_ref[...], ub_ref[...]], axis=1)
+        dn_ref[...] += nt(held[other, :, wide:], both_w)
+        yield True
+
+    def both(i):
+        running = [first(i), second(i)]
+        while running:
+            running = [one for one in running if next(one, False)]
+            yield True
+
+    @pl.when(step == 0)
+    def _():
+        in_turn(first, 1, 1)
+
+    @pl.when(jnp.logical_and(step > 0, step < last))
+    def _():
+        in_turn(both, 1, 1)
+
+    @pl.when(step == last)
+    def _():
+        in_turn(second, 1, 1)
+        out_ref[...] = total[...].astype(BF)
+
+
+def feed_forward(normed, cotangent, middle, pair, down):
+    count, width = normed.shape
+    hidden = down.shape[0]
+    wide = 2 * 128
+    blocks = hidden // wide
+    whole = pl.BlockSpec((count, width), lambda i: (0, 0))
+    now = lambda i: jnp.minimum(i, blocks - 1)
+    past = lambda i: jnp.maximum(i - 1, 0)
+    weights = []
+    for at in (now, past):
+        weights += [
+            pl.BlockSpec((width, wide), lambda i, at=at: (0, at(i))),
+            pl.BlockSpec((width, wide), lambda i, at=at: (0, blocks + at(i))),
+            pl.BlockSpec((wide, width), lambda i, at=at: (at(i), 0)),
+        ]
+    return pl.pallas_call(
+        feed_kernel,
+        grid=(blocks + 1,),
+        in_specs=[whole, whole, whole] + weights,
+        out_specs=[
+            pl.BlockSpec((count, wide), lambda i: (0, now(i))),
+            pl.BlockSpec((2, count, wide), lambda i: (0, 0, now(i))),
+            whole,
+            whole,
+        ],
+        out_shape=[
+            shape((count, hidden), BF),
+            shape((2, count, hidden), BF),
+            shape((count, width), BF),
+            shape((count, width), F32),
+        ],
+        scratch_shapes=[pltpu.VMEM((count, width), F32), pltpu.VMEM((2, count, 3 * wide), BF)],
+        compiler_params=pltpu.CompilerParams(
+            dimension_semantics=("arbitrary",), vmem_limit_bytes=40 * 1024 * 1024
+        ),
+        cost_estimate=cost(25),
+        name="feed_forward",
+    )(*in_hbm(normed, cotangent, middle, pair, pair, down, pair, pair, down))
+
+
 def scan_states(x):
     peers, d, width = x.shape
     return pl.pallas_call(
@@ -783,23 +885,24 @@
         number, mine = here.number[way], here.mine[way]
         if way in "xc" and not self.axes:
             self.total = part.astype(F32)
-            self.got = [here.send(part, way, s) for s in range(1, number)]
-            return
-        if way == "x":
-            axis = len(self.axes)
-            shape = part.shape
-            part = part.reshape(shape[:axis] + (number, shape[axis] // number) + shape[axis + 1 :])
-            self.split = True
+            self.outs = [part] * (number - 1)
         else:
-            axis = self.axes.index(way)
-            self.axes.pop(axis)
-        self.total = lax.dynamic_index_in_dim(part, mine, axis, keepdims=False).astype(F32)
-        self.got = [
-            here.send(
-                lax.dynamic_index_in_dim(part, (mine + s) % number, axis, keepdims=False), way, s
-            )
-            for s in range(1, number)
-        ]
+            if way == "x":
+                axis = len(self.axes)
+                shape = part.shape
+                part = part.reshape(
+                    shape[:axis] + (number, shape[axis] // number) + shape[axis + 1 :]
+                )
+                self.split = True
+            else:
+                axis = self.axes.index(way)
+                self.axes.pop(axis)
+            self.total = lax.dynamic_index_in_dim(part, mine, axis, keepdims=False).astype(F32)
+            self.outs = [
+                lax.dynamic_index_in_dim(part, (mine + s) % number, axis, keepdims=False)
+                for s in range(1, number)
+            ]
+        self.got = [here.send(out, way, s) for s, out in zip(range(1, number), self.outs)]
 
     def begin_x(self, part, *after):
         self.part, self.axes = part, []
@@ -828,19 +931,6 @@
     def step(self, way, *after):
         self.go(way, *after)
         self.end()
-
-    def go_z(self, *after):
-        here = self.here
-        part = hold(self.part, *after)
-        v, w = here.mine["v"], here.mine["w"]
-
-        def at(dv, dw):
-            one = lax.dynamic_index_in_dim(part, (v + dv) % 2, 0, keepdims=False)
-            return lax.dynamic_index_in_dim(one, (w + dw) % 2, 0, keepdims=False)
-
-        self.total = at(0, 0).astype(F32)
-        self.got = [here.send(at(*d), way) for d, way in (((1, 0), "v"), ((1, 1), "u"), ((0, 1), "w"))]
-        self.axes = self.axes[2:]
 
     def rows(self):
         if self.split:
@@ -897,11 +987,6 @@
 
 def rms_norm(values, gain):
     return values * lax.rsqrt(jnp.mean(values * values, axis=-1, keepdims=True) + EPSILON) * gain
-
-
-def swiglu(pair):
-    half = pair.shape[1] // 2
-    return jax.nn.silu(pair[:, :half]) * pair[:, half:]
 
 
 def kv_order(array):
@@ -983,10 +1068,9 @@
         [2 * width, width],
         True,
     )
-    pair_full = gather_apart(here, jnp.concatenate([ffn_gate, ffn_up], axis=1))
-    down_full = gather_apart(here, ffn_down)
     rim_rows = from_behind(hidden_in[row_count - rim :], 1)
     rim_ids = from_behind(numbers[row_count - rim :], 1)
+    pair_full = gather_apart(here, jnp.concatenate([ffn_gate, ffn_up], axis=1))
     first.move("v", "w")
     first.move("vw")
     first.pile()
@@ -1019,6 +1103,7 @@
     kv_pre = jnp.dot(normed_ext, kv_full, preferred_element_type=F32)
     second.move("vw", after=[kv_full])
     second.pile()
+    kv_pre = hold(kv_pre, second.got("z"))
     second.move("zy", "zx", after=[kv_pre])
     beta_pre = jnp.dot(normed_low, extra_full, preferred_element_type=F32)[:, :heads]
     rates = jax.nn.sigmoid(beta_pre)
@@ -1041,6 +1126,8 @@
         1,
     )
     key_low, value_low, kv_mixed, w, u, a, moves = delta_summary(kv_pre, kv_taps, cols, rows, heads)
+    moves = hold(moves, second.got("zy", "zx"))
+    down_full = gather_apart(here, hold(ffn_down, pair_full, moves))
     second.move("zyx", after=[moves] + second.got("zx"))
     second.move("zc", "zyc", "zxc", after=[moves])
     fanout = here.nf // heads
@@ -1065,9 +1152,9 @@
     middle = residual + jnp.dot(gated_low, outw_full, preferred_element_type=F32)
     normed_two, norm_two_back = jax.vjp(partial(rms_norm, gain=ffngain_scale), middle)
     normed_two_low = normed_two.astype(BF)
-    pair_pre = jnp.dot(normed_two_low, pair_full, preferred_element_type=F32)
-    hidden_ff, swiglu_back = jax.vjp(swiglu, pair_pre)
-    hidden_low = hidden_ff.astype(BF)
+    hidden_low, pair_low, output, normed_two_grad = feed_forward(
+        normed_two_low, cotangent, middle, pair_full, down_full
+    )
 
     c = here.mine["c"]
 
@@ -1079,22 +1166,20 @@
     theirs, ours = shares(cotangent, 0, width)
     down_sum = Reduce(here)
     down_sum.swap(contract(hidden_low, theirs, 0, 0))
-    hidden_grad = contract(cotangent, down_full, 1, 1)
-    (pair_grad,) = swiglu_back(hidden_grad)
-    pair_low = pair_grad.astype(BF)
-    down_half = (contract(hidden_low, hold(ours, pair_low), 0, 0) + down_sum.came.astype(F32)).astype(BF)
-    down_apart = scatter_owners(down_half)
-    top_grad = cotangent.astype(F32)
-    normed_two_grad = contract(pair_low, pair_full, 1, 1)
+    theirs, ours = [lax.dynamic_index_in_dim(pair_low, at, 0, keepdims=False) for at in (1 - c, c)]
+    pair_sum = Reduce(here)
+    pair_sum.swap(contract(normed_two_low, theirs, 0, 0))
+    down_theirs, down_ours = shares(cotangent, 0, width)
+    down_sum = Reduce(here)
+    down_sum.swap(contract(hidden_low, down_theirs, 0, 0))
     (middle_back,) = norm_two_back(normed_two_grad)
-    middle_grad = top_grad + middle_back
+    middle_grad = cotangent.astype(F32) + middle_back
     middle_low = middle_grad.astype(BF)
     gated_grad = contract(middle_low, outw_full, 1, 1)
-    theirs, ours = shares(pair_low, 0, 2 * hidden_units)
-    pair_sum = Reduce(here)
-    pair_sum.swap(contract(normed_two_low, theirs, 0, 0))
     pair_half = (contract(normed_two_low, ours, 0, 0) + pair_sum.came.astype(F32)).astype(BF)
     pair_apart = scatter_owners(pair_half)
+    down_half = (contract(hidden_low, down_ours, 0, 0) + down_sum.came.astype(F32)).astype(BF)
+    down_apart = scatter_owners(down_half)
     gated_grad = hold(gated_grad, down_half, pair_half)
     heads_grad, gatepre_low, outgain_grad, local_later = delta_adjoint(
         query_low, key_low, w, cols, rows, gated_grad, attn_heads, qg_pre, outgain_scale, heads
@@ -1107,17 +1192,17 @@
     later = swap(summed_later)
     if fanout > 1:
         later = to_heads(later, fanout)
-    hidden_held, middle_held, gatepre_held = hold((hidden_low, middle_low, gatepre_low), summed_later)
+    middle_held, gatepre_held = hold((middle_low, gatepre_low), summed_later)
     out_grad = contract(gated_low, middle_held, 0, 0)
     gate_grad = contract(normed_low, gatepre_held, 0, 0)
     other_sum = Reduce(here)
     other_sum.swap(by_core(here, gate_grad, out_grad))
-    output = (middle + jnp.dot(hidden_held, down_full, preferred_element_type=F32)).astype(BF)
-    other_sum.take(hold(by_core(here, out_grad, gate_grad), output))
+    other_sum.take(by_core(here, out_grad, gate_grad))
     later = hold(later, other_sum.part)
     other_x, other_y = other_sum.two(width // 2)
     other_x.go("x", later)
     other_y.go("y", later)
+    later = hold(later, *other_x.outs, *other_y.outs)
     state = (query_low, key_low, value_low, w, u, a, fresh, kept, heads_grad, cols, rows)
     mixed_a, beta_a, taps_a = delta_backward(
         0, *state, later, q_mixed, qg_pre, query_taps, kv_mixed, kv_pre, kv_taps, heads
@@ -1136,6 +1221,7 @@
     a_x.go("x", later)
     a_y.go("y", later)
     other_sum.go("w", later)
+    later = hold(later, *a_x.outs, *a_y.outs, *other_sum.outs)
     mixed_b, beta_b, taps_b = delta_backward(
         1, *state, later, q_mixed, qg_pre, query_taps, kv_mixed, kv_pre, kv_taps, heads
     )
@@ -1168,7 +1254,6 @@
     b_sum.go("x")
     a_x.go("y", mixed_b)
     a_y.go("x", mixed_b)
-    other_sum.go("v", mixed_b)
     small_sum.go("x")
     wide_grad = (
         contract(mixed_a[:, cut[0] :], kv_full[:, : 2 * cut[0]], 1, 1)
@@ -1183,7 +1268,8 @@
         + contract(betapre_low, extra_full, 1, 1)
         + contract(gatepre_low, qg_full[:, width:], 1, 1)
     )
-    normed_grad = meet(normed_grad, b_sum, a_x, a_y, other_sum, small_sum)
+    normed_grad = meet(normed_grad, b_sum, a_x, a_y, small_sum)
+    other_sum.go("v", normed_grad)
     a_sum.join(a_x, a_y)
     b_sum.go("y")
     small_sum.go("y")
@@ -1191,25 +1277,25 @@
     a_sum.go("w")
     (input_back,) = jax.vjp(partial(rms_norm, gain=attn_scale), residual)[1](normed_grad)
     input_grad = meet(
-        (middle_grad + input_back).astype(BF), b_sum, a_sum, small_sum, pair_sum
+        (middle_grad + input_back).astype(BF), b_sum, a_sum, other_sum, small_sum, pair_sum
     )
     b_sum.go("w", input_grad)
     a_sum.go("v", input_grad)
     small_sum.go("w", input_grad)
-    down_sum.begin_x(down_apart, input_grad)
     for one in (b_sum, a_sum, small_sum):
         one.end()
-    down_sum.end()
-    b_sum.go("v", a_sum.part, down_sum.part)
+    b_sum.go("v", a_sum.part)
     small_sum.go("v", a_sum.part)
-    pair_part, down_part = hold((pair_sum.part, down_sum.part), a_sum.part)
+    pair_part = hold(pair_sum.part, a_sum.part)
     other = here.send(pair_part, "c")
-    down_total = join_way(here, down_part, "c", 1).astype(F32)
     held = meet(a_sum.part, b_sum, small_sum)
     both = Reduce(here)
     both.part = jnp.concatenate([b_sum.part, held, other_sum.part, small_sum.part], axis=1)
     both.split = True
     both.rows()
+    down_sum.begin_x(down_apart, held)
+    down_sum.end()
+    down_total = join_way(here, down_sum.part, "c", 1).astype(F32)
     hidgate_total = by_core(here, pair_part, other).astype(F32)
     hidup_total = by_core(here, other, pair_part).astype(F32)
     whole = both.other()

time: 512 us -> 501 us (0.979)
  matrix products: 118 us -> 74.5 us
  Pallas kernels: 88.4 us -> 116 us
  waiting for transfers between devices: 110 us -> 124 us
  other arithmetic: 51 us -> 43.1 us
  local copies, waits for them, and re-layouts: 34.8 us -> 40.3 us
  starting transfers between devices: 84 us -> 78.5 us
    pallas_call x0 -> x1, Pallas kernels: none -> 27.9 us  [feed_forward(): pl.pallas_call(feed_kernel, grid=(blocks + 1,), in_specs=[whole, whole, w...]
    dot_general x20 -> x18, matrix products: 84.4 us -> 59.2 us  [contract(): lax.dot_general(left, right, (((left_dim,), (right_dim,)), ((), ())), pre...]
    dot_general x2 -> x0, matrix products: 19.8 us -> none  [the longest x1 11.9 us: on_device(): pair_pre = jnp.dot(normed_two_low, pair_full, preferred_element_type=F32)]
    all_to_all x4, waiting for transfers between devices: 33.1 us -> 20.5 us  [swap(): return lax.all_to_all(value, 'fsdp', 0, 0, tiled=True)]
    convert_element_type x3 -> x1, other arithmetic: 12 us -> 1.32 us  [on_device(): down_total = join_way(here, down_sum.part, 'c', 1).astype(F32)]
    reduce_scatter x2, waiting for transfers between devices: 0.02 us -> 9.3 us  [scatter_owners(): return lax.psum_scatter(array, 'fsdp', scatter_dimension=0, tiled=True)]
    unnamed x176 -> x172, local copies, waits for them, and re-layouts: 17.6 us -> 24.5 us
    ppermute x52, waiting for transfers between devices: 72.8 us -> 79.6 us  [send(): return lax.ppermute(value, axis, pairs)]
  transfers between devices with their start and end apart: 63 -> 63, of which waited for: 20 -> 23; matrix products, arithmetic and copies ran while one was open for 31% -> 25% of each run, Pallas kernels for 18% -> 18%
where the time goes in v5:
time: 501 us; the launch traced here: 492 us
  waiting for transfers between devices  124 us (25%)
  Pallas kernels  116 us (23%)
  starting transfers between devices  78.5 us (16%)
  matrix products  74.5 us (15%)
  other arithmetic  43.1 us (9%)
  local copies, waits for them, and re-layouts  40.3 us (8%)
  between operations  15.7 us (3%)
    ppermute x52, waiting for transfers between devices, send(): return lax.ppermute(value, axis, pairs)  79.6 us
    dot_general x18, matrix products, contract(): lax.dot_general(left, right, (((left_dim,), (right_dim,)), ((), ())), pre...  59.2 us
    ppermute x52, starting transfers between devices, send(): return lax.ppermute(value, axis, pairs)  51.6 us
    pallas_call x2, Pallas kernels, delta_backward(): pl.pallas_call(partial(backward_kernel, heads, part, d), grid=(blocks + 1...  31.6 us
    pallas_call x1, Pallas kernels, feed_forward(): pl.pallas_call(feed_kernel, grid=(blocks + 1,), in_specs=[whole, whole, w...  27.9 us
    unnamed x172, local copies, waits for them, and re-layouts  24.5 us
    pallas_call x1, Pallas kernels, delta_summary(): pl.pallas_call(partial(summary_kernel, heads, d), grid=(blocks,), in_spec...  21.5 us
    all_to_all x4, waiting for transfers between devices, swap(): return lax.all_to_all(value, 'fsdp', 0, 0, tiled=True)  20.5 us
  transfers between devices with their start and end apart: 63, of which 23 were waited for; matrix products, arithmetic and copies ran while one was open for 25% of the time, Pallas kernels for 18%

profile of v5, /device:TPU:0, one launch (start us, length us, event | category | flops | bytes accessed | tf_op | source)
XLA Modules:
  0.0 491.8 jit_solution(10454905710418042389)
XLA Ops:
  7.3 1.9 fusion.67
  10.2 4.1 collective-permute-start.1
  16.0 3.4 collective-permute-start.4
  20.1 2.3 collective-permute-start.3
  23.0 6.9 %collective-permute-done.2 = bf16[32,2176]{1,0:T(8,128)(2,1)S(1)} collective-permute-done((bf16[32,2176]{1,0:T(8,128)(2,1)S(1)}, bf16[32,2176]{1,0:T(8,128)(2,1)S(1)}, u32[]{:S(2)}, u32[]{:S(2)}) %collective-permute-start.2) | collective-permute-done | bytes 139296 | tf_op jit(solution)/shard_map/ppermute | solution.py:762
  34.4 5.7 %collective-permute-done.5.refs_1_ = bf16[4,32,2176]{2,1,0:T(8,128)(2,1)S(1)} collective-permute-done((bf16[4,32,2176]{2,1,0:T(8,128)(2,1)S(1)}, bf16[4,32,2176]{2,1,0:T(8,128)(2,1)S(1)}, u32[]{:S(2)}, u32[]{:S(2)}) %collective-permute-start.5) | collective-permute-done | bytes 557088 | tf_op jit(solution)/shard_map/ppermute | solution.py:762
  40.1 4.2 collective-permute-done.6.refs_2_
  44.3 2.2 collective-permute-start.8
  48.4 2.6 collective-permute-start.13
  51.1 6.0 %collective-permute-start.12 = (bf16[32,3072]{1,0:T(8,128)(2,1)}, bf16[32,3072]{1,0:T(8,128)(2,1)}, u32[]{:S(2)}, u32[]{:S(2)}) collective-permute-start(bf16[32,3072]{1,0:T(8,128)(2,1)} %constant_dynamic-slice_fusion.5), channel_id=1, source_target_pairs={{0,2},{1,3},{2,0},{3,1},{4,6},{5,7},{6,4},{7,5},{8,10},{9,11},{10,... | collective-permute-start | bytes 589832 | tf_op jit(solution)/shard_map/ppermute | solution.py:762
  57.0 6.8 %collective-permute-done.8.refs_4_ = bf16[4,32,2176]{2,1,0:T(8,128)(2,1)} collective-permute-done((bf16[4,32,2176]{2,1,0:T(8,128)(2,1)S(1)}, bf16[4,32,2176]{2,1,0:T(8,128)(2,1)}, u32[]{:S(2)}, u32[]{:S(2)}) %collective-permute-start.8) | collective-permute-done | bytes 557088 | tf_op jit(solution)/shard_map/ppermute | solution.py:762
  69.8 3.4 place_weights.2
  73.2 2.1 copy-done.4
  80.1 6.6 %fusion.103.pre_ref.prev_ref.kvpre_ref.kvrim_ref = f32[520,2048]{1,0:T(8,128)} fusion(bf16[520,1024]{1,0:T(8,128)(2,1)S(1)} %fusion.11, bf16[1024,2048]{1,0:T(8,128)(2,1)} %copy-done.4), kind=kOutput, calls=%fused_computation.231 | convolution fusion | flops 2181038080 | bytes 9519104 | tf_op jit(solution)/shard_map/dot_general | solution.py:1103
  87.3 11.4 %collective-permute-done.14 = bf16[32,3072]{1,0:T(8,128)(2,1)S(1)} collective-permute-done((bf16[32,3072]{1,0:T(8,128)(2,1)}, bf16[32,3072]{1,0:T(8,128)(2,1)S(1)}, u32[]{:S(2)}, u32[]{:S(2)}) %collective-permute-start.14) | collective-permute-done | bytes 196640 | tf_op jit(solution)/shard_map/ppermute | solution.py:762
  100.5 2.4 collective-permute-start.16
  102.9 21.5 %delta_summary.1 = (bf16[512,1024]{1,0:T(8,128)(2,1)}, bf16[512,1024]{1,0:T(8,128)(2,1)}, f32[512,2048]{1,0:T(8,128)}, bf16[512,1024]{1,0:T(8,128)(2,1)}, bf16[5...) custom-call(f32[520,2048]{1,0:T(8,128)} %fusion.103.pre_ref.prev_ref.kvpre_ref.kvrim_ref, ...), custom_call_target="tpu_custom_call" | custom-call | flops 20999999488 | bytes 63000000 | tf_op jit(solution)/shard_map/delta_summary/pallas_call | solution.py:453
  126.0 5.5 %all-to-all-start = ((bf16[8,128,256]{2,1,0:T(8,128)(2,1)}), bf16[8,128,256]{2,1,0:T(8,128)(2,1)S(1)}, u32[]{:S(2)}, u32[]{:S(2)}) async-start(bf16[8,128,256]{2,1,0:T(8,128)(2,1)} %get-tuple-element.122), calls=%async_computation | async-start | bytes 1048576 | tf_op jit(solution)/shard_map/all_to_all | solution.py:1017
  132.4 18.9 %collective-permute-done.17.refs_3_ = bf16[4,32,3072]{2,1,0:T(8,128)(2,1)} collective-permute-done((bf16[4,32,3072]{2,1,0:T(8,128)(2,1)S(1)}, bf16[4,32,3072]{2,1,0:T(8,128)(2,1)}, u32[]{:S(2)}, u32[]{:S(2)}) %collective-permute-start.17) | collective-permute-done | bytes 786464 | tf_op jit(solution)/shard_map/ppermute | solution.py:762
  152.7 2.7 state_prefix.1
  155.4 5.7 %all-to-all-start.1 = ((bf16[8,128,128]{2,1,0:T(8,128)(2,1)}), bf16[8,128,128]{2,1,0:T(8,128)(2,1)S(1)}, u32[]{:S(2)}, u32[]{:S(2)}) async-start(bf16[8,128,128]{2,1,0:T(8,128)(2,1)} %state_prefix.1), calls=%async_computation.1 | async-start | bytes 524288 | tf_op jit(solution)/shard_map/all_to_all | solution.py:1017
  162.8 4.2 place_weights.3
  168.3 1.9 copy-done.6
  170.2 5.6 %fusion.104.pre_ref.prev_ref.gate_ref.qpre_ref.qrim_ref = f32[520,2048]{1,0:T(8,128)} fusion(bf16[520,1024]{1,0:T(8,128)(2,1)} %copy-done.24, bf16[1024,2048]{1,0:T(8,128)(2,1)S(1)} %get-tuple-element.128), kind=kOutput, calls=%fused_computation.232 | convolution fusion | flops 2181038080 | bytes 9519104 | tf_op jit(solution)/shard_map/dot_general | solution.py:1145
  176.6 10.8 %delta_forward.1 = (bf16[512,1024]{1,0:T(8,128)(2,1)}, f32[512,1024]{1,0:T(8,128)}, bf16[512,1024]{1,0:T(8,128)(2,1)}, f32[512,1024]{1,0:T(8,128)}, bf16[512,102...) custom-call(f32[520,2048]{1,0:T(8,128)} %fusion.104.pre_ref.prev_ref.gate_ref.qpre_ref.qrim_ref, ...), custom_call_target="tpu_custom_call" | custom-call | flops 11000000512 | bytes 33000000 | tf_op jit(solution)/shard_map/delta_forward/pallas_call | solution.py:496
  187.5 2.6 multiply_reduce_fusion.1
  192.6 5.8 %all-gather.5.cloned.1.call-done.d_ref.db_ref = bf16[2816,1024]{1,0:T(8,128)(2,1)} async-done(((bf16[88,1024]{1,0:T(8,128)(2,1)}), bf16[2816,1024]{1,0:T(8,128)(2,1)}) %all-gather.5.cloned.1.call-update) | async-done | bytes 5767184 | tf_op jit(solution)/shard_map/all_gather | solution.py:967
  198.5 27.9 %feed_forward.1 = (bf16[512,2816]{1,0:T(8,128)(2,1)}, bf16[2,512,2816]{2,1,0:T(8,128)(2,1)}, bf16[512,1024]{1,0:T(8,128)(2,1)}, f32[512,1024]{1,0:T(8,128)}) custom-call(bf16[512,1024]{1,0:T(8,128)(2,1)} %multiply_convert_fusion.n_ref, bf16[512,1024]{1,0:T(8,128)(2,1)} %e_ref.1, f32[512,1024]{1,0:T(8,128)} %copy-done.17, ...), custom_call_target="tpu_custom_call" | custom-call | flops 24999999488 | bytes 75000000 | tf_op jit(solution)/shard_map/feed_forward/pallas_call | solution.py:692
  226.4 6.8 %convolution_convert_fusion = bf16[1024,2816]{1,0:T(8,128)(2,1)} fusion(bf16[512,1024]{1,0:T(8,128)(2,1)S(1)} %copy-done.50, bf16[2,512,2816]{2,1,0:T(8,128)(2,1)} %get-tuple-element.143, s32[]{:T(128)S(6)} %select_n.640), kind=kOutput, calls=%fused_computation.2 | convolution fusion | flops 2955673600 | bytes 9699332 | tf_op jit(solution)/shard_map/dot_general | solution.py:983
  233.5 5.3 %convolution_convert_fusion.1 = bf16[2816,512]{1,0:T(8,128)(2,1)} fusion(bf16[512,2816]{1,0:T(8,128)(2,1)} %get-tuple-element.142, bf16[512,1024]{1,0:T(8,128)(2,1)} %e_ref.1, s32[]{:T(128)S(6)} %select_n.638), kind=kOutput, calls=%fused_computation.4 | convolution fusion | flops 1477836800 | bytes 6291460 | tf_op jit(solution)/shard_map/dot_general | solution.py:983
  239.0 3.9 collective-permute-done.23
  243.0 7.0 %add_convert_fusion = bf16[1024,2816]{1,0:T(8,128)(2,1)} fusion(bf16[1024,2816]{1,0:T(8,128)(2,1)} %collective-permute-done.23, bf16[512,1024]{1,0:T(8,128)(2,1)S(1)} %copy-done.51, bf16[2,512,2816]{2,1,0:T(8,128)(2,1)S(1)} %copy-done.79, s32[]{:T(128)S(6)} %select_n.639), kind=kOutput, calls=%fused_computation | convolution fusion | flops 2961440768 | bytes 15466500 | tf_op jit(solution)/shard_map/dot_general | solution.py:983
  250.0 2.7 multiply_reduce_fusion
  255.3 2.7 fusion.105.dy_ref
  258.8 5.2 %add_convert_fusion.1 = bf16[2816,512]{1,0:T(8,128)(2,1)} fusion(bf16[2816,512]{1,0:T(8,128)(2,1)} %collective-permute-done.22, bf16[512,2816]{1,0:T(8,128)(2,1)S(1)} %copy-done.77, bf16[512,1024]{1,0:T(8,128)(2,1)S(1)} %copy-done.27, s32[]{:T(128)S(6)} %select_n.637), kind=kOutput, calls=%fused_computation.1 | convolution fusion | flops 1480720384 | bytes 9175044 | tf_op jit(solution)/shard_map/dot_general | solution.py:983
  264.0 10.9 %delta_adjoint.1 = (bf16[512,1024]{1,0:T(8,128)(2,1)}, bf16[512,1024]{1,0:T(8,128)(2,1)}, f32[1,128]{1,0:T(1,128)}, bf16[8,128,128]{2,1,0:T(8,128)(2,1)}) custom-call(bf16[512,1024]{1,0:T(8,128)(2,1)} %get-tuple-element.137.q_ref, bf16[512,1024]{1,0:T(8,128)(2,1)} %get-tuple-element.129.k_ref, bf16[512,1024]{1,0:T(8,128)(2,1)} %get-tuple-element.130.w_ref, ...), custom_call_target="tpu_custom_call" | custom-call | flops 11000000512 | bytes 33000000 | tf_op jit(solution)/shard_map/delta_adjoint/pallas_call | solution.py:532
  274.9 4.6 all-to-all-start.2
  279.5 17.1 %all-to-all-done.2.g_ref = bf16[8,128,128]{2,1,0:T(8,128)(2,1)S(1)} async-done(((bf16[8,128,128]{2,1,0:T(8,128)(2,1)}), bf16[8,128,128]{2,1,0:T(8,128)(2,1)S(1)}, u32[]{:S(2)}, u32[]{:S(2)}) %all-to-all-start.2) | async-done | bytes 262176 | tf_op jit(solution)/shard_map/all_to_all | solution.py:1017
  297.3 2.8 state_suffix.1
  301.7 4.1 select_convert_fusion
  305.7 3.4 all-to-all-start.3
  311.5 4.2 add_convert_fusion.3
  315.7 3.4 all-to-all-done.3.s_ref
  321.9 19.1 %delta_backward.2 = (bf16[520,2304]{1,0:T(8,128)(2,1)}, f32[512,128]{1,0:T(8,128)}, f32[4,2304]{1,0:T(4,128)}) custom-call(bf16[512,1024]{1,0:T(8,128)(2,1)} %get-tuple-element.137.q_ref, bf16[512,1024]{1,0:T(8,128)(2,1)} %get-tuple-element.129.k_ref, bf16[512,1024]{1,0:T(8,128)(2,1)} %get-tuple-element.138.v_ref, ...), custom_call_target="tpu_custom_call" | custom-call | flops 20000000000 | bytes 60000000 | tf_op jit(solution)/shard_map/delta_backward/pallas_call | solution.py:594
  341.8 5.2 %convolution_convert_fusion.2 = bf16[1024,1152]{1,0:T(8,128)(2,1)} fusion(bf16[520,1024]{1,0:T(8,128)(2,1)S(1)} %copy-done.26, bf16[520,2304]{1,0:T(8,128)(2,1)} %get-tuple-element.158, s32[]{:T(128)S(6)} %select_n.647), kind=kOutput, calls=%fused_computation.7 | convolution fusion | flops 1228013568 | bytes 4622340 | tf_op jit(solution)/shard_map/dot_general | solution.py:983
  354.2 4.1 fusion.22
  358.3 3.2 fusion
  361.5 3.9 add_convert_fusion.2
  370.6 12.5 %delta_backward.3 = (bf16[520,768]{1,0:T(8,128)(2,1)}, f32[512,128]{1,0:T(8,128)}, f32[4,768]{1,0:T(4,128)}) custom-call(bf16[512,1024]{1,0:T(8,128)(2,1)} %get-tuple-element.137.q_ref, bf16[512,1024]{1,0:T(8,128)(2,1)} %get-tuple-element.129.k_ref, bf16[512,1024]{1,0:T(8,128)(2,1)} %get-tuple-element.138.v_ref, bf16[512,1024]{1,0:T(8,128)(2,1)} %get-tuple-element.130.w_ref, ...), custom_call_target="tpu_custom_call" | custom-call | flops 12000000000 | bytes 36000000 | tf_op jit(solution)/shard_map/delta_backward/pallas_call | solution.py:594
  389.5 2.0 fusion.33
  393.1 2.0 convolution_convert_fusion.3
  400.4 2.3 fusion.36
  408.6 8.5 %collective-permute-done.35 = bf16[8,1024]{1,0:T(8,128)(2,1)S(1)} collective-permute-done((bf16[8,1024]{1,0:T(8,128)(2,1)S(1)}, bf16[8,1024]{1,0:T(8,128)(2,1)S(1)}, u32[]{:S(2)}, u32[]{:S(2)}) %collective-permute-start.35) | collective-permute-done | bytes 16416 | tf_op jit(solution)/shard_map/ppermute | solution.py:1001
  421.7 2.5 collective-permute-start.42
  427.5 2.0 fusion.14
  429.6 3.4 collective-permute-done.40
  433.7 2.9 collective-permute-done.44
  436.6 2.0 collective-permute-start.48
  441.0 3.3 collective-permute-done.45
  444.3 2.1 collective-permute-done.46
  446.7 2.8 collective-permute-start.47
  451.3 3.6 collective-permute-done.47
  455.3 9.3 %reduce-scatter.5.cloned.1.call-done = bf16[352,512]{1,0:T(8,128)(2,1)} async-done(((bf16[2816,512]{1,0:T(8,128)(2,1)}), bf16[352,512]{1,0:T(8,128)(2,1)}) %reduce-scatter.5.cloned.1.call-update) | async-done | bytes 360464 | tf_op jit(solution)/shard_map/reduce_scatter | solution.py:971
  475.0 3.2 multiply_reduce_fusion.3
  (409 shorter events, 107.1 us)
Async XLA Ops:
  7.2 118.1 %copy-start = (bf16[352,1024]{1,0:T(8,128)(2,1)S(1)}, bf16[352,1024]{1,0:T(8,128)(2,1)}, u32[]{:S(2)}) copy-start(bf16[352,1024]{1,0:T(8,128)(2,1)} %param.26) | copy-start | bytes 2162692
  7.3 118.0 %all-gather.3.cloned.1.call-start = ((), (), s32[]{:S(2)}) async-start(), calls=%async_computation.6 | async-start | bytes 11894784 | tf_op jit(solution)/shard_map/all_gather | solution.py:967
  9.3 189.2 %all-gather.5.cloned.1.call-start = ((), (), s32[]{:S(2)}) async-start(), calls=%async_computation.7 | async-start | bytes 5947392 | tf_op jit(solution)/shard_map/all_gather | solution.py:967
  10.2 12.2 %collective-permute-start.1 = (bf16[32,2176]{1,0:T(8,128)(2,1)S(1)}, bf16[32,2176]{1,0:T(8,128)(2,1)S(1)}, u32[]{:S(2)}, u32[]{:S(2)}) collective-permute-start(bf16[32,2176]{1,0:T(8,128)(2,1)S(1)} %constant_dynamic-slice_fusion.6), channel_id=1, source_target_pairs={{0,4},{1,5},{2,6},{3,7},{4,0},{5,1},{6,2},{7,3},{8,12},{9,13},{10,... | collective-permute-start | bytes 417800 | tf_op jit(solution)/shard_map/ppermute | solution.py:762
  14.3 8.6 %collective-permute-start = (bf16[32,2176]{1,0:T(8,128)(2,1)S(1)}, bf16[32,2176]{1,0:T(8,128)(2,1)S(1)}, u32[]{:S(2)}, u32[]{:S(2)}) collective-permute-start(bf16[32,2176]{1,0:T(8,128)(2,1)S(1)} %constant_dynamic-slice_fusion.6), channel_id=1, source_target_pairs={{0,2},{1,3},{2,0},{3,1},{4,6},{5,7},{6,4},{7,5},{8,10},{9,11},{10,... | collective-permute-start | bytes 417800 | tf_op jit(solution)/shard_map/ppermute | solution.py:762
  16.0 14.0 %collective-permute-start.4 = (s32[8]{0:T(128)S(1)}, s32[8]{0:T(128)S(1)}, u32[]{:S(2)}, u32[]{:S(2)}) collective-permute-start(s32[8]{0:T(128)S(1)} %slice.189), channel_id=1, source_target_pairs={{0,1},{1,2},{2,3},{3,4},{4,5},{5,6},{6,7},{8,9},{9,10},{10,11},{11... | collective-permute-start | bytes 104 | tf_op jit(solution)/shard_map/ppermute | solution.py:1001
  20.1 9.9 %collective-permute-start.3 = (bf16[8,1024]{1,0:T(8,128)(2,1)S(1)}, bf16[8,1024]{1,0:T(8,128)(2,1)S(1)}, u32[]{:S(2)}, u32[]{:S(2)}) collective-permute-start(bf16[8,1024]{1,0:T(8,128)(2,1)S(1)} %slice.188), channel_id=1, source_target_pairs={{0,1},{1,2},{2,3},{3,4},{4,5},{5,6},{6,7},{8,9},{9,10},{10,11},{11... | collective-permute-start | bytes 49160 | tf_op jit(solution)/shard_map/ppermute | solution.py:1001
  22.4 7.4 %collective-permute-start.2 = (bf16[32,2176]{1,0:T(8,128)(2,1)S(1)}, bf16[32,2176]{1,0:T(8,128)(2,1)S(1)}, u32[]{:S(2)}, u32[]{:S(2)}) collective-permute-start(bf16[32,2176]{1,0:T(8,128)(2,1)S(1)} %collective-permute-done.1), channel_id=1, source_target_pairs={{0,2},{1,3},{2,0},{3,1},{4,6},{5,7},{6,4},{7,5},{8,10},{9,11},{10,... | collective-permute-start | bytes 417800 | tf_op jit(solution)/shard_map/ppermute | solution.py:762
  30.0 10.1 %collective-permute-start.5 = (bf16[4,32,2176]{2,1,0:T(8,128)(2,1)S(1)}, bf16[4,32,2176]{2,1,0:T(8,128)(2,1)S(1)}, u32[]{:S(2)}, u32[]{:S(2)}) collective-permute-start(bf16[4,32,2176]{2,1,0:T(8,128)(2,1)S(1)} %pad_maximum_fusion.4.refs_0_), channel_id=1, source_target_pairs={{0,1},{1,0},{2,3},{3,2},{4,5},{5,4},{6,7},{7,6},{8,9},{9,8},{10,11... | collective-permute-start | bytes 1671176 | tf_op jit(solution)/shard_map/ppermute | solution.py:762
  31.5 12.8 %collective-permute-start.6 = (bf16[4,32,2176]{2,1,0:T(8,128)(2,1)S(1)}, bf16[4,32,2176]{2,1,0:T(8,128)(2,1)}, u32[]{:S(2)}, u32[]{:S(2)}) collective-permute-start(bf16[4,32,2176]{2,1,0:T(8,128)(2,1)S(1)} %pad_maximum_fusion.4.refs_0_), channel_id=1, source_target_pairs={{0,16},{8,24},{16,0},{24,8},{1,17},{9,25},{17,1},{25,9},{2,18},{10... | collective-permute-start | bytes 1671176 | tf_op jit(solution)/shard_map/ppermute | solution.py:762
  33.0 11.3 %collective-permute-start.7 = (bf16[4,32,2176]{2,1,0:T(8,128)(2,1)S(1)}, bf16[4,32,2176]{2,1,0:T(8,128)(2,1)}, u32[]{:S(2)}, u32[]{:S(2)}) collective-permute-start(bf16[4,32,2176]{2,1,0:T(8,128)(2,1)S(1)} %pad_maximum_fusion.4.refs_0_), channel_id=1, source_target_pairs={{0,8},{8,0},{16,24},{24,16},{1,9},{9,1},{17,25},{25,17},{2,10},{10... | collective-permute-start | bytes 1671176 | tf_op jit(solution)/shard_map/ppermute | solution.py:762
  44.3 19.5 %collective-permute-start.8 = (bf16[4,32,2176]{2,1,0:T(8,128)(2,1)S(1)}, bf16[4,32,2176]{2,1,0:T(8,128)(2,1)}, u32[]{:S(2)}, u32[]{:S(2)}) collective-permute-start(bf16[4,32,2176]{2,1,0:T(8,128)(2,1)S(1)} %collective-permute-done.5.refs_1_), channel_id=1, source_target_pairs={{0,16},{8,24},{16,0},{24,8},{1,17},{9,25},{17,1},{25,9},{2,18},{10... | collective-permute-start | bytes 1671176 | tf_op jit(solution)/shard_map/ppermute | solution.py:762
  46.5 17.2 %collective-permute-start.10 = (bf16[4,32,2176]{2,1,0:T(8,128)(2,1)}, bf16[4,32,2176]{2,1,0:T(8,128)(2,1)S(1)}, u32[]{:S(2)}, u32[]{:S(2)}) collective-permute-start(bf16[4,32,2176]{2,1,0:T(8,128)(2,1)} %collective-permute-done.6.refs_2_), channel_id=1, source_target_pairs={{0,8},{8,0},{16,24},{24,16},{1,9},{9,1},{17,25},{25,17},{2,10},{10... | collective-permute-start | bytes 1671176 | tf_op jit(solution)/shard_map/ppermute | solution.py:762
  46.5 18.1 %collective-permute-start.9 = (bf16[4,32,2176]{2,1,0:T(8,128)(2,1)S(1)}, bf16[4,32,2176]{2,1,0:T(8,128)(2,1)S(1)}, u32[]{:S(2)}, u32[]{:S(2)}) collective-permute-start(bf16[4,32,2176]{2,1,0:T(8,128)(2,1)S(1)} %collective-permute-done.5.refs_1_), channel_id=1, source_target_pairs={{0,8},{8,0},{16,24},{24,16},{1,9},{9,1},{17,25},{25,17},{2,10},{10... | collective-permute-start | bytes 1671176 | tf_op jit(solution)/shard_map/ppermute | solution.py:762
  48.4 30.7 %collective-permute-start.13 = (bf16[32,3072]{1,0:T(8,128)(2,1)}, bf16[32,3072]{1,0:T(8,128)(2,1)}, u32[]{:S(2)}, u32[]{:S(2)}) collective-permute-start(bf16[32,3072]{1,0:T(8,128)(2,1)} %constant_dynamic-slice_fusion.5), channel_id=1, source_target_pairs={{0,4},{1,5},{2,6},{3,7},{4,0},{5,1},{6,2},{7,3},{8,12},{9,13},{10,... | collective-permute-start | bytes 589832 | tf_op jit(solution)/shard_map/ppermute | solution.py:762
  51.1 36.3 %collective-permute-start.12 = (bf16[32,3072]{1,0:T(8,128)(2,1)}, bf16[32,3072]{1,0:T(8,128)(2,1)}, u32[]{:S(2)}, u32[]{:S(2)}) collective-permute-start(bf16[32,3072]{1,0:T(8,128)(2,1)} %constant_dynamic-slice_fusion.5), channel_id=1, source_target_pairs={{0,2},{1,3},{2,0},{3,1},{4,6},{5,7},{6,4},{7,5},{8,10},{9,11},{10,... | collective-permute-start | bytes 589832 | tf_op jit(solution)/shard_map/ppermute | solution.py:762
  65.4 2.3 collective-permute-start.11
  79.1 19.6 %collective-permute-start.14 = (bf16[32,3072]{1,0:T(8,128)(2,1)}, bf16[32,3072]{1,0:T(8,128)(2,1)S(1)}, u32[]{:S(2)}, u32[]{:S(2)}) collective-permute-start(bf16[32,3072]{1,0:T(8,128)(2,1)} %collective-permute-done.13), channel_id=1, source_target_pairs={{0,2},{1,3},{2,0},{3,1},{4,6},{5,7},{6,4},{7,5},{8,10},{9,11},{10,... | collective-permute-start | bytes 589832 | tf_op jit(solution)/shard_map/ppermute | solution.py:762
  99.8 24.5 %collective-permute-start.15 = (bf16[4,32,3072]{2,1,0:T(8,128)(2,1)S(1)}, bf16[4,32,3072]{2,1,0:T(8,128)(2,1)S(1)}, u32[]{:S(2)}, u32[]{:S(2)}) collective-permute-start(bf16[4,32,3072]{2,1,0:T(8,128)(2,1)S(1)} %pad_maximum_fusion.2.refs_0_), channel_id=1, source_target_pairs={{0,1},{1,0},{2,3},{3,2},{4,5},{5,4},{6,7},{7,6},{8,9},{9,8},{10,11... | collective-permute-start | bytes 2359304 | tf_op jit(solution)/shard_map/ppermute | solution.py:762
  100.5 23.9 %collective-permute-start.16 = (bf16[4,32,3072]{2,1,0:T(8,128)(2,1)S(1)}, bf16[4,32,3072]{2,1,0:T(8,128)(2,1)S(1)}, u32[]{:S(2)}, u32[]{:S(2)}) collective-permute-start(bf16[4,32,3072]{2,1,0:T(8,128)(2,1)S(1)} %pad_maximum_fusion.2.refs_0_), channel_id=1, source_target_pairs={{0,16},{8,24},{16,0},{24,8},{1,17},{9,25},{17,1},{25,9},{2,18},{10... | collective-permute-start | bytes 2359304 | tf_op jit(solution)/shard_map/ppermute | solution.py:762
  126.0 25.4 %all-to-all-start = ((bf16[8,128,256]{2,1,0:T(8,128)(2,1)}), bf16[8,128,256]{2,1,0:T(8,128)(2,1)S(1)}, u32[]{:S(2)}, u32[]{:S(2)}) async-start(bf16[8,128,256]{2,1,0:T(8,128)(2,1)} %get-tuple-element.122), calls=%async_computation | async-start | bytes 1048576 | tf_op jit(solution)/shard_map/all_to_all | solution.py:1017
  131.4 19.9 %collective-permute-start.17 = (bf16[4,32,3072]{2,1,0:T(8,128)(2,1)S(1)}, bf16[4,32,3072]{2,1,0:T(8,128)(2,1)}, u32[]{:S(2)}, u32[]{:S(2)}) collective-permute-start(bf16[4,32,3072]{2,1,0:T(8,128)(2,1)S(1)} %collective-permute-done.15.refs_1_), channel_id=1, source_target_pairs={{0,16},{8,24},{16,0},{24,8},{1,17},{9,25},{17,1},{25,9},{2,18},{10... | collective-permute-start | bytes 2359304 | tf_op jit(solution)/shard_map/ppermute | solution.py:762
  131.9 29.7 %collective-permute-start.20 = (bf16[4,32,3072]{2,1,0:T(8,128)(2,1)}, bf16[4,32,3072]{2,1,0:T(8,128)(2,1)}, u32[]{:S(2)}, u32[]{:S(2)}) collective-permute-start(bf16[4,32,3072]{2,1,0:T(8,128)(2,1)} %copy-done.8), channel_id=1, source_target_pairs={{0,8},{8,0},{16,24},{24,16},{1,9},{9,1},{17,25},{25,17},{2,10},{10... | collective-permute-start | bytes 2359304 | tf_op jit(solution)/shard_map/ppermute | solution.py:762
  131.9 29.7 %collective-permute-start.19 = (bf16[4,32,3072]{2,1,0:T(8,128)(2,1)S(1)}, bf16[4,32,3072]{2,1,0:T(8,128)(2,1)}, u32[]{:S(2)}, u32[]{:S(2)}) collective-permute-start(bf16[4,32,3072]{2,1,0:T(8,128)(2,1)S(1)} %collective-permute-done.15.refs_1_), channel_id=1, source_target_pairs={{0,8},{8,0},{16,24},{24,16},{1,9},{9,1},{17,25},{25,17},{2,10},{10... | collective-permute-start | bytes 2359304 | tf_op jit(solution)/shard_map/ppermute | solution.py:762
  132.4 29.2 %collective-permute-start.18 = (bf16[4,32,3072]{2,1,0:T(8,128)(2,1)S(1)}, bf16[4,32,3072]{2,1,0:T(8,128)(2,1)}, u32[]{:S(2)}, u32[]{:S(2)}) collective-permute-start(bf16[4,32,3072]{2,1,0:T(8,128)(2,1)S(1)} %pad_maximum_fusion.2.refs_0_), channel_id=1, source_target_pairs={{0,8},{8,0},{16,24},{24,16},{1,9},{9,1},{17,25},{25,17},{2,10},{10... | collective-permute-start | bytes 2359304 | tf_op jit(solution)/shard_map/ppermute | solution.py:762
  151.3 10.3 %collective-permute-start.21 = (bf16[4,32,3072]{2,1,0:T(8,128)(2,1)}, bf16[4,32,3072]{2,1,0:T(8,128)(2,1)}, u32[]{:S(2)}, u32[]{:S(2)}) collective-permute-start(bf16[4,32,3072]{2,1,0:T(8,128)(2,1)} %collective-permute-done.17.refs_3_), channel_id=1, source_target_pairs={{0,8},{8,0},{16,24},{24,16},{1,9},{9,1},{17,25},{25,17},{2,10},{10... | collective-permute-start | bytes 2359304 | tf_op jit(solution)/shard_map/ppermute | solution.py:762
  155.4 20.5 %all-to-all-start.1 = ((bf16[8,128,128]{2,1,0:T(8,128)(2,1)}), bf16[8,128,128]{2,1,0:T(8,128)(2,1)S(1)}, u32[]{:S(2)}, u32[]{:S(2)}) async-start(bf16[8,128,128]{2,1,0:T(8,128)(2,1)} %state_prefix.1), calls=%async_computation.1 | async-start | bytes 524288 | tf_op jit(solution)/shard_map/all_to_all | solution.py:1017
  161.1 230.4 %reduce-scatter.3.cloned.1.call-start = ((), (), s32[]{:S(2)}) async-start(), calls=%async_computation.8 | async-start | bytes 6488064 | tf_op jit(solution)/shard_map/reduce_scatter | solution.py:971
  233.2 9.8 %collective-permute-start.23 = (bf16[1024,2816]{1,0:T(8,128)(2,1)}, bf16[1024,2816]{1,0:T(8,128)(2,1)}, u32[]{:S(2)}, u32[]{:S(2)}) collective-permute-start(bf16[1024,2816]{1,0:T(8,128)(2,1)} %convolution_convert_fusion), channel_id=1, source_target_pairs={{0,8},{8,0},{16,24},{24,16},{1,9},{9,1},{17,25},{25,17},{2,10},{10... | collective-permute-start | bytes 17301512 | tf_op jit(solution)/shard_map/ppermute | solution.py:762
  238.8 19.3 %collective-permute-start.22 = (bf16[2816,512]{1,0:T(8,128)(2,1)}, bf16[2816,512]{1,0:T(8,128)(2,1)}, u32[]{:S(2)}, u32[]{:S(2)}) collective-permute-start(bf16[2816,512]{1,0:T(8,128)(2,1)} %convolution_convert_fusion.1), channel_id=1, source_target_pairs={{0,8},{8,0},{16,24},{24,16},{1,9},{9,1},{17,25},{25,17},{2,10},{10... | collective-permute-start | bytes 8650760 | tf_op jit(solution)/shard_map/ppermute | solution.py:762
  274.9 21.7 %all-to-all-start.2 = ((bf16[8,128,128]{2,1,0:T(8,128)(2,1)}), bf16[8,128,128]{2,1,0:T(8,128)(2,1)S(1)}, u32[]{:S(2)}, u32[]{:S(2)}) async-start(bf16[8,128,128]{2,1,0:T(8,128)(2,1)} %get-tuple-element.147), calls=%async_computation.2 | async-start | bytes 524288 | tf_op jit(solution)/shard_map/all_to_all | solution.py:1017
  305.7 4.4 collective-permute-start.24
  305.7 13.3 %all-to-all-start.3 = ((bf16[8,128,128]{2,1,0:T(8,128)(2,1)}), bf16[8,128,128]{2,1,0:T(8,128)(2,1)S(1)}, u32[]{:S(2)}, u32[]{:S(2)}) async-start(bf16[8,128,128]{2,1,0:T(8,128)(2,1)} %state_suffix.1), calls=%async_computation.3 | async-start | bytes 524288 | tf_op jit(solution)/shard_map/all_to_all | solution.py:1017
  309.2 155.5 %reduce-scatter.5.cloned.1.call-start = ((), (), s32[]{:S(2)}) async-start(), calls=%async_computation.9 | async-start | bytes 3244032 | tf_op jit(solution)/shard_map/reduce_scatter | solution.py:971
  319.8 21.2 %collective-permute-start.26 = (bf16[2,2,128,512]{3,2,1,0:T(8,128)(2,1)S(1)}, bf16[2,2,128,512]{3,2,1,0:T(8,128)(2,1)S(1)}, u32[]{:S(2)}, u32[]{:S(2)}) collective-permute-start(bf16[2,2,128,512]{3,2,1,0:T(8,128)(2,1)S(1)} %dynamic-slice_bitcast_fusion.2), channel_id=1, source_target_pairs={{0,1},{1,0},{2,3},{3,2},{4,5},{5,4},{6,7},{7,6},{8,9},{9,8},{10,11... | collective-permute-start | bytes 1572872 | tf_op jit(solution)/shard_map/ppermute | solution.py:762
  321.3 19.8 %collective-permute-start.25 = (bf16[2,2,2,64,512]{4,3,2,1,0:T(8,128)(2,1)S(1)}, bf16[2,2,2,64,512]{4,3,2,1,0:T(8,128)(2,1)S(1)}, u32[]{:S(2)}, u32[]{:S(2)}) collective-permute-start(bf16[2,2,2,64,512]{4,3,2,1,0:T(8,128)(2,1)S(1)} %dynamic-slice_bitcast_fusion.3), channel_id=1, source_target_pairs={{0,16},{8,24},{16,0},{24,8},{1,17},{9,25},{17,1},{25,9},{2,18},{10... | collective-permute-start | bytes 1572872 | tf_op jit(solution)/shard_map/ppermute | solution.py:762
  347.0 14.5 %collective-permute-start.27 = (bf16[1024,1152]{1,0:T(8,128)(2,1)}, bf16[1024,1152]{1,0:T(8,128)(2,1)}, u32[]{:S(2)}, u32[]{:S(2)}) collective-permute-start(bf16[1024,1152]{1,0:T(8,128)(2,1)} %convolution_convert_fusion.2), channel_id=1, source_target_pairs={{0,8},{8,0},{16,24},{24,16},{1,9},{9,1},{17,25},{25,17},{2,10},{10... | collective-permute-start | bytes 7077896 | tf_op jit(solution)/shard_map/ppermute | solution.py:762
  350.6 15.1 %collective-permute-start.29 = (bf16[2,2,64,512]{3,2,1,0:T(8,128)(2,1)S(1)}, bf16[2,2,64,512]{3,2,1,0:T(8,128)(2,1)S(1)}, u32[]{:S(2)}, u32[]{:S(2)}) collective-permute-start(bf16[2,2,64,512]{3,2,1,0:T(8,128)(2,1)S(1)} %dynamic-slice_bitcast_fusion.8), channel_id=1, source_target_pairs={{0,16},{8,24},{16,0},{24,8},{1,17},{9,25},{17,1},{25,9},{2,18},{10... | collective-permute-start | bytes 786440 | tf_op jit(solution)/shard_map/ppermute | solution.py:762
  353.5 12.1 %collective-permute-start.28 = (bf16[2,2,64,512]{3,2,1,0:T(8,128)(2,1)S(1)}, bf16[2,2,64,512]{3,2,1,0:T(8,128)(2,1)S(1)}, u32[]{:S(2)}, u32[]{:S(2)}) collective-permute-start(bf16[2,2,64,512]{3,2,1,0:T(8,128)(2,1)S(1)} %dynamic-slice_bitcast_fusion.9), channel_id=1, source_target_pairs={{0,1},{1,0},{2,3},{3,2},{4,5},{5,4},{6,7},{7,6},{8,9},{9,8},{10,11... | collective-permute-start | bytes 786440 | tf_op jit(solution)/shard_map/ppermute | solution.py:762
  368.4 21.1 %collective-permute-start.30 = (bf16[2,64,1024]{2,1,0:T(8,128)(2,1)S(1)}, bf16[2,64,1024]{2,1,0:T(8,128)(2,1)}, u32[]{:S(2)}, u32[]{:S(2)}) collective-permute-start(bf16[2,64,1024]{2,1,0:T(8,128)(2,1)S(1)} %dynamic-slice_bitcast_fusion.7), channel_id=1, source_target_pairs={{0,2},{1,3},{2,0},{3,1},{4,6},{5,7},{6,4},{7,5},{8,10},{9,11},{10,... | collective-permute-start | bytes 786440 | tf_op jit(solution)/shard_map/ppermute | solution.py:762
  369.1 20.3 %collective-permute-start.32 = (bf16[2,2,128,512]{3,2,1,0:T(8,128)(2,1)}, bf16[2,2,128,512]{3,2,1,0:T(8,128)(2,1)}, u32[]{:S(2)}, u32[]{:S(2)}) collective-permute-start(bf16[2,2,128,512]{3,2,1,0:T(8,128)(2,1)} %dynamic-slice_bitcast_fusion.1), channel_id=1, source_target_pairs={{0,1},{1,0},{2,3},{3,2},{4,5},{5,4},{6,7},{7,6},{8,9},{9,8},{10,11... | collective-permute-start | bytes 1572872 | tf_op jit(solution)/shard_map/ppermute | solution.py:762
  369.8 19.7 %collective-permute-start.31 = (bf16[2,2,2,64,640]{4,3,2,1,0:T(8,128)(2,1)}, bf16[2,2,2,64,640]{4,3,2,1,0:T(8,128)(2,1)}, u32[]{:S(2)}, u32[]{:S(2)}) collective-permute-start(bf16[2,2,2,64,640]{4,3,2,1,0:T(8,128)(2,1)} %dynamic-slice_bitcast_fusion), channel_id=1, source_target_pairs={{0,16},{8,24},{16,0},{24,8},{1,17},{9,25},{17,1},{25,9},{2,18},{10... | collective-permute-start | bytes 1966088 | tf_op jit(solution)/shard_map/ppermute | solution.py:762
  393.0 4.9 collective-permute-start.34
  395.1 4.2 collective-permute-start.33
  398.1 20.4 %collective-permute-start.39 = (bf16[2,2,2,64,128]{4,3,0,1,2:T(8,128)(2,1)S(1)}, bf16[2,2,2,64,128]{4,3,0,1,2:T(8,128)(2,1)S(1)}, u32[]{:S(2)}, u32[]{:S(2)}) collective-permute-start(bf16[2,2,2,64,128]{4,3,0,1,2:T(8,128)(2,1)S(1)} %bitcast.250), channel_id=1, source_target_pairs={{0,16},{8,24},{16,0},{24,8},{1,17},{9,25},{17,1},{25,9},{2,18},{10... | collective-permute-start | bytes 393224 | tf_op jit(solution)/shard_map/ppermute | solution.py:762
  402.8 15.7 %collective-permute-start.38 = (bf16[2,2,64,512]{3,2,1,0:T(8,128)(2,1)S(1)}, bf16[2,2,64,512]{3,2,1,0:T(8,128)(2,1)S(1)}, u32[]{:S(2)}, u32[]{:S(2)}) collective-permute-start(bf16[2,2,64,512]{3,2,1,0:T(8,128)(2,1)S(1)} %dynamic-slice_bitcast_fusion.6), channel_id=1, source_target_pairs={{0,16},{8,24},{16,0},{24,8},{1,17},{9,25},{17,1},{25,9},{2,18},{10... | collective-permute-start | bytes 786440 | tf_op jit(solution)/shard_map/ppermute | solution.py:762
  403.6 14.8 %collective-permute-start.37 = (bf16[2,2,64,640]{3,2,1,0:T(8,128)(2,1)S(1)}, bf16[2,2,64,640]{3,2,1,0:T(8,128)(2,1)S(1)}, u32[]{:S(2)}, u32[]{:S(2)}) collective-permute-start(bf16[2,2,64,640]{3,2,1,0:T(8,128)(2,1)S(1)} %dynamic-slice_bitcast_fusion.4), channel_id=1, source_target_pairs={{0,1},{1,0},{2,3},{3,2},{4,5},{5,4},{6,7},{7,6},{8,9},{9,8},{10,11... | collective-permute-start | bytes 983048 | tf_op jit(solution)/shard_map/ppermute | solution.py:762
  405.8 11.3 %collective-permute-start.35 = (bf16[8,1024]{1,0:T(8,128)(2,1)S(1)}, bf16[8,1024]{1,0:T(8,128)(2,1)S(1)}, u32[]{:S(2)}, u32[]{:S(2)}) collective-permute-start(bf16[8,1024]{1,0:T(8,128)(2,1)S(1)} %slice.353), channel_id=1, source_target_pairs={{1,0},{2,1},{3,2},{4,3},{5,4},{6,5},{7,6},{9,8},{10,9},{11,10},{12... | collective-permute-start | bytes 49160 | tf_op jit(solution)/shard_map/ppermute | solution.py:1001
  407.4 12.0 %collective-permute-start.36 = (bf16[2,2,2,64,384]{4,3,0,1,2:T(8,128)(2,1)S(1)}, bf16[2,2,2,64,384]{4,3,0,1,2:T(8,128)(2,1)S(1)}, u32[]{:S(2)}, u32[]{:S(2)}) collective-permute-start(bf16[2,2,2,64,384]{4,3,0,1,2:T(8,128)(2,1)S(1)} %bitcast.239), channel_id=1, source_target_pairs={{0,16},{8,24},{16,0},{24,8},{1,17},{9,25},{17,1},{25,9},{2,18},{10... | collective-permute-start | bytes 1179656 | tf_op jit(solution)/shard_map/ppermute | solution.py:762
  419.4 17.2 %collective-permute-start.44 = (bf16[128,2816]{1,0:T(8,128)(2,1)S(1)}, bf16[128,2816]{1,0:T(8,128)(2,1)S(1)}, u32[]{:S(2)}, u32[]{:S(2)}) collective-permute-start(bf16[128,2816]{1,0:T(8,128)(2,1)S(1)} %copy-done.55), channel_id=1, source_target_pairs={{0,16},{8,24},{16,0},{24,8},{1,17},{9,25},{17,1},{25,9},{2,18},{10... | collective-permute-start | bytes 2162696 | tf_op jit(solution)/shard_map/ppermute | solution.py:762
  420.2 9.4 %collective-permute-start.43 = (bf16[2,2,64,128]{3,2,0,1:T(8,128)(2,1)S(1)}, bf16[2,2,64,128]{3,2,0,1:T(8,128)(2,1)S(1)}, u32[]{:S(2)}, u32[]{:S(2)}) collective-permute-start(bf16[2,2,64,128]{3,2,0,1:T(8,128)(2,1)S(1)} %dynamic-slice_bitcast_fusion.14), channel_id=1, source_target_pairs={{0,1},{1,0},{2,3},{3,2},{4,5},{5,4},{6,7},{7,6},{8,9},{9,8},{10,11... | collective-permute-start | bytes 196616 | tf_op jit(solution)/shard_map/ppermute | solution.py:762
  421.7 7.8 %collective-permute-start.42 = (bf16[64,1024]{1,0:T(8,128)(2,1)S(1)}, bf16[64,1024]{1,0:T(8,128)(2,1)S(1)}, u32[]{:S(2)}, u32[]{:S(2)}) collective-permute-start(bf16[64,1024]{1,0:T(8,128)(2,1)S(1)} %dynamic-slice_bitcast_fusion.12), channel_id=1, source_target_pairs={{0,4},{1,5},{2,6},{3,7},{4,0},{5,1},{6,2},{7,3},{8,12},{9,13},{10,... | collective-permute-start | bytes 393224 | tf_op jit(solution)/shard_map/ppermute | solution.py:762
  424.6 9.2 %collective-permute-start.41 = (bf16[2,64,1152]{2,1,0:T(8,128)(2,1)S(1)}, bf16[2,64,1152]{2,1,0:T(8,128)(2,1)S(1)}, u32[]{:S(2)}, u32[]{:S(2)}) collective-permute-start(bf16[2,64,1152]{2,1,0:T(8,128)(2,1)S(1)} %dynamic-slice_bitcast_fusion.5), channel_id=1, source_target_pairs={{0,2},{1,3},{2,0},{3,1},{4,6},{5,7},{6,4},{7,5},{8,10},{9,11},{10,... | collective-permute-start | bytes 884744 | tf_op jit(solution)/shard_map/ppermute | solution.py:762
  425.3 7.7 %collective-permute-start.40 = (bf16[2,2,64,384]{3,2,0,1:T(8,128)(2,1)S(1)}, bf16[2,2,64,384]{3,2,0,1:T(8,128)(2,1)S(1)}, u32[]{:S(2)}, u32[]{:S(2)}) collective-permute-start(bf16[2,2,64,384]{3,2,0,1:T(8,128)(2,1)S(1)} %dynamic-slice_bitcast_fusion.10), channel_id=1, source_target_pairs={{0,1},{1,0},{2,3},{3,2},{4,5},{5,4},{6,7},{7,6},{8,9},{9,8},{10,11... | collective-permute-start | bytes 589832 | tf_op jit(solution)/shard_map/ppermute | solution.py:762
  436.6 4.3 collective-permute-start.48
  438.7 7.7 %collective-permute-start.46 = (bf16[64,1152]{1,0:T(8,128)(2,1)S(1)}, bf16[64,1152]{1,0:T(8,128)(2,1)S(1)}, u32[]{:S(2)}, u32[]{:S(2)}) collective-permute-start(bf16[64,1152]{1,0:T(8,128)(2,1)S(1)} %dynamic-slice_bitcast_fusion.11), channel_id=1, source_target_pairs={{0,4},{1,5},{2,6},{3,7},{4,0},{5,1},{6,2},{7,3},{8,12},{9,13},{10,... | collective-permute-start | bytes 442376 | tf_op jit(solution)/shard_map/ppermute | solution.py:762
  439.3 5.0 %collective-permute-start.45 = (bf16[2,64,384]{2,1,0:T(8,128)(2,1)S(1)}, bf16[2,64,384]{2,1,0:T(8,128)(2,1)S(1)}, u32[]{:S(2)}, u32[]{:S(2)}) collective-permute-start(bf16[2,64,384]{2,1,0:T(8,128)(2,1)S(1)} %dynamic-slice_bitcast_fusion.13), channel_id=1, source_target_pairs={{0,2},{1,3},{2,0},{3,1},{4,6},{5,7},{6,4},{7,5},{8,10},{9,11},{10,... | collective-permute-start | bytes 294920 | tf_op jit(solution)/shard_map/ppermute | solution.py:762
  446.5 4.8 collective-permute-start.49
  446.7 8.2 %collective-permute-start.47 = (bf16[64,384]{1,0:T(8,128)(2,1)S(1)}, bf16[64,384]{1,0:T(8,128)(2,1)S(1)}, u32[]{:S(2)}, u32[]{:S(2)}) collective-permute-start(bf16[64,384]{1,0:T(8,128)(2,1)S(1)} %dynamic-slice_bitcast_fusion.15), channel_id=1, source_target_pairs={{0,4},{1,5},{2,6},{3,7},{4,0},{5,1},{6,2},{7,3},{8,12},{9,13},{10,... | collective-permute-start | bytes 147464 | tf_op jit(solution)/shard_map/ppermute | solution.py:762
  455.0 10.4 %collective-permute-start.50 = (bf16[64,2688]{1,0:T(8,128)(2,1)S(1)}, bf16[64,2688]{1,0:T(8,128)(2,1)S(1)}, u32[]{:S(2)}, u32[]{:S(2)}) collective-permute-start(bf16[64,2688]{1,0:T(8,128)(2,1)S(1)} %pad_maximum_fusion.6), channel_id=1, source_target_pairs={{0,16},{8,24},{16,0},{24,8},{1,17},{9,25},{17,1},{25,9},{2,18},{10... | collective-permute-start | bytes 1032200 | tf_op jit(solution)/shard_map/ppermute | solution.py:762
  455.2 19.7 %collective-permute-start.52 = (bf16[128,2816]{1,0:T(8,128)(2,1)S(1)}, bf16[128,2816]{1,0:T(8,128)(2,1)}, u32[]{:S(2)}, u32[]{:S(2)}) collective-permute-start(bf16[128,2816]{1,0:T(8,128)(2,1)S(1)} %add_convert_fusion.5), channel_id=1, source_target_pairs={{0,8},{8,0},{16,24},{24,16},{1,9},{9,1},{17,25},{25,17},{2,10},{10... | collective-permute-start | bytes 2162696 | tf_op jit(solution)/shard_map/ppermute | solution.py:762
  464.6 9.1 %collective-permute-start.53 = (bf16[352,512]{1,0:T(8,128)(2,1)}, bf16[352,512]{1,0:T(8,128)(2,1)}, u32[]{:S(2)}, u32[]{:S(2)}) collective-permute-start(bf16[352,512]{1,0:T(8,128)(2,1)} %reduce-scatter.5.cloned.1.call-done), channel_id=1, source_target_pairs={{0,16},{8,24},{16,0},{24,8},{1,17},{9,25},{17,1},{25,9},{2,18},{10... | collective-permute-start | bytes 1081352 | tf_op jit(solution)/shard_map/ppermute | solution.py:762
  465.5 14.5 %collective-permute-start.51 = (bf16[128,2688]{1,0:T(8,128)(2,1)S(1)}, bf16[128,2688]{1,0:T(8,128)(2,1)S(1)}, u32[]{:S(2)}, u32[]{:S(2)}) collective-permute-start(bf16[128,2688]{1,0:T(8,128)(2,1)S(1)} %maximum_select_fusion.1), channel_id=1, source_target_pairs={{0,8},{8,0},{16,24},{24,16},{1,9},{9,1},{17,25},{25,17},{2,10},{10... | collective-permute-start | bytes 2064392 | tf_op jit(solution)/shard_map/ppermute | solution.py:762
  474.9 3.8 collective-permute-start.54
  (80 other events, 488.6 us)
Sparse Core Ops, SparseCore 0:
  11.5 104.8 all-gather.2
  126.1 72.3 all-gather.4
  250.1 128.8 reduce-scatter.2
  382.4 82.2 reduce-scatter.4

commit v6 on v5

--- a/solution.py
+++ b/solution.py
@@ -1140,10 +1140,11 @@
             axis=2,
         )
     owned = swap(moves)
-    second.move("zyxc", after=[owned])
+    states = scan_states(owned)
+    second.move("zyxc", after=[states])
+    entry = swap(states)
     qg_full, outw_full = second.place()
     qg_pre = jnp.dot(normed_ext, qg_full, preferred_element_type=F32)
-    entry = swap(scan_states(owned))
     if fanout > 1:
         entry = to_heads(entry, fanout)
     query_low, q_mixed, gated_low, attn_heads, fresh, kept = delta_forward(
@@ -1176,11 +1177,12 @@
     middle_grad = cotangent.astype(F32) + middle_back
     middle_low = middle_grad.astype(BF)
     gated_grad = contract(middle_low, outw_full, 1, 1)
+    ours = hold(ours, down_sum.away)
     pair_half = (contract(normed_two_low, ours, 0, 0) + pair_sum.came.astype(F32)).astype(BF)
     pair_apart = scatter_owners(pair_half)
-    down_half = (contract(hidden_low, down_ours, 0, 0) + down_sum.came.astype(F32)).astype(BF)
-    down_apart = scatter_owners(down_half)
-    gated_grad = hold(gated_grad, down_half, pair_half)
+    down_sum.take(contract(hidden_low, down_ours, 0, 0))
+    gated_grad = hold(gated_grad, down_sum.part, pair_half)
+    down_sum.go("x")
     heads_grad, gatepre_low, outgain_grad, local_later = delta_adjoint(
         query_low, key_low, w, cols, rows, gated_grad, attn_heads, qg_pre, outgain_scale, heads
     )
@@ -1188,17 +1190,19 @@
         local_later = to_owners(local_later, fanout)
     came_later = swap(local_later)
 
+    middle_held, gatepre_held = hold((middle_low, gatepre_low), local_later)
+    out_grad = contract(gated_low, middle_held, 0, 0)
+    gate_grad = contract(normed_low, gatepre_held, 0, 0)
+    other_sum = Reduce(here)
+    other_sum.swap(by_core(here, gate_grad, out_grad))
+    came_later = hold(came_later, other_sum.away)
     summed_later = scan_grads(owned, came_later)
     later = swap(summed_later)
     if fanout > 1:
         later = to_heads(later, fanout)
-    middle_held, gatepre_held = hold((middle_low, gatepre_low), summed_later)
-    out_grad = contract(gated_low, middle_held, 0, 0)
-    gate_grad = contract(normed_low, gatepre_held, 0, 0)
-    other_sum = Reduce(here)
-    other_sum.swap(by_core(here, gate_grad, out_grad))
     other_sum.take(by_core(here, out_grad, gate_grad))
-    later = hold(later, other_sum.part)
+    later = meet(hold(later, other_sum.part), down_sum)
+    down_apart = scatter_owners(down_sum.part.reshape(-1, width // 2))
     other_x, other_y = other_sum.two(width // 2)
     other_x.go("x", later)
     other_y.go("y", later)
@@ -1226,6 +1230,13 @@
         1, *state, later, q_mixed, qg_pre, query_taps, kv_mixed, kv_pre, kv_taps, heads
     )
     mixed_b = hold(meet(mixed_b, other_sum, a_x, a_y), pair_apart)
+    a_x.go("y")
+    a_y.go("x")
+    b_sum = Reduce(here)
+    theirs, ours = shares(mixed_b, 0, 3 * cut[1])
+    b_sum.swap(contract(normed_ext, theirs, 0, 0))
+    taps_b, beta_b = hold((taps_b, beta_b), b_sum.away)
+
     def by_kind(first_heads, other_heads):
         pieces = []
         for i in range(3):
@@ -1245,15 +1256,10 @@
     small_sum = Reduce(here)
     small_sum.begin(contract(normed_low, hold(betapre_low, mixed_b), 0, 0) + extra)
     small_sum.both()
-    b_sum = Reduce(here)
-    theirs, ours = shares(mixed_b, 0, 3 * cut[1])
-    b_sum.swap(contract(normed_ext, theirs, 0, 0))
     b_sum.take(contract(normed_ext, ours, 0, 0))
     small_sum.end()
     mixed_b = hold(mixed_b, b_sum.part, small_sum.part)
     b_sum.go("x")
-    a_x.go("y", mixed_b)
-    a_y.go("x", mixed_b)
     small_sum.go("x")
     wide_grad = (
         contract(mixed_a[:, cut[0] :], kv_full[:, : 2 * cut[0]], 1, 1)
@@ -1282,22 +1288,27 @@
     b_sum.go("w", input_grad)
     a_sum.go("v", input_grad)
     small_sum.go("w", input_grad)
-    for one in (b_sum, a_sum, small_sum):
-        one.end()
+    def gain_grad(gain, pairs):
+        total = sum(jnp.sum(weight.astype(F32) * grad, axis=1) for weight, grad in pairs)
+        return total / gain.astype(F32)
+
+    other = here.send(pair_sum.part, "c")
+    hidgate_total = by_core(here, pair_sum.part, other).astype(F32)
+    hidup_total = by_core(here, other, pair_sum.part).astype(F32)
+    ffngain_total = gain_grad(ffn_gain, ((ffn_gate, hidgate_total), (ffn_up, hidup_total)))
+    hidgate_total, hidup_total, ffngain_total = meet(
+        (hidgate_total, hidup_total, ffngain_total), b_sum, a_sum, small_sum
+    )
     b_sum.go("v", a_sum.part)
     small_sum.go("v", a_sum.part)
-    pair_part = hold(pair_sum.part, a_sum.part)
-    other = here.send(pair_part, "c")
     held = meet(a_sum.part, b_sum, small_sum)
     both = Reduce(here)
     both.part = jnp.concatenate([b_sum.part, held, other_sum.part, small_sum.part], axis=1)
     both.split = True
     both.rows()
-    down_sum.begin_x(down_apart, held)
-    down_sum.end()
+    down_sum.part = hold(down_apart, held)
+    down_sum.rows()
     down_total = join_way(here, down_sum.part, "c", 1).astype(F32)
-    hidgate_total = by_core(here, pair_part, other).astype(F32)
-    hidup_total = by_core(here, other, pair_part).astype(F32)
     whole = both.other()
     ends = [0]
     for one in (b_sum, a_sum, other_sum, small_sum):
@@ -1313,14 +1324,9 @@
     extra = both.part[:, ends[3] :].astype(F32)
     beta_total = extra[:, :heads]
 
-    def gain_grad(gain, pairs):
-        total = sum(jnp.sum(weight.astype(F32) * grad, axis=1) for weight, grad in pairs)
-        return total / gain.astype(F32)
-
     attngain_total = gain_grad(
         attn_gain, ((qkv_weight, qkv_total), (beta_weight, beta_total), (gate_weight, gate_total))
     )
-    ffngain_total = gain_grad(ffn_gain, ((ffn_gate, hidgate_total), (ffn_up, hidup_total)))
     flat = extra[:, heads : heads + columns].reshape(-1)
     cut, at = [], 0
     for part in parts:

time: 501 us -> 498 us (level)
  starting transfers between devices: 78.5 us -> 84 us
    all_to_all x4, waiting for transfers between devices: 20.5 us -> 37.9 us  [swap(): return lax.all_to_all(value, 'fsdp', 0, 0, tiled=True)]
    reduce_scatter x2, waiting for transfers between devices: 9.3 us -> 0.04 us  [scatter_owners(): return lax.psum_scatter(array, 'fsdp', scatter_dimension=0, tiled=True)]
    ppermute x52 -> x53, starting transfers between devices: 51.6 us -> 59.3 us  [send(): return lax.ppermute(value, axis, pairs)]
    ppermute x52 -> x53, waiting for transfers between devices: 79.6 us -> 72.4 us  [send(): return lax.ppermute(value, axis, pairs)]
    ppermute x3, waiting for transfers between devices: 8.54 us -> 2.77 us  [from_behind(): lax.ppermute(value, 'fsdp', [(source, source + steps) for source in range...]
    unnamed x172 -> x168, local copies, waits for them, and re-layouts: 24.5 us -> 20.3 us
  transfers between devices with their start and end apart: 63 -> 64, of which waited for: 23 -> 25; matrix products, arithmetic and copies ran while one was open for 25% -> 23% of each run, Pallas kernels for 18% -> 18%
where the time goes in v6:
time: 498 us; the launch traced here: 489 us
  waiting for transfers between devices  122 us (24%)
  Pallas kernels  116 us (23%)
  starting transfers between devices  84 us (17%)
  matrix products  74.1 us (15%)
  other arithmetic  40.8 us (8%)
  local copies, waits for them, and re-layouts  35.7 us (7%)
  between operations  15.8 us (3%)
    ppermute x53, waiting for transfers between devices, send(): return lax.ppermute(value, axis, pairs)  72.4 us
    dot_general x18, matrix products, contract(): lax.dot_general(left, right, (((left_dim,), (right_dim,)), ((), ())), pre...  60 us
    ppermute x53, starting transfers between devices, send(): return lax.ppermute(value, axis, pairs)  59.3 us
    all_to_all x4, waiting for transfers between devices, swap(): return lax.all_to_all(value, 'fsdp', 0, 0, tiled=True)  37.9 us
    pallas_call x2, Pallas kernels, delta_backward(): pl.pallas_call(partial(backward_kernel, heads, part, d), grid=(blocks + 1...  31.6 us
    pallas_call x1, Pallas kernels, feed_forward(): pl.pallas_call(feed_kernel, grid=(blocks + 1,), in_specs=[whole, whole, w...  28 us
    pallas_call x1, Pallas kernels, delta_summary(): pl.pallas_call(partial(summary_kernel, heads, d), grid=(blocks,), in_spec...  21.5 us
    unnamed x168, local copies, waits for them, and re-layouts  20.3 us
  transfers between devices with their start and end apart: 64, of which 25 were waited for; matrix products, arithmetic and copies ran while one was open for 23% of the time, Pallas kernels for 18%

profile of v6, /device:TPU:0, one launch (start us, length us, event | category | flops | bytes accessed | tf_op | source)
XLA Modules:
  0.0 489.0 jit_solution(9667430423705362254)
XLA Ops:
  10.2 4.1 collective-permute-start.1
  16.0 3.4 collective-permute-start.4
  20.1 2.3 collective-permute-start.3
  23.0 6.9 %collective-permute-done.2 = bf16[32,2176]{1,0:T(8,128)(2,1)S(1)} collective-permute-done((bf16[32,2176]{1,0:T(8,128)(2,1)S(1)}, bf16[32,2176]{1,0:T(8,128)(2,1)S(1)}, u32[]{:S(2)}, u32[]{:S(2)}) %collective-permute-start.2) | collective-permute-done | bytes 139296 | tf_op jit(solution)/shard_map/ppermute | solution.py:762
  34.4 5.7 %collective-permute-done.5.refs_1_ = bf16[4,32,2176]{2,1,0:T(8,128)(2,1)S(1)} collective-permute-done((bf16[4,32,2176]{2,1,0:T(8,128)(2,1)S(1)}, bf16[4,32,2176]{2,1,0:T(8,128)(2,1)S(1)}, u32[]{:S(2)}, u32[]{:S(2)}) %collective-permute-start.5) | collective-permute-done | bytes 557088 | tf_op jit(solution)/shard_map/ppermute | solution.py:762
  40.1 4.2 collective-permute-done.6.refs_2_
  44.3 2.2 collective-permute-start.8
  48.4 2.6 collective-permute-start.13
  51.1 6.0 %collective-permute-start.12 = (bf16[32,3072]{1,0:T(8,128)(2,1)}, bf16[32,3072]{1,0:T(8,128)(2,1)}, u32[]{:S(2)}, u32[]{:S(2)}) collective-permute-start(bf16[32,3072]{1,0:T(8,128)(2,1)} %constant_dynamic-slice_fusion.5), channel_id=1, source_target_pairs={{0,2},{1,3},{2,0},{3,1},{4,6},{5,7},{6,4},{7,5},{8,10},{9,11},{10,... | collective-permute-start | bytes 589832 | tf_op jit(solution)/shard_map/ppermute | solution.py:762
  57.0 6.8 %collective-permute-done.8.refs_4_ = bf16[4,32,2176]{2,1,0:T(8,128)(2,1)} collective-permute-done((bf16[4,32,2176]{2,1,0:T(8,128)(2,1)S(1)}, bf16[4,32,2176]{2,1,0:T(8,128)(2,1)}, u32[]{:S(2)}, u32[]{:S(2)}) %collective-permute-start.8) | collective-permute-done | bytes 557088 | tf_op jit(solution)/shard_map/ppermute | solution.py:762
  69.8 3.4 place_weights.2
  80.1 6.7 %fusion.98.pre_ref.prev_ref.kvpre_ref.kvrim_ref = f32[520,2048]{1,0:T(8,128)} fusion(bf16[520,1024]{1,0:T(8,128)(2,1)S(1)} %fusion.7, bf16[1024,2048]{1,0:T(8,128)(2,1)} %copy-done.4), kind=kOutput, calls=%fused_computation.231 | convolution fusion | flops 2181038080 | bytes 9519104 | tf_op jit(solution)/shard_map/dot_general | solution.py:1103
  87.4 11.3 %collective-permute-done.14 = bf16[32,3072]{1,0:T(8,128)(2,1)S(1)} collective-permute-done((bf16[32,3072]{1,0:T(8,128)(2,1)}, bf16[32,3072]{1,0:T(8,128)(2,1)S(1)}, u32[]{:S(2)}, u32[]{:S(2)}) %collective-permute-start.14) | collective-permute-done | bytes 196640 | tf_op jit(solution)/shard_map/ppermute | solution.py:762
  100.4 2.4 collective-permute-start.16
  102.9 21.5 %delta_summary.1 = (bf16[512,1024]{1,0:T(8,128)(2,1)}, bf16[512,1024]{1,0:T(8,128)(2,1)}, f32[512,2048]{1,0:T(8,128)}, bf16[512,1024]{1,0:T(8,128)(2,1)}, bf16[5...) custom-call(f32[520,2048]{1,0:T(8,128)} %fusion.98.pre_ref.prev_ref.kvpre_ref.kvrim_ref, ...), custom_call_target="tpu_custom_call" | custom-call | flops 20999999488 | bytes 63000000 | tf_op jit(solution)/shard_map/delta_summary/pallas_call | solution.py:453
  125.9 5.5 %all-to-all-start = ((bf16[8,128,256]{2,1,0:T(8,128)(2,1)}), bf16[8,128,256]{2,1,0:T(8,128)(2,1)S(1)}, u32[]{:S(2)}, u32[]{:S(2)}) async-start(bf16[8,128,256]{2,1,0:T(8,128)(2,1)} %get-tuple-element.131), calls=%async_computation | async-start | bytes 1048576 | tf_op jit(solution)/shard_map/all_to_all | solution.py:1017
  132.3 16.8 %all-to-all-done.x_ref.t_ref = bf16[8,128,256]{2,1,0:T(8,128)(2,1)S(1)} async-done(((bf16[8,128,256]{2,1,0:T(8,128)(2,1)}), bf16[8,128,256]{2,1,0:T(8,128)(2,1)S(1)}, u32[]{:S(2)}, u32[]{:S(2)}) %all-to-all-start) | async-done | bytes 524320 | tf_op jit(solution)/shard_map/all_to_all | solution.py:1017
  150.0 2.7 state_prefix.1
  154.0 4.4 all-to-all-start.1
  160.0 4.2 place_weights.3
  167.5 4.4 fusion.99.pre_ref.prev_ref.gate_ref.qpre_ref.qrim_ref
  172.9 11.3 %delta_forward.1 = (bf16[512,1024]{1,0:T(8,128)(2,1)}, f32[512,1024]{1,0:T(8,128)}, bf16[512,1024]{1,0:T(8,128)(2,1)}, f32[512,1024]{1,0:T(8,128)}, bf16[512,102...) custom-call(f32[520,2048]{1,0:T(8,128)} %fusion.99.pre_ref.prev_ref.gate_ref.qpre_ref.qrim_ref, ...), custom_call_target="tpu_custom_call" | custom-call | flops 11000000512 | bytes 33000000 | tf_op jit(solution)/shard_map/delta_forward/pallas_call | solution.py:496
  184.2 2.6 multiply_reduce_fusion.1
  189.4 9.2 %all-gather.5.cloned.1.call-done.d_ref.db_ref = bf16[2816,1024]{1,0:T(8,128)(2,1)} async-done(((bf16[88,1024]{1,0:T(8,128)(2,1)}), bf16[2816,1024]{1,0:T(8,128)(2,1)}) %all-gather.5.cloned.1.call-update) | async-done | bytes 5767184 | tf_op jit(solution)/shard_map/all_gather | solution.py:967
  198.6 28.0 %feed_forward.1 = (bf16[512,2816]{1,0:T(8,128)(2,1)}, bf16[2,512,2816]{2,1,0:T(8,128)(2,1)}, bf16[512,1024]{1,0:T(8,128)(2,1)}, f32[512,1024]{1,0:T(8,128)}) custom-call(bf16[512,1024]{1,0:T(8,128)(2,1)} %multiply_convert_fusion.n_ref, bf16[512,1024]{1,0:T(8,128)(2,1)} %e_ref.1, f32[512,1024]{1,0:T(8,128)} %copy-done.17, ...), custom_call_target="tpu_custom_call" | custom-call | flops 24999999488 | bytes 75000000 | tf_op jit(solution)/shard_map/feed_forward/pallas_call | solution.py:692
  226.6 6.8 %convolution_convert_fusion = bf16[1024,2816]{1,0:T(8,128)(2,1)} fusion(bf16[512,1024]{1,0:T(8,128)(2,1)S(1)} %copy-done.44, bf16[2,512,2816]{2,1,0:T(8,128)(2,1)} %get-tuple-element.152, s32[]{:T(128)S(6)} %select_n.653), kind=kOutput, calls=%fused_computation.2 | convolution fusion | flops 2955673600 | bytes 9699332 | tf_op jit(solution)/shard_map/dot_general | solution.py:983
  233.8 5.4 %convolution_convert_fusion.1 = bf16[2816,512]{1,0:T(8,128)(2,1)} fusion(bf16[512,2816]{1,0:T(8,128)(2,1)} %get-tuple-element.151, bf16[512,1024]{1,0:T(8,128)(2,1)} %e_ref.1, s32[]{:T(128)S(6)} %select_n.651), kind=kOutput, calls=%fused_computation.4 | convolution fusion | flops 1477836800 | bytes 6291460 | tf_op jit(solution)/shard_map/dot_general | solution.py:983
  239.3 3.9 collective-permute-done.23
  243.2 7.1 %add_convert_fusion = bf16[1024,2816]{1,0:T(8,128)(2,1)} fusion(bf16[1024,2816]{1,0:T(8,128)(2,1)} %collective-permute-done.23, bf16[512,1024]{1,0:T(8,128)(2,1)S(1)} %copy-done.45, bf16[512,2816]{1,0:T(8,128)(2,1)S(1)} %dynamic-slice_bitcast_fusion), kind=kOutput, calls=%fused_computation | convolution fusion | flops 2961440768 | bytes 15466496 | tf_op jit(solution)/shard_map/dot_general | solution.py:983
  250.7 2.7 multiply_reduce_fusion
  256.0 2.6 fusion.100.dy_ref
  258.8 5.2 %add_convert_fusion.1 = bf16[2816,512]{1,0:T(8,128)(2,1)} fusion(bf16[2816,512]{1,0:T(8,128)(2,1)} %collective-permute-done.22, bf16[512,2816]{1,0:T(8,128)(2,1)S(1)} %copy-done.76, bf16[512,1024]{1,0:T(8,128)(2,1)S(1)} %copy-done.28, s32[]{:T(128)S(6)} %select_n.650), kind=kOutput, calls=%fused_computation.1 | convolution fusion | flops 1480720384 | bytes 9175044 | tf_op jit(solution)/shard_map/dot_general | solution.py:983
  264.0 10.9 %delta_adjoint.1 = (bf16[512,1024]{1,0:T(8,128)(2,1)}, bf16[512,1024]{1,0:T(8,128)(2,1)}, f32[1,128]{1,0:T(1,128)}, bf16[8,128,128]{2,1,0:T(8,128)(2,1)}) custom-call(bf16[512,1024]{1,0:T(8,128)(2,1)} %get-tuple-element.146.q_ref, bf16[512,1024]{1,0:T(8,128)(2,1)} %get-tuple-element.138.k_ref, bf16[512,1024]{1,0:T(8,128)(2,1)} %get-tuple-element.139.w_ref, ...), custom_call_target="tpu_custom_call" | custom-call | flops 11000000512 | bytes 33000000 | tf_op jit(solution)/shard_map/delta_adjoint/pallas_call | solution.py:532
  276.5 4.0 select_convert_fusion
  281.0 2.6 dynamic-slice_bitcast_fusion.1
  285.2 3.6 all-to-all-start.2
  288.8 17.4 %all-to-all-done.2.g_ref = bf16[8,128,128]{2,1,0:T(8,128)(2,1)S(1)} async-done(((bf16[8,128,128]{2,1,0:T(8,128)(2,1)}), bf16[8,128,128]{2,1,0:T(8,128)(2,1)S(1)}, u32[]{:S(2)}, u32[]{:S(2)}) %all-to-all-start.2) | async-done | bytes 262176 | tf_op jit(solution)/shard_map/all_to_all | solution.py:1017
  306.9 2.8 state_suffix.1
  309.7 3.4 all-to-all-start.3
  314.5 4.1 add_convert_fusion.3
  318.6 3.4 all-to-all-done.3.s_ref
  325.9 19.0 %delta_backward.2 = (bf16[520,2304]{1,0:T(8,128)(2,1)}, f32[512,128]{1,0:T(8,128)}, f32[4,2304]{1,0:T(4,128)}) custom-call(bf16[512,1024]{1,0:T(8,128)(2,1)} %get-tuple-element.146.q_ref, bf16[512,1024]{1,0:T(8,128)(2,1)} %get-tuple-element.138.k_ref, bf16[512,1024]{1,0:T(8,128)(2,1)} %get-tuple-element.147.v_ref, ...), custom_call_target="tpu_custom_call" | custom-call | flops 20000000000 | bytes 60000000 | tf_op jit(solution)/shard_map/delta_backward/pallas_call | solution.py:594
  345.0 5.1 %convolution_convert_fusion.2 = bf16[1024,1152]{1,0:T(8,128)(2,1)} fusion(bf16[520,1024]{1,0:T(8,128)(2,1)S(1)} %copy-done.27, bf16[520,2304]{1,0:T(8,128)(2,1)} %get-tuple-element.170, s32[]{:T(128)S(6)} %select_n.660), kind=kOutput, calls=%fused_computation.7 | convolution fusion | flops 1228013568 | bytes 4622340 | tf_op jit(solution)/shard_map/dot_general | solution.py:983
  351.3 3.4 fusion.2
  359.8 4.2 fusion.18
  364.1 3.2 fusion
  367.2 3.9 add_convert_fusion.2
  374.7 12.6 %delta_backward.3 = (bf16[520,768]{1,0:T(8,128)(2,1)}, f32[512,128]{1,0:T(8,128)}, f32[4,768]{1,0:T(4,128)}) custom-call(bf16[512,1024]{1,0:T(8,128)(2,1)} %get-tuple-element.146.q_ref, bf16[512,1024]{1,0:T(8,128)(2,1)} %get-tuple-element.138.k_ref, bf16[512,1024]{1,0:T(8,128)(2,1)} %get-tuple-element.147.v_ref, bf16[512,1024]{1,0:T(8,128)(2,1)} %get-tuple-element.139.w_ref, ...), custom_call_target="tpu_custom_call" | custom-call | flops 12000000000 | bytes 36000000 | tf_op jit(solution)/shard_map/delta_backward/pallas_call | solution.py:594
  387.2 2.1 collective-permute-done.32
  394.0 2.9 convolution_convert_fusion.3
  403.4 2.3 add_convert_fusion.4
  405.7 2.1 fusion.32
  411.5 2.8 collective-permute-done.36
  415.7 5.6 %collective-permute-done.37 = bf16[2,2,2,64,384]{4,3,0,1,2:T(8,128)(2,1)S(1)} collective-permute-done((bf16[2,2,2,64,384]{4,3,0,1,2:T(8,128)(2,1)S(1)}, bf16[2,2,2,64,384]{4,3,0,1,2:T(8,128)(2,1)S(1)}, u32[]{:S(2)}, u32[]{:S(2)}) %collective-permute-start.37) | collective-permute-done | bytes 393248 | tf_op jit(solution)/shard_map/ppermute | solution.py:762
  423.3 2.4 collective-permute-start.44
  429.4 2.1 collective-permute-start.41
  431.6 2.0 fusion.10
  435.2 2.8 collective-permute-done.42
  439.3 2.2 collective-permute-start.49
  445.2 2.1 multiply_reduce_fusion.3
  447.8 3.3 collective-permute-done.47
  451.1 3.1 collective-permute-done.48
  454.5 2.9 collective-permute-start.50
  461.9 8.6 %collective-permute-done.52 = bf16[64,2688]{1,0:T(8,128)(2,1)S(1)} collective-permute-done((bf16[64,2688]{1,0:T(8,128)(2,1)S(1)}, bf16[64,2688]{1,0:T(8,128)(2,1)S(1)}, u32[]{:S(2)}, u32[]{:S(2)}) %collective-permute-start.52) | collective-permute-done | bytes 344096 | tf_op jit(solution)/shard_map/ppermute | solution.py:762
  (411 shorter events, 108.3 us)
Async XLA Ops:
  7.3 118.0 %all-gather.3.cloned.1.call-start = ((), (), s32[]{:S(2)}) async-start(), calls=%async_computation.6 | async-start | bytes 11894784 | tf_op jit(solution)/shard_map/all_gather | solution.py:967
  9.3 189.4 %all-gather.5.cloned.1.call-start = ((), (), s32[]{:S(2)}) async-start(), calls=%async_computation.7 | async-start | bytes 5947392 | tf_op jit(solution)/shard_map/all_gather | solution.py:967
  10.2 12.2 %collective-permute-start.1 = (bf16[32,2176]{1,0:T(8,128)(2,1)S(1)}, bf16[32,2176]{1,0:T(8,128)(2,1)S(1)}, u32[]{:S(2)}, u32[]{:S(2)}) collective-permute-start(bf16[32,2176]{1,0:T(8,128)(2,1)S(1)} %constant_dynamic-slice_fusion.6), channel_id=1, source_target_pairs={{0,4},{1,5},{2,6},{3,7},{4,0},{5,1},{6,2},{7,3},{8,12},{9,13},{10,... | collective-permute-start | bytes 417800 | tf_op jit(solution)/shard_map/ppermute | solution.py:762
  14.3 8.6 %collective-permute-start = (bf16[32,2176]{1,0:T(8,128)(2,1)S(1)}, bf16[32,2176]{1,0:T(8,128)(2,1)S(1)}, u32[]{:S(2)}, u32[]{:S(2)}) collective-permute-start(bf16[32,2176]{1,0:T(8,128)(2,1)S(1)} %constant_dynamic-slice_fusion.6), channel_id=1, source_target_pairs={{0,2},{1,3},{2,0},{3,1},{4,6},{5,7},{6,4},{7,5},{8,10},{9,11},{10,... | collective-permute-start | bytes 417800 | tf_op jit(solution)/shard_map/ppermute | solution.py:762
  16.0 14.0 %collective-permute-start.4 = (s32[8]{0:T(128)S(1)}, s32[8]{0:T(128)S(1)}, u32[]{:S(2)}, u32[]{:S(2)}) collective-permute-start(s32[8]{0:T(128)S(1)} %slice.189), channel_id=1, source_target_pairs={{0,1},{1,2},{2,3},{3,4},{4,5},{5,6},{6,7},{8,9},{9,10},{10,11},{11... | collective-permute-start | bytes 104 | tf_op jit(solution)/shard_map/ppermute | solution.py:1001
  20.1 9.9 %collective-permute-start.3 = (bf16[8,1024]{1,0:T(8,128)(2,1)S(1)}, bf16[8,1024]{1,0:T(8,128)(2,1)S(1)}, u32[]{:S(2)}, u32[]{:S(2)}) collective-permute-start(bf16[8,1024]{1,0:T(8,128)(2,1)S(1)} %slice.188), channel_id=1, source_target_pairs={{0,1},{1,2},{2,3},{3,4},{4,5},{5,6},{6,7},{8,9},{9,10},{10,11},{11... | collective-permute-start | bytes 49160 | tf_op jit(solution)/shard_map/ppermute | solution.py:1001
  22.4 7.4 %collective-permute-start.2 = (bf16[32,2176]{1,0:T(8,128)(2,1)S(1)}, bf16[32,2176]{1,0:T(8,128)(2,1)S(1)}, u32[]{:S(2)}, u32[]{:S(2)}) collective-permute-start(bf16[32,2176]{1,0:T(8,128)(2,1)S(1)} %collective-permute-done.1), channel_id=1, source_target_pairs={{0,2},{1,3},{2,0},{3,1},{4,6},{5,7},{6,4},{7,5},{8,10},{9,11},{10,... | collective-permute-start | bytes 417800 | tf_op jit(solution)/shard_map/ppermute | solution.py:762
  30.0 10.1 %collective-permute-start.5 = (bf16[4,32,2176]{2,1,0:T(8,128)(2,1)S(1)}, bf16[4,32,2176]{2,1,0:T(8,128)(2,1)S(1)}, u32[]{:S(2)}, u32[]{:S(2)}) collective-permute-start(bf16[4,32,2176]{2,1,0:T(8,128)(2,1)S(1)} %pad_maximum_fusion.4.refs_0_), channel_id=1, source_target_pairs={{0,1},{1,0},{2,3},{3,2},{4,5},{5,4},{6,7},{7,6},{8,9},{9,8},{10,11... | collective-permute-start | bytes 1671176 | tf_op jit(solution)/shard_map/ppermute | solution.py:762
  31.5 12.8 %collective-permute-start.6 = (bf16[4,32,2176]{2,1,0:T(8,128)(2,1)S(1)}, bf16[4,32,2176]{2,1,0:T(8,128)(2,1)}, u32[]{:S(2)}, u32[]{:S(2)}) collective-permute-start(bf16[4,32,2176]{2,1,0:T(8,128)(2,1)S(1)} %pad_maximum_fusion.4.refs_0_), channel_id=1, source_target_pairs={{0,16},{8,24},{16,0},{24,8},{1,17},{9,25},{17,1},{25,9},{2,18},{10... | collective-permute-start | bytes 1671176 | tf_op jit(solution)/shard_map/ppermute | solution.py:762
  33.0 11.3 %collective-permute-start.7 = (bf16[4,32,2176]{2,1,0:T(8,128)(2,1)S(1)}, bf16[4,32,2176]{2,1,0:T(8,128)(2,1)}, u32[]{:S(2)}, u32[]{:S(2)}) collective-permute-start(bf16[4,32,2176]{2,1,0:T(8,128)(2,1)S(1)} %pad_maximum_fusion.4.refs_0_), channel_id=1, source_target_pairs={{0,8},{8,0},{16,24},{24,16},{1,9},{9,1},{17,25},{25,17},{2,10},{10... | collective-permute-start | bytes 1671176 | tf_op jit(solution)/shard_map/ppermute | solution.py:762
  44.3 19.5 %collective-permute-start.8 = (bf16[4,32,2176]{2,1,0:T(8,128)(2,1)S(1)}, bf16[4,32,2176]{2,1,0:T(8,128)(2,1)}, u32[]{:S(2)}, u32[]{:S(2)}) collective-permute-start(bf16[4,32,2176]{2,1,0:T(8,128)(2,1)S(1)} %collective-permute-done.5.refs_1_), channel_id=1, source_target_pairs={{0,16},{8,24},{16,0},{24,8},{1,17},{9,25},{17,1},{25,9},{2,18},{10... | collective-permute-start | bytes 1671176 | tf_op jit(solution)/shard_map/ppermute | solution.py:762
  46.5 17.2 %collective-permute-start.10 = (bf16[4,32,2176]{2,1,0:T(8,128)(2,1)}, bf16[4,32,2176]{2,1,0:T(8,128)(2,1)S(1)}, u32[]{:S(2)}, u32[]{:S(2)}) collective-permute-start(bf16[4,32,2176]{2,1,0:T(8,128)(2,1)} %collective-permute-done.6.refs_2_), channel_id=1, source_target_pairs={{0,8},{8,0},{16,24},{24,16},{1,9},{9,1},{17,25},{25,17},{2,10},{10... | collective-permute-start | bytes 1671176 | tf_op jit(solution)/shard_map/ppermute | solution.py:762
  46.5 18.1 %collective-permute-start.9 = (bf16[4,32,2176]{2,1,0:T(8,128)(2,1)S(1)}, bf16[4,32,2176]{2,1,0:T(8,128)(2,1)S(1)}, u32[]{:S(2)}, u32[]{:S(2)}) collective-permute-start(bf16[4,32,2176]{2,1,0:T(8,128)(2,1)S(1)} %collective-permute-done.5.refs_1_), channel_id=1, source_target_pairs={{0,8},{8,0},{16,24},{24,16},{1,9},{9,1},{17,25},{25,17},{2,10},{10... | collective-permute-start | bytes 1671176 | tf_op jit(solution)/shard_map/ppermute | solution.py:762
  48.4 30.7 %collective-permute-start.13 = (bf16[32,3072]{1,0:T(8,128)(2,1)}, bf16[32,3072]{1,0:T(8,128)(2,1)}, u32[]{:S(2)}, u32[]{:S(2)}) collective-permute-start(bf16[32,3072]{1,0:T(8,128)(2,1)} %constant_dynamic-slice_fusion.5), channel_id=1, source_target_pairs={{0,4},{1,5},{2,6},{3,7},{4,0},{5,1},{6,2},{7,3},{8,12},{9,13},{10,... | collective-permute-start | bytes 589832 | tf_op jit(solution)/shard_map/ppermute | solution.py:762
  51.1 36.3 %collective-permute-start.12 = (bf16[32,3072]{1,0:T(8,128)(2,1)}, bf16[32,3072]{1,0:T(8,128)(2,1)}, u32[]{:S(2)}, u32[]{:S(2)}) collective-permute-start(bf16[32,3072]{1,0:T(8,128)(2,1)} %constant_dynamic-slice_fusion.5), channel_id=1, source_target_pairs={{0,2},{1,3},{2,0},{3,1},{4,6},{5,7},{6,4},{7,5},{8,10},{9,11},{10,... | collective-permute-start | bytes 589832 | tf_op jit(solution)/shard_map/ppermute | solution.py:762
  65.4 2.3 collective-permute-start.11
  79.1 19.6 %collective-permute-start.14 = (bf16[32,3072]{1,0:T(8,128)(2,1)}, bf16[32,3072]{1,0:T(8,128)(2,1)S(1)}, u32[]{:S(2)}, u32[]{:S(2)}) collective-permute-start(bf16[32,3072]{1,0:T(8,128)(2,1)} %collective-permute-done.13), channel_id=1, source_target_pairs={{0,2},{1,3},{2,0},{3,1},{4,6},{5,7},{6,4},{7,5},{8,10},{9,11},{10,... | collective-permute-start | bytes 589832 | tf_op jit(solution)/shard_map/ppermute | solution.py:762
  99.9 24.5 %collective-permute-start.15 = (bf16[4,32,3072]{2,1,0:T(8,128)(2,1)S(1)}, bf16[4,32,3072]{2,1,0:T(8,128)(2,1)S(1)}, u32[]{:S(2)}, u32[]{:S(2)}) collective-permute-start(bf16[4,32,3072]{2,1,0:T(8,128)(2,1)S(1)} %pad_maximum_fusion.2.refs_0_), channel_id=1, source_target_pairs={{0,1},{1,0},{2,3},{3,2},{4,5},{5,4},{6,7},{7,6},{8,9},{9,8},{10,11... | collective-permute-start | bytes 2359304 | tf_op jit(solution)/shard_map/ppermute | solution.py:762
  100.4 23.9 %collective-permute-start.16 = (bf16[4,32,3072]{2,1,0:T(8,128)(2,1)S(1)}, bf16[4,32,3072]{2,1,0:T(8,128)(2,1)S(1)}, u32[]{:S(2)}, u32[]{:S(2)}) collective-permute-start(bf16[4,32,3072]{2,1,0:T(8,128)(2,1)S(1)} %pad_maximum_fusion.2.refs_0_), channel_id=1, source_target_pairs={{0,16},{8,24},{16,0},{24,8},{1,17},{9,25},{17,1},{25,9},{2,18},{10... | collective-permute-start | bytes 2359304 | tf_op jit(solution)/shard_map/ppermute | solution.py:762
  125.9 23.2 %all-to-all-start = ((bf16[8,128,256]{2,1,0:T(8,128)(2,1)}), bf16[8,128,256]{2,1,0:T(8,128)(2,1)S(1)}, u32[]{:S(2)}, u32[]{:S(2)}) async-start(bf16[8,128,256]{2,1,0:T(8,128)(2,1)} %get-tuple-element.131), calls=%async_computation | async-start | bytes 1048576 | tf_op jit(solution)/shard_map/all_to_all | solution.py:1017
  131.4 21.2 %collective-permute-start.17 = (bf16[4,32,3072]{2,1,0:T(8,128)(2,1)S(1)}, bf16[4,32,3072]{2,1,0:T(8,128)(2,1)}, u32[]{:S(2)}, u32[]{:S(2)}) collective-permute-start(bf16[4,32,3072]{2,1,0:T(8,128)(2,1)S(1)} %collective-permute-done.15.refs_1_), channel_id=1, source_target_pairs={{0,16},{8,24},{16,0},{24,8},{1,17},{9,25},{17,1},{25,9},{2,18},{10... | collective-permute-start | bytes 2359304 | tf_op jit(solution)/shard_map/ppermute | solution.py:762
  131.8 27.0 %collective-permute-start.20 = (bf16[4,32,3072]{2,1,0:T(8,128)(2,1)}, bf16[4,32,3072]{2,1,0:T(8,128)(2,1)}, u32[]{:S(2)}, u32[]{:S(2)}) collective-permute-start(bf16[4,32,3072]{2,1,0:T(8,128)(2,1)} %copy-done.8), channel_id=1, source_target_pairs={{0,8},{8,0},{16,24},{24,16},{1,9},{9,1},{17,25},{25,17},{2,10},{10... | collective-permute-start | bytes 2359304 | tf_op jit(solution)/shard_map/ppermute | solution.py:762
  131.8 27.0 %collective-permute-start.19 = (bf16[4,32,3072]{2,1,0:T(8,128)(2,1)S(1)}, bf16[4,32,3072]{2,1,0:T(8,128)(2,1)}, u32[]{:S(2)}, u32[]{:S(2)}) collective-permute-start(bf16[4,32,3072]{2,1,0:T(8,128)(2,1)S(1)} %collective-permute-done.15.refs_1_), channel_id=1, source_target_pairs={{0,8},{8,0},{16,24},{24,16},{1,9},{9,1},{17,25},{25,17},{2,10},{10... | collective-permute-start | bytes 2359304 | tf_op jit(solution)/shard_map/ppermute | solution.py:762
  132.3 26.5 %collective-permute-start.18 = (bf16[4,32,3072]{2,1,0:T(8,128)(2,1)S(1)}, bf16[4,32,3072]{2,1,0:T(8,128)(2,1)}, u32[]{:S(2)}, u32[]{:S(2)}) collective-permute-start(bf16[4,32,3072]{2,1,0:T(8,128)(2,1)S(1)} %pad_maximum_fusion.2.refs_0_), channel_id=1, source_target_pairs={{0,8},{8,0},{16,24},{24,16},{1,9},{9,1},{17,25},{25,17},{2,10},{10... | collective-permute-start | bytes 2359304 | tf_op jit(solution)/shard_map/ppermute | solution.py:762
  152.6 6.3 %collective-permute-start.21 = (bf16[4,32,3072]{2,1,0:T(8,128)(2,1)}, bf16[4,32,3072]{2,1,0:T(8,128)(2,1)}, u32[]{:S(2)}, u32[]{:S(2)}) collective-permute-start(bf16[4,32,3072]{2,1,0:T(8,128)(2,1)} %collective-permute-done.17.refs_3_), channel_id=1, source_target_pairs={{0,8},{8,0},{16,24},{24,16},{1,9},{9,1},{17,25},{25,17},{2,10},{10... | collective-permute-start | bytes 2359304 | tf_op jit(solution)/shard_map/ppermute | solution.py:762
  154.0 18.2 %all-to-all-start.1 = ((bf16[8,128,128]{2,1,0:T(8,128)(2,1)}), bf16[8,128,128]{2,1,0:T(8,128)(2,1)S(1)}, u32[]{:S(2)}, u32[]{:S(2)}) async-start(bf16[8,128,128]{2,1,0:T(8,128)(2,1)} %state_prefix.1), calls=%async_computation.1 | async-start | bytes 524288 | tf_op jit(solution)/shard_map/all_to_all | solution.py:1017
  158.3 235.6 %reduce-scatter.3.cloned.1.call-start = ((), (), s32[]{:S(2)}) async-start(), calls=%async_computation.8 | async-start | bytes 6488064 | tf_op jit(solution)/shard_map/reduce_scatter | solution.py:971
  233.5 9.8 %collective-permute-start.23 = (bf16[1024,2816]{1,0:T(8,128)(2,1)}, bf16[1024,2816]{1,0:T(8,128)(2,1)}, u32[]{:S(2)}, u32[]{:S(2)}) collective-permute-start(bf16[1024,2816]{1,0:T(8,128)(2,1)} %convolution_convert_fusion), channel_id=1, source_target_pairs={{0,8},{8,0},{16,24},{24,16},{1,9},{9,1},{17,25},{25,17},{2,10},{10... | collective-permute-start | bytes 17301512 | tf_op jit(solution)/shard_map/ppermute | solution.py:762
  250.3 8.3 %collective-permute-start.22 = (bf16[2816,512]{1,0:T(8,128)(2,1)}, bf16[2816,512]{1,0:T(8,128)(2,1)}, u32[]{:S(2)}, u32[]{:S(2)}) collective-permute-start(bf16[2816,512]{1,0:T(8,128)(2,1)} %convolution_convert_fusion.1), channel_id=1, source_target_pairs={{0,8},{8,0},{16,24},{24,16},{1,9},{9,1},{17,25},{25,17},{2,10},{10... | collective-permute-start | bytes 8650760 | tf_op jit(solution)/shard_map/ppermute | solution.py:762
  280.5 32.6 %collective-permute-start.24 = (bf16[1024,1024]{1,0:T(8,128)(2,1)}, bf16[1024,1024]{1,0:T(8,128)(2,1)S(1)}, u32[]{:S(2)}, u32[]{:S(2)}) collective-permute-start(bf16[1024,1024]{1,0:T(8,128)(2,1)} %get-tuple-element.307), channel_id=1, source_target_pairs={{0,8},{8,0},{16,24},{24,16},{1,9},{9,1},{17,25},{25,17},{2,10},{10... | collective-permute-start | bytes 6291464 | tf_op jit(solution)/shard_map/ppermute | solution.py:762
  283.5 38.5 %collective-permute-start.25 = (bf16[2,2,2,176,512]{4,3,2,1,0:T(8,128)(2,1)}, bf16[2,2,2,176,512]{4,3,2,1,0:T(8,128)(2,1)}, u32[]{:S(2)}, u32[]{:S(2)}) collective-permute-start(bf16[2,2,2,176,512]{4,3,2,1,0:T(8,128)(2,1)} %dynamic-slice_bitcast_fusion.1), channel_id=1, source_target_pairs={{0,16},{8,24},{16,0},{24,8},{1,17},{9,25},{17,1},{25,9},{2,18},{10... | collective-permute-start | bytes 4325384 | tf_op jit(solution)/shard_map/ppermute | solution.py:762
  285.2 21.0 %all-to-all-start.2 = ((bf16[8,128,128]{2,1,0:T(8,128)(2,1)}), bf16[8,128,128]{2,1,0:T(8,128)(2,1)S(1)}, u32[]{:S(2)}, u32[]{:S(2)}) async-start(bf16[8,128,128]{2,1,0:T(8,128)(2,1)} %get-tuple-element.157), calls=%async_computation.2 | async-start | bytes 524288 | tf_op jit(solution)/shard_map/all_to_all | solution.py:1017
  309.7 12.3 %all-to-all-start.3 = ((bf16[8,128,128]{2,1,0:T(8,128)(2,1)}), bf16[8,128,128]{2,1,0:T(8,128)(2,1)S(1)}, u32[]{:S(2)}, u32[]{:S(2)}) async-start(bf16[8,128,128]{2,1,0:T(8,128)(2,1)} %state_suffix.1), calls=%async_computation.3 | async-start | bytes 524288 | tf_op jit(solution)/shard_map/all_to_all | solution.py:1017
  313.1 148.2 %reduce-scatter.5.cloned.1.call-start = ((), (), s32[]{:S(2)}) async-start(), calls=%async_computation.9 | async-start | bytes 1622016 | tf_op jit(solution)/shard_map/reduce_scatter | solution.py:971
  322.8 22.1 %collective-permute-start.27 = (bf16[2,2,128,512]{3,2,1,0:T(8,128)(2,1)S(1)}, bf16[2,2,128,512]{3,2,1,0:T(8,128)(2,1)S(1)}, u32[]{:S(2)}, u32[]{:S(2)}) collective-permute-start(bf16[2,2,128,512]{3,2,1,0:T(8,128)(2,1)S(1)} %dynamic-slice_bitcast_fusion.4), channel_id=1, source_target_pairs={{0,1},{1,0},{2,3},{3,2},{4,5},{5,4},{6,7},{7,6},{8,9},{9,8},{10,11... | collective-permute-start | bytes 1572872 | tf_op jit(solution)/shard_map/ppermute | solution.py:762
  324.3 20.6 %collective-permute-start.26 = (bf16[2,2,2,64,512]{4,3,2,1,0:T(8,128)(2,1)S(1)}, bf16[2,2,2,64,512]{4,3,2,1,0:T(8,128)(2,1)S(1)}, u32[]{:S(2)}, u32[]{:S(2)}) collective-permute-start(bf16[2,2,2,64,512]{4,3,2,1,0:T(8,128)(2,1)S(1)} %dynamic-slice_bitcast_fusion.5), channel_id=1, source_target_pairs={{0,16},{8,24},{16,0},{24,8},{1,17},{9,25},{17,1},{25,9},{2,18},{10... | collective-permute-start | bytes 1572872 | tf_op jit(solution)/shard_map/ppermute | solution.py:762
  350.1 17.2 %collective-permute-start.28 = (bf16[1024,1152]{1,0:T(8,128)(2,1)}, bf16[1024,1152]{1,0:T(8,128)(2,1)}, u32[]{:S(2)}, u32[]{:S(2)}) collective-permute-start(bf16[1024,1152]{1,0:T(8,128)(2,1)} %convolution_convert_fusion.2), channel_id=1, source_target_pairs={{0,8},{8,0},{16,24},{24,16},{1,9},{9,1},{17,25},{25,17},{2,10},{10... | collective-permute-start | bytes 7077896 | tf_op jit(solution)/shard_map/ppermute | solution.py:762
  356.9 14.5 %collective-permute-start.30 = (bf16[2,2,64,512]{3,2,1,0:T(8,128)(2,1)S(1)}, bf16[2,2,64,512]{3,2,1,0:T(8,128)(2,1)S(1)}, u32[]{:S(2)}, u32[]{:S(2)}) collective-permute-start(bf16[2,2,64,512]{3,2,1,0:T(8,128)(2,1)S(1)} %dynamic-slice_bitcast_fusion.10), channel_id=1, source_target_pairs={{0,16},{8,24},{16,0},{24,8},{1,17},{9,25},{17,1},{25,9},{2,18},{10... | collective-permute-start | bytes 786440 | tf_op jit(solution)/shard_map/ppermute | solution.py:762
  359.0 12.4 %collective-permute-start.29 = (bf16[2,2,64,512]{3,2,1,0:T(8,128)(2,1)S(1)}, bf16[2,2,64,512]{3,2,1,0:T(8,128)(2,1)S(1)}, u32[]{:S(2)}, u32[]{:S(2)}) collective-permute-start(bf16[2,2,64,512]{3,2,1,0:T(8,128)(2,1)S(1)} %dynamic-slice_bitcast_fusion.11), channel_id=1, source_target_pairs={{0,1},{1,0},{2,3},{3,2},{4,5},{5,4},{6,7},{7,6},{8,9},{9,8},{10,11... | collective-permute-start | bytes 786440 | tf_op jit(solution)/shard_map/ppermute | solution.py:762
  371.8 15.4 %collective-permute-start.31 = (bf16[2,64,1024]{2,1,0:T(8,128)(2,1)S(1)}, bf16[2,64,1024]{2,1,0:T(8,128)(2,1)S(1)}, u32[]{:S(2)}, u32[]{:S(2)}) collective-permute-start(bf16[2,64,1024]{2,1,0:T(8,128)(2,1)S(1)} %dynamic-slice_bitcast_fusion.9), channel_id=1, source_target_pairs={{0,2},{1,3},{2,0},{3,1},{4,6},{5,7},{6,4},{7,5},{8,10},{9,11},{10,... | collective-permute-start | bytes 786440 | tf_op jit(solution)/shard_map/ppermute | solution.py:762
  372.3 15.0 %collective-permute-start.33 = (bf16[2,2,128,512]{3,2,1,0:T(8,128)(2,1)S(1)}, bf16[2,2,128,512]{3,2,1,0:T(8,128)(2,1)S(1)}, u32[]{:S(2)}, u32[]{:S(2)}) collective-permute-start(bf16[2,2,128,512]{3,2,1,0:T(8,128)(2,1)S(1)} %dynamic-slice_bitcast_fusion.3), channel_id=1, source_target_pairs={{0,1},{1,0},{2,3},{3,2},{4,5},{5,4},{6,7},{7,6},{8,9},{9,8},{10,11... | collective-permute-start | bytes 1572872 | tf_op jit(solution)/shard_map/ppermute | solution.py:762
  372.8 16.6 %collective-permute-start.32 = (bf16[2,2,2,64,640]{4,3,2,1,0:T(8,128)(2,1)S(1)}, bf16[2,2,2,64,640]{4,3,2,1,0:T(8,128)(2,1)S(1)}, u32[]{:S(2)}, u32[]{:S(2)}) collective-permute-start(bf16[2,2,2,64,640]{4,3,2,1,0:T(8,128)(2,1)S(1)} %dynamic-slice_bitcast_fusion.2), channel_id=1, source_target_pairs={{0,16},{8,24},{16,0},{24,8},{1,17},{9,25},{17,1},{25,9},{2,18},{10... | collective-permute-start | bytes 1966088 | tf_op jit(solution)/shard_map/ppermute | solution.py:762
  390.2 25.4 %collective-permute-start.39 = (bf16[2,2,64,512]{3,2,1,0:T(8,128)(2,1)}, bf16[2,2,64,512]{3,2,1,0:T(8,128)(2,1)}, u32[]{:S(2)}, u32[]{:S(2)}) collective-permute-start(bf16[2,2,64,512]{3,2,1,0:T(8,128)(2,1)} %dynamic-slice_bitcast_fusion.8), channel_id=1, source_target_pairs={{0,16},{8,24},{16,0},{24,8},{1,17},{9,25},{17,1},{25,9},{2,18},{10... | collective-permute-start | bytes 786440 | tf_op jit(solution)/shard_map/ppermute | solution.py:762
  392.4 23.3 %collective-permute-start.38 = (bf16[2,2,64,640]{3,2,1,0:T(8,128)(2,1)}, bf16[2,2,64,640]{3,2,1,0:T(8,128)(2,1)S(1)}, u32[]{:S(2)}, u32[]{:S(2)}) collective-permute-start(bf16[2,2,64,640]{3,2,1,0:T(8,128)(2,1)} %dynamic-slice_bitcast_fusion.6), channel_id=1, source_target_pairs={{0,1},{1,0},{2,3},{3,2},{4,5},{5,4},{6,7},{7,6},{8,9},{9,8},{10,11... | collective-permute-start | bytes 983048 | tf_op jit(solution)/shard_map/ppermute | solution.py:762
  396.9 6.5 %collective-permute-start.34 = (bf16[1024,384]{1,0:T(8,128)(2,1)}, bf16[1024,384]{1,0:T(8,128)(2,1)}, u32[]{:S(2)}, u32[]{:S(2)}) collective-permute-start(bf16[1024,384]{1,0:T(8,128)(2,1)} %convolution_convert_fusion.3), channel_id=1, source_target_pairs={{0,8},{8,0},{16,24},{24,16},{1,9},{9,1},{17,25},{25,17},{2,10},{10... | collective-permute-start | bytes 2359304 | tf_op jit(solution)/shard_map/ppermute | solution.py:762
  400.8 1.7 collective-permute-start.35
  402.6 13.0 %collective-permute-start.40 = (bf16[2,2,2,64,128]{4,3,0,1,2:T(8,128)(2,1)S(1)}, bf16[2,2,2,64,128]{4,3,0,1,2:T(8,128)(2,1)S(1)}, u32[]{:S(2)}, u32[]{:S(2)}) collective-permute-start(bf16[2,2,2,64,128]{4,3,0,1,2:T(8,128)(2,1)S(1)} %bitcast.261), channel_id=1, source_target_pairs={{0,16},{8,24},{16,0},{24,8},{1,17},{9,25},{17,1},{25,9},{2,18},{10... | collective-permute-start | bytes 393224 | tf_op jit(solution)/shard_map/ppermute | solution.py:762
  408.5 5.8 %collective-permute-start.36 = (bf16[8,1024]{1,0:T(8,128)(2,1)S(1)}, bf16[8,1024]{1,0:T(8,128)(2,1)S(1)}, u32[]{:S(2)}, u32[]{:S(2)}) collective-permute-start(bf16[8,1024]{1,0:T(8,128)(2,1)S(1)} %slice.353), channel_id=1, source_target_pairs={{1,0},{2,1},{3,2},{4,3},{5,4},{6,5},{7,6},{9,8},{10,9},{11,10},{12... | collective-permute-start | bytes 49160 | tf_op jit(solution)/shard_map/ppermute | solution.py:1001
  410.1 11.2 %collective-permute-start.37 = (bf16[2,2,2,64,384]{4,3,0,1,2:T(8,128)(2,1)S(1)}, bf16[2,2,2,64,384]{4,3,0,1,2:T(8,128)(2,1)S(1)}, u32[]{:S(2)}, u32[]{:S(2)}) collective-permute-start(bf16[2,2,2,64,384]{4,3,0,1,2:T(8,128)(2,1)S(1)} %bitcast.250), channel_id=1, source_target_pairs={{0,16},{8,24},{16,0},{24,8},{1,17},{9,25},{17,1},{25,9},{2,18},{10... | collective-permute-start | bytes 1179656 | tf_op jit(solution)/shard_map/ppermute | solution.py:762
  421.8 17.4 %collective-permute-start.45 = (bf16[128,2816]{1,0:T(8,128)(2,1)S(1)}, bf16[128,2816]{1,0:T(8,128)(2,1)S(1)}, u32[]{:S(2)}, u32[]{:S(2)}) collective-permute-start(bf16[128,2816]{1,0:T(8,128)(2,1)S(1)} %copy-done.49), channel_id=1, source_target_pairs={{0,16},{8,24},{16,0},{24,8},{1,17},{9,25},{17,1},{25,9},{2,18},{10... | collective-permute-start | bytes 2162696 | tf_op jit(solution)/shard_map/ppermute | solution.py:762
  423.3 10.3 %collective-permute-start.44 = (bf16[2,2,64,128]{3,2,0,1:T(8,128)(2,1)S(1)}, bf16[2,2,64,128]{3,2,0,1:T(8,128)(2,1)S(1)}, u32[]{:S(2)}, u32[]{:S(2)}) collective-permute-start(bf16[2,2,64,128]{3,2,0,1:T(8,128)(2,1)S(1)} %dynamic-slice_bitcast_fusion.16), channel_id=1, source_target_pairs={{0,1},{1,0},{2,3},{3,2},{4,5},{5,4},{6,7},{7,6},{8,9},{9,8},{10,11... | collective-permute-start | bytes 196616 | tf_op jit(solution)/shard_map/ppermute | solution.py:762
  425.7 7.9 %collective-permute-start.43 = (bf16[64,1024]{1,0:T(8,128)(2,1)S(1)}, bf16[64,1024]{1,0:T(8,128)(2,1)S(1)}, u32[]{:S(2)}, u32[]{:S(2)}) collective-permute-start(bf16[64,1024]{1,0:T(8,128)(2,1)S(1)} %dynamic-slice_bitcast_fusion.14), channel_id=1, source_target_pairs={{0,4},{1,5},{2,6},{3,7},{4,0},{5,1},{6,2},{7,3},{8,12},{9,13},{10,... | collective-permute-start | bytes 393224 | tf_op jit(solution)/shard_map/ppermute | solution.py:762
  428.3 9.7 %collective-permute-start.42 = (bf16[2,64,1152]{2,1,0:T(8,128)(2,1)S(1)}, bf16[2,64,1152]{2,1,0:T(8,128)(2,1)S(1)}, u32[]{:S(2)}, u32[]{:S(2)}) collective-permute-start(bf16[2,64,1152]{2,1,0:T(8,128)(2,1)S(1)} %dynamic-slice_bitcast_fusion.7), channel_id=1, source_target_pairs={{0,2},{1,3},{2,0},{3,1},{4,6},{5,7},{6,4},{7,5},{8,10},{9,11},{10,... | collective-permute-start | bytes 884744 | tf_op jit(solution)/shard_map/ppermute | solution.py:762
  429.4 5.7 %collective-permute-start.41 = (bf16[2,2,64,384]{3,2,0,1:T(8,128)(2,1)S(1)}, bf16[2,2,64,384]{3,2,0,1:T(8,128)(2,1)S(1)}, u32[]{:S(2)}, u32[]{:S(2)}) collective-permute-start(bf16[2,2,64,384]{3,2,0,1:T(8,128)(2,1)S(1)} %dynamic-slice_bitcast_fusion.12), channel_id=1, source_target_pairs={{0,1},{1,0},{2,3},{3,2},{4,5},{5,4},{6,7},{7,6},{8,9},{9,8},{10,11... | collective-permute-start | bytes 589832 | tf_op jit(solution)/shard_map/ppermute | solution.py:762
  439.3 8.5 %collective-permute-start.49 = (bf16[2,64,128]{2,1,0:T(8,128)(2,1)S(1)}, bf16[2,64,128]{2,1,0:T(8,128)(2,1)S(1)}, u32[]{:S(2)}, u32[]{:S(2)}) collective-permute-start(bf16[2,64,128]{2,1,0:T(8,128)(2,1)S(1)} %dynamic-slice_bitcast_fusion.18), channel_id=1, source_target_pairs={{0,2},{1,3},{2,0},{3,1},{4,6},{5,7},{6,4},{7,5},{8,10},{9,11},{10,... | collective-permute-start | bytes 98312 | tf_op jit(solution)/shard_map/ppermute | solution.py:762
  441.6 3.6 collective-permute-start.46
  441.8 12.4 %collective-permute-start.48 = (bf16[64,1152]{1,0:T(8,128)(2,1)S(1)}, bf16[64,1152]{1,0:T(8,128)(2,1)S(1)}, u32[]{:S(2)}, u32[]{:S(2)}) collective-permute-start(bf16[64,1152]{1,0:T(8,128)(2,1)S(1)} %dynamic-slice_bitcast_fusion.13), channel_id=1, source_target_pairs={{0,4},{1,5},{2,6},{3,7},{4,0},{5,1},{6,2},{7,3},{8,12},{9,13},{10,... | collective-permute-start | bytes 442376 | tf_op jit(solution)/shard_map/ppermute | solution.py:762
  443.9 7.2 %collective-permute-start.47 = (bf16[2,64,384]{2,1,0:T(8,128)(2,1)S(1)}, bf16[2,64,384]{2,1,0:T(8,128)(2,1)S(1)}, u32[]{:S(2)}, u32[]{:S(2)}) collective-permute-start(bf16[2,64,384]{2,1,0:T(8,128)(2,1)S(1)} %dynamic-slice_bitcast_fusion.15), channel_id=1, source_target_pairs={{0,2},{1,3},{2,0},{3,1},{4,6},{5,7},{6,4},{7,5},{8,10},{9,11},{10,... | collective-permute-start | bytes 294920 | tf_op jit(solution)/shard_map/ppermute | solution.py:762
  454.3 4.7 collective-permute-start.51
  454.5 5.1 %collective-permute-start.50 = (bf16[64,384]{1,0:T(8,128)(2,1)S(1)}, bf16[64,384]{1,0:T(8,128)(2,1)S(1)}, u32[]{:S(2)}, u32[]{:S(2)}) collective-permute-start(bf16[64,384]{1,0:T(8,128)(2,1)S(1)} %dynamic-slice_bitcast_fusion.17), channel_id=1, source_target_pairs={{0,4},{1,5},{2,6},{3,7},{4,0},{5,1},{6,2},{7,3},{8,12},{9,13},{10,... | collective-permute-start | bytes 147464 | tf_op jit(solution)/shard_map/ppermute | solution.py:762
  459.7 10.9 %collective-permute-start.52 = (bf16[64,2688]{1,0:T(8,128)(2,1)S(1)}, bf16[64,2688]{1,0:T(8,128)(2,1)S(1)}, u32[]{:S(2)}, u32[]{:S(2)}) collective-permute-start(bf16[64,2688]{1,0:T(8,128)(2,1)S(1)} %pad_maximum_fusion.6), channel_id=1, source_target_pairs={{0,16},{8,24},{16,0},{24,8},{1,17},{9,25},{17,1},{25,9},{2,18},{10... | collective-permute-start | bytes 1032200 | tf_op jit(solution)/shard_map/ppermute | solution.py:762
  461.3 11.2 %collective-permute-start.54 = (bf16[176,512]{1,0:T(8,128)(2,1)}, bf16[176,512]{1,0:T(8,128)(2,1)S(1)}, u32[]{:S(2)}, u32[]{:S(2)}) collective-permute-start(bf16[176,512]{1,0:T(8,128)(2,1)} %reduce-scatter.5.cloned.1.call-done), channel_id=1, source_target_pairs={{0,16},{8,24},{16,0},{24,8},{1,17},{9,25},{17,1},{25,9},{2,18},{10... | collective-permute-start | bytes 540680 | tf_op jit(solution)/shard_map/ppermute | solution.py:762
  470.7 6.6 %collective-permute-start.53 = (bf16[128,2688]{1,0:T(8,128)(2,1)S(1)}, bf16[128,2688]{1,0:T(8,128)(2,1)S(1)}, u32[]{:S(2)}, u32[]{:S(2)}) collective-permute-start(bf16[128,2688]{1,0:T(8,128)(2,1)S(1)} %maximum_select_fusion.1), channel_id=1, source_target_pairs={{0,8},{8,0},{16,24},{24,16},{1,9},{9,1},{17,25},{25,17},{2,10},{10... | collective-permute-start | bytes 2064392 | tf_op jit(solution)/shard_map/ppermute | solution.py:762
  473.6 2.4 collective-permute-start.55
  (79 other events, 778.3 us)
Sparse Core Ops, SparseCore 0:
  11.5 104.8 all-gather.2
  126.1 72.5 all-gather.4
  250.5 126.8 reduce-scatter.2
  381.2 72.0 reduce-scatter.4

commit v7 on v6

--- a/solution.py
+++ b/solution.py
@@ -1180,22 +1180,22 @@
     ours = hold(ours, down_sum.away)
     pair_half = (contract(normed_two_low, ours, 0, 0) + pair_sum.came.astype(F32)).astype(BF)
     pair_apart = scatter_owners(pair_half)
-    down_sum.take(contract(hidden_low, down_ours, 0, 0))
-    gated_grad = hold(gated_grad, down_sum.part, pair_half)
-    down_sum.go("x")
+    gated_grad = hold(gated_grad, pair_half)
     heads_grad, gatepre_low, outgain_grad, local_later = delta_adjoint(
         query_low, key_low, w, cols, rows, gated_grad, attn_heads, qg_pre, outgain_scale, heads
     )
     if fanout > 1:
         local_later = to_owners(local_later, fanout)
     came_later = swap(local_later)
+    down_sum.take(contract(hidden_low, hold(down_ours, local_later), 0, 0))
+    down_sum.go("x")
 
     middle_held, gatepre_held = hold((middle_low, gatepre_low), local_later)
     out_grad = contract(gated_low, middle_held, 0, 0)
     gate_grad = contract(normed_low, gatepre_held, 0, 0)
     other_sum = Reduce(here)
     other_sum.swap(by_core(here, gate_grad, out_grad))
-    came_later = hold(came_later, other_sum.away)
+    came_later = hold(came_later, other_sum.away, *down_sum.outs)
     summed_later = scan_grads(owned, came_later)
     later = swap(summed_later)
     if fanout > 1:

time: 498 us -> 498 us (level)
    unnamed x168 -> x166, local copies, waits for them, and re-layouts: 20.3 us -> 20.4 us
  transfers between devices with their start and end apart: 64 -> 64, of which waited for: 25 -> 25; matrix products, arithmetic and copies ran while one was open for 23% -> 22% of each run, Pallas kernels for 18% -> 18%
where the time goes in v7:
time: 498 us; the launch traced here: 489 us
  waiting for transfers between devices  125 us (25%)
  Pallas kernels  116 us (23%)
  starting transfers between devices  83.4 us (17%)
  matrix products  73.2 us (15%)
  other arithmetic  41.2 us (8%)
  local copies, waits for them, and re-layouts  34.6 us (7%)
  between operations  15.8 us (3%)
    ppermute x53, waiting for transfers between devices, send(): return lax.ppermute(value, axis, pairs)  74.2 us
    dot_general x18, matrix products, contract(): lax.dot_general(left, right, (((left_dim,), (right_dim,)), ((), ())), pre...  59.2 us
    ppermute x53, starting transfers between devices, send(): return lax.ppermute(value, axis, pairs)  58.5 us
    all_to_all x4, waiting for transfers between devices, swap(): return lax.all_to_all(value, 'fsdp', 0, 0, tiled=True)  39 us
    pallas_call x2, Pallas kernels, delta_backward(): pl.pallas_call(partial(backward_kernel, heads, part, d), grid=(blocks + 1...  31.6 us
    pallas_call x1, Pallas kernels, feed_forward(): pl.pallas_call(feed_kernel, grid=(blocks + 1,), in_specs=[whole, whole, w...  28 us
    pallas_call x1, Pallas kernels, delta_summary(): pl.pallas_call(partial(summary_kernel, heads, d), grid=(blocks,), in_spec...  21.5 us
    unnamed x166, local copies, waits for them, and re-layouts  20.4 us
  transfers between devices with their start and end apart: 64, of which 25 were waited for; matrix products, arithmetic and copies ran while one was open for 22% of the time, Pallas kernels for 18%

profile of v7, /device:TPU:0, one launch (start us, length us, event | category | flops | bytes accessed | tf_op | source)
XLA Modules:
  0.0 489.5 jit_solution(18050755139216514431)
XLA Ops:
  10.2 4.1 collective-permute-start.1
  16.0 3.4 collective-permute-start.4
  20.1 2.3 collective-permute-start.3
  23.0 6.9 %collective-permute-done.2 = bf16[32,2176]{1,0:T(8,128)(2,1)S(1)} collective-permute-done((bf16[32,2176]{1,0:T(8,128)(2,1)S(1)}, bf16[32,2176]{1,0:T(8,128)(2,1)S(1)}, u32[]{:S(2)}, u32[]{:S(2)}) %collective-permute-start.2) | collective-permute-done | bytes 139296 | tf_op jit(solution)/shard_map/ppermute | solution.py:762
  34.4 5.7 %collective-permute-done.5.refs_1_ = bf16[4,32,2176]{2,1,0:T(8,128)(2,1)S(1)} collective-permute-done((bf16[4,32,2176]{2,1,0:T(8,128)(2,1)S(1)}, bf16[4,32,2176]{2,1,0:T(8,128)(2,1)S(1)}, u32[]{:S(2)}, u32[]{:S(2)}) %collective-permute-start.5) | collective-permute-done | bytes 557088 | tf_op jit(solution)/shard_map/ppermute | solution.py:762
  40.1 4.2 collective-permute-done.6.refs_2_
  44.3 2.2 collective-permute-start.8
  48.4 2.6 collective-permute-start.13
  51.1 6.0 %collective-permute-start.12 = (bf16[32,3072]{1,0:T(8,128)(2,1)}, bf16[32,3072]{1,0:T(8,128)(2,1)}, u32[]{:S(2)}, u32[]{:S(2)}) collective-permute-start(bf16[32,3072]{1,0:T(8,128)(2,1)} %constant_dynamic-slice_fusion.6), channel_id=1, source_target_pairs={{0,2},{1,3},{2,0},{3,1},{4,6},{5,7},{6,4},{7,5},{8,10},{9,11},{10,... | collective-permute-start | bytes 589832 | tf_op jit(solution)/shard_map/ppermute | solution.py:762
  57.0 6.8 %collective-permute-done.8.refs_4_ = bf16[4,32,2176]{2,1,0:T(8,128)(2,1)} collective-permute-done((bf16[4,32,2176]{2,1,0:T(8,128)(2,1)S(1)}, bf16[4,32,2176]{2,1,0:T(8,128)(2,1)}, u32[]{:S(2)}, u32[]{:S(2)}) %collective-permute-start.8) | collective-permute-done | bytes 557088 | tf_op jit(solution)/shard_map/ppermute | solution.py:762
  69.8 3.4 place_weights.2
  73.2 2.1 copy-done.4
  80.2 6.6 %fusion.93.pre_ref.prev_ref.kvpre_ref.kvrim_ref = f32[520,2048]{1,0:T(8,128)} fusion(bf16[520,1024]{1,0:T(8,128)(2,1)S(1)} %fusion.7, bf16[1024,2048]{1,0:T(8,128)(2,1)} %copy-done.4), kind=kOutput, calls=%fused_computation.229 | convolution fusion | flops 2181038080 | bytes 9519104 | tf_op jit(solution)/shard_map/dot_general | solution.py:1103
  87.4 11.4 %collective-permute-done.14 = bf16[32,3072]{1,0:T(8,128)(2,1)S(1)} collective-permute-done((bf16[32,3072]{1,0:T(8,128)(2,1)}, bf16[32,3072]{1,0:T(8,128)(2,1)S(1)}, u32[]{:S(2)}, u32[]{:S(2)}) %collective-permute-start.14) | collective-permute-done | bytes 196640 | tf_op jit(solution)/shard_map/ppermute | solution.py:762
  100.5 2.4 collective-permute-start.16
  102.9 21.5 %delta_summary.1 = (bf16[512,1024]{1,0:T(8,128)(2,1)}, bf16[512,1024]{1,0:T(8,128)(2,1)}, f32[512,2048]{1,0:T(8,128)}, bf16[512,1024]{1,0:T(8,128)(2,1)}, bf16[5...) custom-call(f32[520,2048]{1,0:T(8,128)} %fusion.93.pre_ref.prev_ref.kvpre_ref.kvrim_ref, ...), custom_call_target="tpu_custom_call" | custom-call | flops 20999999488 | bytes 63000000 | tf_op jit(solution)/shard_map/delta_summary/pallas_call | solution.py:453
  126.0 5.5 %all-to-all-start = ((bf16[8,128,256]{2,1,0:T(8,128)(2,1)}), bf16[8,128,256]{2,1,0:T(8,128)(2,1)S(1)}, u32[]{:S(2)}, u32[]{:S(2)}) async-start(bf16[8,128,256]{2,1,0:T(8,128)(2,1)} %get-tuple-element.132), calls=%async_computation | async-start | bytes 1048576 | tf_op jit(solution)/shard_map/all_to_all | solution.py:1017
  132.4 16.8 %all-to-all-done.x_ref.t_ref = bf16[8,128,256]{2,1,0:T(8,128)(2,1)S(1)} async-done(((bf16[8,128,256]{2,1,0:T(8,128)(2,1)}), bf16[8,128,256]{2,1,0:T(8,128)(2,1)S(1)}, u32[]{:S(2)}, u32[]{:S(2)}) %all-to-all-start) | async-done | bytes 524320 | tf_op jit(solution)/shard_map/all_to_all | solution.py:1017
  150.0 2.7 state_prefix.1
  154.0 4.4 all-to-all-start.1
  160.1 4.2 place_weights.3
  167.5 4.4 fusion.94.pre_ref.prev_ref.gate_ref.qpre_ref.qrim_ref
  173.0 11.3 %delta_forward.1 = (bf16[512,1024]{1,0:T(8,128)(2,1)}, f32[512,1024]{1,0:T(8,128)}, bf16[512,1024]{1,0:T(8,128)(2,1)}, f32[512,1024]{1,0:T(8,128)}, bf16[512,102...) custom-call(f32[520,2048]{1,0:T(8,128)} %fusion.94.pre_ref.prev_ref.gate_ref.qpre_ref.qrim_ref, ...), custom_call_target="tpu_custom_call" | custom-call | flops 11000000512 | bytes 33000000 | tf_op jit(solution)/shard_map/delta_forward/pallas_call | solution.py:496
  184.3 2.6 multiply_reduce_fusion.1
  189.5 9.2 %all-gather.5.cloned.1.call-done.d_ref.db_ref = bf16[2816,1024]{1,0:T(8,128)(2,1)} async-done(((bf16[88,1024]{1,0:T(8,128)(2,1)}), bf16[2816,1024]{1,0:T(8,128)(2,1)}) %all-gather.5.cloned.1.call-update) | async-done | bytes 5767184 | tf_op jit(solution)/shard_map/all_gather | solution.py:967
  198.7 28.0 %feed_forward.1 = (bf16[512,2816]{1,0:T(8,128)(2,1)}, bf16[2,512,2816]{2,1,0:T(8,128)(2,1)}, bf16[512,1024]{1,0:T(8,128)(2,1)}, f32[512,1024]{1,0:T(8,128)}) custom-call(bf16[512,1024]{1,0:T(8,128)(2,1)} %multiply_convert_fusion.n_ref, bf16[512,1024]{1,0:T(8,128)(2,1)} %e_ref.1, f32[512,1024]{1,0:T(8,128)} %copy-done.17, ...), custom_call_target="tpu_custom_call" | custom-call | flops 24999999488 | bytes 75000000 | tf_op jit(solution)/shard_map/feed_forward/pallas_call | solution.py:692
  226.7 6.8 %convolution_convert_fusion = bf16[1024,2816]{1,0:T(8,128)(2,1)} fusion(bf16[512,1024]{1,0:T(8,128)(2,1)S(1)} %copy-done.44, bf16[2,512,2816]{2,1,0:T(8,128)(2,1)} %get-tuple-element.152, s32[]{:T(128)S(6)} %select_n.652), kind=kOutput, calls=%fused_computation.2 | convolution fusion | flops 2955673600 | bytes 9699332 | tf_op jit(solution)/shard_map/dot_general | solution.py:983
  233.8 5.3 %convolution_convert_fusion.1 = bf16[2816,512]{1,0:T(8,128)(2,1)} fusion(bf16[512,2816]{1,0:T(8,128)(2,1)} %get-tuple-element.153, bf16[512,1024]{1,0:T(8,128)(2,1)} %e_ref.1, s32[]{:T(128)S(6)} %select_n.651), kind=kOutput, calls=%fused_computation.4 | convolution fusion | flops 1477836800 | bytes 6291460 | tf_op jit(solution)/shard_map/dot_general | solution.py:983
  239.3 3.9 collective-permute-done.22
  243.2 7.0 %add_convert_fusion = bf16[1024,2816]{1,0:T(8,128)(2,1)} fusion(bf16[1024,2816]{1,0:T(8,128)(2,1)} %collective-permute-done.22, bf16[512,1024]{1,0:T(8,128)(2,1)S(1)} %copy-done.45, bf16[512,2816]{1,0:T(8,128)(2,1)S(1)} %dynamic-slice_bitcast_fusion), kind=kOutput, calls=%fused_computation | convolution fusion | flops 2961440768 | bytes 15466496 | tf_op jit(solution)/shard_map/dot_general | solution.py:983
  250.6 2.7 multiply_reduce_fusion
  256.0 2.7 fusion.95.dy_ref
  258.6 10.9 %delta_adjoint.1 = (bf16[512,1024]{1,0:T(8,128)(2,1)}, bf16[512,1024]{1,0:T(8,128)(2,1)}, f32[1,128]{1,0:T(1,128)}, bf16[8,128,128]{2,1,0:T(8,128)(2,1)}) custom-call(bf16[512,1024]{1,0:T(8,128)(2,1)} %get-tuple-element.147.q_ref, bf16[512,1024]{1,0:T(8,128)(2,1)} %get-tuple-element.139.k_ref, bf16[512,1024]{1,0:T(8,128)(2,1)} %get-tuple-element.140.w_ref, ...), custom_call_target="tpu_custom_call" | custom-call | flops 11000000512 | bytes 33000000 | tf_op jit(solution)/shard_map/delta_adjoint/pallas_call | solution.py:532
  271.2 4.0 select_convert_fusion
  275.4 4.4 add_convert_fusion.1
  283.9 3.9 all-to-all-start.2
  287.8 17.0 %all-to-all-done.2.g_ref = bf16[8,128,128]{2,1,0:T(8,128)(2,1)S(1)} async-done(((bf16[8,128,128]{2,1,0:T(8,128)(2,1)}), bf16[8,128,128]{2,1,0:T(8,128)(2,1)S(1)}, u32[]{:S(2)}, u32[]{:S(2)}) %all-to-all-start.2) | async-done | bytes 262176 | tf_op jit(solution)/shard_map/all_to_all | solution.py:1017
  305.4 2.8 state_suffix.1
  308.3 3.4 all-to-all-start.3
  311.7 4.2 add_convert_fusion.3
  316.0 4.9 %all-to-all-done.3.s_ref = bf16[8,128,128]{2,1,0:T(8,128)(2,1)S(1)} async-done(((bf16[8,128,128]{2,1,0:T(8,128)(2,1)}), bf16[8,128,128]{2,1,0:T(8,128)(2,1)S(1)}, u32[]{:S(2)}, u32[]{:S(2)}) %all-to-all-start.3) | async-done | bytes 262176 | tf_op jit(solution)/shard_map/all_to_all | solution.py:1017
  324.8 19.1 %delta_backward.2 = (bf16[520,2304]{1,0:T(8,128)(2,1)}, f32[512,128]{1,0:T(8,128)}, f32[4,2304]{1,0:T(4,128)}) custom-call(bf16[512,1024]{1,0:T(8,128)(2,1)} %get-tuple-element.147.q_ref, bf16[512,1024]{1,0:T(8,128)(2,1)} %get-tuple-element.139.k_ref, bf16[512,1024]{1,0:T(8,128)(2,1)} %get-tuple-element.148.v_ref, ...), custom_call_target="tpu_custom_call" | custom-call | flops 20000000000 | bytes 60000000 | tf_op jit(solution)/shard_map/delta_backward/pallas_call | solution.py:594
  344.0 5.1 %convolution_convert_fusion.2 = bf16[1024,1152]{1,0:T(8,128)(2,1)} fusion(bf16[520,1024]{1,0:T(8,128)(2,1)S(1)} %copy-done.29, bf16[520,2304]{1,0:T(8,128)(2,1)} %get-tuple-element.172, s32[]{:T(128)S(6)} %select_n.660), kind=kOutput, calls=%fused_computation.7 | convolution fusion | flops 1228013568 | bytes 4622340 | tf_op jit(solution)/shard_map/dot_general | solution.py:983
  350.4 3.7 fusion.2
  358.4 4.1 fusion.18
  362.5 3.2 fusion
  365.7 3.9 add_convert_fusion.2
  373.3 12.5 %delta_backward.3 = (bf16[520,768]{1,0:T(8,128)(2,1)}, f32[512,128]{1,0:T(8,128)}, f32[4,768]{1,0:T(4,128)}) custom-call(bf16[512,1024]{1,0:T(8,128)(2,1)} %get-tuple-element.147.q_ref, bf16[512,1024]{1,0:T(8,128)(2,1)} %get-tuple-element.139.k_ref, bf16[512,1024]{1,0:T(8,128)(2,1)} %get-tuple-element.148.v_ref, bf16[512,1024]{1,0:T(8,128)(2,1)} %get-tuple-element.140.w_ref, ...), custom_call_target="tpu_custom_call" | custom-call | flops 12000000000 | bytes 36000000 | tf_op jit(solution)/shard_map/delta_backward/pallas_call | solution.py:594
  385.9 2.3 collective-permute-done.32
  392.7 2.9 convolution_convert_fusion.3
  401.8 2.3 add_convert_fusion.4
  404.1 2.1 fusion.32
  410.3 2.4 collective-permute-done.36
  414.1 5.6 %collective-permute-done.37 = bf16[2,2,2,64,384]{4,3,0,1,2:T(8,128)(2,1)S(1)} collective-permute-done((bf16[2,2,2,64,384]{4,3,0,1,2:T(8,128)(2,1)S(1)}, bf16[2,2,2,64,384]{4,3,0,1,2:T(8,128)(2,1)S(1)}, u32[]{:S(2)}, u32[]{:S(2)}) %collective-permute-start.37) | collective-permute-done | bytes 393248 | tf_op jit(solution)/shard_map/ppermute | solution.py:762
  422.1 2.4 collective-permute-start.44
  427.9 2.0 collective-permute-start.41
  430.0 2.0 fusion.10
  433.6 3.1 collective-permute-done.42
  437.8 2.6 collective-permute-start.49
  444.0 2.1 multiply_reduce_fusion.3
  446.6 3.7 collective-permute-done.47
  450.3 4.2 collective-permute-done.48
  454.7 3.0 collective-permute-start.50
  462.2 8.8 %collective-permute-done.52 = bf16[64,2688]{1,0:T(8,128)(2,1)S(1)} collective-permute-done((bf16[64,2688]{1,0:T(8,128)(2,1)S(1)}, bf16[64,2688]{1,0:T(8,128)(2,1)S(1)}, u32[]{:S(2)}, u32[]{:S(2)}) %collective-permute-start.52) | collective-permute-done | bytes 344096 | tf_op jit(solution)/shard_map/ppermute | solution.py:762
  (410 shorter events, 106.1 us)
Async XLA Ops:
  7.3 118.0 %all-gather.3.cloned.1.call-start = ((), (), s32[]{:S(2)}) async-start(), calls=%async_computation.6 | async-start | bytes 11894784 | tf_op jit(solution)/shard_map/all_gather | solution.py:967
  9.3 189.5 %all-gather.5.cloned.1.call-start = ((), (), s32[]{:S(2)}) async-start(), calls=%async_computation.7 | async-start | bytes 5947392 | tf_op jit(solution)/shard_map/all_gather | solution.py:967
  10.2 12.2 %collective-permute-start.1 = (bf16[32,2176]{1,0:T(8,128)(2,1)S(1)}, bf16[32,2176]{1,0:T(8,128)(2,1)S(1)}, u32[]{:S(2)}, u32[]{:S(2)}) collective-permute-start(bf16[32,2176]{1,0:T(8,128)(2,1)S(1)} %constant_dynamic-slice_fusion.7), channel_id=1, source_target_pairs={{0,4},{1,5},{2,6},{3,7},{4,0},{5,1},{6,2},{7,3},{8,12},{9,13},{10,... | collective-permute-start | bytes 417800 | tf_op jit(solution)/shard_map/ppermute | solution.py:762
  14.3 8.6 %collective-permute-start = (bf16[32,2176]{1,0:T(8,128)(2,1)S(1)}, bf16[32,2176]{1,0:T(8,128)(2,1)S(1)}, u32[]{:S(2)}, u32[]{:S(2)}) collective-permute-start(bf16[32,2176]{1,0:T(8,128)(2,1)S(1)} %constant_dynamic-slice_fusion.7), channel_id=1, source_target_pairs={{0,2},{1,3},{2,0},{3,1},{4,6},{5,7},{6,4},{7,5},{8,10},{9,11},{10,... | collective-permute-start | bytes 417800 | tf_op jit(solution)/shard_map/ppermute | solution.py:762
  16.0 14.0 %collective-permute-start.4 = (s32[8]{0:T(128)S(1)}, s32[8]{0:T(128)S(1)}, u32[]{:S(2)}, u32[]{:S(2)}) collective-permute-start(s32[8]{0:T(128)S(1)} %slice.189), channel_id=1, source_target_pairs={{0,1},{1,2},{2,3},{3,4},{4,5},{5,6},{6,7},{8,9},{9,10},{10,11},{11... | collective-permute-start | bytes 104 | tf_op jit(solution)/shard_map/ppermute | solution.py:1001
  20.1 9.9 %collective-permute-start.3 = (bf16[8,1024]{1,0:T(8,128)(2,1)S(1)}, bf16[8,1024]{1,0:T(8,128)(2,1)S(1)}, u32[]{:S(2)}, u32[]{:S(2)}) collective-permute-start(bf16[8,1024]{1,0:T(8,128)(2,1)S(1)} %slice.188), channel_id=1, source_target_pairs={{0,1},{1,2},{2,3},{3,4},{4,5},{5,6},{6,7},{8,9},{9,10},{10,11},{11... | collective-permute-start | bytes 49160 | tf_op jit(solution)/shard_map/ppermute | solution.py:1001
  22.4 7.4 %collective-permute-start.2 = (bf16[32,2176]{1,0:T(8,128)(2,1)S(1)}, bf16[32,2176]{1,0:T(8,128)(2,1)S(1)}, u32[]{:S(2)}, u32[]{:S(2)}) collective-permute-start(bf16[32,2176]{1,0:T(8,128)(2,1)S(1)} %collective-permute-done.1), channel_id=1, source_target_pairs={{0,2},{1,3},{2,0},{3,1},{4,6},{5,7},{6,4},{7,5},{8,10},{9,11},{10,... | collective-permute-start | bytes 417800 | tf_op jit(solution)/shard_map/ppermute | solution.py:762
  30.0 10.1 %collective-permute-start.5 = (bf16[4,32,2176]{2,1,0:T(8,128)(2,1)S(1)}, bf16[4,32,2176]{2,1,0:T(8,128)(2,1)S(1)}, u32[]{:S(2)}, u32[]{:S(2)}) collective-permute-start(bf16[4,32,2176]{2,1,0:T(8,128)(2,1)S(1)} %pad_maximum_fusion.4.refs_0_), channel_id=1, source_target_pairs={{0,1},{1,0},{2,3},{3,2},{4,5},{5,4},{6,7},{7,6},{8,9},{9,8},{10,11... | collective-permute-start | bytes 1671176 | tf_op jit(solution)/shard_map/ppermute | solution.py:762
  31.5 12.8 %collective-permute-start.6 = (bf16[4,32,2176]{2,1,0:T(8,128)(2,1)S(1)}, bf16[4,32,2176]{2,1,0:T(8,128)(2,1)}, u32[]{:S(2)}, u32[]{:S(2)}) collective-permute-start(bf16[4,32,2176]{2,1,0:T(8,128)(2,1)S(1)} %pad_maximum_fusion.4.refs_0_), channel_id=1, source_target_pairs={{0,16},{8,24},{16,0},{24,8},{1,17},{9,25},{17,1},{25,9},{2,18},{10... | collective-permute-start | bytes 1671176 | tf_op jit(solution)/shard_map/ppermute | solution.py:762
  33.0 11.3 %collective-permute-start.7 = (bf16[4,32,2176]{2,1,0:T(8,128)(2,1)S(1)}, bf16[4,32,2176]{2,1,0:T(8,128)(2,1)}, u32[]{:S(2)}, u32[]{:S(2)}) collective-permute-start(bf16[4,32,2176]{2,1,0:T(8,128)(2,1)S(1)} %pad_maximum_fusion.4.refs_0_), channel_id=1, source_target_pairs={{0,8},{8,0},{16,24},{24,16},{1,9},{9,1},{17,25},{25,17},{2,10},{10... | collective-permute-start | bytes 1671176 | tf_op jit(solution)/shard_map/ppermute | solution.py:762
  44.3 19.5 %collective-permute-start.8 = (bf16[4,32,2176]{2,1,0:T(8,128)(2,1)S(1)}, bf16[4,32,2176]{2,1,0:T(8,128)(2,1)}, u32[]{:S(2)}, u32[]{:S(2)}) collective-permute-start(bf16[4,32,2176]{2,1,0:T(8,128)(2,1)S(1)} %collective-permute-done.5.refs_1_), channel_id=1, source_target_pairs={{0,16},{8,24},{16,0},{24,8},{1,17},{9,25},{17,1},{25,9},{2,18},{10... | collective-permute-start | bytes 1671176 | tf_op jit(solution)/shard_map/ppermute | solution.py:762
  46.5 17.2 %collective-permute-start.10 = (bf16[4,32,2176]{2,1,0:T(8,128)(2,1)}, bf16[4,32,2176]{2,1,0:T(8,128)(2,1)S(1)}, u32[]{:S(2)}, u32[]{:S(2)}) collective-permute-start(bf16[4,32,2176]{2,1,0:T(8,128)(2,1)} %collective-permute-done.6.refs_2_), channel_id=1, source_target_pairs={{0,8},{8,0},{16,24},{24,16},{1,9},{9,1},{17,25},{25,17},{2,10},{10... | collective-permute-start | bytes 1671176 | tf_op jit(solution)/shard_map/ppermute | solution.py:762
  46.5 18.1 %collective-permute-start.9 = (bf16[4,32,2176]{2,1,0:T(8,128)(2,1)S(1)}, bf16[4,32,2176]{2,1,0:T(8,128)(2,1)S(1)}, u32[]{:S(2)}, u32[]{:S(2)}) collective-permute-start(bf16[4,32,2176]{2,1,0:T(8,128)(2,1)S(1)} %collective-permute-done.5.refs_1_), channel_id=1, source_target_pairs={{0,8},{8,0},{16,24},{24,16},{1,9},{9,1},{17,25},{25,17},{2,10},{10... | collective-permute-start | bytes 1671176 | tf_op jit(solution)/shard_map/ppermute | solution.py:762
  48.4 30.7 %collective-permute-start.13 = (bf16[32,3072]{1,0:T(8,128)(2,1)}, bf16[32,3072]{1,0:T(8,128)(2,1)}, u32[]{:S(2)}, u32[]{:S(2)}) collective-permute-start(bf16[32,3072]{1,0:T(8,128)(2,1)} %constant_dynamic-slice_fusion.6), channel_id=1, source_target_pairs={{0,4},{1,5},{2,6},{3,7},{4,0},{5,1},{6,2},{7,3},{8,12},{9,13},{10,... | collective-permute-start | bytes 589832 | tf_op jit(solution)/shard_map/ppermute | solution.py:762
  51.1 36.3 %collective-permute-start.12 = (bf16[32,3072]{1,0:T(8,128)(2,1)}, bf16[32,3072]{1,0:T(8,128)(2,1)}, u32[]{:S(2)}, u32[]{:S(2)}) collective-permute-start(bf16[32,3072]{1,0:T(8,128)(2,1)} %constant_dynamic-slice_fusion.6), channel_id=1, source_target_pairs={{0,2},{1,3},{2,0},{3,1},{4,6},{5,7},{6,4},{7,5},{8,10},{9,11},{10,... | collective-permute-start | bytes 589832 | tf_op jit(solution)/shard_map/ppermute | solution.py:762
  65.4 2.3 collective-permute-start.11
  79.2 19.6 %collective-permute-start.14 = (bf16[32,3072]{1,0:T(8,128)(2,1)}, bf16[32,3072]{1,0:T(8,128)(2,1)S(1)}, u32[]{:S(2)}, u32[]{:S(2)}) collective-permute-start(bf16[32,3072]{1,0:T(8,128)(2,1)} %collective-permute-done.13), channel_id=1, source_target_pairs={{0,2},{1,3},{2,0},{3,1},{4,6},{5,7},{6,4},{7,5},{8,10},{9,11},{10,... | collective-permute-start | bytes 589832 | tf_op jit(solution)/shard_map/ppermute | solution.py:762
  99.9 24.5 %collective-permute-start.15 = (bf16[4,32,3072]{2,1,0:T(8,128)(2,1)S(1)}, bf16[4,32,3072]{2,1,0:T(8,128)(2,1)S(1)}, u32[]{:S(2)}, u32[]{:S(2)}) collective-permute-start(bf16[4,32,3072]{2,1,0:T(8,128)(2,1)S(1)} %pad_maximum_fusion.2.refs_0_), channel_id=1, source_target_pairs={{0,1},{1,0},{2,3},{3,2},{4,5},{5,4},{6,7},{7,6},{8,9},{9,8},{10,11... | collective-permute-start | bytes 2359304 | tf_op jit(solution)/shard_map/ppermute | solution.py:762
  100.5 23.9 %collective-permute-start.16 = (bf16[4,32,3072]{2,1,0:T(8,128)(2,1)S(1)}, bf16[4,32,3072]{2,1,0:T(8,128)(2,1)S(1)}, u32[]{:S(2)}, u32[]{:S(2)}) collective-permute-start(bf16[4,32,3072]{2,1,0:T(8,128)(2,1)S(1)} %pad_maximum_fusion.2.refs_0_), channel_id=1, source_target_pairs={{0,16},{8,24},{16,0},{24,8},{1,17},{9,25},{17,1},{25,9},{2,18},{10... | collective-permute-start | bytes 2359304 | tf_op jit(solution)/shard_map/ppermute | solution.py:762
  126.0 23.2 %all-to-all-start = ((bf16[8,128,256]{2,1,0:T(8,128)(2,1)}), bf16[8,128,256]{2,1,0:T(8,128)(2,1)S(1)}, u32[]{:S(2)}, u32[]{:S(2)}) async-start(bf16[8,128,256]{2,1,0:T(8,128)(2,1)} %get-tuple-element.132), calls=%async_computation | async-start | bytes 1048576 | tf_op jit(solution)/shard_map/all_to_all | solution.py:1017
  131.5 21.2 %collective-permute-start.17 = (bf16[4,32,3072]{2,1,0:T(8,128)(2,1)S(1)}, bf16[4,32,3072]{2,1,0:T(8,128)(2,1)}, u32[]{:S(2)}, u32[]{:S(2)}) collective-permute-start(bf16[4,32,3072]{2,1,0:T(8,128)(2,1)S(1)} %collective-permute-done.15.refs_1_), channel_id=1, source_target_pairs={{0,16},{8,24},{16,0},{24,8},{1,17},{9,25},{17,1},{25,9},{2,18},{10... | collective-permute-start | bytes 2359304 | tf_op jit(solution)/shard_map/ppermute | solution.py:762
  131.9 27.0 %collective-permute-start.20 = (bf16[4,32,3072]{2,1,0:T(8,128)(2,1)}, bf16[4,32,3072]{2,1,0:T(8,128)(2,1)}, u32[]{:S(2)}, u32[]{:S(2)}) collective-permute-start(bf16[4,32,3072]{2,1,0:T(8,128)(2,1)} %copy-done.8), channel_id=1, source_target_pairs={{0,8},{8,0},{16,24},{24,16},{1,9},{9,1},{17,25},{25,17},{2,10},{10... | collective-permute-start | bytes 2359304 | tf_op jit(solution)/shard_map/ppermute | solution.py:762
  131.9 27.0 %collective-permute-start.19 = (bf16[4,32,3072]{2,1,0:T(8,128)(2,1)S(1)}, bf16[4,32,3072]{2,1,0:T(8,128)(2,1)}, u32[]{:S(2)}, u32[]{:S(2)}) collective-permute-start(bf16[4,32,3072]{2,1,0:T(8,128)(2,1)S(1)} %collective-permute-done.15.refs_1_), channel_id=1, source_target_pairs={{0,8},{8,0},{16,24},{24,16},{1,9},{9,1},{17,25},{25,17},{2,10},{10... | collective-permute-start | bytes 2359304 | tf_op jit(solution)/shard_map/ppermute | solution.py:762
  132.4 26.5 %collective-permute-start.18 = (bf16[4,32,3072]{2,1,0:T(8,128)(2,1)S(1)}, bf16[4,32,3072]{2,1,0:T(8,128)(2,1)}, u32[]{:S(2)}, u32[]{:S(2)}) collective-permute-start(bf16[4,32,3072]{2,1,0:T(8,128)(2,1)S(1)} %pad_maximum_fusion.2.refs_0_), channel_id=1, source_target_pairs={{0,8},{8,0},{16,24},{24,16},{1,9},{9,1},{17,25},{25,17},{2,10},{10... | collective-permute-start | bytes 2359304 | tf_op jit(solution)/shard_map/ppermute | solution.py:762
  152.7 6.2 %collective-permute-start.21 = (bf16[4,32,3072]{2,1,0:T(8,128)(2,1)}, bf16[4,32,3072]{2,1,0:T(8,128)(2,1)}, u32[]{:S(2)}, u32[]{:S(2)}) collective-permute-start(bf16[4,32,3072]{2,1,0:T(8,128)(2,1)} %collective-permute-done.17.refs_3_), channel_id=1, source_target_pairs={{0,8},{8,0},{16,24},{24,16},{1,9},{9,1},{17,25},{25,17},{2,10},{10... | collective-permute-start | bytes 2359304 | tf_op jit(solution)/shard_map/ppermute | solution.py:762
  154.0 18.3 %all-to-all-start.1 = ((bf16[8,128,128]{2,1,0:T(8,128)(2,1)}), bf16[8,128,128]{2,1,0:T(8,128)(2,1)S(1)}, u32[]{:S(2)}, u32[]{:S(2)}) async-start(bf16[8,128,128]{2,1,0:T(8,128)(2,1)} %state_prefix.1), calls=%async_computation.1 | async-start | bytes 524288 | tf_op jit(solution)/shard_map/all_to_all | solution.py:1017
  158.4 234.3 %reduce-scatter.3.cloned.1.call-start = ((), (), s32[]{:S(2)}) async-start(), calls=%async_computation.8 | async-start | bytes 6488064 | tf_op jit(solution)/shard_map/reduce_scatter | solution.py:971
  233.5 9.8 %collective-permute-start.22 = (bf16[1024,2816]{1,0:T(8,128)(2,1)}, bf16[1024,2816]{1,0:T(8,128)(2,1)}, u32[]{:S(2)}, u32[]{:S(2)}) collective-permute-start(bf16[1024,2816]{1,0:T(8,128)(2,1)} %convolution_convert_fusion), channel_id=1, source_target_pairs={{0,8},{8,0},{16,24},{24,16},{1,9},{9,1},{17,25},{25,17},{2,10},{10... | collective-permute-start | bytes 17301512 | tf_op jit(solution)/shard_map/ppermute | solution.py:762
  250.3 25.1 %collective-permute-start.23 = (bf16[2816,512]{1,0:T(8,128)(2,1)}, bf16[2816,512]{1,0:T(8,128)(2,1)}, u32[]{:S(2)}, u32[]{:S(2)}) collective-permute-start(bf16[2816,512]{1,0:T(8,128)(2,1)} %convolution_convert_fusion.1), channel_id=1, source_target_pairs={{0,8},{8,0},{16,24},{24,16},{1,9},{9,1},{17,25},{25,17},{2,10},{10... | collective-permute-start | bytes 8650760 | tf_op jit(solution)/shard_map/ppermute | solution.py:762
  275.2 36.6 %collective-permute-start.24 = (bf16[1024,1024]{1,0:T(8,128)(2,1)}, bf16[1024,1024]{1,0:T(8,128)(2,1)}, u32[]{:S(2)}, u32[]{:S(2)}) collective-permute-start(bf16[1024,1024]{1,0:T(8,128)(2,1)} %get-tuple-element.309), channel_id=1, source_target_pairs={{0,8},{8,0},{16,24},{24,16},{1,9},{9,1},{17,25},{25,17},{2,10},{10... | collective-permute-start | bytes 6291464 | tf_op jit(solution)/shard_map/ppermute | solution.py:762
  282.6 38.2 %collective-permute-start.25 = (bf16[2,2,2,176,512]{4,3,2,1,0:T(8,128)(2,1)}, bf16[2,2,2,176,512]{4,3,2,1,0:T(8,128)(2,1)}, u32[]{:S(2)}, u32[]{:S(2)}) collective-permute-start(bf16[2,2,2,176,512]{4,3,2,1,0:T(8,128)(2,1)} %dynamic-slice_bitcast_fusion.1), channel_id=1, source_target_pairs={{0,16},{8,24},{16,0},{24,8},{1,17},{9,25},{17,1},{25,9},{2,18},{10... | collective-permute-start | bytes 4325384 | tf_op jit(solution)/shard_map/ppermute | solution.py:762
  283.9 20.9 %all-to-all-start.2 = ((bf16[8,128,128]{2,1,0:T(8,128)(2,1)}), bf16[8,128,128]{2,1,0:T(8,128)(2,1)S(1)}, u32[]{:S(2)}, u32[]{:S(2)}) async-start(bf16[8,128,128]{2,1,0:T(8,128)(2,1)} %get-tuple-element.158), calls=%async_computation.2 | async-start | bytes 524288 | tf_op jit(solution)/shard_map/all_to_all | solution.py:1017
  308.3 12.6 %all-to-all-start.3 = ((bf16[8,128,128]{2,1,0:T(8,128)(2,1)}), bf16[8,128,128]{2,1,0:T(8,128)(2,1)S(1)}, u32[]{:S(2)}, u32[]{:S(2)}) async-start(bf16[8,128,128]{2,1,0:T(8,128)(2,1)} %state_suffix.1), calls=%async_computation.3 | async-start | bytes 524288 | tf_op jit(solution)/shard_map/all_to_all | solution.py:1017
  311.7 150.2 %reduce-scatter.5.cloned.1.call-start = ((), (), s32[]{:S(2)}) async-start(), calls=%async_computation.9 | async-start | bytes 1622016 | tf_op jit(solution)/shard_map/reduce_scatter | solution.py:971
  321.6 22.3 %collective-permute-start.27 = (bf16[2,2,128,512]{3,2,1,0:T(8,128)(2,1)S(1)}, bf16[2,2,128,512]{3,2,1,0:T(8,128)(2,1)S(1)}, u32[]{:S(2)}, u32[]{:S(2)}) collective-permute-start(bf16[2,2,128,512]{3,2,1,0:T(8,128)(2,1)S(1)} %dynamic-slice_bitcast_fusion.4), channel_id=1, source_target_pairs={{0,1},{1,0},{2,3},{3,2},{4,5},{5,4},{6,7},{7,6},{8,9},{9,8},{10,11... | collective-permute-start | bytes 1572872 | tf_op jit(solution)/shard_map/ppermute | solution.py:762
  323.1 20.8 %collective-permute-start.26 = (bf16[2,2,2,64,512]{4,3,2,1,0:T(8,128)(2,1)S(1)}, bf16[2,2,2,64,512]{4,3,2,1,0:T(8,128)(2,1)S(1)}, u32[]{:S(2)}, u32[]{:S(2)}) collective-permute-start(bf16[2,2,2,64,512]{4,3,2,1,0:T(8,128)(2,1)S(1)} %dynamic-slice_bitcast_fusion.5), channel_id=1, source_target_pairs={{0,16},{8,24},{16,0},{24,8},{1,17},{9,25},{17,1},{25,9},{2,18},{10... | collective-permute-start | bytes 1572872 | tf_op jit(solution)/shard_map/ppermute | solution.py:762
  349.1 16.6 %collective-permute-start.28 = (bf16[1024,1152]{1,0:T(8,128)(2,1)}, bf16[1024,1152]{1,0:T(8,128)(2,1)}, u32[]{:S(2)}, u32[]{:S(2)}) collective-permute-start(bf16[1024,1152]{1,0:T(8,128)(2,1)} %convolution_convert_fusion.2), channel_id=1, source_target_pairs={{0,8},{8,0},{16,24},{24,16},{1,9},{9,1},{17,25},{25,17},{2,10},{10... | collective-permute-start | bytes 7077896 | tf_op jit(solution)/shard_map/ppermute | solution.py:762
  356.1 13.7 %collective-permute-start.30 = (bf16[2,2,64,512]{3,2,1,0:T(8,128)(2,1)S(1)}, bf16[2,2,64,512]{3,2,1,0:T(8,128)(2,1)S(1)}, u32[]{:S(2)}, u32[]{:S(2)}) collective-permute-start(bf16[2,2,64,512]{3,2,1,0:T(8,128)(2,1)S(1)} %dynamic-slice_bitcast_fusion.10), channel_id=1, source_target_pairs={{0,16},{8,24},{16,0},{24,8},{1,17},{9,25},{17,1},{25,9},{2,18},{10... | collective-permute-start | bytes 786440 | tf_op jit(solution)/shard_map/ppermute | solution.py:762
  357.7 12.2 %collective-permute-start.29 = (bf16[2,2,64,512]{3,2,1,0:T(8,128)(2,1)S(1)}, bf16[2,2,64,512]{3,2,1,0:T(8,128)(2,1)S(1)}, u32[]{:S(2)}, u32[]{:S(2)}) collective-permute-start(bf16[2,2,64,512]{3,2,1,0:T(8,128)(2,1)S(1)} %dynamic-slice_bitcast_fusion.11), channel_id=1, source_target_pairs={{0,1},{1,0},{2,3},{3,2},{4,5},{5,4},{6,7},{7,6},{8,9},{9,8},{10,11... | collective-permute-start | bytes 786440 | tf_op jit(solution)/shard_map/ppermute | solution.py:762
  370.3 15.6 %collective-permute-start.31 = (bf16[2,64,1024]{2,1,0:T(8,128)(2,1)S(1)}, bf16[2,64,1024]{2,1,0:T(8,128)(2,1)S(1)}, u32[]{:S(2)}, u32[]{:S(2)}) collective-permute-start(bf16[2,64,1024]{2,1,0:T(8,128)(2,1)S(1)} %dynamic-slice_bitcast_fusion.9), channel_id=1, source_target_pairs={{0,2},{1,3},{2,0},{3,1},{4,6},{5,7},{6,4},{7,5},{8,10},{9,11},{10,... | collective-permute-start | bytes 786440 | tf_op jit(solution)/shard_map/ppermute | solution.py:762
  371.1 14.8 %collective-permute-start.33 = (bf16[2,2,128,512]{3,2,1,0:T(8,128)(2,1)S(1)}, bf16[2,2,128,512]{3,2,1,0:T(8,128)(2,1)S(1)}, u32[]{:S(2)}, u32[]{:S(2)}) collective-permute-start(bf16[2,2,128,512]{3,2,1,0:T(8,128)(2,1)S(1)} %dynamic-slice_bitcast_fusion.3), channel_id=1, source_target_pairs={{0,1},{1,0},{2,3},{3,2},{4,5},{5,4},{6,7},{7,6},{8,9},{9,8},{10,11... | collective-permute-start | bytes 1572872 | tf_op jit(solution)/shard_map/ppermute | solution.py:762
  371.5 16.6 %collective-permute-start.32 = (bf16[2,2,2,64,640]{4,3,2,1,0:T(8,128)(2,1)S(1)}, bf16[2,2,2,64,640]{4,3,2,1,0:T(8,128)(2,1)S(1)}, u32[]{:S(2)}, u32[]{:S(2)}) collective-permute-start(bf16[2,2,2,64,640]{4,3,2,1,0:T(8,128)(2,1)S(1)} %dynamic-slice_bitcast_fusion.2), channel_id=1, source_target_pairs={{0,16},{8,24},{16,0},{24,8},{1,17},{9,25},{17,1},{25,9},{2,18},{10... | collective-permute-start | bytes 1966088 | tf_op jit(solution)/shard_map/ppermute | solution.py:762
  389.0 25.1 %collective-permute-start.39 = (bf16[2,2,64,512]{3,2,1,0:T(8,128)(2,1)}, bf16[2,2,64,512]{3,2,1,0:T(8,128)(2,1)}, u32[]{:S(2)}, u32[]{:S(2)}) collective-permute-start(bf16[2,2,64,512]{3,2,1,0:T(8,128)(2,1)} %dynamic-slice_bitcast_fusion.8), channel_id=1, source_target_pairs={{0,16},{8,24},{16,0},{24,8},{1,17},{9,25},{17,1},{25,9},{2,18},{10... | collective-permute-start | bytes 786440 | tf_op jit(solution)/shard_map/ppermute | solution.py:762
  391.6 22.4 %collective-permute-start.38 = (bf16[2,2,64,640]{3,2,1,0:T(8,128)(2,1)}, bf16[2,2,64,640]{3,2,1,0:T(8,128)(2,1)S(1)}, u32[]{:S(2)}, u32[]{:S(2)}) collective-permute-start(bf16[2,2,64,640]{3,2,1,0:T(8,128)(2,1)} %dynamic-slice_bitcast_fusion.6), channel_id=1, source_target_pairs={{0,1},{1,0},{2,3},{3,2},{4,5},{5,4},{6,7},{7,6},{8,9},{9,8},{10,11... | collective-permute-start | bytes 983048 | tf_op jit(solution)/shard_map/ppermute | solution.py:762
  395.6 6.2 %collective-permute-start.34 = (bf16[1024,384]{1,0:T(8,128)(2,1)}, bf16[1024,384]{1,0:T(8,128)(2,1)}, u32[]{:S(2)}, u32[]{:S(2)}) collective-permute-start(bf16[1024,384]{1,0:T(8,128)(2,1)} %convolution_convert_fusion.3), channel_id=1, source_target_pairs={{0,8},{8,0},{16,24},{24,16},{1,9},{9,1},{17,25},{25,17},{2,10},{10... | collective-permute-start | bytes 2359304 | tf_op jit(solution)/shard_map/ppermute | solution.py:762
  399.5 1.7 collective-permute-start.35
  401.4 12.7 %collective-permute-start.40 = (bf16[2,2,2,64,128]{4,3,0,1,2:T(8,128)(2,1)S(1)}, bf16[2,2,2,64,128]{4,3,0,1,2:T(8,128)(2,1)S(1)}, u32[]{:S(2)}, u32[]{:S(2)}) collective-permute-start(bf16[2,2,2,64,128]{4,3,0,1,2:T(8,128)(2,1)S(1)} %bitcast.262), channel_id=1, source_target_pairs={{0,16},{8,24},{16,0},{24,8},{1,17},{9,25},{17,1},{25,9},{2,18},{10... | collective-permute-start | bytes 393224 | tf_op jit(solution)/shard_map/ppermute | solution.py:762
  406.9 5.8 %collective-permute-start.36 = (bf16[8,1024]{1,0:T(8,128)(2,1)S(1)}, bf16[8,1024]{1,0:T(8,128)(2,1)S(1)}, u32[]{:S(2)}, u32[]{:S(2)}) collective-permute-start(bf16[8,1024]{1,0:T(8,128)(2,1)S(1)} %slice.353), channel_id=1, source_target_pairs={{1,0},{2,1},{3,2},{4,3},{5,4},{6,5},{7,6},{9,8},{10,9},{11,10},{12... | collective-permute-start | bytes 49160 | tf_op jit(solution)/shard_map/ppermute | solution.py:1001
  408.5 11.2 %collective-permute-start.37 = (bf16[2,2,2,64,384]{4,3,0,1,2:T(8,128)(2,1)S(1)}, bf16[2,2,2,64,384]{4,3,0,1,2:T(8,128)(2,1)S(1)}, u32[]{:S(2)}, u32[]{:S(2)}) collective-permute-start(bf16[2,2,2,64,384]{4,3,0,1,2:T(8,128)(2,1)S(1)} %bitcast.251), channel_id=1, source_target_pairs={{0,16},{8,24},{16,0},{24,8},{1,17},{9,25},{17,1},{25,9},{2,18},{10... | collective-permute-start | bytes 1179656 | tf_op jit(solution)/shard_map/ppermute | solution.py:762
  420.3 17.4 %collective-permute-start.45 = (bf16[128,2816]{1,0:T(8,128)(2,1)S(1)}, bf16[128,2816]{1,0:T(8,128)(2,1)S(1)}, u32[]{:S(2)}, u32[]{:S(2)}) collective-permute-start(bf16[128,2816]{1,0:T(8,128)(2,1)S(1)} %copy-done.49), channel_id=1, source_target_pairs={{0,16},{8,24},{16,0},{24,8},{1,17},{9,25},{17,1},{25,9},{2,18},{10... | collective-permute-start | bytes 2162696 | tf_op jit(solution)/shard_map/ppermute | solution.py:762
  422.1 10.0 %collective-permute-start.44 = (bf16[2,2,64,128]{3,2,0,1:T(8,128)(2,1)S(1)}, bf16[2,2,64,128]{3,2,0,1:T(8,128)(2,1)S(1)}, u32[]{:S(2)}, u32[]{:S(2)}) collective-permute-start(bf16[2,2,64,128]{3,2,0,1:T(8,128)(2,1)S(1)} %dynamic-slice_bitcast_fusion.16), channel_id=1, source_target_pairs={{0,1},{1,0},{2,3},{3,2},{4,5},{5,4},{6,7},{7,6},{8,9},{9,8},{10,11... | collective-permute-start | bytes 196616 | tf_op jit(solution)/shard_map/ppermute | solution.py:762
  424.5 7.5 %collective-permute-start.43 = (bf16[64,1024]{1,0:T(8,128)(2,1)S(1)}, bf16[64,1024]{1,0:T(8,128)(2,1)S(1)}, u32[]{:S(2)}, u32[]{:S(2)}) collective-permute-start(bf16[64,1024]{1,0:T(8,128)(2,1)S(1)} %dynamic-slice_bitcast_fusion.14), channel_id=1, source_target_pairs={{0,4},{1,5},{2,6},{3,7},{4,0},{5,1},{6,2},{7,3},{8,12},{9,13},{10,... | collective-permute-start | bytes 393224 | tf_op jit(solution)/shard_map/ppermute | solution.py:762
  427.6 9.1 %collective-permute-start.42 = (bf16[2,64,1152]{2,1,0:T(8,128)(2,1)S(1)}, bf16[2,64,1152]{2,1,0:T(8,128)(2,1)S(1)}, u32[]{:S(2)}, u32[]{:S(2)}) collective-permute-start(bf16[2,64,1152]{2,1,0:T(8,128)(2,1)S(1)} %dynamic-slice_bitcast_fusion.7), channel_id=1, source_target_pairs={{0,2},{1,3},{2,0},{3,1},{4,6},{5,7},{6,4},{7,5},{8,10},{9,11},{10,... | collective-permute-start | bytes 884744 | tf_op jit(solution)/shard_map/ppermute | solution.py:762
  427.9 5.7 %collective-permute-start.41 = (bf16[2,2,64,384]{3,2,0,1:T(8,128)(2,1)S(1)}, bf16[2,2,64,384]{3,2,0,1:T(8,128)(2,1)S(1)}, u32[]{:S(2)}, u32[]{:S(2)}) collective-permute-start(bf16[2,2,64,384]{3,2,0,1:T(8,128)(2,1)S(1)} %dynamic-slice_bitcast_fusion.12), channel_id=1, source_target_pairs={{0,1},{1,0},{2,3},{3,2},{4,5},{5,4},{6,7},{7,6},{8,9},{9,8},{10,11... | collective-permute-start | bytes 589832 | tf_op jit(solution)/shard_map/ppermute | solution.py:762
  437.8 8.8 %collective-permute-start.49 = (bf16[2,64,128]{2,1,0:T(8,128)(2,1)S(1)}, bf16[2,64,128]{2,1,0:T(8,128)(2,1)S(1)}, u32[]{:S(2)}, u32[]{:S(2)}) collective-permute-start(bf16[2,64,128]{2,1,0:T(8,128)(2,1)S(1)} %dynamic-slice_bitcast_fusion.18), channel_id=1, source_target_pairs={{0,2},{1,3},{2,0},{3,1},{4,6},{5,7},{6,4},{7,5},{8,10},{9,11},{10,... | collective-permute-start | bytes 98312 | tf_op jit(solution)/shard_map/ppermute | solution.py:762
  440.5 3.4 collective-permute-start.46
  440.7 13.8 %collective-permute-start.48 = (bf16[64,1152]{1,0:T(8,128)(2,1)S(1)}, bf16[64,1152]{1,0:T(8,128)(2,1)S(1)}, u32[]{:S(2)}, u32[]{:S(2)}) collective-permute-start(bf16[64,1152]{1,0:T(8,128)(2,1)S(1)} %dynamic-slice_bitcast_fusion.13), channel_id=1, source_target_pairs={{0,4},{1,5},{2,6},{3,7},{4,0},{5,1},{6,2},{7,3},{8,12},{9,13},{10,... | collective-permute-start | bytes 442376 | tf_op jit(solution)/shard_map/ppermute | solution.py:762
  442.4 7.9 %collective-permute-start.47 = (bf16[2,64,384]{2,1,0:T(8,128)(2,1)S(1)}, bf16[2,64,384]{2,1,0:T(8,128)(2,1)S(1)}, u32[]{:S(2)}, u32[]{:S(2)}) collective-permute-start(bf16[2,64,384]{2,1,0:T(8,128)(2,1)S(1)} %dynamic-slice_bitcast_fusion.15), channel_id=1, source_target_pairs={{0,2},{1,3},{2,0},{3,1},{4,6},{5,7},{6,4},{7,5},{8,10},{9,11},{10,... | collective-permute-start | bytes 294920 | tf_op jit(solution)/shard_map/ppermute | solution.py:762
  454.6 4.7 collective-permute-start.51
  454.7 5.1 %collective-permute-start.50 = (bf16[64,384]{1,0:T(8,128)(2,1)S(1)}, bf16[64,384]{1,0:T(8,128)(2,1)S(1)}, u32[]{:S(2)}, u32[]{:S(2)}) collective-permute-start(bf16[64,384]{1,0:T(8,128)(2,1)S(1)} %dynamic-slice_bitcast_fusion.17), channel_id=1, source_target_pairs={{0,4},{1,5},{2,6},{3,7},{4,0},{5,1},{6,2},{7,3},{8,12},{9,13},{10,... | collective-permute-start | bytes 147464 | tf_op jit(solution)/shard_map/ppermute | solution.py:762
  459.9 11.1 %collective-permute-start.52 = (bf16[64,2688]{1,0:T(8,128)(2,1)S(1)}, bf16[64,2688]{1,0:T(8,128)(2,1)S(1)}, u32[]{:S(2)}, u32[]{:S(2)}) collective-permute-start(bf16[64,2688]{1,0:T(8,128)(2,1)S(1)} %pad_maximum_fusion.6), channel_id=1, source_target_pairs={{0,16},{8,24},{16,0},{24,8},{1,17},{9,25},{17,1},{25,9},{2,18},{10... | collective-permute-start | bytes 1032200 | tf_op jit(solution)/shard_map/ppermute | solution.py:762
  461.9 11.0 %collective-permute-start.54 = (bf16[176,512]{1,0:T(8,128)(2,1)}, bf16[176,512]{1,0:T(8,128)(2,1)S(1)}, u32[]{:S(2)}, u32[]{:S(2)}) collective-permute-start(bf16[176,512]{1,0:T(8,128)(2,1)} %reduce-scatter.5.cloned.1.call-done), channel_id=1, source_target_pairs={{0,16},{8,24},{16,0},{24,8},{1,17},{9,25},{17,1},{25,9},{2,18},{10... | collective-permute-start | bytes 540680 | tf_op jit(solution)/shard_map/ppermute | solution.py:762
  471.1 6.6 %collective-permute-start.53 = (bf16[128,2688]{1,0:T(8,128)(2,1)S(1)}, bf16[128,2688]{1,0:T(8,128)(2,1)S(1)}, u32[]{:S(2)}, u32[]{:S(2)}) collective-permute-start(bf16[128,2688]{1,0:T(8,128)(2,1)S(1)} %maximum_select_fusion.1), channel_id=1, source_target_pairs={{0,8},{8,0},{16,24},{24,16},{1,9},{9,1},{17,25},{25,17},{2,10},{10... | collective-permute-start | bytes 2064392 | tf_op jit(solution)/shard_map/ppermute | solution.py:762
  474.0 2.4 collective-permute-start.55
  (78 other events, 772.9 us)
Sparse Core Ops, SparseCore 0:
  11.5 104.8 all-gather.2
  126.1 72.5 all-gather.4
  250.4 127.9 reduce-scatter.2
  382.3 71.9 reduce-scatter.4
